TPU v7x, 32 devices: a whole 2x2x4 slice. The times are simulated.
32 devices in a mesh: dp: 8 (over z, y), head: 4 (over x, core).
Axes of the slice: x: 2, y: 2, z: 4, core: 2. Of those that a mesh axis runs over, the one named last changes fastest.
Arguments:
- q_latent: bfloat16 [768, 65536], P('dp', 'head'), may hold values from -64 to 64
- q_rope: bfloat16 [768, 8192], P('dp', 'head'), may hold values from -6 to 6
- cache_latent: bfloat16 [32, 512, 512], P('dp'), may hold values from -6 to 6
- cache_rope: bfloat16 [32, 64, 512], P('dp'), may hold values from -6 to 6
- lengths: int32 [32], P('dp'), may hold values from 128 to 512
- loads: int32 [8], replicated, may hold values from 1 to 4
- owner_rank: int32 [64], P('dp'), may hold values from 0 to 7, as said below
- owner_pick: int32 [64], P('dp'), may hold values from 0 to 839
- w_uv: bfloat16 [128, 512, 128], P('head'), may hold values from -0.25 to 0.25
- w_out: bfloat16 [16384, 7168], P('head', 'dp'), may hold values from -0.046875 to 0.046875
Outputs:
- layer_out: bfloat16 [768, 7168], P('head', 'dp')
Inputs may be any that keep to these rules, and one draw needn't show every extreme that they name: `owner_rank`: the 8 bundles of one dp rank name distinct owner ranks, and in every draw some rank is named by every dp rank.
All inputs are finite; a program needn't handle non-finite values.
Results may differ from a plain program's by a relative error of at most 0.0064.
Values may be sent and summed in bfloat16 or wider, within the bound.
No kernel may reach another device: no remote copies, remote signals or barrier semaphores. Data moves between devices by JAX's collectives and lax.ppermute only.
A program may use at most 128 MiB of HBM per device.

v0:
```python
import functools
import math

import jax
import jax.numpy as jnp
from jax import lax
from jax.experimental import pallas as pl
from jax.experimental.pallas import tpu as pltpu
from jax.sharding import PartitionSpec as P


ROPE = 64
VD = 128


def ring_order(size):
    fast = 1 << (max(size.bit_length() - 1, 0) // 2)
    slow = size // fast
    if fast == 1 or slow % 2:
        return list(range(size))
    cells = [(z, 0) for z in range(slow)]
    for step, z in enumerate(range(slow - 1, -1, -1)):
        ys = range(1, fast) if step % 2 == 0 else range(fast - 1, 0, -1)
        cells += [(z, y) for y in ys]
    return [z * fast + y for z, y in cells]


def ring_fits(ranks, heads):
    if ranks % 2 or ranks < 4 or ranks % heads or heads & (heads - 1):
        return False
    order, per_head = ring_order(ranks), ranks // heads
    return all(
        order[p - k] // per_head != order[(p + k) % ranks] // per_head
        for p in range(ranks)
        for k in range(1, ranks // 2)
    )


def slot_for(info, loads, width, bundles, requester, owner):
    pick = jnp.int32(0)
    for j in range(bundles):
        hit = info[requester * width + j] == owner
        pick = jnp.where(hit, info[requester * width + bundles + j], pick)
    return lax.rem(pick, loads[owner])


def pack_kernel(info, loads, place, lat_ref, rope_ref, out_ref):
    rows = lat_ref.shape[1]
    out_ref[0, :rows, :] = lat_ref[0]
    out_ref[0, rows:, :] = rope_ref[0]


def pack(info, loads, place, cache_latent, cache_rope, ranks, heads, width, bundles):
    rows = cache_latent.shape[1] // heads
    dims = cache_rope.shape[1] // heads
    wide = cache_latent.shape[2]

    def source(i, info, loads, place):
        return slot_for(info, loads, width, bundles, i, place[0]), place[1], 0

    return pl.pallas_call(
        pack_kernel,
        out_shape=jax.ShapeDtypeStruct((ranks, rows + dims, wide), cache_latent.dtype),
        grid_spec=pltpu.PrefetchScalarGridSpec(
            num_scalar_prefetch=3,
            grid=(ranks,),
            in_specs=[pl.BlockSpec((1, rows, wide), source), pl.BlockSpec((1, dims, wide), source)],
            out_specs=pl.BlockSpec((1, rows + dims, wide), lambda i, *_: (i, 0, 0)),
        ),
        name="pack",
    )(info, loads, place, cache_latent, cache_rope)


def attend_kernel(
    heads, width, bundles, scale, block, info, loads, place, q_ref, qr_ref, *refs
):
    parts = refs[:heads]
    w_ref, out_ref, lat, rope, mixed = refs[heads:]
    b = pl.program_id(0)
    rows = lat.shape[0] // heads
    dims = rope.shape[0] // heads
    for m in range(heads):
        at = jnp.bitwise_xor(place[1], m)
        lat[pl.ds(pl.multiple_of(at * rows, rows), rows), :] = parts[m][0, :rows, :]
        rope[pl.ds(pl.multiple_of(at * dims, dims), dims), :] = parts[m][0, rows:, :]
    base = place[0] * width
    owner = info[base + b]
    slot = lax.rem(info[base + bundles + b], loads[owner])
    length = info[owner * width + 2 * bundles + slot]
    total_rows = q_ref.shape[1]
    live = lax.broadcasted_iota(jnp.int32, (block, lat.shape[0]), 1) < length
    for i in range(total_rows // block):
        at = slice(i * block, (i + 1) * block)
        s = lax.dot_general(
            q_ref[0, at, :], lat[...], (((1,), (1,)), ((), ())), preferred_element_type=jnp.float32
        )
        s = s + jnp.dot(qr_ref[0, at, :], rope[...], preferred_element_type=jnp.float32)
        s = jnp.where(live, s * scale, -1e30)
        w = jnp.exp(s - jnp.max(s, axis=1, keepdims=True))
        w = w * (1.0 / jnp.sum(w, axis=1, keepdims=True))
        o = jnp.dot(w.astype(jnp.bfloat16), lat[...], preferred_element_type=jnp.float32)
        for c in range(mixed.shape[0]):
            piece = o[:, c * 128 : (c + 1) * 128]
            mixed[c, pl.ds(b * total_rows + i * block, block), :] = piece

    @pl.when(b == pl.num_programs(0) - 1)
    def _():
        local_heads, _, value_width = w_ref.shape
        n = mixed.shape[1] // local_heads
        for h in range(local_heads):
            x = jnp.concatenate(
                [mixed[c, pl.ds(h, n, stride=local_heads), :] for c in range(mixed.shape[0])], axis=1
            ).astype(jnp.bfloat16)
            v = jnp.dot(x, w_ref[h], preferred_element_type=jnp.float32)
            out_ref[:, h * value_width : (h + 1) * value_width] = v.astype(jnp.bfloat16)


def attend(info, loads, place, q, qr, parts, w_uv, width, bundles):
    heads = len(parts)
    _, q_rows, wide = q.shape
    _, part_rows, _ = parts[0].shape
    local_heads, _, value_width = w_uv.shape
    dims = qr.shape[2] // heads
    rows = part_rows - dims
    row_count = bundles * q_rows // local_heads

    def theirs(b, info, loads, place):
        return info[place[0] * width + b], 0, 0

    block = math.gcd(q_rows, 128)
    return pl.pallas_call(
        functools.partial(
            attend_kernel, heads, width, bundles, 1.0 / math.sqrt(VD + ROPE), block
        ),
        out_shape=jax.ShapeDtypeStruct((row_count, local_heads * value_width), jnp.bfloat16),
        grid_spec=pltpu.PrefetchScalarGridSpec(
            num_scalar_prefetch=3,
            grid=(bundles,),
            in_specs=[
                pl.BlockSpec((1, q_rows, wide), lambda b, *_: (b, 0, 0)),
                pl.BlockSpec((1, q_rows, qr.shape[2]), lambda b, *_: (b, 0, 0)),
            ]
            + [pl.BlockSpec((1, part_rows, wide), theirs)] * heads
            + [pl.BlockSpec(w_uv.shape, lambda b, *_: (0, 0, 0))],
            out_specs=pl.BlockSpec((row_count, local_heads * value_width), lambda b, *_: (0, 0)),
            scratch_shapes=[
                pltpu.VMEM((rows * heads, wide), jnp.bfloat16),
                pltpu.VMEM((dims * heads, wide), jnp.bfloat16),
                pltpu.VMEM((wide // 128, bundles * q_rows, 128), jnp.float32),
            ],
        ),
        name="attend",
    )(info, loads, place, q, qr, *parts, w_uv)


def local_general(
    q_latent, q_rope, cache_latent, cache_rope, lengths, loads, owner_rank, owner_pick, w_uv, w_out
):
    ranks = lax.axis_size("dp")
    heads = lax.axis_size("head")
    me = lax.axis_index("dp")
    head = lax.axis_index("head")
    bundles = owner_rank.shape[0]
    roll_count = q_latent.shape[0] // bundles
    local_heads = w_uv.shape[0]
    place = jnp.stack([me, head]).astype(jnp.int32)

    facts = jnp.concatenate([owner_rank, owner_pick, lengths])
    width = 32
    facts = jnp.pad(facts, (0, width - facts.shape[0]))
    info = lax.all_to_all(
        jnp.broadcast_to(facts[None], (ranks, width)), "dp", split_axis=0, concat_axis=0, tiled=True
    ).reshape(-1)
    q = q_latent.reshape(bundles, roll_count * local_heads, -1)
    qr = q_rope.reshape(bundles, roll_count * local_heads, -1)

    packed = pack(info, loads, place, cache_latent, cache_rope, ranks, heads, width, bundles)
    mine = lax.all_to_all(packed, "dp", split_axis=0, concat_axis=0, tiled=True)
    parts = [mine]
    bit = heads // 2
    found = {0: mine}
    while bit:
        pairs = [(i, i ^ bit) for i in range(heads)]
        for m in list(found):
            found[m ^ bit] = lax.ppermute(found[m], "head", pairs)
        bit //= 2
    parts = [found[m] for m in range(heads)]
    values = attend(info, loads, place, q, qr, parts, w_uv, width, bundles)

    order = ring_order(ranks)
    ahead = [(order[i], order[(i + 1) % ranks]) for i in range(ranks)]
    behind = [(b, a) for a, b in ahead]
    half = values.shape[1] // 2

    def project(x):
        return jnp.dot(x, w_out, preferred_element_type=jnp.float32).astype(jnp.bfloat16)

    partial = {0: project(values)}
    fore = back = values
    for step in range(1, (ranks + 1) // 2):
        fore = lax.ppermute(fore, "dp", ahead)
        back = lax.ppermute(back, "dp", behind)
        both = project(jnp.concatenate([fore, back], axis=0))
        partial[-step] = both[: values.shape[0]]
        partial[step] = both[values.shape[0] :]
    if ranks % 2 == 0:
        left = lax.ppermute(fore[:, :half], "dp", ahead)
        right = lax.ppermute(back[:, half:], "dp", behind)
        partial[ranks // 2] = project(jnp.concatenate([left, right], axis=1))
    stacked = jnp.stack([partial[k if 2 * k <= ranks else k - ranks] for k in range(ranks)])
    position = [0] * ranks
    for i, r in enumerate(order):
        position[r] = i
    position = jnp.asarray(position, jnp.int32)
    by_rank = stacked[(position - position[me]) % ranks]
    shares = by_rank.reshape(heads, -1, w_out.shape[1])
    got = lax.all_to_all(shares, "head", split_axis=0, concat_axis=0, tiled=True)
    return jnp.sum(got.astype(jnp.float32), axis=0).astype(jnp.bfloat16)


def ring_tables(ranks):
    order = ring_order(ranks)
    where = [order.index(r) for r in range(ranks)]
    offsets = [0]
    for k in range(1, ranks // 2):
        offsets += [-k, k]
    offsets.append(ranks // 2)
    seen = [[order[(where[r] + o) % ranks] for o in offsets] for r in range(ranks)]
    return order, where, offsets, seen


BUNDLE, SLOT, TARGET, OWNER, PLACE, PLAN_ROWS = 0, 1, 2, 3, 4, 8


def plan_kernel(per_head, seen, owner_rank, owner_pick, loads, table):
    ranks = seen.shape[1]
    me, head = lax.axis_index("dp"), lax.axis_index("head")
    table[PLACE, 0] = me
    table[PLACE, 1] = head
    for c in range(ranks):
        owner = seen[me, c]
        bundle, pick = jnp.int32(0), jnp.int32(0)
        for b in range(owner_rank.shape[0]):
            hit = owner_rank[b] == owner
            bundle = jnp.where(hit, b, bundle)
            pick = jnp.where(hit, owner_pick[b], pick)
        table[BUNDLE, c] = bundle
        table[SLOT, c] = lax.rem(pick, loads[owner])
        table[TARGET, c] = lax.div(owner, per_head)
        table[OWNER, c] = owner


def plan_of(seen, owner_rank, owner_pick, loads, per_head):
    smem = pl.BlockSpec(memory_space=pltpu.MemorySpace.SMEM)
    return pl.pallas_call(
        functools.partial(plan_kernel, per_head),
        out_shape=jax.ShapeDtypeStruct((PLAN_ROWS, seen.shape[1]), jnp.int32),
        in_specs=[smem] * 4,
        out_specs=smem,
        name="plan",
    )(seen, owner_rank, owner_pick, loads)


def payload_kernel(lat, rope, out, sems):
    head = lax.axis_index("head")
    dims = rope.shape[1] * (out.shape[1]) // (rope.shape[1] + lat.shape[1])
    rows = out.shape[1] - dims
    copies = [
        pltpu.make_async_copy(
            lat.at[:, pl.ds(pl.multiple_of(head * rows, rows), rows), :],
            out.at[:, pl.ds(0, rows), :],
            sems.at[0],
        ),
        pltpu.make_async_copy(
            rope.at[:, pl.ds(pl.multiple_of(head * dims, dims), dims), :],
            out.at[:, pl.ds(rows, dims), :],
            sems.at[1],
        ),
    ]
    for copy in copies:
        copy.start()
    for copy in copies:
        copy.wait()


def payload_of(cache_latent, cache_rope, heads):
    slots, positions, wide = cache_latent.shape
    rows = (positions + cache_rope.shape[1]) // heads
    return pl.pallas_call(
        payload_kernel,
        out_shape=jax.ShapeDtypeStruct((slots, rows, wide), cache_latent.dtype),
        in_specs=[pl.BlockSpec(memory_space=pl.ANY)] * 2,
        out_specs=pl.BlockSpec(memory_space=pl.ANY),
        scratch_shapes=[pltpu.SemaphoreType.DMA((2,))],
        name="payload",
    )(cache_latent, cache_rope)


def choose_kernel(cut, column, table, a_ref, b_ref, out_ref):
    if cut is None:
        out_ref[0] = a_ref[0]
        out_ref[1] = b_ref[0]
    else:
        first = table[SLOT, column] < cut

        @pl.when(first)
        def _():
            out_ref[0] = a_ref[0]

        @pl.when(jnp.logical_not(first))
        def _():
            out_ref[0] = b_ref[0]


def choose(table, a, b, columns, cut=None):
    _, rows, wide = a.shape
    if cut is None:
        index_a = lambda i, table: (table[SLOT, columns[0]], 0, 0)
        index_b = lambda i, table: (table[SLOT, columns[1]], 0, 0)
    else:
        index_a = lambda i, table: (jnp.minimum(table[SLOT, columns[0]], cut - 1), 0, 0)
        index_b = lambda i, table: (jnp.maximum(table[SLOT, columns[0]] - cut, 0), 0, 0)
    return pl.pallas_call(
        functools.partial(choose_kernel, cut, columns[0]),
        out_shape=jax.ShapeDtypeStruct((len(columns), rows, wide), a.dtype),
        grid_spec=pltpu.PrefetchScalarGridSpec(
            num_scalar_prefetch=1,
            grid=(1,),
            in_specs=[pl.BlockSpec((1, rows, wide), index_a), pl.BlockSpec((1, rows, wide), index_b)],
            out_specs=pl.BlockSpec((len(columns), rows, wide), lambda i, *_: (0, 0, 0)),
        ),
        compiler_params=pltpu.CompilerParams(vmem_limit_bytes=4 * 2**20),
        name="choose",
    )(table, a, b)


def slots_kernel(plan, own, heads, bundles, carried, final, scale, block, table, info, *refs):
    count = len(plan)
    refs = list(refs)
    q_ref, qr_ref = refs.pop(0), refs.pop(0)
    if own:
        full_lat, full_rope = refs.pop(0), refs.pop(0)
    shipped = count - own
    parts = [[refs.pop(0) for _ in range(heads)] for _ in range(shipped)]
    earlier = [refs.pop(0) for _ in carried]
    w_hbm, out_ref, lat, rope, mixed, w_ref, sem = refs[:7]
    i = pl.program_id(0)
    total_rows = q_ref.shape[1]
    w_copy = pltpu.make_async_copy(w_hbm, w_ref, sem)

    @pl.when(i == 0)
    def _():
        w_copy.start()

    rows = lat.shape[0] // heads
    dims = rope.shape[0] // heads

    for j in range(count):

        @pl.when(i == j)
        def _():
            if own and j == 0:
                lat[...] = full_lat[0]
                rope[...] = full_rope[0]
                return
            for m in range(heads):
                part = parts[j - own][m]
                to = jnp.bitwise_xor(table[PLACE, 1], m)
                lat[pl.ds(pl.multiple_of(to * rows, rows), rows), :] = part[0, :rows, :]
                rope[pl.ds(pl.multiple_of(to * dims, dims), dims), :] = part[0, rows:, :]

    column = jnp.int32(plan[0]) + i
    length = info[table[OWNER, column], 0, bundles + table[SLOT, column]]
    live = lax.broadcasted_iota(jnp.int32, (block, lat.shape[0]), 1) < length
    for r in range(total_rows // block):
        at = slice(r * block, (r + 1) * block)
        s = lax.dot_general(
            q_ref[0, at, :], lat[...], (((1,), (1,)), ((), ())), preferred_element_type=jnp.float32
        )
        s = s + jnp.dot(qr_ref[0, at, :], rope[...], preferred_element_type=jnp.float32)
        s = jnp.where(live, s * scale, -1e30)
        w = jnp.exp(s - jnp.max(s, axis=1, keepdims=True))
        w = w * (1.0 / jnp.sum(w, axis=1, keepdims=True))
        o = jnp.dot(w.astype(jnp.bfloat16), lat[...], preferred_element_type=jnp.float32)
        for c in range(mixed.shape[0]):
            mixed[c, pl.ds(i * total_rows + r * block, block), :] = o[:, c * 128 : (c + 1) * 128]

    @pl.when(i == count - 1)
    def _():
        w_copy.wait()
        local_heads, _, value_width = w_ref.shape
        n = mixed.shape[1] // local_heads
        into, at = out_ref, 0
        if final:
            into = refs[7]
            for piece in earlier:
                into[pl.ds(at, piece.shape[0]), :] = piece[...]
                at += piece.shape[0]
        for h in range(local_heads):
            x = jnp.concatenate(
                [mixed[c, pl.ds(h, n, stride=local_heads), :] for c in range(mixed.shape[0])], axis=1
            ).astype(jnp.bfloat16)
            v = jnp.dot(x, w_ref[h], preferred_element_type=jnp.float32)
            into[pl.ds(at, n), h * value_width : (h + 1) * value_width] = v
        if final:
            out_ref[...] = into[...].astype(out_ref.dtype)


def in_hbm(x):
    return pltpu.with_memory_space_constraint(x, pltpu.MemorySpace.HBM)


def attend_slots(plan, table, info, q, qr, full, parts, heads, bundles, w_uv, earlier=None):
    own = 1 if full is not None else 0
    final = earlier is not None
    earlier = list(earlier or ())
    count = len(plan)
    _, q_rows, wide = q.shape
    part_rows = parts[0][0][0].shape[1]
    dims = qr.shape[2] // heads
    rows = part_rows - dims
    block = math.gcd(q_rows, 128)
    local_heads, _, value_width = w_uv.shape
    carried = [e.shape[0] for e in earlier]

    def bundle(i, table, info):
        return table[BUNDLE, plan[0] + i], 0, 0

    in_specs = [
        pl.BlockSpec((1, q_rows, wide), bundle),
        pl.BlockSpec((1, q_rows, qr.shape[2]), bundle),
    ]
    args = [in_hbm(q), in_hbm(qr)]
    if own:
        here = lambda i, table, info: (table[SLOT, plan[0]], 0, 0)
        in_specs += [
            pl.BlockSpec((1, rows * heads, wide), here),
            pl.BlockSpec((1, dims * heads, wide), here),
        ]
        args += [in_hbm(x) for x in full]
    for slot in parts:
        for array, index in slot:
            in_specs.append(
                pl.BlockSpec((1, part_rows, wide), lambda i, *_, index=index: (index, 0, 0))
            )
            args.append(array)
    for piece in earlier:
        in_specs.append(pl.BlockSpec(piece.shape, lambda i, *_: (0, 0)))
        args.append(piece)
    in_specs.append(pl.BlockSpec(memory_space=pl.ANY))
    args.append(in_hbm(w_uv))
    done = sum(carried) + count * q_rows // local_heads
    out_shape = (done, local_heads * value_width)
    scratch = [
        pltpu.VMEM((rows * heads, wide), jnp.bfloat16),
        pltpu.VMEM((dims * heads, wide), jnp.bfloat16),
        pltpu.VMEM((wide // 128, count * q_rows, 128), jnp.float32),
        pltpu.VMEM(w_uv.shape, w_uv.dtype),
        pltpu.SemaphoreType.DMA,
    ]
    if final:
        scratch.append(pltpu.VMEM(out_shape, jnp.float32))
    return pl.pallas_call(
        functools.partial(
            slots_kernel, plan, own, heads, bundles, carried, final,
            1.0 / math.sqrt(VD + ROPE), block,
        ),
        out_shape=jax.ShapeDtypeStruct(out_shape, jnp.bfloat16 if final else jnp.float32),
        grid_spec=pltpu.PrefetchScalarGridSpec(
            num_scalar_prefetch=2,
            grid=(count,),
            in_specs=in_specs,
            out_specs=pl.BlockSpec(out_shape, lambda i, *_: (0, 0)),
            scratch_shapes=scratch,
        ),
        compiler_params=pltpu.CompilerParams(vmem_limit_bytes=24 * 2**20),
        name="attend_slots",
    )(table, info, *args)


def add_in(table, per_head, columns, own, got, before, after):
    part = own[...]
    for g in got:
        part = part + g[...].astype(jnp.float32)
    for y in range(per_head):
        rank = table[PLACE, 1] * per_head + y
        hit = table[OWNER, columns[0]] == rank
        for c in columns[1:]:
            hit = hit | (table[OWNER, c] == rank)
        now = jnp.where(hit, part, 0.0)
        after[y] = now if before is None else before[y] + now


def settle_kernel(heads, per_head, columns, prev_columns, has_total, table, both, *refs):
    refs = list(refs)
    if prev_columns:
        prev_own, prev_got = refs.pop(0), [refs.pop(0) for _ in range(heads - 1)]
        before = refs.pop(0) if has_total else None
    block = both.shape[0] // len(columns)
    sends = len(refs) - 1 - bool(prev_columns)
    own = refs[sends]
    head = table[PLACE, 1]
    if len(columns) == 1:
        own[...] = both[...]
        refs[0][...] = both[...].astype(jnp.bfloat16)
    else:
        for m in range(heads):
            first = table[TARGET, columns[0]] == jnp.bitwise_xor(head, m)
            piece = jnp.where(first, both[:block], both[block:])
            if m == 0:
                own[...] = piece
            else:
                refs[m - 1][...] = piece.astype(jnp.bfloat16)
    if prev_columns:
        add_in(table, per_head, prev_columns, prev_own, prev_got, before, refs[sends + 1])


def settle_step(table, heads, per_head, columns, both, previous):
    n = both.shape[0] // len(columns)
    wide = both.shape[1]
    vmem = pl.BlockSpec(memory_space=pltpu.MemorySpace.VMEM)
    args, prev_columns, has_total = [both], None, False
    if previous is not None:
        prev_columns, prev_own, prev_got, total = previous
        has_total = total is not None
        args += [prev_own, *prev_got] + ([total] if has_total else [])
    sends = 1 if len(columns) == 1 else heads - 1
    out = [jax.ShapeDtypeStruct((n, wide), jnp.bfloat16)] * sends
    out.append(jax.ShapeDtypeStruct((n, wide), jnp.float32))
    if previous is not None:
        out.append(jax.ShapeDtypeStruct((per_head, n, wide), jnp.float32))
    outs = pl.pallas_call(
        functools.partial(settle_kernel, heads, per_head, columns, prev_columns, has_total),
        out_shape=out,
        in_specs=[pl.BlockSpec(memory_space=pltpu.MemorySpace.SMEM)] + [vmem] * len(args),
        out_specs=[vmem] * len(out),
        compiler_params=pltpu.CompilerParams(vmem_limit_bytes=4 * 2**20),
        name="settle",
    )(table, *args)
    to_send = list(outs[:sends]) * (1 if sends > 1 else heads - 1)
    return to_send, outs[sends], outs[sends + 1] if previous is not None else None


def finish_kernel(heads, per_head, columns, roll, table, info, seen, own, *refs):
    got, before, out, total = refs[: heads - 1], refs[heads - 1], refs[heads], refs[heads + 1]
    add_in(table, per_head, columns, own, got, before, total)
    n = total.shape[1]
    slots = n // roll
    to = lax.broadcasted_iota(jnp.int32, (n, n), 0)
    source = lax.broadcasted_iota(jnp.int32, (n, n), 1)
    for y in range(per_head):
        rank = table[PLACE, 1] * per_head + y
        wanted = to
        for b in range(slots):
            place = jnp.int32(0)
            for c in range(slots):
                place = jnp.where(seen[rank, c] == info[rank, 0, b], c, place)
            inside = (to >= b * roll) & (to < (b + 1) * roll)
            wanted = jnp.where(inside, to + (place - b) * roll, wanted)
        pick = jnp.where(wanted == source, 1.0, 0.0).astype(jnp.bfloat16)
        moved = jnp.dot(pick, total[y].astype(jnp.bfloat16), preferred_element_type=jnp.float32)
        out[pl.ds(y * n, n), :] = moved.astype(out.dtype)


def finish(table, info, seen, heads, per_head, columns, roll, own, got, total):
    n, wide = own.shape
    vmem = pl.BlockSpec(memory_space=pltpu.MemorySpace.VMEM)
    smem = pl.BlockSpec(memory_space=pltpu.MemorySpace.SMEM)
    return pl.pallas_call(
        functools.partial(finish_kernel, heads, per_head, columns, roll),
        out_shape=jax.ShapeDtypeStruct((per_head * n, wide), jnp.bfloat16),
        in_specs=[smem] * 3 + [vmem] * (heads + 1),
        out_specs=vmem,
        scratch_shapes=[pltpu.VMEM((per_head, n, wide), jnp.float32)],
        compiler_params=pltpu.CompilerParams(vmem_limit_bytes=6 * 2**20),
        name="finish",
    )(table, info, seen, own, *got, total)


def local_ring(
    q_latent, q_rope, cache_latent, cache_rope, lengths, loads, owner_rank, owner_pick, w_uv, w_out
):
    ranks = lax.axis_size("dp")
    heads = lax.axis_size("head")
    bundles = owner_rank.shape[0]
    local_heads = w_uv.shape[0]
    roll_count = q_latent.shape[0] // bundles
    per_head = ranks // heads
    last = ranks // 2
    order, where, offsets, seen = ring_tables(ranks)
    seen = jnp.asarray(seen, jnp.int32)
    ahead = [(order[i], order[(i + 1) % ranks]) for i in range(ranks)]
    behind = [(b, a) for a, b in ahead]

    def move(x, pairs, axis="dp"):
        return lax.ppermute(x, axis, pairs)

    payload = payload_of(cache_latent, cache_rope, heads)
    slots = payload.shape[0]
    fore, back = move(payload, ahead), move(payload, behind)
    facts = jnp.concatenate([owner_rank, lengths])
    width = 32
    facts = jnp.pad(facts, (0, width - facts.shape[0]))
    info = lax.all_to_all(
        jnp.broadcast_to(facts[None], (ranks, width)), "dp", split_axis=0, concat_axis=0, tiled=True
    )
    info = jnp.maximum(info, 0)[:, None]
    table = plan_of(seen, owner_rank, owner_pick, loads, per_head)
    q = q_latent.reshape(bundles, roll_count * local_heads, -1)
    qr = q_rope.reshape(bundles, roll_count * local_heads, -1)

    def share(chosen):
        found = {0: chosen}
        bit = heads // 2
        while bit:
            pairs = [(i, i ^ bit) for i in range(heads)]
            for m in list(found):
                found[m ^ bit] = move(found[m], pairs, "head")
            bit //= 2
        return [found[m] for m in range(heads)]

    groups = {}
    for k in range(1, last):
        if k > 1:
            fore = move(fore, ahead)
            back = move(back, behind)
        chosen = choose(table, fore, back, [2 * k - 1, 2 * k])
        parts = share(chosen)
        groups[2 * k - 1] = [(p, 0) for p in parts]
        groups[2 * k] = [(p, 1) for p in parts]
    cut = slots // 2
    left = move(fore[:cut], ahead)
    right = move(back[cut:], behind)
    chosen = choose(table, left, right, [2 * last - 1], cut)
    parts = share(chosen)
    groups[2 * last - 1] = [(p, 0) for p in parts]

    def attend(plan, full=None, earlier=None):
        return attend_slots(
            plan, table, info, q, qr, full, [groups[c] for c in plan[(full is not None) :]],
            heads, bundles, w_uv, earlier,
        )

    earlier = [attend([0, 1, 2], (cache_latent, cache_rope))]
    for k in range(2, last):
        earlier.append(attend([2 * k - 1, 2 * k]))
    values = attend([2 * last - 1], None, earlier)
    half = values.shape[1] // 2

    def project(x):
        return jnp.dot(x, w_out, preferred_element_type=jnp.float32)

    def target(p, column):
        return order[(where[p] + offsets[column]) % ranks] // per_head

    def settle(columns, both, previous):
        to_send, own, total = settle_step(table, heads, per_head, columns, both, previous)
        got = []
        for m in range(1, heads):
            pairs = []
            for p in range(ranks):
                for t in sorted({target(p, c) for c in columns}):
                    pairs.append((p * heads + (t ^ m), p * heads + t))
            got.append(move(to_send[m - 1], pairs, ("dp", "head")))
        return columns, own, got, total

    state = settle([0], project(values), None)
    fore = back = values
    for k in range(1, last):
        fore = move(fore, ahead)
        back = move(back, behind)
        both = project(jnp.concatenate([fore, back], axis=0))
        state = settle([2 * k - 1, 2 * k], both, state)
    left = move(fore[:, :half], ahead)
    right = move(back[:, half:], behind)
    ends = project(jnp.concatenate([left, right], axis=1))
    columns, own, got, total = settle([2 * last - 1], ends, state)
    return finish(table, info, seen, heads, per_head, columns, roll_count, own, got, total)


def local(*args):
    ranks, heads = lax.axis_size("dp"), lax.axis_size("head")
    bundles = args[6].shape[0]
    if ranks == bundles and ring_fits(ranks, heads):
        return local_ring(*args)
    return local_general(*args)


def solution(mesh):
    in_specs = (
        P("dp", "head"),
        P("dp", "head"),
        P("dp", None, None),
        P("dp", None, None),
        P("dp"),
        P(),
        P("dp"),
        P("dp"),
        P("head", None, None),
        P("head", "dp"),
    )
    out_specs = P("head", "dp")
    return jax.shard_map(local, mesh=mesh, in_specs=in_specs, out_specs=out_specs, check_vma=False)
```

profile of v0, /device:TPU:0, one launch (start us, length us, event | category | flops | bytes accessed | tf_op | source)
XLA Modules:
  0.0 221.5 jit_solution(6411152215403157270)
XLA Ops:
  0.0 19.0 %payload.1 = bf16[4,144,512]{2,1,0:T(8,128)(2,1)} custom-call(bf16[4,512,512]{2,1,0:T(8,128)(2,1)} %refs_2_.1, bf16[4,64,512]{2,1,0:T(8,128)(2,1)} %refs_3_.1), custom_call_target="tpu_custom_call" | custom-call | tf_op jit(solution)/shard_map/payload/pallas_call | solution.py:289
  19.0 3.0 %collective-permute-start.4 = (bf16[4,144,512]{2,1,0:T(8,128)(2,1)}, bf16[4,144,512]{2,1,0:T(8,128)(2,1)S(1)}, u32[]{:S(2)}, u32[]{:S(2)}) collective-permute-start(bf16[4,144,512]{2,1,0:T(8,128)(2,1)} %payload.1), channel_id=1, source_target_pairs={{8,0},{16,8},{24,16},{28,24},{20,28},{12,20},{4,12},{0,4},{9,1},{1... | collective-permute-start | bytes 1769480 | tf_op jit(solution)/shard_map/ppermute | solution.py:596
  22.2 13.5 %collective-permute-done.4.b_ref = bf16[4,144,512]{2,1,0:T(8,128)(2,1)S(1)} collective-permute-done((bf16[4,144,512]{2,1,0:T(8,128)(2,1)}, bf16[4,144,512]{2,1,0:T(8,128)(2,1)S(1)}, u32[]{:S(2)}, u32[]{:S(2)}) %collective-permute-start.4) | collective-permute-done | bytes 589856 | tf_op jit(solution)/shard_map/ppermute | solution.py:596
  38.5 11.6 %collective-permute-done.5.b_ref = bf16[4,144,512]{2,1,0:T(8,128)(2,1)S(1)} collective-permute-done((bf16[4,144,512]{2,1,0:T(8,128)(2,1)S(1)}, bf16[4,144,512]{2,1,0:T(8,128)(2,1)S(1)}, u32[]{:S(2)}, u32[]{:S(2)}) %collective-permute-start.5) | collective-permute-done | bytes 589856 | tf_op jit(solution)/shard_map/ppermute | solution.py:596
  57.5 6.3 %collective-permute-done.6.b_ref = bf16[4,144,512]{2,1,0:T(8,128)(2,1)S(1)} collective-permute-done((bf16[4,144,512]{2,1,0:T(8,128)(2,1)S(1)}, bf16[4,144,512]{2,1,0:T(8,128)(2,1)S(1)}, u32[]{:S(2)}, u32[]{:S(2)}) %collective-permute-start.6) | collective-permute-done | bytes 589856 | tf_op jit(solution)/shard_map/ppermute | solution.py:596
  74.6 3.7 %collective-permute-done.15.refs_4_.refs_8_ = bf16[2,144,512]{2,1,0:T(8,128)(2,1)S(1)} collective-permute-done((bf16[2,144,512]{2,1,0:T(8,128)(2,1)S(1)}, bf16[2,144,512]{2,1,0:T(8,128)(2,1)S(1)}, u32[]{:S(2)}, u32[]{:S(2)}) %collective-permute-start.15) | collective-permute-done | bytes 294944 | tf_op jit(solution)/shard_map/ppermute | solution.py:596
  78.8 5.8 %collective-permute-done.18.refs_4_.refs_8_ = bf16[2,144,512]{2,1,0:T(8,128)(2,1)S(1)} collective-permute-done((bf16[2,144,512]{2,1,0:T(8,128)(2,1)S(1)}, bf16[2,144,512]{2,1,0:T(8,128)(2,1)S(1)}, u32[]{:S(2)}, u32[]{:S(2)}) %collective-permute-start.18) | collective-permute-done | bytes 294944 | tf_op jit(solution)/shard_map/ppermute | solution.py:596
  85.3 5.5 %all-to-all-start = ((s32[8,1,32]{2,1,0:T(1,128)}), s32[8,1,32]{2,1,0:T(1,128)S(1)}, u32[]{:S(2)}, u32[]{:S(2)}) async-start(s32[8,1,32]{2,1,0:T(1,128)} %broadcast_in_dim.2), calls=%async_computation | async-start | bytes 8192 | tf_op jit(solution)/shard_map/all_to_all | solution.py:604
  90.8 2.6 %reshape.13.refs_1_ = bf16[8,384,64]{2,1,0:T(8,128)(2,1)} reshape(bf16[96,2048]{1,0:T(8,128)(2,1)} %param.12) | data formatting | bytes 786432 | tf_op jit(solution)/shard_map/reshape | solution.py:610
  93.4 5.9 %reshape.12.refs_0_ = bf16[8,384,512]{2,1,0:T(8,128)(2,1)} reshape(bf16[96,16384]{1,0:T(8,128)(2,1)} %param.11) | data formatting | bytes 6291456 | tf_op jit(solution)/shard_map/reshape | solution.py:609
  99.8 9.8 %attend_slots.4.refs_6_ = f32[36,4096]{1,0:T(8,128)S(1)} custom-call(s32[8,8]{1,0:T(8,128)S(1)} %copy-done.2, s32[8,1,32]{2,1,0:T(1,128)S(1)} %broadcast_maximum_fusion.info, bf16[8,384,512]{2,1,0:T(8,128)(2,1)} %reshape.12.refs_0_, bf16[8,384,64]{2,1,0:T(8,128)(2,1)} %reshape.13.refs_1_, bf16[4,512,512]{2,1,0:T(8,128)(2,1)} %refs_2_.1, ...), custom_call_target="tpu_custom_call" | custom-call | tf_op jit(solution)/shard_map/attend_slots/pallas_call | solution.py:463
  109.6 6.9 %attend_slots.5.refs_7_ = f32[24,4096]{1,0:T(8,128)S(1)} custom-call(s32[8,8]{1,0:T(8,128)S(1)} %copy-done.2, s32[8,1,32]{2,1,0:T(1,128)S(1)} %broadcast_maximum_fusion.info, bf16[8,384,512]{2,1,0:T(8,128)(2,1)} %reshape.12.refs_0_, bf16[8,384,64]{2,1,0:T(8,128)(2,1)} %reshape.13.refs_1_, bf16[2,144,512]{2,1,0:T(8,128)(2,1)S(1)} %choose.6.refs_2_.refs_6_, ...), custom_call_target="tpu_custom_call" | custom-call | tf_op jit(solution)/shard_map/attend_slots/pallas_call | solution.py:463
  116.5 7.2 %attend_slots.6.refs_8_ = f32[24,4096]{1,0:T(8,128)S(1)} custom-call(s32[8,8]{1,0:T(8,128)S(1)} %copy-done.2, s32[8,1,32]{2,1,0:T(1,128)S(1)} %broadcast_maximum_fusion.info, bf16[8,384,512]{2,1,0:T(8,128)(2,1)} %reshape.12.refs_0_, bf16[8,384,64]{2,1,0:T(8,128)(2,1)} %reshape.13.refs_1_, bf16[2,144,512]{2,1,0:T(8,128)(2,1)S(1)} %choose.7.refs_2_.refs_6_, ...), custom_call_target="tpu_custom_call" | custom-call | tf_op jit(solution)/shard_map/attend_slots/pallas_call | solution.py:463
  123.8 5.5 %attend_slots.7 = bf16[96,4096]{1,0:T(8,128)(2,1)S(1)} custom-call(s32[8,8]{1,0:T(8,128)S(1)} %copy-done.2, s32[8,1,32]{2,1,0:T(1,128)S(1)} %broadcast_maximum_fusion.info, bf16[8,384,512]{2,1,0:T(8,128)(2,1)} %reshape.12.refs_0_, bf16[8,384,64]{2,1,0:T(8,128)(2,1)} %reshape.13.refs_1_, bf16[1,144,512]{2,1,0:T(8,128)(2,1)} %choose.4.refs_2_, ...), custom_call_target="tpu_custom_call" | custom-call | tf_op jit(solution)/shard_map/attend_slots/pallas_call | solution.py:463
  129.3 2.1 collective-permute-start.24
  131.4 17.7 %collective-permute-done.24 = bf16[96,4096]{1,0:T(8,128)(2,1)S(1)} collective-permute-done((bf16[96,4096]{1,0:T(8,128)(2,1)S(1)}, bf16[96,4096]{1,0:T(8,128)(2,1)S(1)}, u32[]{:S(2)}, u32[]{:S(2)}) %collective-permute-start.24) | collective-permute-done | bytes 786464 | tf_op jit(solution)/shard_map/ppermute | solution.py:596
  157.0 11.1 %collective-permute-done.25 = bf16[96,4096]{1,0:T(8,128)(2,1)S(1)} collective-permute-done((bf16[96,4096]{1,0:T(8,128)(2,1)S(1)}, bf16[96,4096]{1,0:T(8,128)(2,1)S(1)}, u32[]{:S(2)}, u32[]{:S(2)}) %collective-permute-start.25) | collective-permute-done | bytes 786464 | tf_op jit(solution)/shard_map/ppermute | solution.py:596
  179.2 4.7 %collective-permute-done.32.refs_2_ = bf16[96,896]{1,0:T(8,128)(2,1)S(1)} collective-permute-done((bf16[96,896]{1,0:T(8,128)(2,1)S(1)}, bf16[96,896]{1,0:T(8,128)(2,1)S(1)}, u32[]{:S(2)}, u32[]{:S(2)}) %collective-permute-start.32) | collective-permute-done | bytes 172064 | tf_op jit(solution)/shard_map/ppermute | solution.py:596
  183.9 2.7 %collective-permute-done.33.refs_3_ = bf16[96,896]{1,0:T(8,128)(2,1)S(1)} collective-permute-done((bf16[96,896]{1,0:T(8,128)(2,1)S(1)}, bf16[96,896]{1,0:T(8,128)(2,1)S(1)}, u32[]{:S(2)}, u32[]{:S(2)}) %collective-permute-start.33) | collective-permute-done | bytes 172064 | tf_op jit(solution)/shard_map/ppermute | solution.py:596
  187.4 2.5 %collective-permute-start.34 = (bf16[96,896]{1,0:T(8,128)(2,1)S(1)}, bf16[96,896]{1,0:T(8,128)(2,1)S(1)}, u32[]{:S(2)}, u32[]{:S(2)}) collective-permute-start(bf16[96,896]{1,0:T(8,128)(2,1)S(1)} %get-tuple-element.33), channel_id=1, source_target_pairs={{0,1},{3,2},{4,5},{7,6},{9,8},{10,11},{13,12},{14,15},{17,16},{18,... | collective-permute-start | bytes 516104 | tf_op jit(solution)/shard_map/ppermute | solution.py:596
  197.5 5.6 %collective-permute-start.38 = (bf16[96,896]{1,0:T(8,128)(2,1)S(1)}, bf16[96,896]{1,0:T(8,128)(2,1)S(1)}, u32[]{:S(2)}, u32[]{:S(2)}) collective-permute-start(bf16[96,896]{1,0:T(8,128)(2,1)S(1)} %get-tuple-element.39), channel_id=1, source_target_pairs={{0,2},{1,3},{4,6},{5,7},{11,9},{9,11},{15,13},{13,15},{18,16},{16,... | collective-permute-start | bytes 516104 | tf_op jit(solution)/shard_map/ppermute | solution.py:596
  207.9 3.2 %collective-permute-done.39.refs_3_ = bf16[96,896]{1,0:T(8,128)(2,1)S(1)} collective-permute-done((bf16[96,896]{1,0:T(8,128)(2,1)S(1)}, bf16[96,896]{1,0:T(8,128)(2,1)S(1)}, u32[]{:S(2)}, u32[]{:S(2)}) %collective-permute-start.39) | collective-permute-done | bytes 172064 | tf_op jit(solution)/shard_map/ppermute | solution.py:596
  211.9 3.8 %collective-permute-start.42 = (bf16[96,896]{1,0:T(8,128)(2,1)S(1)}, bf16[96,896]{1,0:T(8,128)(2,1)S(1)}, u32[]{:S(2)}, u32[]{:S(2)}) collective-permute-start(bf16[96,896]{1,0:T(8,128)(2,1)S(1)} %get-tuple-element.43), channel_id=1, source_target_pairs={{0,3},{4,7},{9,10},{13,14},{18,17},{22,21},{27,24},{31,28}} | collective-permute-start | bytes 516104 | tf_op jit(solution)/shard_map/ppermute | solution.py:596
  217.1 2.7 %collective-permute-done.42.refs_2_ = bf16[96,896]{1,0:T(8,128)(2,1)S(1)} collective-permute-done((bf16[96,896]{1,0:T(8,128)(2,1)S(1)}, bf16[96,896]{1,0:T(8,128)(2,1)S(1)}, u32[]{:S(2)}, u32[]{:S(2)}) %collective-permute-start.42) | collective-permute-done | bytes 172064 | tf_op jit(solution)/shard_map/ppermute | solution.py:596
  (120 shorter events, 58.7 us)
Async XLA Ops:
  19.0 16.6 %collective-permute-start.4 = (bf16[4,144,512]{2,1,0:T(8,128)(2,1)}, bf16[4,144,512]{2,1,0:T(8,128)(2,1)S(1)}, u32[]{:S(2)}, u32[]{:S(2)}) collective-permute-start(bf16[4,144,512]{2,1,0:T(8,128)(2,1)} %payload.1), channel_id=1, source_target_pairs={{8,0},{16,8},{24,16},{28,24},{20,28},{12,20},{4,12},{0,4},{9,1},{1... | collective-permute-start | bytes 1769480 | tf_op jit(solution)/shard_map/ppermute | solution.py:596
  22.0 15.3 %collective-permute-start = (bf16[4,144,512]{2,1,0:T(8,128)(2,1)}, bf16[4,144,512]{2,1,0:T(8,128)(2,1)S(1)}, u32[]{:S(2)}, u32[]{:S(2)}) collective-permute-start(bf16[4,144,512]{2,1,0:T(8,128)(2,1)} %payload.1), channel_id=1, source_target_pairs={{0,8},{8,16},{16,24},{24,28},{28,20},{20,12},{12,4},{4,0},{1,9},{9... | collective-permute-start | bytes 1769480 | tf_op jit(solution)/shard_map/ppermute | solution.py:596
  35.6 14.5 %collective-permute-start.5 = (bf16[4,144,512]{2,1,0:T(8,128)(2,1)S(1)}, bf16[4,144,512]{2,1,0:T(8,128)(2,1)S(1)}, u32[]{:S(2)}, u32[]{:S(2)}) collective-permute-start(bf16[4,144,512]{2,1,0:T(8,128)(2,1)S(1)} %collective-permute-done.4.b_ref), channel_id=1, source_target_pairs={{8,0},{16,8},{24,16},{28,24},{20,28},{12,20},{4,12},{0,4},{9,1},{1... | collective-permute-start | bytes 1769480 | tf_op jit(solution)/shard_map/ppermute | solution.py:596
  37.3 14.2 %collective-permute-start.1 = (bf16[4,144,512]{2,1,0:T(8,128)(2,1)S(1)}, bf16[4,144,512]{2,1,0:T(8,128)(2,1)S(1)}, u32[]{:S(2)}, u32[]{:S(2)}) collective-permute-start(bf16[4,144,512]{2,1,0:T(8,128)(2,1)S(1)} %collective-permute-done.a_ref), channel_id=1, source_target_pairs={{0,8},{8,16},{16,24},{24,28},{28,20},{20,12},{12,4},{4,0},{1,9},{9... | collective-permute-start | bytes 1769480 | tf_op jit(solution)/shard_map/ppermute | solution.py:596
  50.1 13.6 %collective-permute-start.6 = (bf16[4,144,512]{2,1,0:T(8,128)(2,1)S(1)}, bf16[4,144,512]{2,1,0:T(8,128)(2,1)S(1)}, u32[]{:S(2)}, u32[]{:S(2)}) collective-permute-start(bf16[4,144,512]{2,1,0:T(8,128)(2,1)S(1)} %collective-permute-done.5.b_ref), channel_id=1, source_target_pairs={{8,0},{16,8},{24,16},{28,24},{20,28},{12,20},{4,12},{0,4},{9,1},{1... | collective-permute-start | bytes 1769480 | tf_op jit(solution)/shard_map/ppermute | solution.py:596
  56.0 13.5 %collective-permute-start.12 = (bf16[2,144,512]{2,1,0:T(8,128)(2,1)S(1)}, bf16[2,144,512]{2,1,0:T(8,128)(2,1)S(1)}, u32[]{:S(2)}, u32[]{:S(2)}) collective-permute-start(bf16[2,144,512]{2,1,0:T(8,128)(2,1)S(1)} %choose.5.refs_4_.refs_8_), channel_id=1, source_target_pairs={{0,2},{1,3},{2,0},{3,1},{4,6},{5,7},{6,4},{7,5},{8,10},{9,11},{10,... | collective-permute-start | bytes 884744 | tf_op jit(solution)/shard_map/ppermute | solution.py:596
  70.6 14.0 %collective-permute-start.18 = (bf16[2,144,512]{2,1,0:T(8,128)(2,1)S(1)}, bf16[2,144,512]{2,1,0:T(8,128)(2,1)S(1)}, u32[]{:S(2)}, u32[]{:S(2)}) collective-permute-start(bf16[2,144,512]{2,1,0:T(8,128)(2,1)S(1)} %choose.7.refs_2_.refs_6_), channel_id=1, source_target_pairs={{0,2},{1,3},{2,0},{3,1},{4,6},{5,7},{6,4},{7,5},{8,10},{9,11},{10,... | collective-permute-start | bytes 884744 | tf_op jit(solution)/shard_map/ppermute | solution.py:596
  71.8 27.4 %collective-permute-start.14 = (bf16[2,144,512]{2,1,0:T(8,128)(2,1)S(1)}, bf16[2,144,512]{2,1,0:T(8,128)(2,1)S(1)}, u32[]{:S(2)}, u32[]{:S(2)}) collective-permute-start(bf16[2,144,512]{2,1,0:T(8,128)(2,1)S(1)} %choose.6.refs_2_.refs_6_), channel_id=1, source_target_pairs={{0,1},{1,0},{2,3},{3,2},{4,5},{5,4},{6,7},{7,6},{8,9},{9,8},{10,11... | collective-permute-start | bytes 884744 | tf_op jit(solution)/shard_map/ppermute | solution.py:596
  73.1 26.4 %collective-permute-start.9 = (bf16[1,144,512]{2,1,0:T(8,128)(2,1)}, bf16[1,144,512]{2,1,0:T(8,128)(2,1)}, u32[]{:S(2)}, u32[]{:S(2)}) collective-permute-start(bf16[1,144,512]{2,1,0:T(8,128)(2,1)} %choose.4.refs_2_), channel_id=1, source_target_pairs={{0,2},{1,3},{2,0},{3,1},{4,6},{5,7},{6,4},{7,5},{8,10},{9,11},{10,... | collective-permute-start | bytes 442376 | tf_op jit(solution)/shard_map/ppermute | solution.py:596
  78.3 31.3 %collective-permute-start.16 = (bf16[2,144,512]{2,1,0:T(8,128)(2,1)S(1)}, bf16[2,144,512]{2,1,0:T(8,128)(2,1)S(1)}, u32[]{:S(2)}, u32[]{:S(2)}) collective-permute-start(bf16[2,144,512]{2,1,0:T(8,128)(2,1)S(1)} %collective-permute-done.15.refs_4_.refs_8_), channel_id=1, source_target_pairs={{0,1},{1,0},{2,3},{3,2},{4,5},{5,4},{6,7},{7,6},{8,9},{9,8},{10,11... | collective-permute-start | bytes 884744 | tf_op jit(solution)/shard_map/ppermute | solution.py:596
  78.3 38.2 %collective-permute-start.17 = (bf16[2,144,512]{2,1,0:T(8,128)(2,1)S(1)}, bf16[2,144,512]{2,1,0:T(8,128)(2,1)S(1)}, u32[]{:S(2)}, u32[]{:S(2)}) collective-permute-start(bf16[2,144,512]{2,1,0:T(8,128)(2,1)S(1)} %choose.7.refs_2_.refs_6_), channel_id=1, source_target_pairs={{0,1},{1,0},{2,3},{3,2},{4,5},{5,4},{6,7},{7,6},{8,9},{9,8},{10,11... | collective-permute-start | bytes 884744 | tf_op jit(solution)/shard_map/ppermute | solution.py:596
  84.6 31.9 %collective-permute-start.19 = (bf16[2,144,512]{2,1,0:T(8,128)(2,1)S(1)}, bf16[2,144,512]{2,1,0:T(8,128)(2,1)S(1)}, u32[]{:S(2)}, u32[]{:S(2)}) collective-permute-start(bf16[2,144,512]{2,1,0:T(8,128)(2,1)S(1)} %collective-permute-done.18.refs_4_.refs_8_), channel_id=1, source_target_pairs={{0,1},{1,0},{2,3},{3,2},{4,5},{5,4},{6,7},{7,6},{8,9},{9,8},{10,11... | collective-permute-start | bytes 884744 | tf_op jit(solution)/shard_map/ppermute | solution.py:596
  85.3 14.5 %all-to-all-start = ((s32[8,1,32]{2,1,0:T(1,128)}), s32[8,1,32]{2,1,0:T(1,128)S(1)}, u32[]{:S(2)}, u32[]{:S(2)}) async-start(s32[8,1,32]{2,1,0:T(1,128)} %broadcast_in_dim.2), calls=%async_computation | async-start | bytes 8192 | tf_op jit(solution)/shard_map/all_to_all | solution.py:604
  99.2 24.5 %collective-permute-start.8 = (bf16[1,144,512]{2,1,0:T(8,128)(2,1)}, bf16[1,144,512]{2,1,0:T(8,128)(2,1)}, u32[]{:S(2)}, u32[]{:S(2)}) collective-permute-start(bf16[1,144,512]{2,1,0:T(8,128)(2,1)} %choose.4.refs_2_), channel_id=1, source_target_pairs={{0,1},{1,0},{2,3},{3,2},{4,5},{5,4},{6,7},{7,6},{8,9},{9,8},{10,11... | collective-permute-start | bytes 442376 | tf_op jit(solution)/shard_map/ppermute | solution.py:596
  99.5 24.3 %collective-permute-start.10 = (bf16[1,144,512]{2,1,0:T(8,128)(2,1)}, bf16[1,144,512]{2,1,0:T(8,128)(2,1)}, u32[]{:S(2)}, u32[]{:S(2)}) collective-permute-start(bf16[1,144,512]{2,1,0:T(8,128)(2,1)} %collective-permute-done.9.refs_4_), channel_id=1, source_target_pairs={{0,1},{1,0},{2,3},{3,2},{4,5},{5,4},{6,7},{7,6},{8,9},{9,8},{10,11... | collective-permute-start | bytes 442376 | tf_op jit(solution)/shard_map/ppermute | solution.py:596
  129.3 19.8 %collective-permute-start.24 = (bf16[96,4096]{1,0:T(8,128)(2,1)S(1)}, bf16[96,4096]{1,0:T(8,128)(2,1)S(1)}, u32[]{:S(2)}, u32[]{:S(2)}) collective-permute-start(bf16[96,4096]{1,0:T(8,128)(2,1)S(1)} %attend_slots.7), channel_id=1, source_target_pairs={{8,0},{16,8},{24,16},{28,24},{20,28},{12,20},{4,12},{0,4},{9,1},{1... | collective-permute-start | bytes 2359304 | tf_op jit(solution)/shard_map/ppermute | solution.py:596
  131.4 19.5 %collective-permute-start.20 = (bf16[96,4096]{1,0:T(8,128)(2,1)S(1)}, bf16[96,4096]{1,0:T(8,128)(2,1)S(1)}, u32[]{:S(2)}, u32[]{:S(2)}) collective-permute-start(bf16[96,4096]{1,0:T(8,128)(2,1)S(1)} %attend_slots.7), channel_id=1, source_target_pairs={{0,8},{8,16},{16,24},{24,28},{28,20},{20,12},{12,4},{4,0},{1,9},{9... | collective-permute-start | bytes 2359304 | tf_op jit(solution)/shard_map/ppermute | solution.py:596
  149.1 18.9 %collective-permute-start.25 = (bf16[96,4096]{1,0:T(8,128)(2,1)S(1)}, bf16[96,4096]{1,0:T(8,128)(2,1)S(1)}, u32[]{:S(2)}, u32[]{:S(2)}) collective-permute-start(bf16[96,4096]{1,0:T(8,128)(2,1)S(1)} %collective-permute-done.24), channel_id=1, source_target_pairs={{8,0},{16,8},{24,16},{28,24},{20,28},{12,20},{4,12},{0,4},{9,1},{1... | collective-permute-start | bytes 2359304 | tf_op jit(solution)/shard_map/ppermute | solution.py:596
  150.9 18.7 %collective-permute-start.21 = (bf16[96,4096]{1,0:T(8,128)(2,1)S(1)}, bf16[96,4096]{1,0:T(8,128)(2,1)S(1)}, u32[]{:S(2)}, u32[]{:S(2)}) collective-permute-start(bf16[96,4096]{1,0:T(8,128)(2,1)S(1)} %collective-permute-done.20), channel_id=1, source_target_pairs={{0,8},{8,16},{16,24},{24,28},{28,20},{20,12},{12,4},{4,0},{1,9},{9... | collective-permute-start | bytes 2359304 | tf_op jit(solution)/shard_map/ppermute | solution.py:596
  153.1 18.8 %collective-permute-start.30 = (bf16[96,896]{1,0:T(8,128)(2,1)S(1)}, bf16[96,896]{1,0:T(8,128)(2,1)S(1)}, u32[]{:S(2)}, u32[]{:S(2)}) collective-permute-start(bf16[96,896]{1,0:T(8,128)(2,1)S(1)} %get-tuple-element.26), channel_id=1, source_target_pairs={{3,0},{7,4},{10,9},{14,13},{17,18},{21,22},{24,27},{28,31}} | collective-permute-start | bytes 516104 | tf_op jit(solution)/shard_map/ppermute | solution.py:596
  154.4 17.6 %collective-permute-start.29 = (bf16[96,896]{1,0:T(8,128)(2,1)S(1)}, bf16[96,896]{1,0:T(8,128)(2,1)S(1)}, u32[]{:S(2)}, u32[]{:S(2)}) collective-permute-start(bf16[96,896]{1,0:T(8,128)(2,1)S(1)} %get-tuple-element.26), channel_id=1, source_target_pairs={{2,0},{6,4},{11,9},{15,13},{16,18},{20,22},{25,27},{29,31}} | collective-permute-start | bytes 516104 | tf_op jit(solution)/shard_map/ppermute | solution.py:596
  155.7 16.3 %collective-permute-start.28 = (bf16[96,896]{1,0:T(8,128)(2,1)S(1)}, bf16[96,896]{1,0:T(8,128)(2,1)S(1)}, u32[]{:S(2)}, u32[]{:S(2)}) collective-permute-start(bf16[96,896]{1,0:T(8,128)(2,1)S(1)} %get-tuple-element.26), channel_id=1, source_target_pairs={{1,0},{5,4},{8,9},{12,13},{19,18},{23,22},{26,27},{30,31}} | collective-permute-start | bytes 516104 | tf_op jit(solution)/shard_map/ppermute | solution.py:596
  168.1 23.8 %collective-permute-start.26 = (bf16[96,4096]{1,0:T(8,128)(2,1)S(1)}, bf16[96,4096]{1,0:T(8,128)(2,1)S(1)}, u32[]{:S(2)}, u32[]{:S(2)}) collective-permute-start(bf16[96,4096]{1,0:T(8,128)(2,1)S(1)} %collective-permute-done.25), channel_id=1, source_target_pairs={{8,0},{16,8},{24,16},{28,24},{20,28},{12,20},{4,12},{0,4},{9,1},{1... | collective-permute-start | bytes 2359304 | tf_op jit(solution)/shard_map/ppermute | solution.py:596
  169.6 23.9 %collective-permute-start.22 = (bf16[96,4096]{1,0:T(8,128)(2,1)S(1)}, bf16[96,4096]{1,0:T(8,128)(2,1)S(1)}, u32[]{:S(2)}, u32[]{:S(2)}) collective-permute-start(bf16[96,4096]{1,0:T(8,128)(2,1)S(1)} %collective-permute-done.21), channel_id=1, source_target_pairs={{0,8},{8,16},{16,24},{24,28},{28,20},{20,12},{12,4},{4,0},{1,9},{9... | collective-permute-start | bytes 2359304 | tf_op jit(solution)/shard_map/ppermute | solution.py:596
  (32 other events, 327.4 us)
where the time goes:
time: 223 us; the launch traced here: 222 us
  waiting for transfers between devices  85.3 us (38%)
  Pallas kernels  58.7 us (26%)
  starting transfers between devices  55.5 us (25%)
  local copies, waits for them, and re-layouts  13.5 us (6%)
  matrix products  7.98 us (4%)
    ppermute x43, waiting for transfers between devices, move(): return lax.ppermute(x, axis, pairs)  85.3 us
    ppermute x43, starting transfers between devices, move(): return lax.ppermute(x, axis, pairs)  50 us
    pallas_call x4, Pallas kernels, attend_slots(): pl.pallas_call(functools.partial(slots_kernel, plan, own, heads, bundles,...  29.4 us
    pallas_call x1, Pallas kernels, payload_of(): pl.pallas_call(payload_kernel, out_shape=jax.ShapeDtypeStruct((slots, row...  19 us
    dot_general x5, matrix products, project(): return jnp.dot(x, w_out, preferred_element_type=jnp.float32)  7.98 us
    reshape x1, local copies, waits for them, and re-layouts, local_ring(): q = q_latent.reshape(bundles, roll_count * local_heads, -1)  5.87 us
    all_to_all x1, starting transfers between devices, local_ring(): lax.all_to_all(jnp.broadcast_to(facts[None], (ranks, width)), 'dp', split...  5.5 us
  transfers between devices with their start and end apart: 44, of which 15 were waited for; matrix products, arithmetic and copies ran while one was open for 8% of the time, Pallas kernels for 14%

commit v1 on v0

--- a/solution.py
+++ b/solution.py
@@ -218,6 +218,10 @@
     return jnp.sum(got.astype(jnp.float32), axis=0).astype(jnp.bfloat16)
 
 
+def in_hbm(x):
+    return pltpu.with_memory_space_constraint(x, pltpu.MemorySpace.HBM)
+
+
 def ring_tables(ranks):
     order = ring_order(ranks)
     where = [order.index(r) for r in range(ranks)]
@@ -290,10 +294,11 @@
         payload_kernel,
         out_shape=jax.ShapeDtypeStruct((slots, rows, wide), cache_latent.dtype),
         in_specs=[pl.BlockSpec(memory_space=pl.ANY)] * 2,
-        out_specs=pl.BlockSpec(memory_space=pl.ANY),
+        out_specs=pl.BlockSpec(memory_space=pltpu.MemorySpace.VMEM),
         scratch_shapes=[pltpu.SemaphoreType.DMA((2,))],
+        compiler_params=pltpu.CompilerParams(vmem_limit_bytes=4 * 2**20),
         name="payload",
-    )(cache_latent, cache_rope)
+    )(in_hbm(cache_latent), in_hbm(cache_rope))
 
 
 def choose_kernel(cut, column, table, a_ref, b_ref, out_ref):
@@ -404,10 +409,6 @@
             into[pl.ds(at, n), h * value_width : (h + 1) * value_width] = v
         if final:
             out_ref[...] = into[...].astype(out_ref.dtype)
-
-
-def in_hbm(x):
-    return pltpu.with_memory_space_constraint(x, pltpu.MemorySpace.HBM)
 
 
 def attend_slots(plan, table, info, q, qr, full, parts, heads, bundles, w_uv, earlier=None):
@@ -541,9 +542,11 @@
     return to_send, outs[sends], outs[sends + 1] if previous is not None else None
 
 
-def finish_kernel(heads, per_head, columns, roll, table, info, seen, own, *refs):
-    got, before, out, total = refs[: heads - 1], refs[heads - 1], refs[heads], refs[heads + 1]
-    add_in(table, per_head, columns, own, got, before, total)
+def finish_kernel(heads, per_head, steps, roll, table, info, seen, before, *refs):
+    out, total = refs[heads * len(steps) :]
+    for i, columns in enumerate(steps):
+        own, *got = refs[heads * i : heads * (i + 1)]
+        add_in(table, per_head, columns, own, got, total if i else before, total)
     n = total.shape[1]
     slots = n // roll
     to = lax.broadcasted_iota(jnp.int32, (n, n), 0)
@@ -562,19 +565,21 @@
         out[pl.ds(y * n, n), :] = moved.astype(out.dtype)
 
 
-def finish(table, info, seen, heads, per_head, columns, roll, own, got, total):
-    n, wide = own.shape
+def finish(table, info, seen, heads, per_head, roll, total, states):
+    _, n, wide = total.shape
+    steps = [state[0] for state in states]
+    args = [x for _, own, got in states for x in (own, *got)]
     vmem = pl.BlockSpec(memory_space=pltpu.MemorySpace.VMEM)
     smem = pl.BlockSpec(memory_space=pltpu.MemorySpace.SMEM)
     return pl.pallas_call(
-        functools.partial(finish_kernel, heads, per_head, columns, roll),
+        functools.partial(finish_kernel, heads, per_head, steps, roll),
         out_shape=jax.ShapeDtypeStruct((per_head * n, wide), jnp.bfloat16),
-        in_specs=[smem] * 3 + [vmem] * (heads + 1),
+        in_specs=[smem] * 3 + [vmem] * (1 + len(args)),
         out_specs=vmem,
         scratch_shapes=[pltpu.VMEM((per_head, n, wide), jnp.float32)],
         compiler_params=pltpu.CompilerParams(vmem_limit_bytes=6 * 2**20),
         name="finish",
-    )(table, info, seen, own, *got, total)
+    )(table, info, seen, total, *args)
 
 
 def local_ring(
@@ -674,8 +679,9 @@
     left = move(fore[:, :half], ahead)
     right = move(back[:, half:], behind)
     ends = project(jnp.concatenate([left, right], axis=1))
-    columns, own, got, total = settle([2 * last - 1], ends, state)
-    return finish(table, info, seen, heads, per_head, columns, roll_count, own, got, total)
+    *before, total = state
+    *final, _ = settle([2 * last - 1], ends, None)
+    return finish(table, info, seen, heads, per_head, roll_count, total, [before, final])
 
 
 def local(*args):

time: 223 us -> 199 us (0.89)
  Pallas kernels: 58.7 us -> 40.7 us
  starting transfers between devices: 55.5 us -> 52.9 us
  waiting for transfers between devices: 85.3 us -> 82.9 us
    pallas_call x1, Pallas kernels: 19 us -> 1.06 us  [payload_of(): pl.pallas_call(payload_kernel, out_shape=jax.ShapeDtypeStruct((slots, row...]
    ppermute x43, starting transfers between devices: 50 us -> 47.4 us  [move(): return lax.ppermute(x, axis, pairs)]
    ppermute x43, waiting for transfers between devices: 85.3 us -> 82.9 us  [move(): return lax.ppermute(x, axis, pairs)]
  transfers between devices with their start and end apart: 44 -> 44, of which waited for: 15 -> 14; matrix products, arithmetic and copies ran while one was open for 8% -> 9% of each run, Pallas kernels for 14% -> 16%
where the time goes in v1:
time: 199 us
  waiting for transfers between devices  82.9 us (42%)
  starting transfers between devices  52.9 us (27%)
  Pallas kernels  40.7 us (20%)
  local copies, waits for them, and re-layouts  13.5 us (7%)
  matrix products  7.99 us (4%)
    ppermute x43, waiting for transfers between devices, move(): return lax.ppermute(x, axis, pairs)  82.9 us
    ppermute x43, starting transfers between devices, move(): return lax.ppermute(x, axis, pairs)  47.4 us
    pallas_call x4, Pallas kernels, attend_slots(): pl.pallas_call(functools.partial(slots_kernel, plan, own, heads, bundles,...  29.4 us
    dot_general x5, matrix products, project(): return jnp.dot(x, w_out, preferred_element_type=jnp.float32)  7.99 us
    reshape x1, local copies, waits for them, and re-layouts, local_ring(): q = q_latent.reshape(bundles, roll_count * local_heads, -1)  5.87 us
    all_to_all x1, starting transfers between devices, local_ring(): lax.all_to_all(jnp.broadcast_to(facts[None], (ranks, width)), 'dp', split...  5.5 us
    unnamed x24, local copies, waits for them, and re-layouts  4.33 us
  transfers between devices with their start and end apart: 44, of which 14 were waited for; matrix products, arithmetic and copies ran while one was open for 9% of the time, Pallas kernels for 16%

profile of v1, /device:TPU:0, one launch (start us, length us, event | category | flops | bytes accessed | tf_op | source)
XLA Modules:
  0.0 198.6 jit_solution(15495629044998259791)
XLA Ops:
  1.1 3.0 %collective-permute-start.4 = (bf16[4,144,512]{2,1,0:T(8,128)(2,1)S(1)}, bf16[4,144,512]{2,1,0:T(8,128)(2,1)S(1)}, u32[]{:S(2)}, u32[]{:S(2)}) collective-permute-start(bf16[4,144,512]{2,1,0:T(8,128)(2,1)S(1)} %payload.1), channel_id=1, source_target_pairs={{8,0},{16,8},{24,16},{28,24},{20,28},{12,20},{4,12},{0,4},{9,1},{1... | collective-permute-start | bytes 1769480 | tf_op jit(solution)/shard_map/ppermute | solution.py:601
  4.2 13.3 %collective-permute-done.4.b_ref = bf16[4,144,512]{2,1,0:T(8,128)(2,1)S(1)} collective-permute-done((bf16[4,144,512]{2,1,0:T(8,128)(2,1)S(1)}, bf16[4,144,512]{2,1,0:T(8,128)(2,1)S(1)}, u32[]{:S(2)}, u32[]{:S(2)}) %collective-permute-start.4) | collective-permute-done | bytes 589856 | tf_op jit(solution)/shard_map/ppermute | solution.py:601
  20.4 11.6 %collective-permute-done.5.b_ref = bf16[4,144,512]{2,1,0:T(8,128)(2,1)S(1)} collective-permute-done((bf16[4,144,512]{2,1,0:T(8,128)(2,1)S(1)}, bf16[4,144,512]{2,1,0:T(8,128)(2,1)S(1)}, u32[]{:S(2)}, u32[]{:S(2)}) %collective-permute-start.5) | collective-permute-done | bytes 589856 | tf_op jit(solution)/shard_map/ppermute | solution.py:601
  39.3 6.3 %collective-permute-done.6.b_ref = bf16[4,144,512]{2,1,0:T(8,128)(2,1)S(1)} collective-permute-done((bf16[4,144,512]{2,1,0:T(8,128)(2,1)S(1)}, bf16[4,144,512]{2,1,0:T(8,128)(2,1)S(1)}, u32[]{:S(2)}, u32[]{:S(2)}) %collective-permute-start.6) | collective-permute-done | bytes 589856 | tf_op jit(solution)/shard_map/ppermute | solution.py:601
  56.5 3.7 %collective-permute-done.15.refs_4_.refs_8_ = bf16[2,144,512]{2,1,0:T(8,128)(2,1)S(1)} collective-permute-done((bf16[2,144,512]{2,1,0:T(8,128)(2,1)S(1)}, bf16[2,144,512]{2,1,0:T(8,128)(2,1)S(1)}, u32[]{:S(2)}, u32[]{:S(2)}) %collective-permute-start.15) | collective-permute-done | bytes 294944 | tf_op jit(solution)/shard_map/ppermute | solution.py:601
  60.7 5.8 %collective-permute-done.18.refs_4_.refs_8_ = bf16[2,144,512]{2,1,0:T(8,128)(2,1)S(1)} collective-permute-done((bf16[2,144,512]{2,1,0:T(8,128)(2,1)S(1)}, bf16[2,144,512]{2,1,0:T(8,128)(2,1)S(1)}, u32[]{:S(2)}, u32[]{:S(2)}) %collective-permute-start.18) | collective-permute-done | bytes 294944 | tf_op jit(solution)/shard_map/ppermute | solution.py:601
  67.2 5.5 %all-to-all-start = ((s32[8,1,32]{2,1,0:T(1,128)}), s32[8,1,32]{2,1,0:T(1,128)S(1)}, u32[]{:S(2)}, u32[]{:S(2)}) async-start(s32[8,1,32]{2,1,0:T(1,128)} %broadcast_in_dim.2), calls=%async_computation | async-start | bytes 8192 | tf_op jit(solution)/shard_map/all_to_all | solution.py:609
  72.7 2.6 %reshape.13.refs_1_ = bf16[8,384,64]{2,1,0:T(8,128)(2,1)} reshape(bf16[96,2048]{1,0:T(8,128)(2,1)} %param.12) | data formatting | bytes 786432 | tf_op jit(solution)/shard_map/reshape | solution.py:615
  75.2 5.9 %reshape.12.refs_0_ = bf16[8,384,512]{2,1,0:T(8,128)(2,1)} reshape(bf16[96,16384]{1,0:T(8,128)(2,1)} %param.11) | data formatting | bytes 6291456 | tf_op jit(solution)/shard_map/reshape | solution.py:614
  81.6 9.8 %attend_slots.4.refs_6_ = f32[36,4096]{1,0:T(8,128)S(1)} custom-call(s32[8,8]{1,0:T(8,128)S(1)} %copy-done.2, s32[8,1,32]{2,1,0:T(1,128)S(1)} %broadcast_maximum_fusion.info, bf16[8,384,512]{2,1,0:T(8,128)(2,1)} %reshape.12.refs_0_, bf16[8,384,64]{2,1,0:T(8,128)(2,1)} %reshape.13.refs_1_, bf16[4,512,512]{2,1,0:T(8,128)(2,1)} %refs_2_.1, ...), custom_call_target="tpu_custom_call" | custom-call | tf_op jit(solution)/shard_map/attend_slots/pallas_call | solution.py:464
  91.4 6.9 %attend_slots.5.refs_7_ = f32[24,4096]{1,0:T(8,128)S(1)} custom-call(s32[8,8]{1,0:T(8,128)S(1)} %copy-done.2, s32[8,1,32]{2,1,0:T(1,128)S(1)} %broadcast_maximum_fusion.info, bf16[8,384,512]{2,1,0:T(8,128)(2,1)} %reshape.12.refs_0_, bf16[8,384,64]{2,1,0:T(8,128)(2,1)} %reshape.13.refs_1_, bf16[2,144,512]{2,1,0:T(8,128)(2,1)S(1)} %choose.6.refs_2_.refs_6_, ...), custom_call_target="tpu_custom_call" | custom-call | tf_op jit(solution)/shard_map/attend_slots/pallas_call | solution.py:464
  98.4 7.2 %attend_slots.6.refs_8_ = f32[24,4096]{1,0:T(8,128)S(1)} custom-call(s32[8,8]{1,0:T(8,128)S(1)} %copy-done.2, s32[8,1,32]{2,1,0:T(1,128)S(1)} %broadcast_maximum_fusion.info, bf16[8,384,512]{2,1,0:T(8,128)(2,1)} %reshape.12.refs_0_, bf16[8,384,64]{2,1,0:T(8,128)(2,1)} %reshape.13.refs_1_, bf16[2,144,512]{2,1,0:T(8,128)(2,1)S(1)} %choose.7.refs_2_.refs_6_, ...), custom_call_target="tpu_custom_call" | custom-call | tf_op jit(solution)/shard_map/attend_slots/pallas_call | solution.py:464
  105.7 5.5 %attend_slots.7 = bf16[96,4096]{1,0:T(8,128)(2,1)S(1)} custom-call(s32[8,8]{1,0:T(8,128)S(1)} %copy-done.2, s32[8,1,32]{2,1,0:T(1,128)S(1)} %broadcast_maximum_fusion.info, bf16[8,384,512]{2,1,0:T(8,128)(2,1)} %reshape.12.refs_0_, bf16[8,384,64]{2,1,0:T(8,128)(2,1)} %reshape.13.refs_1_, bf16[1,144,512]{2,1,0:T(8,128)(2,1)} %choose.4.refs_2_, ...), custom_call_target="tpu_custom_call" | custom-call | tf_op jit(solution)/shard_map/attend_slots/pallas_call | solution.py:464
  111.2 2.1 %collective-permute-start.23 = (bf16[96,4096]{1,0:T(8,128)(2,1)S(1)}, bf16[96,4096]{1,0:T(8,128)(2,1)S(1)}, u32[]{:S(2)}, u32[]{:S(2)}) collective-permute-start(bf16[96,4096]{1,0:T(8,128)(2,1)S(1)} %attend_slots.7), channel_id=1, source_target_pairs={{8,0},{16,8},{24,16},{28,24},{20,28},{12,20},{4,12},{0,4},{9,1},{1... | collective-permute-start | bytes 2359304 | tf_op jit(solution)/shard_map/ppermute | solution.py:601
  113.3 17.7 %collective-permute-done.23 = bf16[96,4096]{1,0:T(8,128)(2,1)S(1)} collective-permute-done((bf16[96,4096]{1,0:T(8,128)(2,1)S(1)}, bf16[96,4096]{1,0:T(8,128)(2,1)S(1)}, u32[]{:S(2)}, u32[]{:S(2)}) %collective-permute-start.23) | collective-permute-done | bytes 786464 | tf_op jit(solution)/shard_map/ppermute | solution.py:601
  138.9 11.1 %collective-permute-done.24 = bf16[96,4096]{1,0:T(8,128)(2,1)S(1)} collective-permute-done((bf16[96,4096]{1,0:T(8,128)(2,1)S(1)}, bf16[96,4096]{1,0:T(8,128)(2,1)S(1)}, u32[]{:S(2)}, u32[]{:S(2)}) %collective-permute-start.24) | collective-permute-done | bytes 786464 | tf_op jit(solution)/shard_map/ppermute | solution.py:601
  154.7 1.9 collective-permute-start.29
  161.1 4.7 %collective-permute-done.30.refs_2_ = bf16[96,896]{1,0:T(8,128)(2,1)S(1)} collective-permute-done((bf16[96,896]{1,0:T(8,128)(2,1)S(1)}, bf16[96,896]{1,0:T(8,128)(2,1)S(1)}, u32[]{:S(2)}, u32[]{:S(2)}) %collective-permute-start.30) | collective-permute-done | bytes 172064 | tf_op jit(solution)/shard_map/ppermute | solution.py:601
  165.7 2.7 %collective-permute-done.31.refs_3_ = bf16[96,896]{1,0:T(8,128)(2,1)S(1)} collective-permute-done((bf16[96,896]{1,0:T(8,128)(2,1)S(1)}, bf16[96,896]{1,0:T(8,128)(2,1)S(1)}, u32[]{:S(2)}, u32[]{:S(2)}) %collective-permute-start.31) | collective-permute-done | bytes 172064 | tf_op jit(solution)/shard_map/ppermute | solution.py:601
  169.3 2.5 %collective-permute-start.32 = (bf16[96,896]{1,0:T(8,128)(2,1)S(1)}, bf16[96,896]{1,0:T(8,128)(2,1)S(1)}, u32[]{:S(2)}, u32[]{:S(2)}) collective-permute-start(bf16[96,896]{1,0:T(8,128)(2,1)S(1)} %get-tuple-element.32), channel_id=1, source_target_pairs={{0,1},{3,2},{4,5},{7,6},{9,8},{10,11},{13,12},{14,15},{17,16},{18,... | collective-permute-start | bytes 516104 | tf_op jit(solution)/shard_map/ppermute | solution.py:601
  179.4 5.6 %collective-permute-start.36 = (bf16[96,896]{1,0:T(8,128)(2,1)S(1)}, bf16[96,896]{1,0:T(8,128)(2,1)S(1)}, u32[]{:S(2)}, u32[]{:S(2)}) collective-permute-start(bf16[96,896]{1,0:T(8,128)(2,1)S(1)} %get-tuple-element.39), channel_id=1, source_target_pairs={{0,2},{1,3},{4,6},{5,7},{11,9},{9,11},{15,13},{13,15},{18,16},{16,... | collective-permute-start | bytes 516104 | tf_op jit(solution)/shard_map/ppermute | solution.py:601
  191.4 2.1 %collective-permute-done.37.refs_3_ = bf16[96,896]{1,0:T(8,128)(2,1)S(1)} collective-permute-done((bf16[96,896]{1,0:T(8,128)(2,1)S(1)}, bf16[96,896]{1,0:T(8,128)(2,1)S(1)}, u32[]{:S(2)}, u32[]{:S(2)}) %collective-permute-start.37) | collective-permute-done | bytes 172064 | tf_op jit(solution)/shard_map/ppermute | solution.py:601
  193.5 3.2 %collective-permute-done.42.refs_7_ = bf16[96,896]{1,0:T(8,128)(2,1)S(1)} collective-permute-done((bf16[96,896]{1,0:T(8,128)(2,1)S(1)}, bf16[96,896]{1,0:T(8,128)(2,1)S(1)}, u32[]{:S(2)}, u32[]{:S(2)}) %collective-permute-start.42) | collective-permute-done | bytes 172064 | tf_op jit(solution)/shard_map/ppermute | solution.py:601
  196.7 1.9 finish.1
  (120 shorter events, 55.5 us)
Async XLA Ops:
  1.1 16.4 %collective-permute-start.4 = (bf16[4,144,512]{2,1,0:T(8,128)(2,1)S(1)}, bf16[4,144,512]{2,1,0:T(8,128)(2,1)S(1)}, u32[]{:S(2)}, u32[]{:S(2)}) collective-permute-start(bf16[4,144,512]{2,1,0:T(8,128)(2,1)S(1)} %payload.1), channel_id=1, source_target_pairs={{8,0},{16,8},{24,16},{28,24},{20,28},{12,20},{4,12},{0,4},{9,1},{1... | collective-permute-start | bytes 1769480 | tf_op jit(solution)/shard_map/ppermute | solution.py:601
  4.1 15.1 %collective-permute-start = (bf16[4,144,512]{2,1,0:T(8,128)(2,1)S(1)}, bf16[4,144,512]{2,1,0:T(8,128)(2,1)S(1)}, u32[]{:S(2)}, u32[]{:S(2)}) collective-permute-start(bf16[4,144,512]{2,1,0:T(8,128)(2,1)S(1)} %payload.1), channel_id=1, source_target_pairs={{0,8},{8,16},{16,24},{24,28},{28,20},{20,12},{12,4},{4,0},{1,9},{9... | collective-permute-start | bytes 1769480 | tf_op jit(solution)/shard_map/ppermute | solution.py:601
  17.5 14.5 %collective-permute-start.5 = (bf16[4,144,512]{2,1,0:T(8,128)(2,1)S(1)}, bf16[4,144,512]{2,1,0:T(8,128)(2,1)S(1)}, u32[]{:S(2)}, u32[]{:S(2)}) collective-permute-start(bf16[4,144,512]{2,1,0:T(8,128)(2,1)S(1)} %collective-permute-done.4.b_ref), channel_id=1, source_target_pairs={{8,0},{16,8},{24,16},{28,24},{20,28},{12,20},{4,12},{0,4},{9,1},{1... | collective-permute-start | bytes 1769480 | tf_op jit(solution)/shard_map/ppermute | solution.py:601
  19.2 14.2 %collective-permute-start.1 = (bf16[4,144,512]{2,1,0:T(8,128)(2,1)S(1)}, bf16[4,144,512]{2,1,0:T(8,128)(2,1)S(1)}, u32[]{:S(2)}, u32[]{:S(2)}) collective-permute-start(bf16[4,144,512]{2,1,0:T(8,128)(2,1)S(1)} %collective-permute-done.a_ref), channel_id=1, source_target_pairs={{0,8},{8,16},{16,24},{24,28},{28,20},{20,12},{12,4},{4,0},{1,9},{9... | collective-permute-start | bytes 1769480 | tf_op jit(solution)/shard_map/ppermute | solution.py:601
  32.0 13.6 %collective-permute-start.6 = (bf16[4,144,512]{2,1,0:T(8,128)(2,1)S(1)}, bf16[4,144,512]{2,1,0:T(8,128)(2,1)S(1)}, u32[]{:S(2)}, u32[]{:S(2)}) collective-permute-start(bf16[4,144,512]{2,1,0:T(8,128)(2,1)S(1)} %collective-permute-done.5.b_ref), channel_id=1, source_target_pairs={{8,0},{16,8},{24,16},{28,24},{20,28},{12,20},{4,12},{0,4},{9,1},{1... | collective-permute-start | bytes 1769480 | tf_op jit(solution)/shard_map/ppermute | solution.py:601
  37.9 13.5 %collective-permute-start.12 = (bf16[2,144,512]{2,1,0:T(8,128)(2,1)S(1)}, bf16[2,144,512]{2,1,0:T(8,128)(2,1)S(1)}, u32[]{:S(2)}, u32[]{:S(2)}) collective-permute-start(bf16[2,144,512]{2,1,0:T(8,128)(2,1)S(1)} %choose.5.refs_4_.refs_8_), channel_id=1, source_target_pairs={{0,2},{1,3},{2,0},{3,1},{4,6},{5,7},{6,4},{7,5},{8,10},{9,11},{10,... | collective-permute-start | bytes 884744 | tf_op jit(solution)/shard_map/ppermute | solution.py:601
  52.4 14.0 %collective-permute-start.18 = (bf16[2,144,512]{2,1,0:T(8,128)(2,1)S(1)}, bf16[2,144,512]{2,1,0:T(8,128)(2,1)S(1)}, u32[]{:S(2)}, u32[]{:S(2)}) collective-permute-start(bf16[2,144,512]{2,1,0:T(8,128)(2,1)S(1)} %choose.7.refs_2_.refs_6_), channel_id=1, source_target_pairs={{0,2},{1,3},{2,0},{3,1},{4,6},{5,7},{6,4},{7,5},{8,10},{9,11},{10,... | collective-permute-start | bytes 884744 | tf_op jit(solution)/shard_map/ppermute | solution.py:601
  53.7 27.4 %collective-permute-start.14 = (bf16[2,144,512]{2,1,0:T(8,128)(2,1)S(1)}, bf16[2,144,512]{2,1,0:T(8,128)(2,1)S(1)}, u32[]{:S(2)}, u32[]{:S(2)}) collective-permute-start(bf16[2,144,512]{2,1,0:T(8,128)(2,1)S(1)} %choose.6.refs_2_.refs_6_), channel_id=1, source_target_pairs={{0,1},{1,0},{2,3},{3,2},{4,5},{5,4},{6,7},{7,6},{8,9},{9,8},{10,11... | collective-permute-start | bytes 884744 | tf_op jit(solution)/shard_map/ppermute | solution.py:601
  55.0 26.4 %collective-permute-start.9 = (bf16[1,144,512]{2,1,0:T(8,128)(2,1)}, bf16[1,144,512]{2,1,0:T(8,128)(2,1)}, u32[]{:S(2)}, u32[]{:S(2)}) collective-permute-start(bf16[1,144,512]{2,1,0:T(8,128)(2,1)} %choose.4.refs_2_), channel_id=1, source_target_pairs={{0,2},{1,3},{2,0},{3,1},{4,6},{5,7},{6,4},{7,5},{8,10},{9,11},{10,... | collective-permute-start | bytes 442376 | tf_op jit(solution)/shard_map/ppermute | solution.py:601
  60.1 31.3 %collective-permute-start.16 = (bf16[2,144,512]{2,1,0:T(8,128)(2,1)S(1)}, bf16[2,144,512]{2,1,0:T(8,128)(2,1)S(1)}, u32[]{:S(2)}, u32[]{:S(2)}) collective-permute-start(bf16[2,144,512]{2,1,0:T(8,128)(2,1)S(1)} %collective-permute-done.15.refs_4_.refs_8_), channel_id=1, source_target_pairs={{0,1},{1,0},{2,3},{3,2},{4,5},{5,4},{6,7},{7,6},{8,9},{9,8},{10,11... | collective-permute-start | bytes 884744 | tf_op jit(solution)/shard_map/ppermute | solution.py:601
  60.1 38.2 %collective-permute-start.17 = (bf16[2,144,512]{2,1,0:T(8,128)(2,1)S(1)}, bf16[2,144,512]{2,1,0:T(8,128)(2,1)S(1)}, u32[]{:S(2)}, u32[]{:S(2)}) collective-permute-start(bf16[2,144,512]{2,1,0:T(8,128)(2,1)S(1)} %choose.7.refs_2_.refs_6_), channel_id=1, source_target_pairs={{0,1},{1,0},{2,3},{3,2},{4,5},{5,4},{6,7},{7,6},{8,9},{9,8},{10,11... | collective-permute-start | bytes 884744 | tf_op jit(solution)/shard_map/ppermute | solution.py:601
  66.5 31.9 %collective-permute-start.19 = (bf16[2,144,512]{2,1,0:T(8,128)(2,1)S(1)}, bf16[2,144,512]{2,1,0:T(8,128)(2,1)S(1)}, u32[]{:S(2)}, u32[]{:S(2)}) collective-permute-start(bf16[2,144,512]{2,1,0:T(8,128)(2,1)S(1)} %collective-permute-done.18.refs_4_.refs_8_), channel_id=1, source_target_pairs={{0,1},{1,0},{2,3},{3,2},{4,5},{5,4},{6,7},{7,6},{8,9},{9,8},{10,11... | collective-permute-start | bytes 884744 | tf_op jit(solution)/shard_map/ppermute | solution.py:601
  67.2 14.5 %all-to-all-start = ((s32[8,1,32]{2,1,0:T(1,128)}), s32[8,1,32]{2,1,0:T(1,128)S(1)}, u32[]{:S(2)}, u32[]{:S(2)}) async-start(s32[8,1,32]{2,1,0:T(1,128)} %broadcast_in_dim.2), calls=%async_computation | async-start | bytes 8192 | tf_op jit(solution)/shard_map/all_to_all | solution.py:609
  81.1 24.5 %collective-permute-start.8 = (bf16[1,144,512]{2,1,0:T(8,128)(2,1)}, bf16[1,144,512]{2,1,0:T(8,128)(2,1)}, u32[]{:S(2)}, u32[]{:S(2)}) collective-permute-start(bf16[1,144,512]{2,1,0:T(8,128)(2,1)} %choose.4.refs_2_), channel_id=1, source_target_pairs={{0,1},{1,0},{2,3},{3,2},{4,5},{5,4},{6,7},{7,6},{8,9},{9,8},{10,11... | collective-permute-start | bytes 442376 | tf_op jit(solution)/shard_map/ppermute | solution.py:601
  81.3 24.3 %collective-permute-start.10 = (bf16[1,144,512]{2,1,0:T(8,128)(2,1)}, bf16[1,144,512]{2,1,0:T(8,128)(2,1)}, u32[]{:S(2)}, u32[]{:S(2)}) collective-permute-start(bf16[1,144,512]{2,1,0:T(8,128)(2,1)} %collective-permute-done.9.refs_4_), channel_id=1, source_target_pairs={{0,1},{1,0},{2,3},{3,2},{4,5},{5,4},{6,7},{7,6},{8,9},{9,8},{10,11... | collective-permute-start | bytes 442376 | tf_op jit(solution)/shard_map/ppermute | solution.py:601
  111.2 19.9 %collective-permute-start.23 = (bf16[96,4096]{1,0:T(8,128)(2,1)S(1)}, bf16[96,4096]{1,0:T(8,128)(2,1)S(1)}, u32[]{:S(2)}, u32[]{:S(2)}) collective-permute-start(bf16[96,4096]{1,0:T(8,128)(2,1)S(1)} %attend_slots.7), channel_id=1, source_target_pairs={{8,0},{16,8},{24,16},{28,24},{20,28},{12,20},{4,12},{0,4},{9,1},{1... | collective-permute-start | bytes 2359304 | tf_op jit(solution)/shard_map/ppermute | solution.py:601
  113.2 19.5 %collective-permute-start.20 = (bf16[96,4096]{1,0:T(8,128)(2,1)S(1)}, bf16[96,4096]{1,0:T(8,128)(2,1)S(1)}, u32[]{:S(2)}, u32[]{:S(2)}) collective-permute-start(bf16[96,4096]{1,0:T(8,128)(2,1)S(1)} %attend_slots.7), channel_id=1, source_target_pairs={{0,8},{8,16},{16,24},{24,28},{28,20},{20,12},{12,4},{4,0},{1,9},{9... | collective-permute-start | bytes 2359304 | tf_op jit(solution)/shard_map/ppermute | solution.py:601
  131.0 18.9 %collective-permute-start.24 = (bf16[96,4096]{1,0:T(8,128)(2,1)S(1)}, bf16[96,4096]{1,0:T(8,128)(2,1)S(1)}, u32[]{:S(2)}, u32[]{:S(2)}) collective-permute-start(bf16[96,4096]{1,0:T(8,128)(2,1)S(1)} %collective-permute-done.23), channel_id=1, source_target_pairs={{8,0},{16,8},{24,16},{28,24},{20,28},{12,20},{4,12},{0,4},{9,1},{1... | collective-permute-start | bytes 2359304 | tf_op jit(solution)/shard_map/ppermute | solution.py:601
  132.8 18.7 %collective-permute-start.21 = (bf16[96,4096]{1,0:T(8,128)(2,1)S(1)}, bf16[96,4096]{1,0:T(8,128)(2,1)S(1)}, u32[]{:S(2)}, u32[]{:S(2)}) collective-permute-start(bf16[96,4096]{1,0:T(8,128)(2,1)S(1)} %collective-permute-done.20), channel_id=1, source_target_pairs={{0,8},{8,16},{16,24},{24,28},{28,20},{20,12},{12,4},{4,0},{1,9},{9... | collective-permute-start | bytes 2359304 | tf_op jit(solution)/shard_map/ppermute | solution.py:601
  135.0 18.9 %collective-permute-start.28 = (bf16[96,896]{1,0:T(8,128)(2,1)S(1)}, bf16[96,896]{1,0:T(8,128)(2,1)S(1)}, u32[]{:S(2)}, u32[]{:S(2)}) collective-permute-start(bf16[96,896]{1,0:T(8,128)(2,1)S(1)} %get-tuple-element.25), channel_id=1, source_target_pairs={{3,0},{7,4},{10,9},{14,13},{17,18},{21,22},{24,27},{28,31}} | collective-permute-start | bytes 516104 | tf_op jit(solution)/shard_map/ppermute | solution.py:601
  136.3 17.6 %collective-permute-start.27 = (bf16[96,896]{1,0:T(8,128)(2,1)S(1)}, bf16[96,896]{1,0:T(8,128)(2,1)S(1)}, u32[]{:S(2)}, u32[]{:S(2)}) collective-permute-start(bf16[96,896]{1,0:T(8,128)(2,1)S(1)} %get-tuple-element.25), channel_id=1, source_target_pairs={{2,0},{6,4},{11,9},{15,13},{16,18},{20,22},{25,27},{29,31}} | collective-permute-start | bytes 516104 | tf_op jit(solution)/shard_map/ppermute | solution.py:601
  137.6 16.3 %collective-permute-start.26 = (bf16[96,896]{1,0:T(8,128)(2,1)S(1)}, bf16[96,896]{1,0:T(8,128)(2,1)S(1)}, u32[]{:S(2)}, u32[]{:S(2)}) collective-permute-start(bf16[96,896]{1,0:T(8,128)(2,1)S(1)} %get-tuple-element.25), channel_id=1, source_target_pairs={{1,0},{5,4},{8,9},{12,13},{19,18},{23,22},{26,27},{30,31}} | collective-permute-start | bytes 516104 | tf_op jit(solution)/shard_map/ppermute | solution.py:601
  150.0 23.8 %collective-permute-start.25 = (bf16[96,4096]{1,0:T(8,128)(2,1)S(1)}, bf16[96,4096]{1,0:T(8,128)(2,1)S(1)}, u32[]{:S(2)}, u32[]{:S(2)}) collective-permute-start(bf16[96,4096]{1,0:T(8,128)(2,1)S(1)} %collective-permute-done.24), channel_id=1, source_target_pairs={{8,0},{16,8},{24,16},{28,24},{20,28},{12,20},{4,12},{0,4},{9,1},{1... | collective-permute-start | bytes 2359304 | tf_op jit(solution)/shard_map/ppermute | solution.py:601
  151.4 23.9 %collective-permute-start.22 = (bf16[96,4096]{1,0:T(8,128)(2,1)S(1)}, bf16[96,4096]{1,0:T(8,128)(2,1)S(1)}, u32[]{:S(2)}, u32[]{:S(2)}) collective-permute-start(bf16[96,4096]{1,0:T(8,128)(2,1)S(1)} %collective-permute-done.21), channel_id=1, source_target_pairs={{0,8},{8,16},{16,24},{24,28},{28,20},{20,12},{12,4},{4,0},{1,9},{9... | collective-permute-start | bytes 2359304 | tf_op jit(solution)/shard_map/ppermute | solution.py:601
  (32 other events, 332.6 us)

commit v2 on v1

--- a/solution.py
+++ b/solution.py
@@ -234,6 +234,14 @@
 
 
 BUNDLE, SLOT, TARGET, OWNER, PLACE, PLAN_ROWS = 0, 1, 2, 3, 4, 8
+
+
+def chunk_plans(ranks):
+    middle = ranks // 2
+    return {
+        "p": [list(range(middle - 1)), [middle - 1]],
+        "s": [list(range(middle, ranks - 1)), [ranks - 1]],
+    }
 
 
 def plan_kernel(per_head, seen, owner_rank, owner_pick, loads, table):
@@ -646,14 +654,18 @@
             heads, bundles, w_uv, earlier,
         )
 
-    earlier = [attend([0, 1, 2], (cache_latent, cache_rope))]
-    for k in range(2, last):
-        earlier.append(attend([2 * k - 1, 2 * k]))
-    values = attend([2 * last - 1], None, earlier)
-    half = values.shape[1] // 2
-
-    def project(x):
-        return jnp.dot(x, w_out, preferred_element_type=jnp.float32)
+    chunks = []
+    for tag, plans in chunk_plans(ranks).items():
+        earlier = []
+        for n, plan in enumerate(plans):
+            full = (cache_latent, cache_rope) if plan[0] == 0 else None
+            carried = earlier if n == len(plans) - 1 else None
+            earlier.append(attend(plan, full, carried))
+        chunks.append((tag, earlier[-1]))
+    half = chunks[0][1].shape[1] // 2
+
+    def project(pieces):
+        return jnp.dot(jnp.concatenate(pieces), w_out, preferred_element_type=jnp.float32)
 
     def target(p, column):
         return order[(where[p] + offsets[column]) % ranks] // per_head
@@ -669,16 +681,22 @@
             got.append(move(to_send[m - 1], pairs, ("dp", "head")))
         return columns, own, got, total
 
-    state = settle([0], project(values), None)
-    fore = back = values
+    arrived = {}
+    for tag, values in chunks:
+        fore = back = values
+        for k in range(1, last):
+            fore = move(fore, ahead)
+            back = move(back, behind)
+            arrived[tag, k] = fore, back
+        fore, back = fore[:, :half], back[:, half:]
+        left = move(fore, ahead)
+        right = move(back, behind)
+        arrived[tag, last] = (jnp.concatenate([left, right], axis=1),)
+    state = settle([0], project([values for _, values in chunks]), None)
     for k in range(1, last):
-        fore = move(fore, ahead)
-        back = move(back, behind)
-        both = project(jnp.concatenate([fore, back], axis=0))
-        state = settle([2 * k - 1, 2 * k], both, state)
-    left = move(fore[:, :half], ahead)
-    right = move(back[:, half:], behind)
-    ends = project(jnp.concatenate([left, right], axis=1))
+        pieces = [arrived[tag, k][side] for side in (0, 1) for tag, _ in chunks]
+        state = settle([2 * k - 1, 2 * k], project(pieces), state)
+    ends = project([arrived[tag, last][0] for tag, _ in chunks])
     *before, total = state
     *final, _ = settle([2 * last - 1], ends, None)
     return finish(table, info, seen, heads, per_head, roll_count, total, [before, final])

time: 199 us -> 189 us (0.950)
  waiting for transfers between devices: 82.9 us -> 60.2 us
  starting transfers between devices: 52.9 us -> 64.5 us
    ppermute x43 -> x51, waiting for transfers between devices: 82.9 us -> 60.2 us  [move(): return lax.ppermute(x, axis, pairs)]
    ppermute x43 -> x51, starting transfers between devices: 47.4 us -> 59 us  [move(): return lax.ppermute(x, axis, pairs)]
  transfers between devices with their start and end apart: 44 -> 52, of which waited for: 14 -> 14; matrix products, arithmetic and copies ran while one was open for 9% -> 9% of each run, Pallas kernels for 16% -> 20%
where the time goes in v2:
time: 189 us; the launch traced here: 188 us
  starting transfers between devices  64.5 us (34%)
  waiting for transfers between devices  60.2 us (32%)
  Pallas kernels  41 us (22%)
  local copies, waits for them, and re-layouts  13.5 us (7%)
  matrix products  7.92 us (4%)
    ppermute x51, waiting for transfers between devices, move(): return lax.ppermute(x, axis, pairs)  60.2 us
    ppermute x51, starting transfers between devices, move(): return lax.ppermute(x, axis, pairs)  59 us
    pallas_call x4, Pallas kernels, attend_slots(): pl.pallas_call(functools.partial(slots_kernel, plan, own, heads, bundles,...  29.7 us
    dot_general x5, matrix products, project(): jnp.dot(jnp.concatenate(pieces), w_out, preferred_element_type=jnp.float32)  7.92 us
    reshape x1, local copies, waits for them, and re-layouts, local_ring(): q = q_latent.reshape(bundles, roll_count * local_heads, -1)  5.85 us
    all_to_all x1, starting transfers between devices, local_ring(): lax.all_to_all(jnp.broadcast_to(facts[None], (ranks, width)), 'dp', split...  5.5 us
    unnamed x24, local copies, waits for them, and re-layouts  4.35 us
  transfers between devices with their start and end apart: 52, of which 14 were waited for; matrix products, arithmetic and copies ran while one was open for 9% of the time, Pallas kernels for 20%

profile of v2, /device:TPU:0, one launch (start us, length us, event | category | flops | bytes accessed | tf_op | source)
XLA Modules:
  0.0 187.8 jit_solution(1135802462235035504)
XLA Ops:
  1.1 3.0 %collective-permute-start.2 = (bf16[4,144,512]{2,1,0:T(8,128)(2,1)S(1)}, bf16[4,144,512]{2,1,0:T(8,128)(2,1)S(1)}, u32[]{:S(2)}, u32[]{:S(2)}) collective-permute-start(bf16[4,144,512]{2,1,0:T(8,128)(2,1)S(1)} %payload.1), channel_id=1, source_target_pairs={{8,0},{16,8},{24,16},{28,24},{20,28},{12,20},{4,12},{0,4},{9,1},{1... | collective-permute-start | bytes 1769480 | tf_op jit(solution)/shard_map/ppermute | solution.py:609
  4.2 13.3 %collective-permute-done.2.b_ref = bf16[4,144,512]{2,1,0:T(8,128)(2,1)S(1)} collective-permute-done((bf16[4,144,512]{2,1,0:T(8,128)(2,1)S(1)}, bf16[4,144,512]{2,1,0:T(8,128)(2,1)S(1)}, u32[]{:S(2)}, u32[]{:S(2)}) %collective-permute-start.2) | collective-permute-done | bytes 589856 | tf_op jit(solution)/shard_map/ppermute | solution.py:609
  20.4 11.6 %collective-permute-done.3.b_ref = bf16[4,144,512]{2,1,0:T(8,128)(2,1)S(1)} collective-permute-done((bf16[4,144,512]{2,1,0:T(8,128)(2,1)S(1)}, bf16[4,144,512]{2,1,0:T(8,128)(2,1)S(1)}, u32[]{:S(2)}, u32[]{:S(2)}) %collective-permute-start.3) | collective-permute-done | bytes 589856 | tf_op jit(solution)/shard_map/ppermute | solution.py:609
  39.3 6.3 %collective-permute-done.15.b_ref = bf16[4,144,512]{2,1,0:T(8,128)(2,1)S(1)} collective-permute-done((bf16[4,144,512]{2,1,0:T(8,128)(2,1)S(1)}, bf16[4,144,512]{2,1,0:T(8,128)(2,1)S(1)}, u32[]{:S(2)}, u32[]{:S(2)}) %collective-permute-start.15) | collective-permute-done | bytes 589856 | tf_op jit(solution)/shard_map/ppermute | solution.py:609
  56.5 3.7 %collective-permute-done.5.refs_4_ = bf16[2,144,512]{2,1,0:T(8,128)(2,1)S(1)} collective-permute-done((bf16[2,144,512]{2,1,0:T(8,128)(2,1)S(1)}, bf16[2,144,512]{2,1,0:T(8,128)(2,1)S(1)}, u32[]{:S(2)}, u32[]{:S(2)}) %collective-permute-start.5) | collective-permute-done | bytes 294944 | tf_op jit(solution)/shard_map/ppermute | solution.py:609
  60.7 5.8 %collective-permute-done.21.refs_8_.refs_12_ = bf16[2,144,512]{2,1,0:T(8,128)(2,1)S(1)} collective-permute-done((bf16[2,144,512]{2,1,0:T(8,128)(2,1)S(1)}, bf16[2,144,512]{2,1,0:T(8,128)(2,1)S(1)}, u32[]{:S(2)}, u32[]{:S(2)}) %collective-permute-start.21) | collective-permute-done | bytes 294944 | tf_op jit(solution)/shard_map/ppermute | solution.py:609
  67.2 5.5 %all-to-all-start = ((s32[8,1,32]{2,1,0:T(1,128)}), s32[8,1,32]{2,1,0:T(1,128)S(1)}, u32[]{:S(2)}, u32[]{:S(2)}) async-start(s32[8,1,32]{2,1,0:T(1,128)} %broadcast_in_dim.2), calls=%async_computation | async-start | bytes 8192 | tf_op jit(solution)/shard_map/all_to_all | solution.py:617
  72.7 2.6 %reshape.13.refs_1_ = bf16[8,384,64]{2,1,0:T(8,128)(2,1)} reshape(bf16[96,2048]{1,0:T(8,128)(2,1)} %param.12) | data formatting | bytes 786432 | tf_op jit(solution)/shard_map/reshape | solution.py:623
  75.2 5.8 %reshape.12.refs_0_ = bf16[8,384,512]{2,1,0:T(8,128)(2,1)} reshape(bf16[96,16384]{1,0:T(8,128)(2,1)} %param.11) | data formatting | bytes 6291456 | tf_op jit(solution)/shard_map/reshape | solution.py:622
  81.6 9.8 %attend_slots.4.refs_6_ = f32[36,4096]{1,0:T(8,128)S(1)} custom-call(s32[8,8]{1,0:T(8,128)S(1)} %copy-done.2, s32[8,1,32]{2,1,0:T(1,128)S(1)} %broadcast_maximum_fusion.info, bf16[8,384,512]{2,1,0:T(8,128)(2,1)} %reshape.12.refs_0_, bf16[8,384,64]{2,1,0:T(8,128)(2,1)} %reshape.13.refs_1_, bf16[4,512,512]{2,1,0:T(8,128)(2,1)} %refs_2_.1, ...), custom_call_target="tpu_custom_call" | custom-call | tf_op jit(solution)/shard_map/attend_slots/pallas_call | solution.py:472
  91.4 5.2 %attend_slots.5 = bf16[48,4096]{1,0:T(8,128)(2,1)S(1)} custom-call(s32[8,8]{1,0:T(8,128)S(1)} %copy-done.2, s32[8,1,32]{2,1,0:T(1,128)S(1)} %broadcast_maximum_fusion.info, bf16[8,384,512]{2,1,0:T(8,128)(2,1)} %reshape.12.refs_0_, bf16[8,384,64]{2,1,0:T(8,128)(2,1)} %reshape.13.refs_1_, bf16[2,144,512]{2,1,0:T(8,128)(2,1)S(1)} %choose.4.refs_2_, ...), custom_call_target="tpu_custom_call" | custom-call | tf_op jit(solution)/shard_map/attend_slots/pallas_call | solution.py:472
  96.7 2.1 %collective-permute-start.26 = (bf16[48,4096]{1,0:T(8,128)(2,1)S(1)}, bf16[48,4096]{1,0:T(8,128)(2,1)S(1)}, u32[]{:S(2)}, u32[]{:S(2)}) collective-permute-start(bf16[48,4096]{1,0:T(8,128)(2,1)S(1)} %attend_slots.5), channel_id=1, source_target_pairs={{8,0},{16,8},{24,16},{28,24},{20,28},{12,20},{4,12},{0,4},{9,1},{1... | collective-permute-start | bytes 1179656 | tf_op jit(solution)/shard_map/ppermute | solution.py:609
  99.0 9.5 %attend_slots.6.refs_6_ = f32[36,4096]{1,0:T(8,128)S(1)} custom-call(s32[8,8]{1,0:T(8,128)S(1)} %copy-done.2, s32[8,1,32]{2,1,0:T(1,128)S(1)} %broadcast_maximum_fusion.info, bf16[8,384,512]{2,1,0:T(8,128)(2,1)} %reshape.12.refs_0_, bf16[8,384,64]{2,1,0:T(8,128)(2,1)} %reshape.13.refs_1_, bf16[2,144,512]{2,1,0:T(8,128)(2,1)S(1)} %choose.4.refs_2_, ...), custom_call_target="tpu_custom_call" | custom-call | tf_op jit(solution)/shard_map/attend_slots/pallas_call | solution.py:472
  108.6 5.1 %attend_slots.7 = bf16[48,4096]{1,0:T(8,128)(2,1)S(1)} custom-call(s32[8,8]{1,0:T(8,128)S(1)} %copy-done.2, s32[8,1,32]{2,1,0:T(1,128)S(1)} %broadcast_maximum_fusion.info, bf16[8,384,512]{2,1,0:T(8,128)(2,1)} %reshape.12.refs_0_, bf16[8,384,64]{2,1,0:T(8,128)(2,1)} %reshape.13.refs_1_, bf16[1,144,512]{2,1,0:T(8,128)(2,1)} %choose.6.refs_2_, ...), custom_call_target="tpu_custom_call" | custom-call | tf_op jit(solution)/shard_map/attend_slots/pallas_call | solution.py:472
  122.2 2.3 %collective-permute-done.34.refs_3_ = bf16[96,896]{1,0:T(8,128)(2,1)S(1)} collective-permute-done((bf16[96,896]{1,0:T(8,128)(2,1)S(1)}, bf16[96,896]{1,0:T(8,128)(2,1)S(1)}, u32[]{:S(2)}, u32[]{:S(2)}) %collective-permute-start.34) | collective-permute-done | bytes 172064 | tf_op jit(solution)/shard_map/ppermute | solution.py:609
  132.4 2.5 %collective-permute-start.35 = (bf16[96,896]{1,0:T(8,128)(2,1)S(1)}, bf16[96,896]{1,0:T(8,128)(2,1)S(1)}, u32[]{:S(2)}, u32[]{:S(2)}) collective-permute-start(bf16[96,896]{1,0:T(8,128)(2,1)S(1)} %get-tuple-element.27), channel_id=1, source_target_pairs={{1,0},{0,1},{5,4},{4,5},{9,8},{11,10},{13,12},{15,14},{16,17},{18,... | collective-permute-start | bytes 516104 | tf_op jit(solution)/shard_map/ppermute | solution.py:609
  136.2 2.0 %collective-permute-start.28 = (bf16[48,4096]{1,0:T(8,128)(2,1)S(1)}, bf16[48,4096]{1,0:T(8,128)(2,1)S(1)}, u32[]{:S(2)}, u32[]{:S(2)}) collective-permute-start(bf16[48,4096]{1,0:T(8,128)(2,1)S(1)} %collective-permute-done.27), channel_id=1, source_target_pairs={{8,0},{16,8},{24,16},{28,24},{20,28},{12,20},{4,12},{0,4},{9,1},{1... | collective-permute-start | bytes 1179656 | tf_op jit(solution)/shard_map/ppermute | solution.py:609
  139.5 3.6 %collective-permute-done.36.refs_2_ = bf16[96,896]{1,0:T(8,128)(2,1)S(1)} collective-permute-done((bf16[96,896]{1,0:T(8,128)(2,1)S(1)}, bf16[96,896]{1,0:T(8,128)(2,1)S(1)}, u32[]{:S(2)}, u32[]{:S(2)}) %collective-permute-start.36) | collective-permute-done | bytes 172064 | tf_op jit(solution)/shard_map/ppermute | solution.py:609
  148.3 2.7 %collective-permute-done.37.refs_3_ = bf16[96,896]{1,0:T(8,128)(2,1)S(1)} collective-permute-done((bf16[96,896]{1,0:T(8,128)(2,1)S(1)}, bf16[96,896]{1,0:T(8,128)(2,1)S(1)}, u32[]{:S(2)}, u32[]{:S(2)}) %collective-permute-start.37) | collective-permute-done | bytes 172064 | tf_op jit(solution)/shard_map/ppermute | solution.py:609
  156.3 3.1 %collective-permute-done.31 = bf16[48,4096]{1,0:T(8,128)(2,1)S(1)} collective-permute-done((bf16[48,4096]{1,0:T(8,128)(2,1)S(1)}, bf16[48,4096]{1,0:T(8,128)(2,1)S(1)}, u32[]{:S(2)}, u32[]{:S(2)}) %collective-permute-start.31) | collective-permute-done | bytes 393248 | tf_op jit(solution)/shard_map/ppermute | solution.py:609
  161.7 2.5 %collective-permute-start.47 = (bf16[48,2048]{1,0:T(8,128)(2,1)S(1)}, bf16[48,2048]{1,0:T(8,128)(2,1)S(1)}, u32[]{:S(2)}, u32[]{:S(2)}) collective-permute-start(bf16[48,2048]{1,0:T(8,128)(2,1)S(1)} %slice.29), channel_id=1, source_target_pairs={{8,0},{16,8},{24,16},{28,24},{20,28},{12,20},{4,12},{0,4},{9,1},{1... | collective-permute-start | bytes 589832 | tf_op jit(solution)/shard_map/ppermute | solution.py:609
  167.9 6.3 %collective-permute-start.42 = (bf16[96,896]{1,0:T(8,128)(2,1)S(1)}, bf16[96,896]{1,0:T(8,128)(2,1)S(1)}, u32[]{:S(2)}, u32[]{:S(2)}) collective-permute-start(bf16[96,896]{1,0:T(8,128)(2,1)S(1)} %get-tuple-element.39), channel_id=1, source_target_pairs={{0,2},{1,3},{4,6},{5,7},{11,9},{9,11},{15,13},{13,15},{18,16},{16,... | collective-permute-start | bytes 516104 | tf_op jit(solution)/shard_map/ppermute | solution.py:609
  180.2 2.4 %collective-permute-done.43.refs_3_ = bf16[96,896]{1,0:T(8,128)(2,1)S(1)} collective-permute-done((bf16[96,896]{1,0:T(8,128)(2,1)S(1)}, bf16[96,896]{1,0:T(8,128)(2,1)S(1)}, u32[]{:S(2)}, u32[]{:S(2)}) %collective-permute-start.43) | collective-permute-done | bytes 172064 | tf_op jit(solution)/shard_map/ppermute | solution.py:609
  182.6 3.2 %collective-permute-done.50.refs_7_ = bf16[96,896]{1,0:T(8,128)(2,1)S(1)} collective-permute-done((bf16[96,896]{1,0:T(8,128)(2,1)S(1)}, bf16[96,896]{1,0:T(8,128)(2,1)S(1)}, u32[]{:S(2)}, u32[]{:S(2)}) %collective-permute-start.50) | collective-permute-done | bytes 172064 | tf_op jit(solution)/shard_map/ppermute | solution.py:609
  (138 shorter events, 67.3 us)
Async XLA Ops:
  1.1 16.4 %collective-permute-start.2 = (bf16[4,144,512]{2,1,0:T(8,128)(2,1)S(1)}, bf16[4,144,512]{2,1,0:T(8,128)(2,1)S(1)}, u32[]{:S(2)}, u32[]{:S(2)}) collective-permute-start(bf16[4,144,512]{2,1,0:T(8,128)(2,1)S(1)} %payload.1), channel_id=1, source_target_pairs={{8,0},{16,8},{24,16},{28,24},{20,28},{12,20},{4,12},{0,4},{9,1},{1... | collective-permute-start | bytes 1769480 | tf_op jit(solution)/shard_map/ppermute | solution.py:609
  4.1 15.1 %collective-permute-start = (bf16[4,144,512]{2,1,0:T(8,128)(2,1)S(1)}, bf16[4,144,512]{2,1,0:T(8,128)(2,1)S(1)}, u32[]{:S(2)}, u32[]{:S(2)}) collective-permute-start(bf16[4,144,512]{2,1,0:T(8,128)(2,1)S(1)} %payload.1), channel_id=1, source_target_pairs={{0,8},{8,16},{16,24},{24,28},{28,20},{20,12},{12,4},{4,0},{1,9},{9... | collective-permute-start | bytes 1769480 | tf_op jit(solution)/shard_map/ppermute | solution.py:609
  17.5 14.5 %collective-permute-start.3 = (bf16[4,144,512]{2,1,0:T(8,128)(2,1)S(1)}, bf16[4,144,512]{2,1,0:T(8,128)(2,1)S(1)}, u32[]{:S(2)}, u32[]{:S(2)}) collective-permute-start(bf16[4,144,512]{2,1,0:T(8,128)(2,1)S(1)} %collective-permute-done.2.b_ref), channel_id=1, source_target_pairs={{8,0},{16,8},{24,16},{28,24},{20,28},{12,20},{4,12},{0,4},{9,1},{1... | collective-permute-start | bytes 1769480 | tf_op jit(solution)/shard_map/ppermute | solution.py:609
  19.2 14.2 %collective-permute-start.1 = (bf16[4,144,512]{2,1,0:T(8,128)(2,1)S(1)}, bf16[4,144,512]{2,1,0:T(8,128)(2,1)S(1)}, u32[]{:S(2)}, u32[]{:S(2)}) collective-permute-start(bf16[4,144,512]{2,1,0:T(8,128)(2,1)S(1)} %collective-permute-done.a_ref), channel_id=1, source_target_pairs={{0,8},{8,16},{16,24},{24,28},{28,20},{20,12},{12,4},{4,0},{1,9},{9... | collective-permute-start | bytes 1769480 | tf_op jit(solution)/shard_map/ppermute | solution.py:609
  52.4 14.0 %collective-permute-start.21 = (bf16[2,144,512]{2,1,0:T(8,128)(2,1)S(1)}, bf16[2,144,512]{2,1,0:T(8,128)(2,1)S(1)}, u32[]{:S(2)}, u32[]{:S(2)}) collective-permute-start(bf16[2,144,512]{2,1,0:T(8,128)(2,1)S(1)} %choose.7.refs_6_.refs_10_), channel_id=1, source_target_pairs={{0,2},{1,3},{2,0},{3,1},{4,6},{5,7},{6,4},{7,5},{8,10},{9,11},{10,... | collective-permute-start | bytes 884744 | tf_op jit(solution)/shard_map/ppermute | solution.py:609
  53.7 27.4 %collective-permute-start.4 = (bf16[2,144,512]{2,1,0:T(8,128)(2,1)S(1)}, bf16[2,144,512]{2,1,0:T(8,128)(2,1)S(1)}, u32[]{:S(2)}, u32[]{:S(2)}) collective-permute-start(bf16[2,144,512]{2,1,0:T(8,128)(2,1)S(1)} %choose.4.refs_2_), channel_id=1, source_target_pairs={{0,1},{1,0},{2,3},{3,2},{4,5},{5,4},{6,7},{7,6},{8,9},{9,8},{10,11... | collective-permute-start | bytes 884744 | tf_op jit(solution)/shard_map/ppermute | solution.py:609
  55.0 26.3 %collective-permute-start.18 = (bf16[1,144,512]{2,1,0:T(8,128)(2,1)}, bf16[1,144,512]{2,1,0:T(8,128)(2,1)}, u32[]{:S(2)}, u32[]{:S(2)}) collective-permute-start(bf16[1,144,512]{2,1,0:T(8,128)(2,1)} %choose.6.refs_2_), channel_id=1, source_target_pairs={{0,2},{1,3},{2,0},{3,1},{4,6},{5,7},{6,4},{7,5},{8,10},{9,11},{10,... | collective-permute-start | bytes 442376 | tf_op jit(solution)/shard_map/ppermute | solution.py:609
  60.1 31.3 %collective-permute-start.6 = (bf16[2,144,512]{2,1,0:T(8,128)(2,1)S(1)}, bf16[2,144,512]{2,1,0:T(8,128)(2,1)S(1)}, u32[]{:S(2)}, u32[]{:S(2)}) collective-permute-start(bf16[2,144,512]{2,1,0:T(8,128)(2,1)S(1)} %collective-permute-done.5.refs_4_), channel_id=1, source_target_pairs={{0,1},{1,0},{2,3},{3,2},{4,5},{5,4},{6,7},{7,6},{8,9},{9,8},{10,11... | collective-permute-start | bytes 884744 | tf_op jit(solution)/shard_map/ppermute | solution.py:609
  60.1 38.6 %collective-permute-start.20 = (bf16[2,144,512]{2,1,0:T(8,128)(2,1)S(1)}, bf16[2,144,512]{2,1,0:T(8,128)(2,1)S(1)}, u32[]{:S(2)}, u32[]{:S(2)}) collective-permute-start(bf16[2,144,512]{2,1,0:T(8,128)(2,1)S(1)} %choose.7.refs_6_.refs_10_), channel_id=1, source_target_pairs={{0,1},{1,0},{2,3},{3,2},{4,5},{5,4},{6,7},{7,6},{8,9},{9,8},{10,11... | collective-permute-start | bytes 884744 | tf_op jit(solution)/shard_map/ppermute | solution.py:609
  66.5 32.6 %collective-permute-start.22 = (bf16[2,144,512]{2,1,0:T(8,128)(2,1)S(1)}, bf16[2,144,512]{2,1,0:T(8,128)(2,1)S(1)}, u32[]{:S(2)}, u32[]{:S(2)}) collective-permute-start(bf16[2,144,512]{2,1,0:T(8,128)(2,1)S(1)} %collective-permute-done.21.refs_8_.refs_12_), channel_id=1, source_target_pairs={{0,1},{1,0},{2,3},{3,2},{4,5},{5,4},{6,7},{7,6},{8,9},{9,8},{10,11... | collective-permute-start | bytes 884744 | tf_op jit(solution)/shard_map/ppermute | solution.py:609
  67.2 14.5 %all-to-all-start = ((s32[8,1,32]{2,1,0:T(1,128)}), s32[8,1,32]{2,1,0:T(1,128)S(1)}, u32[]{:S(2)}, u32[]{:S(2)}) async-start(s32[8,1,32]{2,1,0:T(1,128)} %broadcast_in_dim.2), calls=%async_computation | async-start | bytes 8192 | tf_op jit(solution)/shard_map/all_to_all | solution.py:617
  81.1 27.5 %collective-permute-start.17 = (bf16[1,144,512]{2,1,0:T(8,128)(2,1)}, bf16[1,144,512]{2,1,0:T(8,128)(2,1)}, u32[]{:S(2)}, u32[]{:S(2)}) collective-permute-start(bf16[1,144,512]{2,1,0:T(8,128)(2,1)} %choose.6.refs_2_), channel_id=1, source_target_pairs={{0,1},{1,0},{2,3},{3,2},{4,5},{5,4},{6,7},{7,6},{8,9},{9,8},{10,11... | collective-permute-start | bytes 442376 | tf_op jit(solution)/shard_map/ppermute | solution.py:609
  81.3 27.2 %collective-permute-start.19 = (bf16[1,144,512]{2,1,0:T(8,128)(2,1)}, bf16[1,144,512]{2,1,0:T(8,128)(2,1)}, u32[]{:S(2)}, u32[]{:S(2)}) collective-permute-start(bf16[1,144,512]{2,1,0:T(8,128)(2,1)} %collective-permute-done.18.refs_4_), channel_id=1, source_target_pairs={{0,1},{1,0},{2,3},{3,2},{4,5},{5,4},{6,7},{7,6},{8,9},{9,8},{10,11... | collective-permute-start | bytes 442376 | tf_op jit(solution)/shard_map/ppermute | solution.py:609
  96.7 22.3 %collective-permute-start.26 = (bf16[48,4096]{1,0:T(8,128)(2,1)S(1)}, bf16[48,4096]{1,0:T(8,128)(2,1)S(1)}, u32[]{:S(2)}, u32[]{:S(2)}) collective-permute-start(bf16[48,4096]{1,0:T(8,128)(2,1)S(1)} %attend_slots.5), channel_id=1, source_target_pairs={{8,0},{16,8},{24,16},{28,24},{20,28},{12,20},{4,12},{0,4},{9,1},{1... | collective-permute-start | bytes 1179656 | tf_op jit(solution)/shard_map/ppermute | solution.py:609
  98.8 21.5 %collective-permute-start.10 = (bf16[48,4096]{1,0:T(8,128)(2,1)S(1)}, bf16[48,4096]{1,0:T(8,128)(2,1)S(1)}, u32[]{:S(2)}, u32[]{:S(2)}) collective-permute-start(bf16[48,4096]{1,0:T(8,128)(2,1)S(1)} %attend_slots.5), channel_id=1, source_target_pairs={{0,8},{8,16},{16,24},{24,28},{28,20},{20,12},{12,4},{4,0},{1,9},{9... | collective-permute-start | bytes 1179656 | tf_op jit(solution)/shard_map/ppermute | solution.py:609
  120.3 14.6 %collective-permute-start.27 = (bf16[48,4096]{1,0:T(8,128)(2,1)S(1)}, bf16[48,4096]{1,0:T(8,128)(2,1)S(1)}, u32[]{:S(2)}, u32[]{:S(2)}) collective-permute-start(bf16[48,4096]{1,0:T(8,128)(2,1)S(1)} %collective-permute-done.26), channel_id=1, source_target_pairs={{8,0},{16,8},{24,16},{28,24},{20,28},{12,20},{4,12},{0,4},{9,1},{1... | collective-permute-start | bytes 1179656 | tf_op jit(solution)/shard_map/ppermute | solution.py:609
  127.6 16.8 %collective-permute-start.30 = (bf16[48,4096]{1,0:T(8,128)(2,1)S(1)}, bf16[48,4096]{1,0:T(8,128)(2,1)S(1)}, u32[]{:S(2)}, u32[]{:S(2)}) collective-permute-start(bf16[48,4096]{1,0:T(8,128)(2,1)S(1)} %collective-permute-done.29), channel_id=1, source_target_pairs={{8,0},{16,8},{24,16},{28,24},{20,28},{12,20},{4,12},{0,4},{9,1},{1... | collective-permute-start | bytes 1179656 | tf_op jit(solution)/shard_map/ppermute | solution.py:609
  129.4 16.7 %collective-permute-start.24 = (bf16[48,4096]{1,0:T(8,128)(2,1)S(1)}, bf16[48,4096]{1,0:T(8,128)(2,1)S(1)}, u32[]{:S(2)}, u32[]{:S(2)}) collective-permute-start(bf16[48,4096]{1,0:T(8,128)(2,1)S(1)} %collective-permute-done.23), channel_id=1, source_target_pairs={{0,8},{8,16},{16,24},{24,28},{28,20},{20,12},{12,4},{4,0},{1,9},{9... | collective-permute-start | bytes 1179656 | tf_op jit(solution)/shard_map/ppermute | solution.py:609
  136.2 17.0 %collective-permute-start.28 = (bf16[48,4096]{1,0:T(8,128)(2,1)S(1)}, bf16[48,4096]{1,0:T(8,128)(2,1)S(1)}, u32[]{:S(2)}, u32[]{:S(2)}) collective-permute-start(bf16[48,4096]{1,0:T(8,128)(2,1)S(1)} %collective-permute-done.27), channel_id=1, source_target_pairs={{8,0},{16,8},{24,16},{28,24},{20,28},{12,20},{4,12},{0,4},{9,1},{1... | collective-permute-start | bytes 1179656 | tf_op jit(solution)/shard_map/ppermute | solution.py:609
  138.2 16.3 %collective-permute-start.12 = (bf16[48,4096]{1,0:T(8,128)(2,1)S(1)}, bf16[48,4096]{1,0:T(8,128)(2,1)S(1)}, u32[]{:S(2)}, u32[]{:S(2)}) collective-permute-start(bf16[48,4096]{1,0:T(8,128)(2,1)S(1)} %collective-permute-done.11), channel_id=1, source_target_pairs={{0,8},{8,16},{16,24},{24,28},{28,20},{20,12},{12,4},{4,0},{1,9},{9... | collective-permute-start | bytes 1179656 | tf_op jit(solution)/shard_map/ppermute | solution.py:609
  144.4 15.1 %collective-permute-start.31 = (bf16[48,4096]{1,0:T(8,128)(2,1)S(1)}, bf16[48,4096]{1,0:T(8,128)(2,1)S(1)}, u32[]{:S(2)}, u32[]{:S(2)}) collective-permute-start(bf16[48,4096]{1,0:T(8,128)(2,1)S(1)} %collective-permute-done.30), channel_id=1, source_target_pairs={{8,0},{16,8},{24,16},{28,24},{20,28},{12,20},{4,12},{0,4},{9,1},{1... | collective-permute-start | bytes 1179656 | tf_op jit(solution)/shard_map/ppermute | solution.py:609
  146.2 14.8 %collective-permute-start.25 = (bf16[48,4096]{1,0:T(8,128)(2,1)S(1)}, bf16[48,4096]{1,0:T(8,128)(2,1)S(1)}, u32[]{:S(2)}, u32[]{:S(2)}) collective-permute-start(bf16[48,4096]{1,0:T(8,128)(2,1)S(1)} %collective-permute-done.24), channel_id=1, source_target_pairs={{0,8},{8,16},{16,24},{24,28},{28,20},{20,12},{12,4},{4,0},{1,9},{9... | collective-permute-start | bytes 1179656 | tf_op jit(solution)/shard_map/ppermute | solution.py:609
  159.5 14.7 %collective-permute-start.44 = (bf16[48,2048]{1,0:T(8,128)(2,1)S(1)}, bf16[48,2048]{1,0:T(8,128)(2,1)S(1)}, u32[]{:S(2)}, u32[]{:S(2)}) collective-permute-start(bf16[48,2048]{1,0:T(8,128)(2,1)S(1)} %slice.26), channel_id=1, source_target_pairs={{0,8},{8,16},{16,24},{24,28},{28,20},{20,12},{12,4},{4,0},{1,9},{9... | collective-permute-start | bytes 589832 | tf_op jit(solution)/shard_map/ppermute | solution.py:609
  161.7 13.9 %collective-permute-start.47 = (bf16[48,2048]{1,0:T(8,128)(2,1)S(1)}, bf16[48,2048]{1,0:T(8,128)(2,1)S(1)}, u32[]{:S(2)}, u32[]{:S(2)}) collective-permute-start(bf16[48,2048]{1,0:T(8,128)(2,1)S(1)} %slice.29), channel_id=1, source_target_pairs={{8,0},{16,8},{24,16},{28,24},{20,28},{12,20},{4,12},{0,4},{9,1},{1... | collective-permute-start | bytes 589832 | tf_op jit(solution)/shard_map/ppermute | solution.py:609
  (40 other events, 405.2 us)

commit v3 on v2

--- a/solution.py
+++ b/solution.py
@@ -347,142 +347,118 @@
     )(table, a, b)
 
 
-def slots_kernel(plan, own, heads, bundles, carried, final, scale, block, table, info, *refs):
-    count = len(plan)
+def slots_kernel(plan, own, indices, bundles, final, scale, table, info, *refs):
+    count, heads = len(plan), len(indices[0])
     refs = list(refs)
-    q_ref, qr_ref = refs.pop(0), refs.pop(0)
+    q_ref, qr_ref, w_ref = refs.pop(0), refs.pop(0), refs.pop(0)
     if own:
         full_lat, full_rope = refs.pop(0), refs.pop(0)
-    shipped = count - own
-    parts = [[refs.pop(0) for _ in range(heads)] for _ in range(shipped)]
-    earlier = [refs.pop(0) for _ in carried]
-    w_hbm, out_ref, lat, rope, mixed, w_ref, sem = refs[:7]
-    i = pl.program_id(0)
+    parts = [[(refs.pop(0), index) for index in slot] for slot in indices]
+    lat, rope, mixed = refs.pop(-3), refs.pop(-2), refs.pop(-1)
+    if own:
+        own_lat, own_rope, sems = refs.pop(-3), refs.pop(-2), refs.pop(-1)
+        slot = table[SLOT, plan[0]]
+        copies = [
+            pltpu.make_async_copy(full_lat.at[slot], own_lat, sems.at[0]),
+            pltpu.make_async_copy(full_rope.at[slot], own_rope, sems.at[1]),
+        ]
+        for copy in copies:
+            copy.start()
+    into = refs.pop(-1) if final else None
+    out_ref = refs.pop(-1)
+    earlier = refs
     total_rows = q_ref.shape[1]
-    w_copy = pltpu.make_async_copy(w_hbm, w_ref, sem)
-
-    @pl.when(i == 0)
-    def _():
-        w_copy.start()
-
     rows = lat.shape[0] // heads
     dims = rope.shape[0] // heads
 
-    for j in range(count):
-
-        @pl.when(i == j)
-        def _():
-            if own and j == 0:
-                lat[...] = full_lat[0]
-                rope[...] = full_rope[0]
-                return
-            for m in range(heads):
-                part = parts[j - own][m]
-                to = jnp.bitwise_xor(table[PLACE, 1], m)
-                lat[pl.ds(pl.multiple_of(to * rows, rows), rows), :] = part[0, :rows, :]
-                rope[pl.ds(pl.multiple_of(to * dims, dims), dims), :] = part[0, rows:, :]
-
-    column = jnp.int32(plan[0]) + i
-    length = info[table[OWNER, column], 0, bundles + table[SLOT, column]]
-    live = lax.broadcasted_iota(jnp.int32, (block, lat.shape[0]), 1) < length
-    for r in range(total_rows // block):
-        at = slice(r * block, (r + 1) * block)
+    def bundle(i, _):
+        j = lax.rem(i + own, count)
+        for at in range(count):
+
+            @pl.when(j == at)
+            def _():
+                if own and at == 0:
+                    for copy in copies:
+                        copy.wait()
+                    lat[...] = own_lat[...]
+                    rope[...] = own_rope[...]
+                    return
+                for m, (part, index) in enumerate(parts[at - own]):
+                    to = jnp.bitwise_xor(table[PLACE, 1], m)
+                    lat[pl.ds(pl.multiple_of(to * rows, rows), rows), :] = part[index, :rows, :]
+                    rope[pl.ds(pl.multiple_of(to * dims, dims), dims), :] = part[index, rows:, :]
+
+        column = plan[0] + j
+        length = info[table[OWNER, column], 0, bundles + table[SLOT, column]]
+        b = table[BUNDLE, column]
+        past = lax.broadcasted_iota(jnp.int32, (1, lat.shape[0]), 1) >= length
         s = lax.dot_general(
-            q_ref[0, at, :], lat[...], (((1,), (1,)), ((), ())), preferred_element_type=jnp.float32
+            q_ref[b], lat[...], (((1,), (1,)), ((), ())), preferred_element_type=jnp.float32
         )
-        s = s + jnp.dot(qr_ref[0, at, :], rope[...], preferred_element_type=jnp.float32)
-        s = jnp.where(live, s * scale, -1e30)
-        w = jnp.exp(s - jnp.max(s, axis=1, keepdims=True))
+        s = s + jnp.dot(qr_ref[b], rope[...], preferred_element_type=jnp.float32)
+        s = s + jnp.where(past, -1e30, 0.0)
+        w = jnp.exp((s - jnp.max(s, axis=1, keepdims=True)) * scale)
         w = w * (1.0 / jnp.sum(w, axis=1, keepdims=True))
         o = jnp.dot(w.astype(jnp.bfloat16), lat[...], preferred_element_type=jnp.float32)
+        start = pl.multiple_of(j * total_rows, total_rows)
         for c in range(mixed.shape[0]):
-            mixed[c, pl.ds(i * total_rows + r * block, block), :] = o[:, c * 128 : (c + 1) * 128]
-
-    @pl.when(i == count - 1)
-    def _():
-        w_copy.wait()
-        local_heads, _, value_width = w_ref.shape
-        n = mixed.shape[1] // local_heads
-        into, at = out_ref, 0
-        if final:
-            into = refs[7]
-            for piece in earlier:
-                into[pl.ds(at, piece.shape[0]), :] = piece[...]
-                at += piece.shape[0]
-        for h in range(local_heads):
-            x = jnp.concatenate(
-                [mixed[c, pl.ds(h, n, stride=local_heads), :] for c in range(mixed.shape[0])], axis=1
-            ).astype(jnp.bfloat16)
-            v = jnp.dot(x, w_ref[h], preferred_element_type=jnp.float32)
-            into[pl.ds(at, n), h * value_width : (h + 1) * value_width] = v
-        if final:
-            out_ref[...] = into[...].astype(out_ref.dtype)
-
-
-def attend_slots(plan, table, info, q, qr, full, parts, heads, bundles, w_uv, earlier=None):
+            mixed[c, pl.ds(start, total_rows), :] = o[:, c * 128 : (c + 1) * 128]
+        return 0
+
+    lax.fori_loop(0, count, bundle, 0)
+    local_heads, _, value_width = w_ref.shape
+    n = mixed.shape[1] // local_heads
+    at = 0
+    if final:
+        for piece in earlier:
+            into[pl.ds(at, piece.shape[0]), :] = piece[...]
+            at += piece.shape[0]
+    else:
+        into = out_ref
+    for h in range(local_heads):
+        x = jnp.concatenate(
+            [mixed[c, pl.ds(h, n, stride=local_heads), :] for c in range(mixed.shape[0])], axis=1
+        ).astype(jnp.bfloat16)
+        v = jnp.dot(x, w_ref[h], preferred_element_type=jnp.float32)
+        into[pl.ds(at, n), h * value_width : (h + 1) * value_width] = v
+    if final:
+        out_ref[...] = into[...].astype(out_ref.dtype)
+
+
+def attend_slots(plan, table, info, q, qr, full, parts, bundles, w_uv, earlier=None):
     own = 1 if full is not None else 0
     final = earlier is not None
     earlier = list(earlier or ())
-    count = len(plan)
+    count, heads = len(plan), len(parts[0])
     _, q_rows, wide = q.shape
-    part_rows = parts[0][0][0].shape[1]
-    dims = qr.shape[2] // heads
-    rows = part_rows - dims
-    block = math.gcd(q_rows, 128)
+    dims = qr.shape[2]
+    positions = (parts[0][0][0].shape[1] - dims // heads) * heads
     local_heads, _, value_width = w_uv.shape
-    carried = [e.shape[0] for e in earlier]
-
-    def bundle(i, table, info):
-        return table[BUNDLE, plan[0] + i], 0, 0
-
-    in_specs = [
-        pl.BlockSpec((1, q_rows, wide), bundle),
-        pl.BlockSpec((1, q_rows, qr.shape[2]), bundle),
-    ]
-    args = [in_hbm(q), in_hbm(qr)]
+    vmem = pl.BlockSpec(memory_space=pltpu.MemorySpace.VMEM)
+    smem = pl.BlockSpec(memory_space=pltpu.MemorySpace.SMEM)
+    args, in_specs = [q, qr, w_uv], [vmem] * 3
     if own:
-        here = lambda i, table, info: (table[SLOT, plan[0]], 0, 0)
-        in_specs += [
-            pl.BlockSpec((1, rows * heads, wide), here),
-            pl.BlockSpec((1, dims * heads, wide), here),
-        ]
         args += [in_hbm(x) for x in full]
-    for slot in parts:
-        for array, index in slot:
-            in_specs.append(
-                pl.BlockSpec((1, part_rows, wide), lambda i, *_, index=index: (index, 0, 0))
-            )
-            args.append(array)
-    for piece in earlier:
-        in_specs.append(pl.BlockSpec(piece.shape, lambda i, *_: (0, 0)))
-        args.append(piece)
-    in_specs.append(pl.BlockSpec(memory_space=pl.ANY))
-    args.append(in_hbm(w_uv))
-    done = sum(carried) + count * q_rows // local_heads
+        in_specs += [pl.BlockSpec(memory_space=pl.ANY)] * 2
+    args += [array for slot in parts for array, _ in slot] + earlier
+    in_specs += [vmem] * (len(args) - len(in_specs))
+    done = sum(e.shape[0] for e in earlier) + count * q_rows // local_heads
     out_shape = (done, local_heads * value_width)
-    scratch = [
-        pltpu.VMEM((rows * heads, wide), jnp.bfloat16),
-        pltpu.VMEM((dims * heads, wide), jnp.bfloat16),
-        pltpu.VMEM((wide // 128, count * q_rows, 128), jnp.float32),
-        pltpu.VMEM(w_uv.shape, w_uv.dtype),
-        pltpu.SemaphoreType.DMA,
-    ]
-    if final:
-        scratch.append(pltpu.VMEM(out_shape, jnp.float32))
+    caches = [pltpu.VMEM((positions, wide), jnp.bfloat16), pltpu.VMEM((dims, wide), jnp.bfloat16)]
+    scratch = [pltpu.VMEM(out_shape, jnp.float32)] if final else []
+    if own:
+        scratch += caches + [pltpu.SemaphoreType.DMA((2,))]
+    scratch += caches + [pltpu.VMEM((wide // 128, count * q_rows, 128), jnp.float32)]
     return pl.pallas_call(
         functools.partial(
-            slots_kernel, plan, own, heads, bundles, carried, final,
-            1.0 / math.sqrt(VD + ROPE), block,
+            slots_kernel, plan, own, [[index for _, index in slot] for slot in parts], bundles,
+            final, 1.0 / math.sqrt(VD + ROPE),
         ),
         out_shape=jax.ShapeDtypeStruct(out_shape, jnp.bfloat16 if final else jnp.float32),
-        grid_spec=pltpu.PrefetchScalarGridSpec(
-            num_scalar_prefetch=2,
-            grid=(count,),
-            in_specs=in_specs,
-            out_specs=pl.BlockSpec(out_shape, lambda i, *_: (0, 0)),
-            scratch_shapes=scratch,
-        ),
-        compiler_params=pltpu.CompilerParams(vmem_limit_bytes=24 * 2**20),
+        in_specs=[smem] * 2 + in_specs,
+        out_specs=vmem,
+        scratch_shapes=scratch,
+        compiler_params=pltpu.CompilerParams(vmem_limit_bytes=14 * 2**20),
         name="attend_slots",
     )(table, info, *args)
 
@@ -651,7 +627,7 @@
     def attend(plan, full=None, earlier=None):
         return attend_slots(
             plan, table, info, q, qr, full, [groups[c] for c in plan[(full is not None) :]],
-            heads, bundles, w_uv, earlier,
+            bundles, w_uv, earlier,
         )
 
     chunks = []

time: 189 us -> 183 us (0.968)
  Pallas kernels: 41 us -> 32.1 us
  local copies, waits for them, and re-layouts: 13.5 us -> 18.5 us
    pallas_call x4, Pallas kernels: 29.7 us -> 19.3 us  [attend_slots(): pl.pallas_call(functools.partial(slots_kernel, plan, own, [[index for _,...]
    unnamed x24 -> x40, local copies, waits for them, and re-layouts: 4.35 us -> 10.9 us
  transfers between devices with their start and end apart: 52 -> 52, of which waited for: 14 -> 13; matrix products, arithmetic and copies ran while one was open for 9% -> 9% of each run, Pallas kernels for 20% -> 16%
where the time goes in v3:
time: 183 us; the launch traced here: 182 us
  starting transfers between devices  64.3 us (35%)
  waiting for transfers between devices  58.5 us (32%)
  Pallas kernels  32.1 us (18%)
  local copies, waits for them, and re-layouts  18.5 us (10%)
  matrix products  7.97 us (4%)
    ppermute x51, starting transfers between devices, move(): return lax.ppermute(x, axis, pairs)  58.8 us
    ppermute x51, waiting for transfers between devices, move(): return lax.ppermute(x, axis, pairs)  58.5 us
    pallas_call x4, Pallas kernels, attend_slots(): pl.pallas_call(functools.partial(slots_kernel, plan, own, [[index for _,...  19.3 us
    unnamed x40, local copies, waits for them, and re-layouts  10.9 us
    dot_general x5, matrix products, project(): jnp.dot(jnp.concatenate(pieces), w_out, preferred_element_type=jnp.float32)  7.97 us
    all_to_all x1, starting transfers between devices, local_ring(): lax.all_to_all(jnp.broadcast_to(facts[None], (ranks, width)), 'dp', split...  5.5 us
    pallas_call x4, Pallas kernels, choose(): pl.pallas_call(functools.partial(choose_kernel, cut, columns[0]), out_sha...  4.59 us
    reshape x1, local copies, waits for them, and re-layouts, local_ring(): q = q_latent.reshape(bundles, roll_count * local_heads, -1)  4.2 us
  transfers between devices with their start and end apart: 52, of which 13 were waited for; matrix products, arithmetic and copies ran while one was open for 9% of the time, Pallas kernels for 16%

profile of v3, /device:TPU:0, one launch (start us, length us, event | category | flops | bytes accessed | tf_op | source)
XLA Modules:
  0.0 182.0 jit_solution(7119872877099825103)
XLA Ops:
  1.1 3.0 %collective-permute-start.2 = (bf16[4,144,512]{2,1,0:T(8,128)(2,1)S(1)}, bf16[4,144,512]{2,1,0:T(8,128)(2,1)S(1)}, u32[]{:S(2)}, u32[]{:S(2)}) collective-permute-start(bf16[4,144,512]{2,1,0:T(8,128)(2,1)S(1)} %payload.1), channel_id=1, source_target_pairs={{8,0},{16,8},{24,16},{28,24},{20,28},{12,20},{4,12},{0,4},{9,1},{1... | collective-permute-start | bytes 1769480 | tf_op jit(solution)/shard_map/ppermute | solution.py:585
  4.2 13.3 %collective-permute-done.2.b_ref = bf16[4,144,512]{2,1,0:T(8,128)(2,1)S(1)} collective-permute-done((bf16[4,144,512]{2,1,0:T(8,128)(2,1)S(1)}, bf16[4,144,512]{2,1,0:T(8,128)(2,1)S(1)}, u32[]{:S(2)}, u32[]{:S(2)}) %collective-permute-start.2) | collective-permute-done | bytes 589856 | tf_op jit(solution)/shard_map/ppermute | solution.py:585
  20.4 11.6 %collective-permute-done.3.b_ref = bf16[4,144,512]{2,1,0:T(8,128)(2,1)S(1)} collective-permute-done((bf16[4,144,512]{2,1,0:T(8,128)(2,1)S(1)}, bf16[4,144,512]{2,1,0:T(8,128)(2,1)S(1)}, u32[]{:S(2)}, u32[]{:S(2)}) %collective-permute-start.3) | collective-permute-done | bytes 589856 | tf_op jit(solution)/shard_map/ppermute | solution.py:585
  39.3 6.3 %collective-permute-done.15.b_ref = bf16[4,144,512]{2,1,0:T(8,128)(2,1)S(1)} collective-permute-done((bf16[4,144,512]{2,1,0:T(8,128)(2,1)S(1)}, bf16[4,144,512]{2,1,0:T(8,128)(2,1)S(1)}, u32[]{:S(2)}, u32[]{:S(2)}) %collective-permute-start.15) | collective-permute-done | bytes 589856 | tf_op jit(solution)/shard_map/ppermute | solution.py:585
  57.2 2.8 %collective-permute-done.5.refs_5_ = bf16[2,144,512]{2,1,0:T(8,128)(2,1)} collective-permute-done((bf16[2,144,512]{2,1,0:T(8,128)(2,1)}, bf16[2,144,512]{2,1,0:T(8,128)(2,1)}, u32[]{:S(2)}, u32[]{:S(2)}) %collective-permute-start.5) | collective-permute-done | bytes 294944 | tf_op jit(solution)/shard_map/ppermute | solution.py:585
  61.3 5.1 %collective-permute-done.21.refs_9_.refs_13_ = bf16[2,144,512]{2,1,0:T(8,128)(2,1)} collective-permute-done((bf16[2,144,512]{2,1,0:T(8,128)(2,1)}, bf16[2,144,512]{2,1,0:T(8,128)(2,1)}, u32[]{:S(2)}, u32[]{:S(2)}) %collective-permute-start.21) | collective-permute-done | bytes 294944 | tf_op jit(solution)/shard_map/ppermute | solution.py:585
  67.0 5.5 %all-to-all-start = ((s32[8,1,32]{2,1,0:T(1,128)}), s32[8,1,32]{2,1,0:T(1,128)S(1)}, u32[]{:S(2)}, u32[]{:S(2)}) async-start(s32[8,1,32]{2,1,0:T(1,128)} %broadcast_in_dim.2), calls=%async_computation | async-start | bytes 8192 | tf_op jit(solution)/shard_map/all_to_all | solution.py:593
  72.6 2.6 %reshape.13.refs_1_ = bf16[8,384,64]{2,1,0:T(8,128)(2,1)} reshape(bf16[96,2048]{1,0:T(8,128)(2,1)} %param.12) | data formatting | bytes 786432 | tf_op jit(solution)/shard_map/reshape | solution.py:599
  75.2 4.2 %reshape.12.refs_0_ = bf16[8,384,512]{2,1,0:T(8,128)(2,1)S(1)} reshape(bf16[96,16384]{1,0:T(8,128)(2,1)} %param.11) | data formatting | bytes 6291456 | tf_op jit(solution)/shard_map/reshape | solution.py:598
  80.0 2.2 %copy-done = bf16[32,512,128]{2,1,0:T(8,128)(2,1)S(1)} copy-done((bf16[32,512,128]{2,1,0:T(8,128)(2,1)S(1)}, bf16[32,512,128]{2,1,0:T(8,128)(2,1)}, u32[]{:S(2)}) %copy-start) | copy-done | bytes 4194328
  86.2 6.0 %attend_slots.4.refs_7_ = f32[36,4096]{1,0:T(8,128)S(1)} custom-call(s32[8,8]{1,0:T(8,128)S(1)} %copy-done.12, s32[8,1,32]{2,1,0:T(1,128)S(1)} %broadcast_maximum_fusion.info, bf16[8,384,512]{2,1,0:T(8,128)(2,1)S(1)} %reshape.12.refs_0_, bf16[8,384,64]{2,1,0:T(8,128)(2,1)S(1)} %copy-done.2, bf16[32,512,128]{2,1,0:T(8,128)(2,1)S(1)} %copy-done, ...), custom_call_target="tpu_custom_call" | custom-call | tf_op jit(solution)/shard_map/attend_slots/pallas_call | solution.py:452
  92.3 3.1 %attend_slots.5 = bf16[48,4096]{1,0:T(8,128)(2,1)S(1)} custom-call(s32[8,8]{1,0:T(8,128)S(1)} %copy-done.12, s32[8,1,32]{2,1,0:T(1,128)S(1)} %broadcast_maximum_fusion.info, bf16[8,384,512]{2,1,0:T(8,128)(2,1)S(1)} %reshape.12.refs_0_, bf16[8,384,64]{2,1,0:T(8,128)(2,1)S(1)} %copy-done.3, bf16[32,512,128]{2,1,0:T(8,128)(2,1)S(1)} %copy-done.1, ...), custom_call_target="tpu_custom_call" | custom-call | tf_op jit(solution)/shard_map/attend_slots/pallas_call | solution.py:452
  95.4 2.1 %collective-permute-start.26 = (bf16[48,4096]{1,0:T(8,128)(2,1)S(1)}, bf16[48,4096]{1,0:T(8,128)(2,1)S(1)}, u32[]{:S(2)}, u32[]{:S(2)}) collective-permute-start(bf16[48,4096]{1,0:T(8,128)(2,1)S(1)} %attend_slots.5), channel_id=1, source_target_pairs={{8,0},{16,8},{24,16},{28,24},{20,28},{12,20},{4,12},{0,4},{9,1},{1... | collective-permute-start | bytes 1179656 | tf_op jit(solution)/shard_map/ppermute | solution.py:585
  97.8 7.3 %attend_slots.6.refs_7_ = f32[36,4096]{1,0:T(8,128)S(1)} custom-call(s32[8,8]{1,0:T(8,128)S(1)} %copy-done.12, s32[8,1,32]{2,1,0:T(1,128)S(1)} %broadcast_maximum_fusion.info, bf16[8,384,512]{2,1,0:T(8,128)(2,1)S(1)} %reshape.12.refs_0_, bf16[8,384,64]{2,1,0:T(8,128)(2,1)S(1)} %copy-done.3, bf16[32,512,128]{2,1,0:T(8,128)(2,1)S(1)} %copy-done.1, ...), custom_call_target="tpu_custom_call" | custom-call | tf_op jit(solution)/shard_map/attend_slots/pallas_call | solution.py:452
  105.1 2.9 %attend_slots.7 = bf16[48,4096]{1,0:T(8,128)(2,1)S(1)} custom-call(s32[8,8]{1,0:T(8,128)S(1)} %copy-done.12, s32[8,1,32]{2,1,0:T(1,128)S(1)} %broadcast_maximum_fusion.info, bf16[8,384,512]{2,1,0:T(8,128)(2,1)S(1)} %reshape.12.refs_0_, bf16[8,384,64]{2,1,0:T(8,128)(2,1)S(1)} %copy-done.3, bf16[32,512,128]{2,1,0:T(8,128)(2,1)S(1)} %copy-done.1, ...), custom_call_target="tpu_custom_call" | custom-call | tf_op jit(solution)/shard_map/attend_slots/pallas_call | solution.py:452
  116.4 2.3 %collective-permute-done.34.refs_3_ = bf16[96,896]{1,0:T(8,128)(2,1)S(1)} collective-permute-done((bf16[96,896]{1,0:T(8,128)(2,1)S(1)}, bf16[96,896]{1,0:T(8,128)(2,1)S(1)}, u32[]{:S(2)}, u32[]{:S(2)}) %collective-permute-start.34) | collective-permute-done | bytes 172064 | tf_op jit(solution)/shard_map/ppermute | solution.py:585
  126.6 2.5 %collective-permute-start.35 = (bf16[96,896]{1,0:T(8,128)(2,1)S(1)}, bf16[96,896]{1,0:T(8,128)(2,1)S(1)}, u32[]{:S(2)}, u32[]{:S(2)}) collective-permute-start(bf16[96,896]{1,0:T(8,128)(2,1)S(1)} %get-tuple-element.27), channel_id=1, source_target_pairs={{1,0},{0,1},{5,4},{4,5},{9,8},{11,10},{13,12},{15,14},{16,17},{18,... | collective-permute-start | bytes 516104 | tf_op jit(solution)/shard_map/ppermute | solution.py:585
  133.8 3.6 %collective-permute-done.36.refs_2_ = bf16[96,896]{1,0:T(8,128)(2,1)S(1)} collective-permute-done((bf16[96,896]{1,0:T(8,128)(2,1)S(1)}, bf16[96,896]{1,0:T(8,128)(2,1)S(1)}, u32[]{:S(2)}, u32[]{:S(2)}) %collective-permute-start.36) | collective-permute-done | bytes 172064 | tf_op jit(solution)/shard_map/ppermute | solution.py:585
  142.5 2.7 %collective-permute-done.37.refs_3_ = bf16[96,896]{1,0:T(8,128)(2,1)S(1)} collective-permute-done((bf16[96,896]{1,0:T(8,128)(2,1)S(1)}, bf16[96,896]{1,0:T(8,128)(2,1)S(1)}, u32[]{:S(2)}, u32[]{:S(2)}) %collective-permute-start.37) | collective-permute-done | bytes 172064 | tf_op jit(solution)/shard_map/ppermute | solution.py:585
  150.6 3.1 %collective-permute-done.31 = bf16[48,4096]{1,0:T(8,128)(2,1)S(1)} collective-permute-done((bf16[48,4096]{1,0:T(8,128)(2,1)S(1)}, bf16[48,4096]{1,0:T(8,128)(2,1)S(1)}, u32[]{:S(2)}, u32[]{:S(2)}) %collective-permute-start.31) | collective-permute-done | bytes 393248 | tf_op jit(solution)/shard_map/ppermute | solution.py:585
  156.0 2.5 %collective-permute-start.47 = (bf16[48,2048]{1,0:T(8,128)(2,1)S(1)}, bf16[48,2048]{1,0:T(8,128)(2,1)S(1)}, u32[]{:S(2)}, u32[]{:S(2)}) collective-permute-start(bf16[48,2048]{1,0:T(8,128)(2,1)S(1)} %slice.29), channel_id=1, source_target_pairs={{8,0},{16,8},{24,16},{28,24},{20,28},{12,20},{4,12},{0,4},{9,1},{1... | collective-permute-start | bytes 589832 | tf_op jit(solution)/shard_map/ppermute | solution.py:585
  162.2 6.2 %collective-permute-start.42 = (bf16[96,896]{1,0:T(8,128)(2,1)S(1)}, bf16[96,896]{1,0:T(8,128)(2,1)S(1)}, u32[]{:S(2)}, u32[]{:S(2)}) collective-permute-start(bf16[96,896]{1,0:T(8,128)(2,1)S(1)} %get-tuple-element.39), channel_id=1, source_target_pairs={{0,2},{1,3},{4,6},{5,7},{11,9},{9,11},{15,13},{13,15},{18,16},{16,... | collective-permute-start | bytes 516104 | tf_op jit(solution)/shard_map/ppermute | solution.py:585
  174.5 2.4 %collective-permute-done.43.refs_3_ = bf16[96,896]{1,0:T(8,128)(2,1)S(1)} collective-permute-done((bf16[96,896]{1,0:T(8,128)(2,1)S(1)}, bf16[96,896]{1,0:T(8,128)(2,1)S(1)}, u32[]{:S(2)}, u32[]{:S(2)}) %collective-permute-start.43) | collective-permute-done | bytes 172064 | tf_op jit(solution)/shard_map/ppermute | solution.py:585
  176.9 3.2 %collective-permute-done.50.refs_7_ = bf16[96,896]{1,0:T(8,128)(2,1)S(1)} collective-permute-done((bf16[96,896]{1,0:T(8,128)(2,1)S(1)}, bf16[96,896]{1,0:T(8,128)(2,1)S(1)}, u32[]{:S(2)}, u32[]{:S(2)}) %collective-permute-start.50) | collective-permute-done | bytes 172064 | tf_op jit(solution)/shard_map/ppermute | solution.py:585
  (154 shorter events, 74.8 us)
Async XLA Ops:
  1.1 16.4 %collective-permute-start.2 = (bf16[4,144,512]{2,1,0:T(8,128)(2,1)S(1)}, bf16[4,144,512]{2,1,0:T(8,128)(2,1)S(1)}, u32[]{:S(2)}, u32[]{:S(2)}) collective-permute-start(bf16[4,144,512]{2,1,0:T(8,128)(2,1)S(1)} %payload.1), channel_id=1, source_target_pairs={{8,0},{16,8},{24,16},{28,24},{20,28},{12,20},{4,12},{0,4},{9,1},{1... | collective-permute-start | bytes 1769480 | tf_op jit(solution)/shard_map/ppermute | solution.py:585
  4.1 15.1 %collective-permute-start = (bf16[4,144,512]{2,1,0:T(8,128)(2,1)S(1)}, bf16[4,144,512]{2,1,0:T(8,128)(2,1)S(1)}, u32[]{:S(2)}, u32[]{:S(2)}) collective-permute-start(bf16[4,144,512]{2,1,0:T(8,128)(2,1)S(1)} %payload.1), channel_id=1, source_target_pairs={{0,8},{8,16},{16,24},{24,28},{28,20},{20,12},{12,4},{4,0},{1,9},{9... | collective-permute-start | bytes 1769480 | tf_op jit(solution)/shard_map/ppermute | solution.py:585
  17.5 14.5 %collective-permute-start.3 = (bf16[4,144,512]{2,1,0:T(8,128)(2,1)S(1)}, bf16[4,144,512]{2,1,0:T(8,128)(2,1)S(1)}, u32[]{:S(2)}, u32[]{:S(2)}) collective-permute-start(bf16[4,144,512]{2,1,0:T(8,128)(2,1)S(1)} %collective-permute-done.2.b_ref), channel_id=1, source_target_pairs={{8,0},{16,8},{24,16},{28,24},{20,28},{12,20},{4,12},{0,4},{9,1},{1... | collective-permute-start | bytes 1769480 | tf_op jit(solution)/shard_map/ppermute | solution.py:585
  19.2 14.2 %collective-permute-start.1 = (bf16[4,144,512]{2,1,0:T(8,128)(2,1)S(1)}, bf16[4,144,512]{2,1,0:T(8,128)(2,1)S(1)}, u32[]{:S(2)}, u32[]{:S(2)}) collective-permute-start(bf16[4,144,512]{2,1,0:T(8,128)(2,1)S(1)} %collective-permute-done.a_ref), channel_id=1, source_target_pairs={{0,8},{8,16},{16,24},{24,28},{28,20},{20,12},{12,4},{4,0},{1,9},{9... | collective-permute-start | bytes 1769480 | tf_op jit(solution)/shard_map/ppermute | solution.py:585
  53.7 25.7 %collective-permute-start.4 = (bf16[2,144,512]{2,1,0:T(8,128)(2,1)}, bf16[2,144,512]{2,1,0:T(8,128)(2,1)}, u32[]{:S(2)}, u32[]{:S(2)}) collective-permute-start(bf16[2,144,512]{2,1,0:T(8,128)(2,1)} %choose.4.refs_3_), channel_id=1, source_target_pairs={{0,1},{1,0},{2,3},{3,2},{4,5},{5,4},{6,7},{7,6},{8,9},{9,8},{10,11... | collective-permute-start | bytes 884744 | tf_op jit(solution)/shard_map/ppermute | solution.py:585
  55.7 24.0 %collective-permute-start.18 = (bf16[1,144,512]{2,1,0:T(8,128)(2,1)}, bf16[1,144,512]{2,1,0:T(8,128)(2,1)}, u32[]{:S(2)}, u32[]{:S(2)}) collective-permute-start(bf16[1,144,512]{2,1,0:T(8,128)(2,1)} %choose.6.refs_3_), channel_id=1, source_target_pairs={{0,2},{1,3},{2,0},{3,1},{4,6},{5,7},{6,4},{7,5},{8,10},{9,11},{10,... | collective-permute-start | bytes 442376 | tf_op jit(solution)/shard_map/ppermute | solution.py:585
  60.0 32.2 %collective-permute-start.6 = (bf16[2,144,512]{2,1,0:T(8,128)(2,1)}, bf16[2,144,512]{2,1,0:T(8,128)(2,1)}, u32[]{:S(2)}, u32[]{:S(2)}) collective-permute-start(bf16[2,144,512]{2,1,0:T(8,128)(2,1)} %collective-permute-done.5.refs_5_), channel_id=1, source_target_pairs={{0,1},{1,0},{2,3},{3,2},{4,5},{5,4},{6,7},{7,6},{8,9},{9,8},{10,11... | collective-permute-start | bytes 884744 | tf_op jit(solution)/shard_map/ppermute | solution.py:585
  60.8 36.8 %collective-permute-start.20 = (bf16[2,144,512]{2,1,0:T(8,128)(2,1)}, bf16[2,144,512]{2,1,0:T(8,128)(2,1)}, u32[]{:S(2)}, u32[]{:S(2)}) collective-permute-start(bf16[2,144,512]{2,1,0:T(8,128)(2,1)} %choose.7.refs_7_.refs_11_), channel_id=1, source_target_pairs={{0,1},{1,0},{2,3},{3,2},{4,5},{5,4},{6,7},{7,6},{8,9},{9,8},{10,11... | collective-permute-start | bytes 884744 | tf_op jit(solution)/shard_map/ppermute | solution.py:585
  66.3 31.4 %collective-permute-start.22 = (bf16[2,144,512]{2,1,0:T(8,128)(2,1)}, bf16[2,144,512]{2,1,0:T(8,128)(2,1)}, u32[]{:S(2)}, u32[]{:S(2)}) collective-permute-start(bf16[2,144,512]{2,1,0:T(8,128)(2,1)} %collective-permute-done.21.refs_9_.refs_13_), channel_id=1, source_target_pairs={{0,1},{1,0},{2,3},{3,2},{4,5},{5,4},{6,7},{7,6},{8,9},{9,8},{10,11... | collective-permute-start | bytes 884744 | tf_op jit(solution)/shard_map/ppermute | solution.py:585
  79.4 25.7 %collective-permute-start.17 = (bf16[1,144,512]{2,1,0:T(8,128)(2,1)}, bf16[1,144,512]{2,1,0:T(8,128)(2,1)}, u32[]{:S(2)}, u32[]{:S(2)}) collective-permute-start(bf16[1,144,512]{2,1,0:T(8,128)(2,1)} %choose.6.refs_3_), channel_id=1, source_target_pairs={{0,1},{1,0},{2,3},{3,2},{4,5},{5,4},{6,7},{7,6},{8,9},{9,8},{10,11... | collective-permute-start | bytes 442376 | tf_op jit(solution)/shard_map/ppermute | solution.py:585
  79.7 25.4 %collective-permute-start.19 = (bf16[1,144,512]{2,1,0:T(8,128)(2,1)}, bf16[1,144,512]{2,1,0:T(8,128)(2,1)}, u32[]{:S(2)}, u32[]{:S(2)}) collective-permute-start(bf16[1,144,512]{2,1,0:T(8,128)(2,1)} %collective-permute-done.18.refs_5_), channel_id=1, source_target_pairs={{0,1},{1,0},{2,3},{3,2},{4,5},{5,4},{6,7},{7,6},{8,9},{9,8},{10,11... | collective-permute-start | bytes 442376 | tf_op jit(solution)/shard_map/ppermute | solution.py:585
  95.4 17.8 %collective-permute-start.26 = (bf16[48,4096]{1,0:T(8,128)(2,1)S(1)}, bf16[48,4096]{1,0:T(8,128)(2,1)S(1)}, u32[]{:S(2)}, u32[]{:S(2)}) collective-permute-start(bf16[48,4096]{1,0:T(8,128)(2,1)S(1)} %attend_slots.5), channel_id=1, source_target_pairs={{8,0},{16,8},{24,16},{28,24},{20,28},{12,20},{4,12},{0,4},{9,1},{1... | collective-permute-start | bytes 1179656 | tf_op jit(solution)/shard_map/ppermute | solution.py:585
  97.5 17.1 %collective-permute-start.10 = (bf16[48,4096]{1,0:T(8,128)(2,1)S(1)}, bf16[48,4096]{1,0:T(8,128)(2,1)S(1)}, u32[]{:S(2)}, u32[]{:S(2)}) collective-permute-start(bf16[48,4096]{1,0:T(8,128)(2,1)S(1)} %attend_slots.5), channel_id=1, source_target_pairs={{0,8},{8,16},{16,24},{24,28},{28,20},{20,12},{12,4},{4,0},{1,9},{9... | collective-permute-start | bytes 1179656 | tf_op jit(solution)/shard_map/ppermute | solution.py:585
  108.0 13.9 %collective-permute-start.29 = (bf16[48,4096]{1,0:T(8,128)(2,1)S(1)}, bf16[48,4096]{1,0:T(8,128)(2,1)S(1)}, u32[]{:S(2)}, u32[]{:S(2)}) collective-permute-start(bf16[48,4096]{1,0:T(8,128)(2,1)S(1)} %attend_slots.7), channel_id=1, source_target_pairs={{8,0},{16,8},{24,16},{28,24},{20,28},{12,20},{4,12},{0,4},{9,1},{1... | collective-permute-start | bytes 1179656 | tf_op jit(solution)/shard_map/ppermute | solution.py:585
  109.8 13.9 %collective-permute-start.23 = (bf16[48,4096]{1,0:T(8,128)(2,1)S(1)}, bf16[48,4096]{1,0:T(8,128)(2,1)S(1)}, u32[]{:S(2)}, u32[]{:S(2)}) collective-permute-start(bf16[48,4096]{1,0:T(8,128)(2,1)S(1)} %attend_slots.7), channel_id=1, source_target_pairs={{0,8},{8,16},{16,24},{24,28},{28,20},{20,12},{12,4},{4,0},{1,9},{9... | collective-permute-start | bytes 1179656 | tf_op jit(solution)/shard_map/ppermute | solution.py:585
  114.6 14.6 %collective-permute-start.27 = (bf16[48,4096]{1,0:T(8,128)(2,1)S(1)}, bf16[48,4096]{1,0:T(8,128)(2,1)S(1)}, u32[]{:S(2)}, u32[]{:S(2)}) collective-permute-start(bf16[48,4096]{1,0:T(8,128)(2,1)S(1)} %collective-permute-done.26), channel_id=1, source_target_pairs={{8,0},{16,8},{24,16},{28,24},{20,28},{12,20},{4,12},{0,4},{9,1},{1... | collective-permute-start | bytes 1179656 | tf_op jit(solution)/shard_map/ppermute | solution.py:585
  121.9 16.7 %collective-permute-start.30 = (bf16[48,4096]{1,0:T(8,128)(2,1)S(1)}, bf16[48,4096]{1,0:T(8,128)(2,1)S(1)}, u32[]{:S(2)}, u32[]{:S(2)}) collective-permute-start(bf16[48,4096]{1,0:T(8,128)(2,1)S(1)} %collective-permute-done.29), channel_id=1, source_target_pairs={{8,0},{16,8},{24,16},{28,24},{20,28},{12,20},{4,12},{0,4},{9,1},{1... | collective-permute-start | bytes 1179656 | tf_op jit(solution)/shard_map/ppermute | solution.py:585
  123.7 16.7 %collective-permute-start.24 = (bf16[48,4096]{1,0:T(8,128)(2,1)S(1)}, bf16[48,4096]{1,0:T(8,128)(2,1)S(1)}, u32[]{:S(2)}, u32[]{:S(2)}) collective-permute-start(bf16[48,4096]{1,0:T(8,128)(2,1)S(1)} %collective-permute-done.23), channel_id=1, source_target_pairs={{0,8},{8,16},{16,24},{24,28},{28,20},{20,12},{12,4},{4,0},{1,9},{9... | collective-permute-start | bytes 1179656 | tf_op jit(solution)/shard_map/ppermute | solution.py:585
  130.5 17.0 %collective-permute-start.28 = (bf16[48,4096]{1,0:T(8,128)(2,1)S(1)}, bf16[48,4096]{1,0:T(8,128)(2,1)S(1)}, u32[]{:S(2)}, u32[]{:S(2)}) collective-permute-start(bf16[48,4096]{1,0:T(8,128)(2,1)S(1)} %collective-permute-done.27), channel_id=1, source_target_pairs={{8,0},{16,8},{24,16},{28,24},{20,28},{12,20},{4,12},{0,4},{9,1},{1... | collective-permute-start | bytes 1179656 | tf_op jit(solution)/shard_map/ppermute | solution.py:585
  132.5 16.3 %collective-permute-start.12 = (bf16[48,4096]{1,0:T(8,128)(2,1)S(1)}, bf16[48,4096]{1,0:T(8,128)(2,1)S(1)}, u32[]{:S(2)}, u32[]{:S(2)}) collective-permute-start(bf16[48,4096]{1,0:T(8,128)(2,1)S(1)} %collective-permute-done.11), channel_id=1, source_target_pairs={{0,8},{8,16},{16,24},{24,28},{28,20},{20,12},{12,4},{4,0},{1,9},{9... | collective-permute-start | bytes 1179656 | tf_op jit(solution)/shard_map/ppermute | solution.py:585
  138.6 15.1 %collective-permute-start.31 = (bf16[48,4096]{1,0:T(8,128)(2,1)S(1)}, bf16[48,4096]{1,0:T(8,128)(2,1)S(1)}, u32[]{:S(2)}, u32[]{:S(2)}) collective-permute-start(bf16[48,4096]{1,0:T(8,128)(2,1)S(1)} %collective-permute-done.30), channel_id=1, source_target_pairs={{8,0},{16,8},{24,16},{28,24},{20,28},{12,20},{4,12},{0,4},{9,1},{1... | collective-permute-start | bytes 1179656 | tf_op jit(solution)/shard_map/ppermute | solution.py:585
  140.4 14.8 %collective-permute-start.25 = (bf16[48,4096]{1,0:T(8,128)(2,1)S(1)}, bf16[48,4096]{1,0:T(8,128)(2,1)S(1)}, u32[]{:S(2)}, u32[]{:S(2)}) collective-permute-start(bf16[48,4096]{1,0:T(8,128)(2,1)S(1)} %collective-permute-done.24), channel_id=1, source_target_pairs={{0,8},{8,16},{16,24},{24,28},{28,20},{20,12},{12,4},{4,0},{1,9},{9... | collective-permute-start | bytes 1179656 | tf_op jit(solution)/shard_map/ppermute | solution.py:585
  153.7 14.7 %collective-permute-start.44 = (bf16[48,2048]{1,0:T(8,128)(2,1)S(1)}, bf16[48,2048]{1,0:T(8,128)(2,1)S(1)}, u32[]{:S(2)}, u32[]{:S(2)}) collective-permute-start(bf16[48,2048]{1,0:T(8,128)(2,1)S(1)} %slice.26), channel_id=1, source_target_pairs={{0,8},{8,16},{16,24},{24,28},{28,20},{20,12},{12,4},{4,0},{1,9},{9... | collective-permute-start | bytes 589832 | tf_op jit(solution)/shard_map/ppermute | solution.py:585
  156.0 13.9 %collective-permute-start.47 = (bf16[48,2048]{1,0:T(8,128)(2,1)S(1)}, bf16[48,2048]{1,0:T(8,128)(2,1)S(1)}, u32[]{:S(2)}, u32[]{:S(2)}) collective-permute-start(bf16[48,2048]{1,0:T(8,128)(2,1)S(1)} %slice.29), channel_id=1, source_target_pairs={{8,0},{16,8},{24,16},{28,24},{20,28},{12,20},{4,12},{0,4},{9,1},{1... | collective-permute-start | bytes 589832 | tf_op jit(solution)/shard_map/ppermute | solution.py:585
  (48 other events, 417.3 us)

commit v4 on v3

--- a/solution.py
+++ b/solution.py
@@ -309,48 +309,81 @@
     )(in_hbm(cache_latent), in_hbm(cache_rope))
 
 
-def choose_kernel(cut, column, table, a_ref, b_ref, out_ref):
-    if cut is None:
-        out_ref[0] = a_ref[0]
-        out_ref[1] = b_ref[0]
+def upper(rows):
+    return (rows // 2 + 15) // 16 * 16
+
+
+def relay_kernel(bundles, offsets, table, info, loads, seen, fore, back, *outs):
+    chosen, sends = outs[0], outs[1:]
+    me = table[PLACE, 0]
+    last = len(offsets) // 2
+    rows = fore.shape[1]
+    for side, (way, arrived, out) in enumerate(((1, fore, sends[0]), (-1, back, sends[1]))):
+        chosen[side] = arrived[table[SLOT, offsets.index(-way)]]
+        owner = seen[me, offsets.index(-way)]
+        for d in range(2, last + 1):
+            asker = seen[me, offsets.index(way * (d - 1))]
+            pick = jnp.int32(0)
+            for b in range(bundles):
+                hit = info[asker, 0, b] == owner
+                pick = jnp.where(hit, info[asker, 0, bundles + b], pick)
+            slot = lax.rem(pick, loads[owner])
+            start = (d - 2) * rows
+            if d < last:
+                out[pl.ds(start, rows), :] = arrived[slot]
+            elif way == 1:
+                out[pl.ds(start, upper(rows)), :] = arrived[slot, : upper(rows), :]
+            else:
+                out[pl.ds(start, rows - upper(rows)), :] = arrived[slot, upper(rows) :, :]
+
+
+def relay(table, info, loads, seen, bundles, offsets, fore, back):
+    _, rows, wide = fore.shape
+    full = (len(offsets) // 2 - 2) * rows
+    vmem = pl.BlockSpec(memory_space=pltpu.MemorySpace.VMEM)
+    smem = pl.BlockSpec(memory_space=pltpu.MemorySpace.SMEM)
+    return pl.pallas_call(
+        functools.partial(relay_kernel, bundles, offsets),
+        out_shape=[
+            jax.ShapeDtypeStruct((2, rows, wide), fore.dtype),
+            jax.ShapeDtypeStruct((full + upper(rows), wide), fore.dtype),
+            jax.ShapeDtypeStruct((full + rows - upper(rows), wide), fore.dtype),
+        ],
+        in_specs=[smem] * 4 + [vmem] * 2,
+        out_specs=[vmem] * 3,
+        compiler_params=pltpu.CompilerParams(vmem_limit_bytes=6 * 2**20),
+        name="relay",
+    )(table, info, loads, seen, fore, back)
+
+
+def join_kernel(rows, fore, back, out):
+    if out.shape[0] == 2:
+        out[0] = fore[:rows, :]
+        out[1] = back[:rows, :]
     else:
-        first = table[SLOT, column] < cut
-
-        @pl.when(first)
-        def _():
-            out_ref[0] = a_ref[0]
-
-        @pl.when(jnp.logical_not(first))
-        def _():
-            out_ref[0] = b_ref[0]
-
-
-def choose(table, a, b, columns, cut=None):
-    _, rows, wide = a.shape
-    if cut is None:
-        index_a = lambda i, table: (table[SLOT, columns[0]], 0, 0)
-        index_b = lambda i, table: (table[SLOT, columns[1]], 0, 0)
-    else:
-        index_a = lambda i, table: (jnp.minimum(table[SLOT, columns[0]], cut - 1), 0, 0)
-        index_b = lambda i, table: (jnp.maximum(table[SLOT, columns[0]] - cut, 0), 0, 0)
+        out[0, : fore.shape[0], :] = fore[...]
+        out[0, fore.shape[0] :, :] = back[...]
+
+
+def join(count, rows, fore, back):
+    vmem = pl.BlockSpec(memory_space=pltpu.MemorySpace.VMEM)
     return pl.pallas_call(
-        functools.partial(choose_kernel, cut, columns[0]),
-        out_shape=jax.ShapeDtypeStruct((len(columns), rows, wide), a.dtype),
-        grid_spec=pltpu.PrefetchScalarGridSpec(
-            num_scalar_prefetch=1,
-            grid=(1,),
-            in_specs=[pl.BlockSpec((1, rows, wide), index_a), pl.BlockSpec((1, rows, wide), index_b)],
-            out_specs=pl.BlockSpec((len(columns), rows, wide), lambda i, *_: (0, 0, 0)),
-        ),
+        functools.partial(join_kernel, rows),
+        out_shape=jax.ShapeDtypeStruct((count, rows, fore.shape[1]), fore.dtype),
+        in_specs=[vmem] * 2,
+        out_specs=vmem,
         compiler_params=pltpu.CompilerParams(vmem_limit_bytes=4 * 2**20),
-        name="choose",
-    )(table, a, b)
+        name="join",
+    )(fore, back)
 
 
 def slots_kernel(plan, own, indices, bundles, final, scale, table, info, *refs):
     count, heads = len(plan), len(indices[0])
     refs = list(refs)
-    q_ref, qr_ref, w_ref = refs.pop(0), refs.pop(0), refs.pop(0)
+    q_ref, qr_ref, w_hbm = refs.pop(0), refs.pop(0), refs.pop(0)
+    w_ref, w_sem = refs.pop(-2), refs.pop(-1)
+    w_copy = pltpu.make_async_copy(w_hbm, w_ref, w_sem)
+    w_copy.start()
     if own:
         full_lat, full_rope = refs.pop(0), refs.pop(0)
     parts = [[(refs.pop(0), index) for index in slot] for slot in indices]
@@ -389,7 +422,7 @@
                     rope[pl.ds(pl.multiple_of(to * dims, dims), dims), :] = part[index, rows:, :]
 
         column = plan[0] + j
-        length = info[table[OWNER, column], 0, bundles + table[SLOT, column]]
+        length = info[table[OWNER, column], 0, 2 * bundles + table[SLOT, column]]
         b = table[BUNDLE, column]
         past = lax.broadcasted_iota(jnp.int32, (1, lat.shape[0]), 1) >= length
         s = lax.dot_general(
@@ -406,6 +439,7 @@
         return 0
 
     lax.fori_loop(0, count, bundle, 0)
+    w_copy.wait()
     local_heads, _, value_width = w_ref.shape
     n = mixed.shape[1] // local_heads
     at = 0
@@ -436,7 +470,7 @@
     local_heads, _, value_width = w_uv.shape
     vmem = pl.BlockSpec(memory_space=pltpu.MemorySpace.VMEM)
     smem = pl.BlockSpec(memory_space=pltpu.MemorySpace.SMEM)
-    args, in_specs = [q, qr, w_uv], [vmem] * 3
+    args, in_specs = [q, qr, in_hbm(w_uv)], [vmem, vmem, pl.BlockSpec(memory_space=pl.ANY)]
     if own:
         args += [in_hbm(x) for x in full]
         in_specs += [pl.BlockSpec(memory_space=pl.ANY)] * 2
@@ -449,6 +483,7 @@
     if own:
         scratch += caches + [pltpu.SemaphoreType.DMA((2,))]
     scratch += caches + [pltpu.VMEM((wide // 128, count * q_rows, 128), jnp.float32)]
+    scratch += [pltpu.VMEM(w_uv.shape, w_uv.dtype), pltpu.SemaphoreType.DMA]
     return pl.pallas_call(
         functools.partial(
             slots_kernel, plan, own, [[index for _, index in slot] for slot in parts], bundles,
@@ -458,7 +493,7 @@
         in_specs=[smem] * 2 + in_specs,
         out_specs=vmem,
         scratch_shapes=scratch,
-        compiler_params=pltpu.CompilerParams(vmem_limit_bytes=14 * 2**20),
+        compiler_params=pltpu.CompilerParams(vmem_limit_bytes=18 * 2**20),
         name="attend_slots",
     )(table, info, *args)
 
@@ -585,9 +620,8 @@
         return lax.ppermute(x, axis, pairs)
 
     payload = payload_of(cache_latent, cache_rope, heads)
-    slots = payload.shape[0]
     fore, back = move(payload, ahead), move(payload, behind)
-    facts = jnp.concatenate([owner_rank, lengths])
+    facts = jnp.concatenate([owner_rank, owner_pick, lengths])
     width = 32
     facts = jnp.pad(facts, (0, width - facts.shape[0]))
     info = lax.all_to_all(
@@ -608,21 +642,20 @@
             bit //= 2
         return [found[m] for m in range(heads)]
 
+    rows = payload.shape[1]
+    chosen, fore, back = relay(table, info, loads, seen, bundles, offsets, fore, back)
     groups = {}
-    for k in range(1, last):
+    for k in range(1, last + 1):
         if k > 1:
+            if k > 2:
+                fore, back = fore[rows:], back[rows:]
             fore = move(fore, ahead)
             back = move(back, behind)
-        chosen = choose(table, fore, back, [2 * k - 1, 2 * k])
+            chosen = join(2 if k < last else 1, rows, fore, back)
         parts = share(chosen)
         groups[2 * k - 1] = [(p, 0) for p in parts]
-        groups[2 * k] = [(p, 1) for p in parts]
-    cut = slots // 2
-    left = move(fore[:cut], ahead)
-    right = move(back[cut:], behind)
-    chosen = choose(table, left, right, [2 * last - 1], cut)
-    parts = share(chosen)
-    groups[2 * last - 1] = [(p, 0) for p in parts]
+        if k < last:
+            groups[2 * k] = [(p, 1) for p in parts]
 
     def attend(plan, full=None, earlier=None):
         return attend_slots(

time: 183 us -> 169 us (0.923)
  waiting for transfers between devices: 58.5 us -> 49.2 us
  starting transfers between devices: 64.3 us -> 59.8 us
    ppermute x51, waiting for transfers between devices: 58.5 us -> 41.4 us  [move(): return lax.ppermute(x, axis, pairs)]
    all_to_all x1, waiting for transfers between devices: 0.01 us -> 7.73 us  [local_ring(): lax.all_to_all(jnp.broadcast_to(facts[None], (ranks, width)), 'dp', split...]
    ppermute x51, starting transfers between devices: 58.8 us -> 53.5 us  [move(): return lax.ppermute(x, axis, pairs)]
    pallas_call x4, Pallas kernels: 19.3 us -> 22.5 us  [attend_slots(): pl.pallas_call(functools.partial(slots_kernel, plan, own, [[index for _,...]
    pallas_call x4, Pallas kernels: 4.59 us -> 2.29 us  [the longest x3 1.43 us: join(): pl.pallas_call(functools.partial(join_kernel, rows), out_shape=jax.ShapeD...]
    unnamed x40 -> x38, local copies, waits for them, and re-layouts: 10.9 us -> 9.16 us
  transfers between devices with their start and end apart: 52 -> 52, of which waited for: 13 -> 16; matrix products, arithmetic and copies ran while one was open for 9% -> 10% of each run, Pallas kernels for 16% -> 17%
where the time goes in v4:
time: 169 us; the launch traced here: 168 us
  starting transfers between devices  59.8 us (35%)
  waiting for transfers between devices  49.2 us (29%)
  Pallas kernels  33 us (20%)
  local copies, waits for them, and re-layouts  16.7 us (10%)
  matrix products  7.92 us (5%)
    ppermute x51, starting transfers between devices, move(): return lax.ppermute(x, axis, pairs)  53.5 us
    ppermute x51, waiting for transfers between devices, move(): return lax.ppermute(x, axis, pairs)  41.4 us
    pallas_call x4, Pallas kernels, attend_slots(): pl.pallas_call(functools.partial(slots_kernel, plan, own, [[index for _,...  22.5 us
    unnamed x38, local copies, waits for them, and re-layouts  9.16 us
    dot_general x5, matrix products, project(): jnp.dot(jnp.concatenate(pieces), w_out, preferred_element_type=jnp.float32)  7.92 us
    all_to_all x1, waiting for transfers between devices, local_ring(): lax.all_to_all(jnp.broadcast_to(facts[None], (ranks, width)), 'dp', split...  7.73 us
    all_to_all x1, starting transfers between devices, local_ring(): lax.all_to_all(jnp.broadcast_to(facts[None], (ranks, width)), 'dp', split...  6.28 us
    reshape x1, local copies, waits for them, and re-layouts, local_ring(): q = q_latent.reshape(bundles, roll_count * local_heads, -1)  4.2 us
  transfers between devices with their start and end apart: 52, of which 16 were waited for; matrix products, arithmetic and copies ran while one was open for 10% of the time, Pallas kernels for 17%

profile of v4, /device:TPU:0, one launch (start us, length us, event | category | flops | bytes accessed | tf_op | source)
XLA Modules:
  0.0 167.9 jit_solution(8107579310285595591)
XLA Ops:
  1.1 3.1 %collective-permute-start = (bf16[4,144,512]{2,1,0:T(8,128)(2,1)S(1)}, bf16[4,144,512]{2,1,0:T(8,128)(2,1)S(1)}, u32[]{:S(2)}, u32[]{:S(2)}) collective-permute-start(bf16[4,144,512]{2,1,0:T(8,128)(2,1)S(1)} %payload.1), channel_id=1, source_target_pairs={{0,8},{8,16},{16,24},{24,28},{28,20},{20,12},{12,4},{4,0},{1,9},{9... | collective-permute-start | bytes 1769480 | tf_op jit(solution)/shard_map/ppermute | solution.py:620
  5.5 6.3 %all-to-all-start = ((s32[8,1,32]{2,1,0:T(1,128)}), s32[8,1,32]{2,1,0:T(1,128)S(1)}, u32[]{:S(2)}, u32[]{:S(2)}) async-start(s32[8,1,32]{2,1,0:T(1,128)} %broadcast_in_dim.2), calls=%async_computation | async-start | bytes 8192 | tf_op jit(solution)/shard_map/all_to_all | solution.py:627
  13.3 7.7 %all-to-all-done = s32[8,1,32]{2,1,0:T(1,128)S(1)} async-done(((s32[8,1,32]{2,1,0:T(1,128)}), s32[8,1,32]{2,1,0:T(1,128)S(1)}, u32[]{:S(2)}, u32[]{:S(2)}) %all-to-all-start) | async-done | bytes 1056 | tf_op jit(solution)/shard_map/all_to_all | solution.py:627
  27.5 5.5 %collective-permute-done.2.fore = bf16[368,512]{1,0:T(8,128)(2,1)S(1)} collective-permute-done((bf16[368,512]{1,0:T(8,128)(2,1)S(1)}, bf16[368,512]{1,0:T(8,128)(2,1)S(1)}, u32[]{:S(2)}, u32[]{:S(2)}) %collective-permute-start.2) | collective-permute-done | bytes 376864 | tf_op jit(solution)/shard_map/ppermute | solution.py:620
  36.8 2.8 %collective-permute-done.15.back = bf16[208,512]{1,0:T(8,128)(2,1)S(1)} collective-permute-done((bf16[208,512]{1,0:T(8,128)(2,1)S(1)}, bf16[208,512]{1,0:T(8,128)(2,1)S(1)}, u32[]{:S(2)}, u32[]{:S(2)}) %collective-permute-start.15) | collective-permute-done | bytes 213024 | tf_op jit(solution)/shard_map/ppermute | solution.py:620
  44.3 2.1 %collective-permute-done.16.back = bf16[64,512]{1,0:T(8,128)(2,1)S(1)} collective-permute-done((bf16[64,512]{1,0:T(8,128)(2,1)S(1)}, bf16[64,512]{1,0:T(8,128)(2,1)S(1)}, u32[]{:S(2)}, u32[]{:S(2)}) %collective-permute-start.16) | collective-permute-done | bytes 65568 | tf_op jit(solution)/shard_map/ppermute | solution.py:620
  47.2 3.6 %collective-permute-done.14.fore = bf16[80,512]{1,0:T(8,128)(2,1)S(1)} collective-permute-done((bf16[80,512]{1,0:T(8,128)(2,1)S(1)}, bf16[80,512]{1,0:T(8,128)(2,1)S(1)}, u32[]{:S(2)}, u32[]{:S(2)}) %collective-permute-start.14) | collective-permute-done | bytes 81952 | tf_op jit(solution)/shard_map/ppermute | solution.py:620
  55.0 4.1 %collective-permute-done.18.refs_5_ = bf16[1,144,512]{2,1,0:T(8,128)(2,1)} collective-permute-done((bf16[1,144,512]{2,1,0:T(8,128)(2,1)}, bf16[1,144,512]{2,1,0:T(8,128)(2,1)}, u32[]{:S(2)}, u32[]{:S(2)}) %collective-permute-start.18) | collective-permute-done | bytes 147488 | tf_op jit(solution)/shard_map/ppermute | solution.py:620
  59.2 4.2 %reshape.12.refs_0_ = bf16[8,384,512]{2,1,0:T(8,128)(2,1)S(1)} reshape(bf16[96,16384]{1,0:T(8,128)(2,1)} %param.11) | data formatting | bytes 6291456 | tf_op jit(solution)/shard_map/reshape | solution.py:632
  63.4 2.6 %reshape.13.refs_1_ = bf16[8,384,64]{2,1,0:T(8,128)(2,1)} reshape(bf16[96,2048]{1,0:T(8,128)(2,1)} %param.12) | data formatting | bytes 786432 | tf_op jit(solution)/shard_map/reshape | solution.py:633
  71.0 6.3 %attend_slots.4.refs_7_ = f32[36,4096]{1,0:T(8,128)S(1)} custom-call(s32[8,8]{1,0:T(8,128)S(1)} %copy-done.13, s32[8,1,32]{2,1,0:T(1,128)S(1)} %broadcast_maximum_fusion.info, bf16[8,384,512]{2,1,0:T(8,128)(2,1)S(1)} %reshape.12.refs_0_, bf16[8,384,64]{2,1,0:T(8,128)(2,1)S(1)} %copy-done, bf16[32,512,128]{2,1,0:T(8,128)(2,1)} %refs_2_.7, ...), custom_call_target="tpu_custom_call" | custom-call | tf_op jit(solution)/shard_map/attend_slots/pallas_call | solution.py:487
  77.3 4.8 %attend_slots.5 = bf16[48,4096]{1,0:T(8,128)(2,1)S(1)} custom-call(s32[8,8]{1,0:T(8,128)S(1)} %copy-done.13, s32[8,1,32]{2,1,0:T(1,128)S(1)} %broadcast_maximum_fusion.info, bf16[8,384,512]{2,1,0:T(8,128)(2,1)S(1)} %reshape.12.refs_0_, bf16[8,384,64]{2,1,0:T(8,128)(2,1)S(1)} %copy-done, bf16[32,512,128]{2,1,0:T(8,128)(2,1)} %refs_2_.7, ...), custom_call_target="tpu_custom_call" | custom-call | tf_op jit(solution)/shard_map/attend_slots/pallas_call | solution.py:487
  84.3 7.0 %attend_slots.6.refs_7_ = f32[36,4096]{1,0:T(8,128)S(1)} custom-call(s32[8,8]{1,0:T(8,128)S(1)} %copy-done.13, s32[8,1,32]{2,1,0:T(1,128)S(1)} %broadcast_maximum_fusion.info, bf16[8,384,512]{2,1,0:T(8,128)(2,1)S(1)} %reshape.12.refs_0_, bf16[8,384,64]{2,1,0:T(8,128)(2,1)S(1)} %copy-done.1, bf16[32,512,128]{2,1,0:T(8,128)(2,1)} %refs_2_.7, ...), custom_call_target="tpu_custom_call" | custom-call | tf_op jit(solution)/shard_map/attend_slots/pallas_call | solution.py:487
  91.3 4.4 %attend_slots.7 = bf16[48,4096]{1,0:T(8,128)(2,1)S(1)} custom-call(s32[8,8]{1,0:T(8,128)S(1)} %copy-done.13, s32[8,1,32]{2,1,0:T(1,128)S(1)} %broadcast_maximum_fusion.info, bf16[8,384,512]{2,1,0:T(8,128)(2,1)S(1)} %reshape.12.refs_0_, bf16[8,384,64]{2,1,0:T(8,128)(2,1)S(1)} %copy-done.1, bf16[32,512,128]{2,1,0:T(8,128)(2,1)} %refs_2_.7, ...), custom_call_target="tpu_custom_call" | custom-call | tf_op jit(solution)/shard_map/attend_slots/pallas_call | solution.py:487
  105.1 4.3 %collective-permute-done.33.refs_2_ = bf16[96,896]{1,0:T(8,128)(2,1)S(1)} collective-permute-done((bf16[96,896]{1,0:T(8,128)(2,1)S(1)}, bf16[96,896]{1,0:T(8,128)(2,1)S(1)}, u32[]{:S(2)}, u32[]{:S(2)}) %collective-permute-start.33) | collective-permute-done | bytes 172064 | tf_op jit(solution)/shard_map/ppermute | solution.py:620
  117.4 3.2 %collective-permute-done.11 = bf16[48,4096]{1,0:T(8,128)(2,1)S(1)} collective-permute-done((bf16[48,4096]{1,0:T(8,128)(2,1)S(1)}, bf16[48,4096]{1,0:T(8,128)(2,1)S(1)}, u32[]{:S(2)}, u32[]{:S(2)}) %collective-permute-start.11) | collective-permute-done | bytes 393248 | tf_op jit(solution)/shard_map/ppermute | solution.py:620
  121.8 2.4 %collective-permute-start.28 = (bf16[48,4096]{1,0:T(8,128)(2,1)S(1)}, bf16[48,4096]{1,0:T(8,128)(2,1)S(1)}, u32[]{:S(2)}, u32[]{:S(2)}) collective-permute-start(bf16[48,4096]{1,0:T(8,128)(2,1)S(1)} %collective-permute-done.27), channel_id=1, source_target_pairs={{8,0},{16,8},{24,16},{28,24},{20,28},{12,20},{4,12},{0,4},{9,1},{1... | collective-permute-start | bytes 1179656 | tf_op jit(solution)/shard_map/ppermute | solution.py:620
  130.9 3.0 %collective-permute-done.28 = bf16[48,4096]{1,0:T(8,128)(2,1)S(1)} collective-permute-done((bf16[48,4096]{1,0:T(8,128)(2,1)S(1)}, bf16[48,4096]{1,0:T(8,128)(2,1)S(1)}, u32[]{:S(2)}, u32[]{:S(2)}) %collective-permute-start.28) | collective-permute-done | bytes 393248 | tf_op jit(solution)/shard_map/ppermute | solution.py:620
  137.4 3.6 %collective-permute-done.31 = bf16[48,4096]{1,0:T(8,128)(2,1)S(1)} collective-permute-done((bf16[48,4096]{1,0:T(8,128)(2,1)S(1)}, bf16[48,4096]{1,0:T(8,128)(2,1)S(1)}, u32[]{:S(2)}, u32[]{:S(2)}) %collective-permute-start.31) | collective-permute-done | bytes 393248 | tf_op jit(solution)/shard_map/ppermute | solution.py:620
  141.9 2.2 %collective-permute-done.25 = bf16[48,4096]{1,0:T(8,128)(2,1)S(1)} collective-permute-done((bf16[48,4096]{1,0:T(8,128)(2,1)S(1)}, bf16[48,4096]{1,0:T(8,128)(2,1)S(1)}, u32[]{:S(2)}, u32[]{:S(2)}) %collective-permute-start.25) | collective-permute-done | bytes 393248 | tf_op jit(solution)/shard_map/ppermute | solution.py:620
  144.1 2.1 %collective-permute-start.47 = (bf16[48,2048]{1,0:T(8,128)(2,1)S(1)}, bf16[48,2048]{1,0:T(8,128)(2,1)S(1)}, u32[]{:S(2)}, u32[]{:S(2)}) collective-permute-start(bf16[48,2048]{1,0:T(8,128)(2,1)S(1)} %slice.39), channel_id=1, source_target_pairs={{8,0},{16,8},{24,16},{28,24},{20,28},{12,20},{4,12},{0,4},{9,1},{1... | collective-permute-start | bytes 589832 | tf_op jit(solution)/shard_map/ppermute | solution.py:620
  149.6 4.7 %collective-permute-start.42 = (bf16[96,896]{1,0:T(8,128)(2,1)S(1)}, bf16[96,896]{1,0:T(8,128)(2,1)S(1)}, u32[]{:S(2)}, u32[]{:S(2)}) collective-permute-start(bf16[96,896]{1,0:T(8,128)(2,1)S(1)} %get-tuple-element.45), channel_id=1, source_target_pairs={{0,2},{1,3},{4,6},{5,7},{11,9},{9,11},{15,13},{13,15},{18,16},{16,... | collective-permute-start | bytes 516104 | tf_op jit(solution)/shard_map/ppermute | solution.py:620
  159.0 2.5 %collective-permute-start.50 = (bf16[96,896]{1,0:T(8,128)(2,1)S(1)}, bf16[96,896]{1,0:T(8,128)(2,1)S(1)}, u32[]{:S(2)}, u32[]{:S(2)}) collective-permute-start(bf16[96,896]{1,0:T(8,128)(2,1)S(1)} %get-tuple-element.48), channel_id=1, source_target_pairs={{0,3},{4,7},{9,10},{13,14},{18,17},{22,21},{27,24},{31,28}} | collective-permute-start | bytes 516104 | tf_op jit(solution)/shard_map/ppermute | solution.py:620
  162.7 3.2 %collective-permute-done.50.refs_7_ = bf16[96,896]{1,0:T(8,128)(2,1)S(1)} collective-permute-done((bf16[96,896]{1,0:T(8,128)(2,1)S(1)}, bf16[96,896]{1,0:T(8,128)(2,1)S(1)}, u32[]{:S(2)}, u32[]{:S(2)}) %collective-permute-start.50) | collective-permute-done | bytes 172064 | tf_op jit(solution)/shard_map/ppermute | solution.py:620
  (154 shorter events, 71.4 us)
Async XLA Ops:
  1.1 20.0 %collective-permute-start = (bf16[4,144,512]{2,1,0:T(8,128)(2,1)S(1)}, bf16[4,144,512]{2,1,0:T(8,128)(2,1)S(1)}, u32[]{:S(2)}, u32[]{:S(2)}) collective-permute-start(bf16[4,144,512]{2,1,0:T(8,128)(2,1)S(1)} %payload.1), channel_id=1, source_target_pairs={{0,8},{8,16},{16,24},{24,28},{28,20},{20,12},{12,4},{4,0},{1,9},{9... | collective-permute-start | bytes 1769480 | tf_op jit(solution)/shard_map/ppermute | solution.py:620
  4.2 16.9 %collective-permute-start.1 = (bf16[4,144,512]{2,1,0:T(8,128)(2,1)S(1)}, bf16[4,144,512]{2,1,0:T(8,128)(2,1)S(1)}, u32[]{:S(2)}, u32[]{:S(2)}) collective-permute-start(bf16[4,144,512]{2,1,0:T(8,128)(2,1)S(1)} %payload.1), channel_id=1, source_target_pairs={{8,0},{16,8},{24,16},{28,24},{20,28},{12,20},{4,12},{0,4},{9,1},{1... | collective-permute-start | bytes 1769480 | tf_op jit(solution)/shard_map/ppermute | solution.py:620
  5.5 15.5 %all-to-all-start = ((s32[8,1,32]{2,1,0:T(1,128)}), s32[8,1,32]{2,1,0:T(1,128)S(1)}, u32[]{:S(2)}, u32[]{:S(2)}) async-start(s32[8,1,32]{2,1,0:T(1,128)} %broadcast_in_dim.2), calls=%async_computation | async-start | bytes 8192 | tf_op jit(solution)/shard_map/all_to_all | solution.py:627
  26.0 15.8 %collective-permute-start.8 = (bf16[2,144,512]{2,1,0:T(8,128)(2,1)S(1)}, bf16[2,144,512]{2,1,0:T(8,128)(2,1)S(1)}, u32[]{:S(2)}, u32[]{:S(2)}) collective-permute-start(bf16[2,144,512]{2,1,0:T(8,128)(2,1)S(1)} %get-tuple-element.29.refs_5_.refs_9_), channel_id=1, source_target_pairs={{0,2},{1,3},{2,0},{3,1},{4,6},{5,7},{6,4},{7,5},{8,10},{9,11},{10,... | collective-permute-start | bytes 884744 | tf_op jit(solution)/shard_map/ppermute | solution.py:620
  35.3 12.0 %collective-permute-start.5 = (bf16[2,144,512]{2,1,0:T(8,128)(2,1)S(1)}, bf16[2,144,512]{2,1,0:T(8,128)(2,1)}, u32[]{:S(2)}, u32[]{:S(2)}) collective-permute-start(bf16[2,144,512]{2,1,0:T(8,128)(2,1)S(1)} %join.3.refs_3_), channel_id=1, source_target_pairs={{0,2},{1,3},{2,0},{3,1},{4,6},{5,7},{6,4},{7,5},{8,10},{9,11},{10,... | collective-permute-start | bytes 884744 | tf_op jit(solution)/shard_map/ppermute | solution.py:620
  47.2 30.1 %collective-permute-start.6 = (bf16[2,144,512]{2,1,0:T(8,128)(2,1)}, bf16[2,144,512]{2,1,0:T(8,128)(2,1)}, u32[]{:S(2)}, u32[]{:S(2)}) collective-permute-start(bf16[2,144,512]{2,1,0:T(8,128)(2,1)} %collective-permute-done.5.refs_5_), channel_id=1, source_target_pairs={{0,1},{1,0},{2,3},{3,2},{4,5},{5,4},{6,7},{7,6},{8,9},{9,8},{10,11... | collective-permute-start | bytes 884744 | tf_op jit(solution)/shard_map/ppermute | solution.py:620
  50.9 32.8 %collective-permute-start.20 = (bf16[2,144,512]{2,1,0:T(8,128)(2,1)}, bf16[2,144,512]{2,1,0:T(8,128)(2,1)}, u32[]{:S(2)}, u32[]{:S(2)}) collective-permute-start(bf16[2,144,512]{2,1,0:T(8,128)(2,1)} %join.5.refs_7_.refs_11_), channel_id=1, source_target_pairs={{0,1},{1,0},{2,3},{3,2},{4,5},{5,4},{6,7},{7,6},{8,9},{9,8},{10,11... | collective-permute-start | bytes 884744 | tf_op jit(solution)/shard_map/ppermute | solution.py:620
  51.2 33.1 %collective-permute-start.22 = (bf16[2,144,512]{2,1,0:T(8,128)(2,1)}, bf16[2,144,512]{2,1,0:T(8,128)(2,1)}, u32[]{:S(2)}, u32[]{:S(2)}) collective-permute-start(bf16[2,144,512]{2,1,0:T(8,128)(2,1)} %collective-permute-done.21.refs_9_.refs_13_), channel_id=1, source_target_pairs={{0,1},{1,0},{2,3},{3,2},{4,5},{5,4},{6,7},{7,6},{8,9},{9,8},{10,11... | collective-permute-start | bytes 884744 | tf_op jit(solution)/shard_map/ppermute | solution.py:620
  54.8 36.5 %collective-permute-start.17 = (bf16[1,144,512]{2,1,0:T(8,128)(2,1)}, bf16[1,144,512]{2,1,0:T(8,128)(2,1)}, u32[]{:S(2)}, u32[]{:S(2)}) collective-permute-start(bf16[1,144,512]{2,1,0:T(8,128)(2,1)} %join.4.refs_3_), channel_id=1, source_target_pairs={{0,1},{1,0},{2,3},{3,2},{4,5},{5,4},{6,7},{7,6},{8,9},{9,8},{10,11... | collective-permute-start | bytes 442376 | tf_op jit(solution)/shard_map/ppermute | solution.py:620
  59.2 32.1 %collective-permute-start.19 = (bf16[1,144,512]{2,1,0:T(8,128)(2,1)}, bf16[1,144,512]{2,1,0:T(8,128)(2,1)}, u32[]{:S(2)}, u32[]{:S(2)}) collective-permute-start(bf16[1,144,512]{2,1,0:T(8,128)(2,1)} %collective-permute-done.18.refs_5_), channel_id=1, source_target_pairs={{0,1},{1,0},{2,3},{3,2},{4,5},{5,4},{6,7},{7,6},{8,9},{9,8},{10,11... | collective-permute-start | bytes 442376 | tf_op jit(solution)/shard_map/ppermute | solution.py:620
  82.2 18.8 %collective-permute-start.26 = (bf16[48,4096]{1,0:T(8,128)(2,1)S(1)}, bf16[48,4096]{1,0:T(8,128)(2,1)S(1)}, u32[]{:S(2)}, u32[]{:S(2)}) collective-permute-start(bf16[48,4096]{1,0:T(8,128)(2,1)S(1)} %attend_slots.5), channel_id=1, source_target_pairs={{8,0},{16,8},{24,16},{28,24},{20,28},{12,20},{4,12},{0,4},{9,1},{1... | collective-permute-start | bytes 1179656 | tf_op jit(solution)/shard_map/ppermute | solution.py:620
  83.7 18.6 %collective-permute-start.10 = (bf16[48,4096]{1,0:T(8,128)(2,1)S(1)}, bf16[48,4096]{1,0:T(8,128)(2,1)S(1)}, u32[]{:S(2)}, u32[]{:S(2)}) collective-permute-start(bf16[48,4096]{1,0:T(8,128)(2,1)S(1)} %attend_slots.5), channel_id=1, source_target_pairs={{0,8},{8,16},{16,24},{24,28},{28,20},{20,12},{12,4},{4,0},{1,9},{9... | collective-permute-start | bytes 1179656 | tf_op jit(solution)/shard_map/ppermute | solution.py:620
  95.7 13.7 %collective-permute-start.29 = (bf16[48,4096]{1,0:T(8,128)(2,1)S(1)}, bf16[48,4096]{1,0:T(8,128)(2,1)S(1)}, u32[]{:S(2)}, u32[]{:S(2)}) collective-permute-start(bf16[48,4096]{1,0:T(8,128)(2,1)S(1)} %attend_slots.7), channel_id=1, source_target_pairs={{8,0},{16,8},{24,16},{28,24},{20,28},{12,20},{4,12},{0,4},{9,1},{1... | collective-permute-start | bytes 1179656 | tf_op jit(solution)/shard_map/ppermute | solution.py:620
  97.2 14.2 %collective-permute-start.23 = (bf16[48,4096]{1,0:T(8,128)(2,1)S(1)}, bf16[48,4096]{1,0:T(8,128)(2,1)S(1)}, u32[]{:S(2)}, u32[]{:S(2)}) collective-permute-start(bf16[48,4096]{1,0:T(8,128)(2,1)S(1)} %attend_slots.7), channel_id=1, source_target_pairs={{0,8},{8,16},{16,24},{24,28},{28,20},{20,12},{12,4},{4,0},{1,9},{9... | collective-permute-start | bytes 1179656 | tf_op jit(solution)/shard_map/ppermute | solution.py:620
  103.7 12.4 %collective-permute-start.27 = (bf16[48,4096]{1,0:T(8,128)(2,1)S(1)}, bf16[48,4096]{1,0:T(8,128)(2,1)S(1)}, u32[]{:S(2)}, u32[]{:S(2)}) collective-permute-start(bf16[48,4096]{1,0:T(8,128)(2,1)S(1)} %collective-permute-done.26), channel_id=1, source_target_pairs={{8,0},{16,8},{24,16},{28,24},{20,28},{12,20},{4,12},{0,4},{9,1},{1... | collective-permute-start | bytes 1179656 | tf_op jit(solution)/shard_map/ppermute | solution.py:620
  109.4 15.3 %collective-permute-start.30 = (bf16[48,4096]{1,0:T(8,128)(2,1)S(1)}, bf16[48,4096]{1,0:T(8,128)(2,1)S(1)}, u32[]{:S(2)}, u32[]{:S(2)}) collective-permute-start(bf16[48,4096]{1,0:T(8,128)(2,1)S(1)} %collective-permute-done.29), channel_id=1, source_target_pairs={{8,0},{16,8},{24,16},{28,24},{20,28},{12,20},{4,12},{0,4},{9,1},{1... | collective-permute-start | bytes 1179656 | tf_op jit(solution)/shard_map/ppermute | solution.py:620
  111.5 15.3 %collective-permute-start.24 = (bf16[48,4096]{1,0:T(8,128)(2,1)S(1)}, bf16[48,4096]{1,0:T(8,128)(2,1)S(1)}, u32[]{:S(2)}, u32[]{:S(2)}) collective-permute-start(bf16[48,4096]{1,0:T(8,128)(2,1)S(1)} %collective-permute-done.23), channel_id=1, source_target_pairs={{0,8},{8,16},{16,24},{24,28},{28,20},{20,12},{12,4},{4,0},{1,9},{9... | collective-permute-start | bytes 1179656 | tf_op jit(solution)/shard_map/ppermute | solution.py:620
  121.8 12.0 %collective-permute-start.28 = (bf16[48,4096]{1,0:T(8,128)(2,1)S(1)}, bf16[48,4096]{1,0:T(8,128)(2,1)S(1)}, u32[]{:S(2)}, u32[]{:S(2)}) collective-permute-start(bf16[48,4096]{1,0:T(8,128)(2,1)S(1)} %collective-permute-done.27), channel_id=1, source_target_pairs={{8,0},{16,8},{24,16},{28,24},{20,28},{12,20},{4,12},{0,4},{9,1},{1... | collective-permute-start | bytes 1179656 | tf_op jit(solution)/shard_map/ppermute | solution.py:620
  124.7 12.0 %collective-permute-start.12 = (bf16[48,4096]{1,0:T(8,128)(2,1)S(1)}, bf16[48,4096]{1,0:T(8,128)(2,1)S(1)}, u32[]{:S(2)}, u32[]{:S(2)}) collective-permute-start(bf16[48,4096]{1,0:T(8,128)(2,1)S(1)} %collective-permute-done.11), channel_id=1, source_target_pairs={{0,8},{8,16},{16,24},{24,28},{28,20},{20,12},{12,4},{4,0},{1,9},{9... | collective-permute-start | bytes 1179656 | tf_op jit(solution)/shard_map/ppermute | solution.py:620
  124.7 16.3 %collective-permute-start.31 = (bf16[48,4096]{1,0:T(8,128)(2,1)S(1)}, bf16[48,4096]{1,0:T(8,128)(2,1)S(1)}, u32[]{:S(2)}, u32[]{:S(2)}) collective-permute-start(bf16[48,4096]{1,0:T(8,128)(2,1)S(1)} %collective-permute-done.30), channel_id=1, source_target_pairs={{8,0},{16,8},{24,16},{28,24},{20,28},{12,20},{4,12},{0,4},{9,1},{1... | collective-permute-start | bytes 1179656 | tf_op jit(solution)/shard_map/ppermute | solution.py:620
  126.8 17.3 %collective-permute-start.25 = (bf16[48,4096]{1,0:T(8,128)(2,1)S(1)}, bf16[48,4096]{1,0:T(8,128)(2,1)S(1)}, u32[]{:S(2)}, u32[]{:S(2)}) collective-permute-start(bf16[48,4096]{1,0:T(8,128)(2,1)S(1)} %collective-permute-done.24), channel_id=1, source_target_pairs={{0,8},{8,16},{16,24},{24,28},{28,20},{20,12},{12,4},{4,0},{1,9},{9... | collective-permute-start | bytes 1179656 | tf_op jit(solution)/shard_map/ppermute | solution.py:620
  129.5 14.6 %collective-permute-start.38 = (bf16[96,896]{1,0:T(8,128)(2,1)S(1)}, bf16[96,896]{1,0:T(8,128)(2,1)S(1)}, u32[]{:S(2)}, u32[]{:S(2)}) collective-permute-start(bf16[96,896]{1,0:T(8,128)(2,1)S(1)} %get-tuple-element.38), channel_id=1, source_target_pairs={{0,1},{3,2},{4,5},{7,6},{9,8},{10,11},{13,12},{14,15},{17,16},{18,... | collective-permute-start | bytes 516104 | tf_op jit(solution)/shard_map/ppermute | solution.py:620
  133.9 12.3 %collective-permute-start.39 = (bf16[96,896]{1,0:T(8,128)(2,1)S(1)}, bf16[96,896]{1,0:T(8,128)(2,1)S(1)}, u32[]{:S(2)}, u32[]{:S(2)}) collective-permute-start(bf16[96,896]{1,0:T(8,128)(2,1)S(1)} %get-tuple-element.39), channel_id=1, source_target_pairs={{3,1},{0,2},{7,5},{4,6},{10,8},{9,11},{14,12},{13,15},{18,16},{17,... | collective-permute-start | bytes 516104 | tf_op jit(solution)/shard_map/ppermute | solution.py:620
  149.6 12.0 %collective-permute-start.42 = (bf16[96,896]{1,0:T(8,128)(2,1)S(1)}, bf16[96,896]{1,0:T(8,128)(2,1)S(1)}, u32[]{:S(2)}, u32[]{:S(2)}) collective-permute-start(bf16[96,896]{1,0:T(8,128)(2,1)S(1)} %get-tuple-element.45), channel_id=1, source_target_pairs={{0,2},{1,3},{4,6},{5,7},{11,9},{9,11},{15,13},{13,15},{18,16},{16,... | collective-permute-start | bytes 516104 | tf_op jit(solution)/shard_map/ppermute | solution.py:620
  (47 other events, 366.9 us)

commit v5 on v4

--- a/solution.py
+++ b/solution.py
@@ -381,9 +381,11 @@
     count, heads = len(plan), len(indices[0])
     refs = list(refs)
     q_ref, qr_ref, w_hbm = refs.pop(0), refs.pop(0), refs.pop(0)
-    w_ref, w_sem = refs.pop(-2), refs.pop(-1)
-    w_copy = pltpu.make_async_copy(w_hbm, w_ref, w_sem)
-    w_copy.start()
+    w_ref = w_hbm
+    if count > 1:
+        w_ref, w_sem = refs.pop(-2), refs.pop(-1)
+        w_copy = pltpu.make_async_copy(w_hbm, w_ref, w_sem)
+        w_copy.start()
     if own:
         full_lat, full_rope = refs.pop(0), refs.pop(0)
     parts = [[(refs.pop(0), index) for index in slot] for slot in indices]
@@ -439,7 +441,8 @@
         return 0
 
     lax.fori_loop(0, count, bundle, 0)
-    w_copy.wait()
+    if count > 1:
+        w_copy.wait()
     local_heads, _, value_width = w_ref.shape
     n = mixed.shape[1] // local_heads
     at = 0
@@ -470,7 +473,9 @@
     local_heads, _, value_width = w_uv.shape
     vmem = pl.BlockSpec(memory_space=pltpu.MemorySpace.VMEM)
     smem = pl.BlockSpec(memory_space=pltpu.MemorySpace.SMEM)
-    args, in_specs = [q, qr, in_hbm(w_uv)], [vmem, vmem, pl.BlockSpec(memory_space=pl.ANY)]
+    fetch = count > 1
+    args = [q, qr, in_hbm(w_uv) if fetch else w_uv]
+    in_specs = [vmem, vmem, pl.BlockSpec(memory_space=pl.ANY) if fetch else vmem]
     if own:
         args += [in_hbm(x) for x in full]
         in_specs += [pl.BlockSpec(memory_space=pl.ANY)] * 2
@@ -483,7 +488,8 @@
     if own:
         scratch += caches + [pltpu.SemaphoreType.DMA((2,))]
     scratch += caches + [pltpu.VMEM((wide // 128, count * q_rows, 128), jnp.float32)]
-    scratch += [pltpu.VMEM(w_uv.shape, w_uv.dtype), pltpu.SemaphoreType.DMA]
+    if fetch:
+        scratch += [pltpu.VMEM(w_uv.shape, w_uv.dtype), pltpu.SemaphoreType.DMA]
     return pl.pallas_call(
         functools.partial(
             slots_kernel, plan, own, [[index for _, index in slot] for slot in parts], bundles,
@@ -493,7 +499,7 @@
         in_specs=[smem] * 2 + in_specs,
         out_specs=vmem,
         scratch_shapes=scratch,
-        compiler_params=pltpu.CompilerParams(vmem_limit_bytes=18 * 2**20),
+        compiler_params=pltpu.CompilerParams(vmem_limit_bytes=(18 if fetch else 12) * 2**20),
         name="attend_slots",
     )(table, info, *args)
 
@@ -680,7 +686,10 @@
         return order[(where[p] + offsets[column]) % ranks] // per_head
 
     def settle(columns, both, previous):
-        to_send, own, total = settle_step(table, heads, per_head, columns, both, previous)
+        if previous is None and len(columns) == 1:
+            to_send, own, total = [both.astype(jnp.bfloat16)] * (heads - 1), both, None
+        else:
+            to_send, own, total = settle_step(table, heads, per_head, columns, both, previous)
         got = []
         for m in range(1, heads):
             pairs = []
@@ -693,13 +702,22 @@
     arrived = {}
     for tag, values in chunks:
         fore = back = values
-        for k in range(1, last):
+        for k in range(1, last - 1):
             fore = move(fore, ahead)
             back = move(back, behind)
             arrived[tag, k] = fore, back
-        fore, back = fore[:, :half], back[:, half:]
-        left = move(fore, ahead)
-        right = move(back, behind)
+        fore_on, fore_end = fore[:, :half], fore[:, half:]
+        back_on, back_end = back[:, half:], back[:, :half]
+        fore_on = move(fore_on, ahead)
+        back_on = move(back_on, behind)
+        fore_end = move(fore_end, ahead)
+        back_end = move(back_end, behind)
+        arrived[tag, last - 1] = (
+            jnp.concatenate([fore_on, fore_end], axis=1),
+            jnp.concatenate([back_end, back_on], axis=1),
+        )
+        left = move(fore_on, ahead)
+        right = move(back_on, behind)
         arrived[tag, last] = (jnp.concatenate([left, right], axis=1),)
     state = settle([0], project([values for _, values in chunks]), None)
     for k in range(1, last):

time: 169 us -> 178 us (1.053)
  starting transfers between devices: 59.8 us -> 68.3 us
  waiting for transfers between devices: 49.2 us -> 54.3 us
  Pallas kernels: 33 us -> 28.7 us
    ppermute x51 -> x55, starting transfers between devices: 53.5 us -> 62 us  [move(): return lax.ppermute(x, axis, pairs)]
    ppermute x51 -> x55, waiting for transfers between devices: 41.4 us -> 46.6 us  [move(): return lax.ppermute(x, axis, pairs)]
    pallas_call x4, Pallas kernels: 22.5 us -> 19.5 us  [attend_slots(): pl.pallas_call(functools.partial(slots_kernel, plan, own, [[index for _,...]
    pallas_call x5 -> x3, Pallas kernels: 3.75 us -> 2.47 us  [settle_step(): pl.pallas_call(functools.partial(settle_kernel, heads, per_head, columns,...]
    unnamed x38 -> x42, local copies, waits for them, and re-layouts: 9.16 us -> 9.19 us
  transfers between devices with their start and end apart: 52 -> 56, of which waited for: 16 -> 17; matrix products, arithmetic and copies ran while one was open for 10% -> 9% of each run, Pallas kernels for 17% -> 14%
where the time goes in v5:
time: 178 us; the launch traced here: 177 us
  starting transfers between devices  68.3 us (38%)
  waiting for transfers between devices  54.3 us (31%)
  Pallas kernels  28.7 us (16%)
  local copies, waits for them, and re-layouts  16.7 us (9%)
  matrix products  7.93 us (4%)
    ppermute x55, starting transfers between devices, move(): return lax.ppermute(x, axis, pairs)  62 us
    ppermute x55, waiting for transfers between devices, move(): return lax.ppermute(x, axis, pairs)  46.6 us
    pallas_call x4, Pallas kernels, attend_slots(): pl.pallas_call(functools.partial(slots_kernel, plan, own, [[index for _,...  19.5 us
    unnamed x42, local copies, waits for them, and re-layouts  9.19 us
    dot_general x5, matrix products, project(): jnp.dot(jnp.concatenate(pieces), w_out, preferred_element_type=jnp.float32)  7.93 us
    all_to_all x1, waiting for transfers between devices, local_ring(): lax.all_to_all(jnp.broadcast_to(facts[None], (ranks, width)), 'dp', split...  7.73 us
    all_to_all x1, starting transfers between devices, local_ring(): lax.all_to_all(jnp.broadcast_to(facts[None], (ranks, width)), 'dp', split...  6.28 us
    reshape x1, local copies, waits for them, and re-layouts, local_ring(): q = q_latent.reshape(bundles, roll_count * local_heads, -1)  4.2 us
  transfers between devices with their start and end apart: 56, of which 17 were waited for; matrix products, arithmetic and copies ran while one was open for 9% of the time, Pallas kernels for 14%

profile of v5, /device:TPU:0, one launch (start us, length us, event | category | flops | bytes accessed | tf_op | source)
XLA Modules:
  0.0 177.3 jit_solution(14911032672017122511)
XLA Ops:
  1.1 3.1 %collective-permute-start = (bf16[4,144,512]{2,1,0:T(8,128)(2,1)S(1)}, bf16[4,144,512]{2,1,0:T(8,128)(2,1)S(1)}, u32[]{:S(2)}, u32[]{:S(2)}) collective-permute-start(bf16[4,144,512]{2,1,0:T(8,128)(2,1)S(1)} %payload.1), channel_id=1, source_target_pairs={{0,8},{8,16},{16,24},{24,28},{28,20},{20,12},{12,4},{4,0},{1,9},{9... | collective-permute-start | bytes 1769480 | tf_op jit(solution)/shard_map/ppermute | solution.py:626
  5.5 6.3 %all-to-all-start = ((s32[8,1,32]{2,1,0:T(1,128)}), s32[8,1,32]{2,1,0:T(1,128)S(1)}, u32[]{:S(2)}, u32[]{:S(2)}) async-start(s32[8,1,32]{2,1,0:T(1,128)} %broadcast_in_dim.2), calls=%async_computation | async-start | bytes 8192 | tf_op jit(solution)/shard_map/all_to_all | solution.py:633
  13.3 7.7 %all-to-all-done = s32[8,1,32]{2,1,0:T(1,128)S(1)} async-done(((s32[8,1,32]{2,1,0:T(1,128)}), s32[8,1,32]{2,1,0:T(1,128)S(1)}, u32[]{:S(2)}, u32[]{:S(2)}) %all-to-all-start) | async-done | bytes 1056 | tf_op jit(solution)/shard_map/all_to_all | solution.py:633
  27.5 5.5 %collective-permute-done.2.fore = bf16[368,512]{1,0:T(8,128)(2,1)S(1)} collective-permute-done((bf16[368,512]{1,0:T(8,128)(2,1)S(1)}, bf16[368,512]{1,0:T(8,128)(2,1)S(1)}, u32[]{:S(2)}, u32[]{:S(2)}) %collective-permute-start.2) | collective-permute-done | bytes 376864 | tf_op jit(solution)/shard_map/ppermute | solution.py:626
  36.8 2.8 %collective-permute-done.16.back = bf16[208,512]{1,0:T(8,128)(2,1)S(1)} collective-permute-done((bf16[208,512]{1,0:T(8,128)(2,1)S(1)}, bf16[208,512]{1,0:T(8,128)(2,1)S(1)}, u32[]{:S(2)}, u32[]{:S(2)}) %collective-permute-start.16) | collective-permute-done | bytes 213024 | tf_op jit(solution)/shard_map/ppermute | solution.py:626
  44.3 2.1 %collective-permute-done.17.back = bf16[64,512]{1,0:T(8,128)(2,1)S(1)} collective-permute-done((bf16[64,512]{1,0:T(8,128)(2,1)S(1)}, bf16[64,512]{1,0:T(8,128)(2,1)S(1)}, u32[]{:S(2)}, u32[]{:S(2)}) %collective-permute-start.17) | collective-permute-done | bytes 65568 | tf_op jit(solution)/shard_map/ppermute | solution.py:626
  47.2 3.6 %collective-permute-done.15.fore = bf16[80,512]{1,0:T(8,128)(2,1)S(1)} collective-permute-done((bf16[80,512]{1,0:T(8,128)(2,1)S(1)}, bf16[80,512]{1,0:T(8,128)(2,1)S(1)}, u32[]{:S(2)}, u32[]{:S(2)}) %collective-permute-start.15) | collective-permute-done | bytes 81952 | tf_op jit(solution)/shard_map/ppermute | solution.py:626
  55.0 4.1 %collective-permute-done.19.refs_5_ = bf16[1,144,512]{2,1,0:T(8,128)(2,1)} collective-permute-done((bf16[1,144,512]{2,1,0:T(8,128)(2,1)}, bf16[1,144,512]{2,1,0:T(8,128)(2,1)}, u32[]{:S(2)}, u32[]{:S(2)}) %collective-permute-start.19) | collective-permute-done | bytes 147488 | tf_op jit(solution)/shard_map/ppermute | solution.py:626
  59.2 4.2 %reshape.12.refs_0_ = bf16[8,384,512]{2,1,0:T(8,128)(2,1)S(1)} reshape(bf16[96,16384]{1,0:T(8,128)(2,1)} %param.11) | data formatting | bytes 6291456 | tf_op jit(solution)/shard_map/reshape | solution.py:638
  63.4 2.6 %reshape.13.refs_1_ = bf16[8,384,64]{2,1,0:T(8,128)(2,1)} reshape(bf16[96,2048]{1,0:T(8,128)(2,1)} %param.12) | data formatting | bytes 786432 | tf_op jit(solution)/shard_map/reshape | solution.py:639
  71.0 6.6 %attend_slots.4.refs_7_ = f32[36,4096]{1,0:T(8,128)S(1)} custom-call(s32[8,8]{1,0:T(8,128)S(1)} %copy-done.15, s32[8,1,32]{2,1,0:T(1,128)S(1)} %broadcast_maximum_fusion.info, bf16[8,384,512]{2,1,0:T(8,128)(2,1)S(1)} %reshape.12.refs_0_, bf16[8,384,64]{2,1,0:T(8,128)(2,1)S(1)} %copy-done.2, bf16[32,512,128]{2,1,0:T(8,128)(2,1)} %refs_2_.7, ...), custom_call_target="tpu_custom_call" | custom-call | tf_op jit(solution)/shard_map/attend_slots/pallas_call | solution.py:493
  77.6 2.9 %attend_slots.5 = bf16[48,4096]{1,0:T(8,128)(2,1)S(1)} custom-call(s32[8,8]{1,0:T(8,128)S(1)} %copy-done.15, s32[8,1,32]{2,1,0:T(1,128)S(1)} %broadcast_maximum_fusion.info, bf16[8,384,512]{2,1,0:T(8,128)(2,1)S(1)} %reshape.12.refs_0_, bf16[8,384,64]{2,1,0:T(8,128)(2,1)S(1)} %copy-done.2, bf16[32,512,128]{2,1,0:T(8,128)(2,1)S(1)} %copy-done, ...), custom_call_target="tpu_custom_call" | custom-call | tf_op jit(solution)/shard_map/attend_slots/pallas_call | solution.py:493
  82.7 7.1 %attend_slots.6.refs_7_ = f32[36,4096]{1,0:T(8,128)S(1)} custom-call(s32[8,8]{1,0:T(8,128)S(1)} %copy-done.15, s32[8,1,32]{2,1,0:T(1,128)S(1)} %broadcast_maximum_fusion.info, bf16[8,384,512]{2,1,0:T(8,128)(2,1)S(1)} %reshape.12.refs_0_, bf16[8,384,64]{2,1,0:T(8,128)(2,1)S(1)} %copy-done.3, bf16[32,512,128]{2,1,0:T(8,128)(2,1)} %refs_2_.7, ...), custom_call_target="tpu_custom_call" | custom-call | tf_op jit(solution)/shard_map/attend_slots/pallas_call | solution.py:493
  89.9 2.9 %attend_slots.7 = bf16[48,4096]{1,0:T(8,128)(2,1)S(1)} custom-call(s32[8,8]{1,0:T(8,128)S(1)} %copy-done.15, s32[8,1,32]{2,1,0:T(1,128)S(1)} %broadcast_maximum_fusion.info, bf16[8,384,512]{2,1,0:T(8,128)(2,1)S(1)} %reshape.12.refs_0_, bf16[8,384,64]{2,1,0:T(8,128)(2,1)S(1)} %copy-done.3, bf16[32,512,128]{2,1,0:T(8,128)(2,1)S(1)} %copy-done.1, ...), custom_call_target="tpu_custom_call" | custom-call | tf_op jit(solution)/shard_map/attend_slots/pallas_call | solution.py:493
  100.0 3.8 %collective-permute-done.32 = bf16[48,4096]{1,0:T(8,128)(2,1)S(1)} collective-permute-done((bf16[48,4096]{1,0:T(8,128)(2,1)S(1)}, bf16[48,4096]{1,0:T(8,128)(2,1)S(1)}, u32[]{:S(2)}, u32[]{:S(2)}) %collective-permute-start.32) | collective-permute-done | bytes 393248 | tf_op jit(solution)/shard_map/ppermute | solution.py:626
  108.5 1.9 %collective-permute-start.39 = (bf16[96,896]{1,0:T(8,128)(2,1)S(1)}, bf16[96,896]{1,0:T(8,128)(2,1)S(1)}, u32[]{:S(2)}, u32[]{:S(2)}) collective-permute-start(bf16[96,896]{1,0:T(8,128)(2,1)S(1)} %get-tuple-element.27), channel_id=1, source_target_pairs={{1,0},{0,1},{5,4},{4,5},{9,8},{11,10},{13,12},{15,14},{16,17},{18,... | collective-permute-start | bytes 516104 | tf_op jit(solution)/shard_map/ppermute | solution.py:626
  116.1 9.6 %collective-permute-done.33 = bf16[48,4096]{1,0:T(8,128)(2,1)S(1)} collective-permute-done((bf16[48,4096]{1,0:T(8,128)(2,1)S(1)}, bf16[48,4096]{1,0:T(8,128)(2,1)S(1)}, u32[]{:S(2)}, u32[]{:S(2)}) %collective-permute-start.33) | collective-permute-done | bytes 393248 | tf_op jit(solution)/shard_map/ppermute | solution.py:626
  139.1 2.8 %collective-permute-done.12 = bf16[48,2048]{1,0:T(8,128)(2,1)S(1)} collective-permute-done((bf16[48,2048]{1,0:T(8,128)(2,1)S(1)}, bf16[48,2048]{1,0:T(8,128)(2,1)S(1)}, u32[]{:S(2)}, u32[]{:S(2)}) %collective-permute-start.12) | collective-permute-done | bytes 196640 | tf_op jit(solution)/shard_map/ppermute | solution.py:626
  144.9 2.9 %collective-permute-done.43.refs_2_ = bf16[96,896]{1,0:T(8,128)(2,1)S(1)} collective-permute-done((bf16[96,896]{1,0:T(8,128)(2,1)S(1)}, bf16[96,896]{1,0:T(8,128)(2,1)S(1)}, u32[]{:S(2)}, u32[]{:S(2)}) %collective-permute-start.43) | collective-permute-done | bytes 172064 | tf_op jit(solution)/shard_map/ppermute | solution.py:626
  147.8 2.0 %collective-permute-start.49 = (bf16[48,2048]{1,0:T(8,128)(2,1)S(1)}, bf16[48,2048]{1,0:T(8,128)(2,1)S(1)}, u32[]{:S(2)}, u32[]{:S(2)}) collective-permute-start(bf16[48,2048]{1,0:T(8,128)(2,1)S(1)} %collective-permute-done.31), channel_id=1, source_target_pairs={{8,0},{16,8},{24,16},{28,24},{20,28},{12,20},{4,12},{0,4},{9,1},{1... | collective-permute-start | bytes 589832 | tf_op jit(solution)/shard_map/ppermute | solution.py:626
  152.6 2.4 %collective-permute-start.50 = (bf16[48,2048]{1,0:T(8,128)(2,1)S(1)}, bf16[48,2048]{1,0:T(8,128)(2,1)S(1)}, u32[]{:S(2)}, u32[]{:S(2)}) collective-permute-start(bf16[48,2048]{1,0:T(8,128)(2,1)S(1)} %collective-permute-done.26), channel_id=1, source_target_pairs={{0,8},{8,16},{16,24},{24,28},{28,20},{20,12},{12,4},{4,0},{1,9},{9... | collective-permute-start | bytes 589832 | tf_op jit(solution)/shard_map/ppermute | solution.py:626
  158.3 5.4 %collective-permute-start.46 = (bf16[96,896]{1,0:T(8,128)(2,1)S(1)}, bf16[96,896]{1,0:T(8,128)(2,1)S(1)}, u32[]{:S(2)}, u32[]{:S(2)}) collective-permute-start(bf16[96,896]{1,0:T(8,128)(2,1)S(1)} %get-tuple-element.39), channel_id=1, source_target_pairs={{0,2},{1,3},{4,6},{5,7},{11,9},{9,11},{15,13},{13,15},{18,16},{16,... | collective-permute-start | bytes 516104 | tf_op jit(solution)/shard_map/ppermute | solution.py:626
  167.8 2.5 %collective-permute-start.54 = (bf16[96,896]{1,0:T(8,128)(2,1)S(1)}, bf16[96,896]{1,0:T(8,128)(2,1)S(1)}, u32[]{:S(2)}, u32[]{:S(2)}) collective-permute-start(bf16[96,896]{1,0:T(8,128)(2,1)S(1)} %get-tuple-element.51), channel_id=1, source_target_pairs={{0,3},{4,7},{9,10},{13,14},{18,17},{22,21},{27,24},{31,28}} | collective-permute-start | bytes 516104 | tf_op jit(solution)/shard_map/ppermute | solution.py:626
  172.2 3.2 %collective-permute-done.54.refs_7_ = bf16[96,896]{1,0:T(8,128)(2,1)S(1)} collective-permute-done((bf16[96,896]{1,0:T(8,128)(2,1)S(1)}, bf16[96,896]{1,0:T(8,128)(2,1)S(1)}, u32[]{:S(2)}, u32[]{:S(2)}) %collective-permute-start.54) | collective-permute-done | bytes 172064 | tf_op jit(solution)/shard_map/ppermute | solution.py:626
  (164 shorter events, 78.5 us)
Async XLA Ops:
  1.1 20.0 %collective-permute-start = (bf16[4,144,512]{2,1,0:T(8,128)(2,1)S(1)}, bf16[4,144,512]{2,1,0:T(8,128)(2,1)S(1)}, u32[]{:S(2)}, u32[]{:S(2)}) collective-permute-start(bf16[4,144,512]{2,1,0:T(8,128)(2,1)S(1)} %payload.1), channel_id=1, source_target_pairs={{0,8},{8,16},{16,24},{24,28},{28,20},{20,12},{12,4},{4,0},{1,9},{9... | collective-permute-start | bytes 1769480 | tf_op jit(solution)/shard_map/ppermute | solution.py:626
  4.2 16.9 %collective-permute-start.1 = (bf16[4,144,512]{2,1,0:T(8,128)(2,1)S(1)}, bf16[4,144,512]{2,1,0:T(8,128)(2,1)S(1)}, u32[]{:S(2)}, u32[]{:S(2)}) collective-permute-start(bf16[4,144,512]{2,1,0:T(8,128)(2,1)S(1)} %payload.1), channel_id=1, source_target_pairs={{8,0},{16,8},{24,16},{28,24},{20,28},{12,20},{4,12},{0,4},{9,1},{1... | collective-permute-start | bytes 1769480 | tf_op jit(solution)/shard_map/ppermute | solution.py:626
  5.5 15.5 %all-to-all-start = ((s32[8,1,32]{2,1,0:T(1,128)}), s32[8,1,32]{2,1,0:T(1,128)S(1)}, u32[]{:S(2)}, u32[]{:S(2)}) async-start(s32[8,1,32]{2,1,0:T(1,128)} %broadcast_in_dim.2), calls=%async_computation | async-start | bytes 8192 | tf_op jit(solution)/shard_map/all_to_all | solution.py:633
  26.0 15.8 %collective-permute-start.8 = (bf16[2,144,512]{2,1,0:T(8,128)(2,1)S(1)}, bf16[2,144,512]{2,1,0:T(8,128)(2,1)S(1)}, u32[]{:S(2)}, u32[]{:S(2)}) collective-permute-start(bf16[2,144,512]{2,1,0:T(8,128)(2,1)S(1)} %get-tuple-element.25.refs_5_.refs_9_), channel_id=1, source_target_pairs={{0,2},{1,3},{2,0},{3,1},{4,6},{5,7},{6,4},{7,5},{8,10},{9,11},{10,... | collective-permute-start | bytes 884744 | tf_op jit(solution)/shard_map/ppermute | solution.py:626
  35.3 11.9 %collective-permute-start.5 = (bf16[2,144,512]{2,1,0:T(8,128)(2,1)S(1)}, bf16[2,144,512]{2,1,0:T(8,128)(2,1)}, u32[]{:S(2)}, u32[]{:S(2)}) collective-permute-start(bf16[2,144,512]{2,1,0:T(8,128)(2,1)S(1)} %join.3.refs_3_), channel_id=1, source_target_pairs={{0,2},{1,3},{2,0},{3,1},{4,6},{5,7},{6,4},{7,5},{8,10},{9,11},{10,... | collective-permute-start | bytes 884744 | tf_op jit(solution)/shard_map/ppermute | solution.py:626
  47.2 30.4 %collective-permute-start.6 = (bf16[2,144,512]{2,1,0:T(8,128)(2,1)}, bf16[2,144,512]{2,1,0:T(8,128)(2,1)}, u32[]{:S(2)}, u32[]{:S(2)}) collective-permute-start(bf16[2,144,512]{2,1,0:T(8,128)(2,1)} %collective-permute-done.5.refs_5_), channel_id=1, source_target_pairs={{0,1},{1,0},{2,3},{3,2},{4,5},{5,4},{6,7},{7,6},{8,9},{9,8},{10,11... | collective-permute-start | bytes 884744 | tf_op jit(solution)/shard_map/ppermute | solution.py:626
  50.8 31.3 %collective-permute-start.21 = (bf16[2,144,512]{2,1,0:T(8,128)(2,1)}, bf16[2,144,512]{2,1,0:T(8,128)(2,1)}, u32[]{:S(2)}, u32[]{:S(2)}) collective-permute-start(bf16[2,144,512]{2,1,0:T(8,128)(2,1)} %join.5.refs_7_.refs_11_), channel_id=1, source_target_pairs={{0,1},{1,0},{2,3},{3,2},{4,5},{5,4},{6,7},{7,6},{8,9},{9,8},{10,11... | collective-permute-start | bytes 884744 | tf_op jit(solution)/shard_map/ppermute | solution.py:626
  51.2 31.5 %collective-permute-start.23 = (bf16[2,144,512]{2,1,0:T(8,128)(2,1)}, bf16[2,144,512]{2,1,0:T(8,128)(2,1)}, u32[]{:S(2)}, u32[]{:S(2)}) collective-permute-start(bf16[2,144,512]{2,1,0:T(8,128)(2,1)} %collective-permute-done.22.refs_9_.refs_13_), channel_id=1, source_target_pairs={{0,1},{1,0},{2,3},{3,2},{4,5},{5,4},{6,7},{7,6},{8,9},{9,8},{10,11... | collective-permute-start | bytes 884744 | tf_op jit(solution)/shard_map/ppermute | solution.py:626
  54.8 35.0 %collective-permute-start.18 = (bf16[1,144,512]{2,1,0:T(8,128)(2,1)}, bf16[1,144,512]{2,1,0:T(8,128)(2,1)}, u32[]{:S(2)}, u32[]{:S(2)}) collective-permute-start(bf16[1,144,512]{2,1,0:T(8,128)(2,1)} %join.4.refs_3_), channel_id=1, source_target_pairs={{0,1},{1,0},{2,3},{3,2},{4,5},{5,4},{6,7},{7,6},{8,9},{9,8},{10,11... | collective-permute-start | bytes 442376 | tf_op jit(solution)/shard_map/ppermute | solution.py:626
  59.2 30.6 %collective-permute-start.20 = (bf16[1,144,512]{2,1,0:T(8,128)(2,1)}, bf16[1,144,512]{2,1,0:T(8,128)(2,1)}, u32[]{:S(2)}, u32[]{:S(2)}) collective-permute-start(bf16[1,144,512]{2,1,0:T(8,128)(2,1)} %collective-permute-done.19.refs_5_), channel_id=1, source_target_pairs={{0,1},{1,0},{2,3},{3,2},{4,5},{5,4},{6,7},{7,6},{8,9},{9,8},{10,11... | collective-permute-start | bytes 442376 | tf_op jit(solution)/shard_map/ppermute | solution.py:626
  80.6 16.7 %collective-permute-start.28 = (bf16[48,4096]{1,0:T(8,128)(2,1)S(1)}, bf16[48,4096]{1,0:T(8,128)(2,1)S(1)}, u32[]{:S(2)}, u32[]{:S(2)}) collective-permute-start(bf16[48,4096]{1,0:T(8,128)(2,1)S(1)} %attend_slots.5), channel_id=1, source_target_pairs={{8,0},{16,8},{24,16},{28,24},{20,28},{12,20},{4,12},{0,4},{9,1},{1... | collective-permute-start | bytes 1179656 | tf_op jit(solution)/shard_map/ppermute | solution.py:626
  82.1 16.6 %collective-permute-start.10 = (bf16[48,4096]{1,0:T(8,128)(2,1)S(1)}, bf16[48,4096]{1,0:T(8,128)(2,1)S(1)}, u32[]{:S(2)}, u32[]{:S(2)}) collective-permute-start(bf16[48,4096]{1,0:T(8,128)(2,1)S(1)} %attend_slots.5), channel_id=1, source_target_pairs={{0,8},{8,16},{16,24},{24,28},{28,20},{20,12},{12,4},{4,0},{1,9},{9... | collective-permute-start | bytes 1179656 | tf_op jit(solution)/shard_map/ppermute | solution.py:626
  108.5 21.5 %collective-permute-start.39 = (bf16[96,896]{1,0:T(8,128)(2,1)S(1)}, bf16[96,896]{1,0:T(8,128)(2,1)S(1)}, u32[]{:S(2)}, u32[]{:S(2)}) collective-permute-start(bf16[96,896]{1,0:T(8,128)(2,1)S(1)} %get-tuple-element.27), channel_id=1, source_target_pairs={{1,0},{0,1},{5,4},{4,5},{9,8},{11,10},{13,12},{15,14},{16,17},{18,... | collective-permute-start | bytes 516104 | tf_op jit(solution)/shard_map/ppermute | solution.py:626
  110.4 21.0 %collective-permute-start.40 = (bf16[96,896]{1,0:T(8,128)(2,1)S(1)}, bf16[96,896]{1,0:T(8,128)(2,1)S(1)}, u32[]{:S(2)}, u32[]{:S(2)}) collective-permute-start(bf16[96,896]{1,0:T(8,128)(2,1)S(1)} %get-tuple-element.28), channel_id=1, source_target_pairs={{2,0},{3,1},{6,4},{7,5},{10,8},{8,10},{14,12},{12,14},{19,17},{17,... | collective-permute-start | bytes 516104 | tf_op jit(solution)/shard_map/ppermute | solution.py:626
  111.7 19.9 %collective-permute-start.41 = (bf16[96,896]{1,0:T(8,128)(2,1)S(1)}, bf16[96,896]{1,0:T(8,128)(2,1)S(1)}, u32[]{:S(2)}, u32[]{:S(2)}) collective-permute-start(bf16[96,896]{1,0:T(8,128)(2,1)S(1)} %get-tuple-element.29), channel_id=1, source_target_pairs={{3,0},{2,1},{7,4},{6,5},{11,8},{9,10},{15,12},{13,14},{18,17},{16,... | collective-permute-start | bytes 516104 | tf_op jit(solution)/shard_map/ppermute | solution.py:626
  114.0 11.8 %collective-permute-start.33 = (bf16[48,4096]{1,0:T(8,128)(2,1)S(1)}, bf16[48,4096]{1,0:T(8,128)(2,1)S(1)}, u32[]{:S(2)}, u32[]{:S(2)}) collective-permute-start(bf16[48,4096]{1,0:T(8,128)(2,1)S(1)} %collective-permute-done.32), channel_id=1, source_target_pairs={{8,0},{16,8},{24,16},{28,24},{20,28},{12,20},{4,12},{0,4},{9,1},{1... | collective-permute-start | bytes 1179656 | tf_op jit(solution)/shard_map/ppermute | solution.py:626
  115.4 12.0 %collective-permute-start.25 = (bf16[48,4096]{1,0:T(8,128)(2,1)S(1)}, bf16[48,4096]{1,0:T(8,128)(2,1)S(1)}, u32[]{:S(2)}, u32[]{:S(2)}) collective-permute-start(bf16[48,4096]{1,0:T(8,128)(2,1)S(1)} %collective-permute-done.24), channel_id=1, source_target_pairs={{0,8},{8,16},{16,24},{24,28},{28,20},{20,12},{12,4},{4,0},{1,9},{9... | collective-permute-start | bytes 1179656 | tf_op jit(solution)/shard_map/ppermute | solution.py:626
  133.9 15.9 %collective-permute-start.35 = (bf16[48,2048]{1,0:T(8,128)(2,1)S(1)}, bf16[48,2048]{1,0:T(8,128)(2,1)S(1)}, u32[]{:S(2)}, u32[]{:S(2)}) collective-permute-start(bf16[48,2048]{1,0:T(8,128)(2,1)S(1)} %get-tuple-element.48), channel_id=1, source_target_pairs={{8,0},{16,8},{24,16},{28,24},{20,28},{12,20},{4,12},{0,4},{9,1},{1... | collective-permute-start | bytes 589832 | tf_op jit(solution)/shard_map/ppermute | solution.py:626
  136.6 14.1 %collective-permute-start.34 = (bf16[48,2048]{1,0:T(8,128)(2,1)S(1)}, bf16[48,2048]{1,0:T(8,128)(2,1)S(1)}, u32[]{:S(2)}, u32[]{:S(2)}) collective-permute-start(bf16[48,2048]{1,0:T(8,128)(2,1)S(1)} %get-tuple-element.47), channel_id=1, source_target_pairs={{8,0},{16,8},{24,16},{28,24},{20,28},{12,20},{4,12},{0,4},{9,1},{1... | collective-permute-start | bytes 589832 | tf_op jit(solution)/shard_map/ppermute | solution.py:626
  137.8 13.5 %collective-permute-start.27 = (bf16[48,2048]{1,0:T(8,128)(2,1)S(1)}, bf16[48,2048]{1,0:T(8,128)(2,1)S(1)}, u32[]{:S(2)}, u32[]{:S(2)}) collective-permute-start(bf16[48,2048]{1,0:T(8,128)(2,1)S(1)} %get-tuple-element.44), channel_id=1, source_target_pairs={{0,8},{8,16},{16,24},{24,28},{28,20},{20,12},{12,4},{4,0},{1,9},{9... | collective-permute-start | bytes 589832 | tf_op jit(solution)/shard_map/ppermute | solution.py:626
  149.8 13.9 %collective-permute-start.48 = (bf16[48,2048]{1,0:T(8,128)(2,1)S(1)}, bf16[48,2048]{1,0:T(8,128)(2,1)S(1)}, u32[]{:S(2)}, u32[]{:S(2)}) collective-permute-start(bf16[48,2048]{1,0:T(8,128)(2,1)S(1)} %collective-permute-done.12), channel_id=1, source_target_pairs={{0,8},{8,16},{16,24},{24,28},{28,20},{20,12},{12,4},{4,0},{1,9},{9... | collective-permute-start | bytes 589832 | tf_op jit(solution)/shard_map/ppermute | solution.py:626
  151.3 13.8 %collective-permute-start.51 = (bf16[48,2048]{1,0:T(8,128)(2,1)S(1)}, bf16[48,2048]{1,0:T(8,128)(2,1)S(1)}, u32[]{:S(2)}, u32[]{:S(2)}) collective-permute-start(bf16[48,2048]{1,0:T(8,128)(2,1)S(1)} %collective-permute-done.35), channel_id=1, source_target_pairs={{8,0},{16,8},{24,16},{28,24},{20,28},{12,20},{4,12},{0,4},{9,1},{1... | collective-permute-start | bytes 589832 | tf_op jit(solution)/shard_map/ppermute | solution.py:626
  152.6 12.6 %collective-permute-start.50 = (bf16[48,2048]{1,0:T(8,128)(2,1)S(1)}, bf16[48,2048]{1,0:T(8,128)(2,1)S(1)}, u32[]{:S(2)}, u32[]{:S(2)}) collective-permute-start(bf16[48,2048]{1,0:T(8,128)(2,1)S(1)} %collective-permute-done.26), channel_id=1, source_target_pairs={{0,8},{8,16},{16,24},{24,28},{28,20},{20,12},{12,4},{4,0},{1,9},{9... | collective-permute-start | bytes 589832 | tf_op jit(solution)/shard_map/ppermute | solution.py:626
  158.3 12.1 %collective-permute-start.46 = (bf16[96,896]{1,0:T(8,128)(2,1)S(1)}, bf16[96,896]{1,0:T(8,128)(2,1)S(1)}, u32[]{:S(2)}, u32[]{:S(2)}) collective-permute-start(bf16[96,896]{1,0:T(8,128)(2,1)S(1)} %get-tuple-element.39), channel_id=1, source_target_pairs={{0,2},{1,3},{4,6},{5,7},{11,9},{9,11},{15,13},{13,15},{18,16},{16,... | collective-permute-start | bytes 516104 | tf_op jit(solution)/shard_map/ppermute | solution.py:626
  (53 other events, 420.0 us)

commit v6 on v5

--- a/solution.py
+++ b/solution.py
@@ -517,60 +517,62 @@
         after[y] = now if before is None else before[y] + now
 
 
-def settle_kernel(heads, per_head, columns, prev_columns, has_total, table, both, *refs):
+def settle_kernel(masks, per_head, columns, prev_columns, has_total, table, both, near, *refs):
     refs = list(refs)
     if prev_columns:
-        prev_own, prev_got = refs.pop(0), [refs.pop(0) for _ in range(heads - 1)]
+        prev_own, prev_got = refs.pop(0), [refs.pop(0) for _ in masks]
         before = refs.pop(0) if has_total else None
     block = both.shape[0] // len(columns)
-    sends = len(refs) - 1 - bool(prev_columns)
+    sends = 1 if len(columns) == 1 else len(masks)
     own = refs[sends]
     head = table[PLACE, 1]
+    chip = both[...].astype(jnp.float32) + near[...].astype(jnp.float32)
     if len(columns) == 1:
-        own[...] = both[...]
-        refs[0][...] = both[...].astype(jnp.bfloat16)
+        own[...] = chip
+        refs[0][...] = chip.astype(jnp.bfloat16)
     else:
-        for m in range(heads):
+        for k, m in enumerate((0, *masks)):
             first = table[TARGET, columns[0]] == jnp.bitwise_xor(head, m)
-            piece = jnp.where(first, both[:block], both[block:])
+            piece = jnp.where(first, chip[:block], chip[block:])
             if m == 0:
                 own[...] = piece
             else:
-                refs[m - 1][...] = piece.astype(jnp.bfloat16)
+                refs[k - 1][...] = piece.astype(jnp.bfloat16)
     if prev_columns:
         add_in(table, per_head, prev_columns, prev_own, prev_got, before, refs[sends + 1])
 
 
-def settle_step(table, heads, per_head, columns, both, previous):
+def settle_step(table, masks, per_head, columns, both, near, previous):
     n = both.shape[0] // len(columns)
     wide = both.shape[1]
     vmem = pl.BlockSpec(memory_space=pltpu.MemorySpace.VMEM)
-    args, prev_columns, has_total = [both], None, False
+    args, prev_columns, has_total = [both, near], None, False
     if previous is not None:
         prev_columns, prev_own, prev_got, total = previous
         has_total = total is not None
         args += [prev_own, *prev_got] + ([total] if has_total else [])
-    sends = 1 if len(columns) == 1 else heads - 1
+    sends = 1 if len(columns) == 1 else len(masks)
     out = [jax.ShapeDtypeStruct((n, wide), jnp.bfloat16)] * sends
     out.append(jax.ShapeDtypeStruct((n, wide), jnp.float32))
     if previous is not None:
         out.append(jax.ShapeDtypeStruct((per_head, n, wide), jnp.float32))
     outs = pl.pallas_call(
-        functools.partial(settle_kernel, heads, per_head, columns, prev_columns, has_total),
+        functools.partial(settle_kernel, masks, per_head, columns, prev_columns, has_total),
         out_shape=out,
         in_specs=[pl.BlockSpec(memory_space=pltpu.MemorySpace.SMEM)] + [vmem] * len(args),
         out_specs=[vmem] * len(out),
         compiler_params=pltpu.CompilerParams(vmem_limit_bytes=4 * 2**20),
         name="settle",
     )(table, *args)
-    to_send = list(outs[:sends]) * (1 if sends > 1 else heads - 1)
+    to_send = list(outs[:sends]) * (1 if len(columns) > 1 else len(masks))
     return to_send, outs[sends], outs[sends + 1] if previous is not None else None
 
 
-def finish_kernel(heads, per_head, steps, roll, table, info, seen, before, *refs):
-    out, total = refs[heads * len(steps) :]
+def finish_kernel(per_head, steps, roll, table, info, seen, before, *refs):
+    *refs, out, total = refs
+    each = len(refs) // len(steps)
     for i, columns in enumerate(steps):
-        own, *got = refs[heads * i : heads * (i + 1)]
+        own, *got = refs[each * i : each * (i + 1)]
         add_in(table, per_head, columns, own, got, total if i else before, total)
     n = total.shape[1]
     slots = n // roll
@@ -590,14 +592,14 @@
         out[pl.ds(y * n, n), :] = moved.astype(out.dtype)
 
 
-def finish(table, info, seen, heads, per_head, roll, total, states):
+def finish(table, info, seen, per_head, roll, total, states):
     _, n, wide = total.shape
     steps = [state[0] for state in states]
     args = [x for _, own, got in states for x in (own, *got)]
     vmem = pl.BlockSpec(memory_space=pltpu.MemorySpace.VMEM)
     smem = pl.BlockSpec(memory_space=pltpu.MemorySpace.SMEM)
     return pl.pallas_call(
-        functools.partial(finish_kernel, heads, per_head, steps, roll),
+        functools.partial(finish_kernel, per_head, steps, roll),
         out_shape=jax.ShapeDtypeStruct((per_head * n, wide), jnp.bfloat16),
         in_specs=[smem] * 3 + [vmem] * (1 + len(args)),
         out_specs=vmem,
@@ -680,42 +682,46 @@
     half = chunks[0][1].shape[1] // 2
 
     def project(pieces):
-        return jnp.dot(jnp.concatenate(pieces), w_out, preferred_element_type=jnp.float32)
+        product = jnp.dot(jnp.concatenate(pieces), w_out, preferred_element_type=jnp.float32)
+        return product.astype(jnp.bfloat16)
 
     def target(p, column):
         return order[(where[p] + offsets[column]) % ranks] // per_head
 
+    masks = list(range(2, heads, 2))
+
     def settle(columns, both, previous):
-        if previous is None and len(columns) == 1:
-            to_send, own, total = [both.astype(jnp.bfloat16)] * (heads - 1), both, None
-        else:
-            to_send, own, total = settle_step(table, heads, per_head, columns, both, previous)
+        near = move(both, [(i, i ^ 1) for i in range(heads)], "head")
+        to_send, own, total = settle_step(table, masks, per_head, columns, both, near, previous)
         got = []
-        for m in range(1, heads):
+        for k, m in enumerate(masks):
             pairs = []
             for p in range(ranks):
                 for t in sorted({target(p, c) for c in columns}):
                     pairs.append((p * heads + (t ^ m), p * heads + t))
-            got.append(move(to_send[m - 1], pairs, ("dp", "head")))
+            got.append(move(to_send[k], pairs, ("dp", "head")))
         return columns, own, got, total
 
     arrived = {}
     for tag, values in chunks:
         fore = back = values
-        for k in range(1, last - 1):
+        for k in range(1, last):
+            if k == last - 1 and tag == chunks[-1][0]:
+                break
             fore = move(fore, ahead)
             back = move(back, behind)
             arrived[tag, k] = fore, back
         fore_on, fore_end = fore[:, :half], fore[:, half:]
         back_on, back_end = back[:, half:], back[:, :half]
-        fore_on = move(fore_on, ahead)
-        back_on = move(back_on, behind)
-        fore_end = move(fore_end, ahead)
-        back_end = move(back_end, behind)
-        arrived[tag, last - 1] = (
-            jnp.concatenate([fore_on, fore_end], axis=1),
-            jnp.concatenate([back_end, back_on], axis=1),
-        )
+        if k == last - 1 and (tag, k) not in arrived:
+            fore_on = move(fore_on, ahead)
+            back_on = move(back_on, behind)
+            fore_end = move(fore_end, ahead)
+            back_end = move(back_end, behind)
+            arrived[tag, k] = (
+                jnp.concatenate([fore_on, fore_end], axis=1),
+                jnp.concatenate([back_end, back_on], axis=1),
+            )
         left = move(fore_on, ahead)
         right = move(back_on, behind)
         arrived[tag, last] = (jnp.concatenate([left, right], axis=1),)
@@ -726,7 +732,7 @@
     ends = project([arrived[tag, last][0] for tag, _ in chunks])
     *before, total = state
     *final, _ = settle([2 * last - 1], ends, None)
-    return finish(table, info, seen, heads, per_head, roll_count, total, [before, final])
+    return finish(table, info, seen, per_head, roll_count, total, [before, final])
 
 
 def local(*args):

time: 178 us -> 165 us (0.927)
  starting transfers between devices: 68.3 us -> 53.4 us
    ppermute x55 -> x48, starting transfers between devices: 62 us -> 47.2 us  [move(): return lax.ppermute(x, axis, pairs)]
    pallas_call x4 -> x6, Pallas kernels: 4.38 us -> 5.47 us  [the longest x5 3.67 us: settle_step(): pl.pallas_call(functools.partial(settle_kernel, masks, per_head, columns,...]
    ppermute x55 -> x48, waiting for transfers between devices: 46.6 us -> 46.8 us  [move(): return lax.ppermute(x, axis, pairs)]
  transfers between devices with their start and end apart: 56 -> 49, of which waited for: 17 -> 17; matrix products, arithmetic and copies ran while one was open for 9% -> 10% of each run, Pallas kernels for 14% -> 16%
where the time goes in v6:
time: 165 us; the launch traced here: 164 us
  waiting for transfers between devices  54.5 us (33%)
  starting transfers between devices  53.4 us (32%)
  Pallas kernels  29.8 us (18%)
  local copies, waits for them, and re-layouts  16.8 us (10%)
  matrix products  8.13 us (5%)
    ppermute x48, starting transfers between devices, move(): return lax.ppermute(x, axis, pairs)  47.2 us
    ppermute x48, waiting for transfers between devices, move(): return lax.ppermute(x, axis, pairs)  46.8 us
    pallas_call x4, Pallas kernels, attend_slots(): pl.pallas_call(functools.partial(slots_kernel, plan, own, [[index for _,...  19.5 us
    unnamed x42, local copies, waits for them, and re-layouts  9.2 us
    dot_general x5, matrix products, project(): jnp.dot(jnp.concatenate(pieces), w_out, preferred_element_type=jnp.float32)  8.13 us
    all_to_all x1, waiting for transfers between devices, local_ring(): lax.all_to_all(jnp.broadcast_to(facts[None], (ranks, width)), 'dp', split...  7.73 us
    all_to_all x1, starting transfers between devices, local_ring(): lax.all_to_all(jnp.broadcast_to(facts[None], (ranks, width)), 'dp', split...  6.28 us
    reshape x1, local copies, waits for them, and re-layouts, local_ring(): q = q_latent.reshape(bundles, roll_count * local_heads, -1)  4.2 us
  transfers between devices with their start and end apart: 49, of which 17 were waited for; matrix products, arithmetic and copies ran while one was open for 10% of the time, Pallas kernels for 16%

profile of v6, /device:TPU:0, one launch (start us, length us, event | category | flops | bytes accessed | tf_op | source)
XLA Modules:
  0.0 163.9 jit_solution(10966890551678833411)
XLA Ops:
  1.1 3.1 %collective-permute-start = (bf16[4,144,512]{2,1,0:T(8,128)(2,1)S(1)}, bf16[4,144,512]{2,1,0:T(8,128)(2,1)S(1)}, u32[]{:S(2)}, u32[]{:S(2)}) collective-permute-start(bf16[4,144,512]{2,1,0:T(8,128)(2,1)S(1)} %payload.1), channel_id=1, source_target_pairs={{0,8},{8,16},{16,24},{24,28},{28,20},{20,12},{12,4},{4,0},{1,9},{9... | collective-permute-start | bytes 1769480 | tf_op jit(solution)/shard_map/ppermute | solution.py:628
  5.5 6.3 %all-to-all-start = ((s32[8,1,32]{2,1,0:T(1,128)}), s32[8,1,32]{2,1,0:T(1,128)S(1)}, u32[]{:S(2)}, u32[]{:S(2)}) async-start(s32[8,1,32]{2,1,0:T(1,128)} %broadcast_in_dim.2), calls=%async_computation | async-start | bytes 8192 | tf_op jit(solution)/shard_map/all_to_all | solution.py:635
  13.3 7.7 %all-to-all-done = s32[8,1,32]{2,1,0:T(1,128)S(1)} async-done(((s32[8,1,32]{2,1,0:T(1,128)}), s32[8,1,32]{2,1,0:T(1,128)S(1)}, u32[]{:S(2)}, u32[]{:S(2)}) %all-to-all-start) | async-done | bytes 1056 | tf_op jit(solution)/shard_map/all_to_all | solution.py:635
  27.5 5.5 %collective-permute-done.2.fore = bf16[368,512]{1,0:T(8,128)(2,1)S(1)} collective-permute-done((bf16[368,512]{1,0:T(8,128)(2,1)S(1)}, bf16[368,512]{1,0:T(8,128)(2,1)S(1)}, u32[]{:S(2)}, u32[]{:S(2)}) %collective-permute-start.2) | collective-permute-done | bytes 376864 | tf_op jit(solution)/shard_map/ppermute | solution.py:628
  36.8 2.8 %collective-permute-done.15.back = bf16[208,512]{1,0:T(8,128)(2,1)S(1)} collective-permute-done((bf16[208,512]{1,0:T(8,128)(2,1)S(1)}, bf16[208,512]{1,0:T(8,128)(2,1)S(1)}, u32[]{:S(2)}, u32[]{:S(2)}) %collective-permute-start.15) | collective-permute-done | bytes 213024 | tf_op jit(solution)/shard_map/ppermute | solution.py:628
  44.3 2.1 %collective-permute-done.16.back = bf16[64,512]{1,0:T(8,128)(2,1)S(1)} collective-permute-done((bf16[64,512]{1,0:T(8,128)(2,1)S(1)}, bf16[64,512]{1,0:T(8,128)(2,1)S(1)}, u32[]{:S(2)}, u32[]{:S(2)}) %collective-permute-start.16) | collective-permute-done | bytes 65568 | tf_op jit(solution)/shard_map/ppermute | solution.py:628
  47.2 3.6 %collective-permute-done.14.fore = bf16[80,512]{1,0:T(8,128)(2,1)S(1)} collective-permute-done((bf16[80,512]{1,0:T(8,128)(2,1)S(1)}, bf16[80,512]{1,0:T(8,128)(2,1)S(1)}, u32[]{:S(2)}, u32[]{:S(2)}) %collective-permute-start.14) | collective-permute-done | bytes 81952 | tf_op jit(solution)/shard_map/ppermute | solution.py:628
  55.1 4.1 %collective-permute-done.18.refs_5_ = bf16[1,144,512]{2,1,0:T(8,128)(2,1)} collective-permute-done((bf16[1,144,512]{2,1,0:T(8,128)(2,1)}, bf16[1,144,512]{2,1,0:T(8,128)(2,1)}, u32[]{:S(2)}, u32[]{:S(2)}) %collective-permute-start.18) | collective-permute-done | bytes 147488 | tf_op jit(solution)/shard_map/ppermute | solution.py:628
  59.2 4.2 %reshape.12.refs_0_ = bf16[8,384,512]{2,1,0:T(8,128)(2,1)S(1)} reshape(bf16[96,16384]{1,0:T(8,128)(2,1)} %param.11) | data formatting | bytes 6291456 | tf_op jit(solution)/shard_map/reshape | solution.py:640
  63.4 2.6 %reshape.13.refs_1_ = bf16[8,384,64]{2,1,0:T(8,128)(2,1)} reshape(bf16[96,2048]{1,0:T(8,128)(2,1)} %param.12) | data formatting | bytes 786432 | tf_op jit(solution)/shard_map/reshape | solution.py:641
  71.0 6.6 %attend_slots.4.refs_7_ = f32[36,4096]{1,0:T(8,128)S(1)} custom-call(s32[8,8]{1,0:T(8,128)S(1)} %copy-done.15, s32[8,1,32]{2,1,0:T(1,128)S(1)} %broadcast_maximum_fusion.info, bf16[8,384,512]{2,1,0:T(8,128)(2,1)S(1)} %reshape.12.refs_0_, bf16[8,384,64]{2,1,0:T(8,128)(2,1)S(1)} %copy-done.2, bf16[32,512,128]{2,1,0:T(8,128)(2,1)} %refs_2_.7, ...), custom_call_target="tpu_custom_call" | custom-call | tf_op jit(solution)/shard_map/attend_slots/pallas_call | solution.py:493
  77.7 3.0 %attend_slots.5 = bf16[48,4096]{1,0:T(8,128)(2,1)S(1)} custom-call(s32[8,8]{1,0:T(8,128)S(1)} %copy-done.15, s32[8,1,32]{2,1,0:T(1,128)S(1)} %broadcast_maximum_fusion.info, bf16[8,384,512]{2,1,0:T(8,128)(2,1)S(1)} %reshape.12.refs_0_, bf16[8,384,64]{2,1,0:T(8,128)(2,1)S(1)} %copy-done.2, bf16[32,512,128]{2,1,0:T(8,128)(2,1)S(1)} %copy-done, ...), custom_call_target="tpu_custom_call" | custom-call | tf_op jit(solution)/shard_map/attend_slots/pallas_call | solution.py:493
  82.8 7.1 %attend_slots.6.refs_7_ = f32[36,4096]{1,0:T(8,128)S(1)} custom-call(s32[8,8]{1,0:T(8,128)S(1)} %copy-done.15, s32[8,1,32]{2,1,0:T(1,128)S(1)} %broadcast_maximum_fusion.info, bf16[8,384,512]{2,1,0:T(8,128)(2,1)S(1)} %reshape.12.refs_0_, bf16[8,384,64]{2,1,0:T(8,128)(2,1)S(1)} %copy-done.3, bf16[32,512,128]{2,1,0:T(8,128)(2,1)} %refs_2_.7, ...), custom_call_target="tpu_custom_call" | custom-call | tf_op jit(solution)/shard_map/attend_slots/pallas_call | solution.py:493
  89.9 2.9 %attend_slots.7 = bf16[48,4096]{1,0:T(8,128)(2,1)S(1)} custom-call(s32[8,8]{1,0:T(8,128)S(1)} %copy-done.15, s32[8,1,32]{2,1,0:T(1,128)S(1)} %broadcast_maximum_fusion.info, bf16[8,384,512]{2,1,0:T(8,128)(2,1)S(1)} %reshape.12.refs_0_, bf16[8,384,64]{2,1,0:T(8,128)(2,1)S(1)} %copy-done.3, bf16[32,512,128]{2,1,0:T(8,128)(2,1)S(1)} %copy-done.1, ...), custom_call_target="tpu_custom_call" | custom-call | tf_op jit(solution)/shard_map/attend_slots/pallas_call | solution.py:493
  98.3 6.5 %collective-permute-done.30 = bf16[48,4096]{1,0:T(8,128)(2,1)S(1)} collective-permute-done((bf16[48,4096]{1,0:T(8,128)(2,1)S(1)}, bf16[48,4096]{1,0:T(8,128)(2,1)S(1)}, u32[]{:S(2)}, u32[]{:S(2)}) %collective-permute-start.30) | collective-permute-done | bytes 393248 | tf_op jit(solution)/shard_map/ppermute | solution.py:628
  110.2 6.0 %collective-permute-done.38.refs_1_ = bf16[96,896]{1,0:T(8,128)(2,1)S(1)} collective-permute-done((bf16[96,896]{1,0:T(8,128)(2,1)S(1)}, bf16[96,896]{1,0:T(8,128)(2,1)S(1)}, u32[]{:S(2)}, u32[]{:S(2)}) %collective-permute-start.38) | collective-permute-done | bytes 172064 | tf_op jit(solution)/shard_map/ppermute | solution.py:628
  116.2 2.0 %collective-permute-start.29 = (bf16[48,4096]{1,0:T(8,128)(2,1)S(1)}, bf16[48,4096]{1,0:T(8,128)(2,1)S(1)}, u32[]{:S(2)}, u32[]{:S(2)}) collective-permute-start(bf16[48,4096]{1,0:T(8,128)(2,1)S(1)} %collective-permute-done.28), channel_id=1, source_target_pairs={{8,0},{16,8},{24,16},{28,24},{20,28},{12,20},{4,12},{0,4},{9,1},{1... | collective-permute-start | bytes 1179656 | tf_op jit(solution)/shard_map/ppermute | solution.py:628
  123.2 4.0 %collective-permute-done.24 = bf16[48,4096]{1,0:T(8,128)(2,1)S(1)} collective-permute-done((bf16[48,4096]{1,0:T(8,128)(2,1)S(1)}, bf16[48,4096]{1,0:T(8,128)(2,1)S(1)}, u32[]{:S(2)}, u32[]{:S(2)}) %collective-permute-start.24) | collective-permute-done | bytes 393248 | tf_op jit(solution)/shard_map/ppermute | solution.py:628
  127.2 2.1 %collective-permute-start.32 = (bf16[48,2048]{1,0:T(8,128)(2,1)S(1)}, bf16[48,2048]{1,0:T(8,128)(2,1)S(1)}, u32[]{:S(2)}, u32[]{:S(2)}) collective-permute-start(bf16[48,2048]{1,0:T(8,128)(2,1)S(1)} %get-tuple-element.39), channel_id=1, source_target_pairs={{8,0},{16,8},{24,16},{28,24},{20,28},{12,20},{4,12},{0,4},{9,1},{1... | collective-permute-start | bytes 589832 | tf_op jit(solution)/shard_map/ppermute | solution.py:628
  130.7 3.4 %collective-permute-done.12 = bf16[48,4096]{1,0:T(8,128)(2,1)S(1)} collective-permute-done((bf16[48,4096]{1,0:T(8,128)(2,1)S(1)}, bf16[48,4096]{1,0:T(8,128)(2,1)S(1)}, u32[]{:S(2)}, u32[]{:S(2)}) %collective-permute-start.12) | collective-permute-done | bytes 393248 | tf_op jit(solution)/shard_map/ppermute | solution.py:628
  134.1 2.5 %collective-permute-start.25 = (bf16[48,2048]{1,0:T(8,128)(2,1)S(1)}, bf16[48,2048]{1,0:T(8,128)(2,1)S(1)}, u32[]{:S(2)}, u32[]{:S(2)}) collective-permute-start(bf16[48,2048]{1,0:T(8,128)(2,1)S(1)} %get-tuple-element.37), channel_id=1, source_target_pairs={{0,8},{8,16},{16,24},{24,28},{28,20},{20,12},{12,4},{4,0},{1,9},{9... | collective-permute-start | bytes 589832 | tf_op jit(solution)/shard_map/ppermute | solution.py:628
  142.5 2.5 %collective-permute-start.44 = (bf16[48,2048]{1,0:T(8,128)(2,1)S(1)}, bf16[48,2048]{1,0:T(8,128)(2,1)S(1)}, u32[]{:S(2)}, u32[]{:S(2)}) collective-permute-start(bf16[48,2048]{1,0:T(8,128)(2,1)S(1)} %collective-permute-done.25), channel_id=1, source_target_pairs={{0,8},{8,16},{16,24},{24,28},{28,20},{20,12},{12,4},{4,0},{1,9},{9... | collective-permute-start | bytes 589832 | tf_op jit(solution)/shard_map/ppermute | solution.py:628
  153.4 3.9 %collective-permute-start.41 = (bf16[96,896]{1,0:T(8,128)(2,1)S(1)}, bf16[96,896]{1,0:T(8,128)(2,1)S(1)}, u32[]{:S(2)}, u32[]{:S(2)}) collective-permute-start(bf16[96,896]{1,0:T(8,128)(2,1)S(1)} %get-tuple-element.34), channel_id=1, source_target_pairs={{0,2},{1,3},{4,6},{5,7},{11,9},{9,11},{15,13},{13,15},{18,16},{16,... | collective-permute-start | bytes 516104 | tf_op jit(solution)/shard_map/ppermute | solution.py:628
  158.7 3.4 %collective-permute-done.41.refs_1_ = bf16[96,896]{1,0:T(8,128)(2,1)S(1)} collective-permute-done((bf16[96,896]{1,0:T(8,128)(2,1)S(1)}, bf16[96,896]{1,0:T(8,128)(2,1)S(1)}, u32[]{:S(2)}, u32[]{:S(2)}) %collective-permute-start.41) | collective-permute-done | bytes 172064 | tf_op jit(solution)/shard_map/ppermute | solution.py:628
  (152 shorter events, 65.4 us)
Async XLA Ops:
  1.1 20.0 %collective-permute-start = (bf16[4,144,512]{2,1,0:T(8,128)(2,1)S(1)}, bf16[4,144,512]{2,1,0:T(8,128)(2,1)S(1)}, u32[]{:S(2)}, u32[]{:S(2)}) collective-permute-start(bf16[4,144,512]{2,1,0:T(8,128)(2,1)S(1)} %payload.1), channel_id=1, source_target_pairs={{0,8},{8,16},{16,24},{24,28},{28,20},{20,12},{12,4},{4,0},{1,9},{9... | collective-permute-start | bytes 1769480 | tf_op jit(solution)/shard_map/ppermute | solution.py:628
  4.2 16.9 %collective-permute-start.1 = (bf16[4,144,512]{2,1,0:T(8,128)(2,1)S(1)}, bf16[4,144,512]{2,1,0:T(8,128)(2,1)S(1)}, u32[]{:S(2)}, u32[]{:S(2)}) collective-permute-start(bf16[4,144,512]{2,1,0:T(8,128)(2,1)S(1)} %payload.1), channel_id=1, source_target_pairs={{8,0},{16,8},{24,16},{28,24},{20,28},{12,20},{4,12},{0,4},{9,1},{1... | collective-permute-start | bytes 1769480 | tf_op jit(solution)/shard_map/ppermute | solution.py:628
  5.5 15.5 %all-to-all-start = ((s32[8,1,32]{2,1,0:T(1,128)}), s32[8,1,32]{2,1,0:T(1,128)S(1)}, u32[]{:S(2)}, u32[]{:S(2)}) async-start(s32[8,1,32]{2,1,0:T(1,128)} %broadcast_in_dim.2), calls=%async_computation | async-start | bytes 8192 | tf_op jit(solution)/shard_map/all_to_all | solution.py:635
  26.1 15.8 %collective-permute-start.8 = (bf16[2,144,512]{2,1,0:T(8,128)(2,1)S(1)}, bf16[2,144,512]{2,1,0:T(8,128)(2,1)S(1)}, u32[]{:S(2)}, u32[]{:S(2)}) collective-permute-start(bf16[2,144,512]{2,1,0:T(8,128)(2,1)S(1)} %get-tuple-element.23.refs_5_.refs_9_), channel_id=1, source_target_pairs={{0,2},{1,3},{2,0},{3,1},{4,6},{5,7},{6,4},{7,5},{8,10},{9,11},{10,... | collective-permute-start | bytes 884744 | tf_op jit(solution)/shard_map/ppermute | solution.py:628
  35.3 12.0 %collective-permute-start.5 = (bf16[2,144,512]{2,1,0:T(8,128)(2,1)S(1)}, bf16[2,144,512]{2,1,0:T(8,128)(2,1)}, u32[]{:S(2)}, u32[]{:S(2)}) collective-permute-start(bf16[2,144,512]{2,1,0:T(8,128)(2,1)S(1)} %join.3.refs_3_), channel_id=1, source_target_pairs={{0,2},{1,3},{2,0},{3,1},{4,6},{5,7},{6,4},{7,5},{8,10},{9,11},{10,... | collective-permute-start | bytes 884744 | tf_op jit(solution)/shard_map/ppermute | solution.py:628
  47.2 30.4 %collective-permute-start.6 = (bf16[2,144,512]{2,1,0:T(8,128)(2,1)}, bf16[2,144,512]{2,1,0:T(8,128)(2,1)}, u32[]{:S(2)}, u32[]{:S(2)}) collective-permute-start(bf16[2,144,512]{2,1,0:T(8,128)(2,1)} %collective-permute-done.5.refs_5_), channel_id=1, source_target_pairs={{0,1},{1,0},{2,3},{3,2},{4,5},{5,4},{6,7},{7,6},{8,9},{9,8},{10,11... | collective-permute-start | bytes 884744 | tf_op jit(solution)/shard_map/ppermute | solution.py:628
  50.9 31.3 %collective-permute-start.20 = (bf16[2,144,512]{2,1,0:T(8,128)(2,1)}, bf16[2,144,512]{2,1,0:T(8,128)(2,1)}, u32[]{:S(2)}, u32[]{:S(2)}) collective-permute-start(bf16[2,144,512]{2,1,0:T(8,128)(2,1)} %join.5.refs_7_.refs_11_), channel_id=1, source_target_pairs={{0,1},{1,0},{2,3},{3,2},{4,5},{5,4},{6,7},{7,6},{8,9},{9,8},{10,11... | collective-permute-start | bytes 884744 | tf_op jit(solution)/shard_map/ppermute | solution.py:628
  51.2 31.5 %collective-permute-start.22 = (bf16[2,144,512]{2,1,0:T(8,128)(2,1)}, bf16[2,144,512]{2,1,0:T(8,128)(2,1)}, u32[]{:S(2)}, u32[]{:S(2)}) collective-permute-start(bf16[2,144,512]{2,1,0:T(8,128)(2,1)} %collective-permute-done.21.refs_9_.refs_13_), channel_id=1, source_target_pairs={{0,1},{1,0},{2,3},{3,2},{4,5},{5,4},{6,7},{7,6},{8,9},{9,8},{10,11... | collective-permute-start | bytes 884744 | tf_op jit(solution)/shard_map/ppermute | solution.py:628
  54.8 35.1 %collective-permute-start.17 = (bf16[1,144,512]{2,1,0:T(8,128)(2,1)}, bf16[1,144,512]{2,1,0:T(8,128)(2,1)}, u32[]{:S(2)}, u32[]{:S(2)}) collective-permute-start(bf16[1,144,512]{2,1,0:T(8,128)(2,1)} %join.4.refs_3_), channel_id=1, source_target_pairs={{0,1},{1,0},{2,3},{3,2},{4,5},{5,4},{6,7},{7,6},{8,9},{9,8},{10,11... | collective-permute-start | bytes 442376 | tf_op jit(solution)/shard_map/ppermute | solution.py:628
  59.2 30.7 %collective-permute-start.19 = (bf16[1,144,512]{2,1,0:T(8,128)(2,1)}, bf16[1,144,512]{2,1,0:T(8,128)(2,1)}, u32[]{:S(2)}, u32[]{:S(2)}) collective-permute-start(bf16[1,144,512]{2,1,0:T(8,128)(2,1)} %collective-permute-done.18.refs_5_), channel_id=1, source_target_pairs={{0,1},{1,0},{2,3},{3,2},{4,5},{5,4},{6,7},{7,6},{8,9},{9,8},{10,11... | collective-permute-start | bytes 442376 | tf_op jit(solution)/shard_map/ppermute | solution.py:628
  80.7 15.6 %collective-permute-start.27 = (bf16[48,4096]{1,0:T(8,128)(2,1)S(1)}, bf16[48,4096]{1,0:T(8,128)(2,1)S(1)}, u32[]{:S(2)}, u32[]{:S(2)}) collective-permute-start(bf16[48,4096]{1,0:T(8,128)(2,1)S(1)} %attend_slots.5), channel_id=1, source_target_pairs={{8,0},{16,8},{24,16},{28,24},{20,28},{12,20},{4,12},{0,4},{9,1},{1... | collective-permute-start | bytes 1179656 | tf_op jit(solution)/shard_map/ppermute | solution.py:628
  82.2 15.6 %collective-permute-start.10 = (bf16[48,4096]{1,0:T(8,128)(2,1)S(1)}, bf16[48,4096]{1,0:T(8,128)(2,1)S(1)}, u32[]{:S(2)}, u32[]{:S(2)}) collective-permute-start(bf16[48,4096]{1,0:T(8,128)(2,1)S(1)} %attend_slots.5), channel_id=1, source_target_pairs={{0,8},{8,16},{16,24},{24,28},{28,20},{20,12},{12,4},{4,0},{1,9},{9... | collective-permute-start | bytes 1179656 | tf_op jit(solution)/shard_map/ppermute | solution.py:628
  92.8 12.0 %collective-permute-start.30 = (bf16[48,4096]{1,0:T(8,128)(2,1)S(1)}, bf16[48,4096]{1,0:T(8,128)(2,1)S(1)}, u32[]{:S(2)}, u32[]{:S(2)}) collective-permute-start(bf16[48,4096]{1,0:T(8,128)(2,1)S(1)} %attend_slots.7), channel_id=1, source_target_pairs={{8,0},{16,8},{24,16},{28,24},{20,28},{12,20},{4,12},{0,4},{9,1},{1... | collective-permute-start | bytes 1179656 | tf_op jit(solution)/shard_map/ppermute | solution.py:628
  94.3 12.0 %collective-permute-start.23 = (bf16[48,4096]{1,0:T(8,128)(2,1)S(1)}, bf16[48,4096]{1,0:T(8,128)(2,1)S(1)}, u32[]{:S(2)}, u32[]{:S(2)}) collective-permute-start(bf16[48,4096]{1,0:T(8,128)(2,1)S(1)} %attend_slots.7), channel_id=1, source_target_pairs={{0,8},{8,16},{16,24},{24,28},{28,20},{20,12},{12,4},{4,0},{1,9},{9... | collective-permute-start | bytes 1179656 | tf_op jit(solution)/shard_map/ppermute | solution.py:628
  96.1 12.1 %collective-permute-start.37 = (bf16[96,896]{1,0:T(8,128)(2,1)S(1)}, bf16[96,896]{1,0:T(8,128)(2,1)S(1)}, u32[]{:S(2)}, u32[]{:S(2)}) collective-permute-start(bf16[96,896]{1,0:T(8,128)(2,1)S(1)} %convolution_convert_fusion.1.both), channel_id=1, source_target_pairs={{0,1},{1,0},{2,3},{3,2},{4,5},{5,4},{6,7},{7,6},{8,9},{9,8},{10,11... | collective-permute-start | bytes 516104 | tf_op jit(solution)/shard_map/ppermute | solution.py:628
  96.2 20.0 %collective-permute-start.28 = (bf16[48,4096]{1,0:T(8,128)(2,1)S(1)}, bf16[48,4096]{1,0:T(8,128)(2,1)S(1)}, u32[]{:S(2)}, u32[]{:S(2)}) collective-permute-start(bf16[48,4096]{1,0:T(8,128)(2,1)S(1)} %collective-permute-done.27), channel_id=1, source_target_pairs={{8,0},{16,8},{24,16},{28,24},{20,28},{12,20},{4,12},{0,4},{9,1},{1... | collective-permute-start | bytes 1179656 | tf_op jit(solution)/shard_map/ppermute | solution.py:628
  97.7 20.5 %collective-permute-start.11 = (bf16[48,4096]{1,0:T(8,128)(2,1)S(1)}, bf16[48,4096]{1,0:T(8,128)(2,1)S(1)}, u32[]{:S(2)}, u32[]{:S(2)}) collective-permute-start(bf16[48,4096]{1,0:T(8,128)(2,1)S(1)} %collective-permute-done.10), channel_id=1, source_target_pairs={{0,8},{8,16},{16,24},{24,28},{28,20},{20,12},{12,4},{4,0},{1,9},{9... | collective-permute-start | bytes 1179656 | tf_op jit(solution)/shard_map/ppermute | solution.py:628
  104.8 16.9 %collective-permute-start.31 = (bf16[48,4096]{1,0:T(8,128)(2,1)S(1)}, bf16[48,4096]{1,0:T(8,128)(2,1)S(1)}, u32[]{:S(2)}, u32[]{:S(2)}) collective-permute-start(bf16[48,4096]{1,0:T(8,128)(2,1)S(1)} %collective-permute-done.30), channel_id=1, source_target_pairs={{8,0},{16,8},{24,16},{28,24},{20,28},{12,20},{4,12},{0,4},{9,1},{1... | collective-permute-start | bytes 1179656 | tf_op jit(solution)/shard_map/ppermute | solution.py:628
  116.2 11.0 %collective-permute-start.24 = (bf16[48,4096]{1,0:T(8,128)(2,1)S(1)}, bf16[48,4096]{1,0:T(8,128)(2,1)S(1)}, u32[]{:S(2)}, u32[]{:S(2)}) collective-permute-start(bf16[48,4096]{1,0:T(8,128)(2,1)S(1)} %collective-permute-done.23), channel_id=1, source_target_pairs={{0,8},{8,16},{16,24},{24,28},{28,20},{20,12},{12,4},{4,0},{1,9},{9... | collective-permute-start | bytes 1179656 | tf_op jit(solution)/shard_map/ppermute | solution.py:628
  116.2 13.9 %collective-permute-start.29 = (bf16[48,4096]{1,0:T(8,128)(2,1)S(1)}, bf16[48,4096]{1,0:T(8,128)(2,1)S(1)}, u32[]{:S(2)}, u32[]{:S(2)}) collective-permute-start(bf16[48,4096]{1,0:T(8,128)(2,1)S(1)} %collective-permute-done.28), channel_id=1, source_target_pairs={{8,0},{16,8},{24,16},{28,24},{20,28},{12,20},{4,12},{0,4},{9,1},{1... | collective-permute-start | bytes 1179656 | tf_op jit(solution)/shard_map/ppermute | solution.py:628
  118.2 15.9 %collective-permute-start.12 = (bf16[48,4096]{1,0:T(8,128)(2,1)S(1)}, bf16[48,4096]{1,0:T(8,128)(2,1)S(1)}, u32[]{:S(2)}, u32[]{:S(2)}) collective-permute-start(bf16[48,4096]{1,0:T(8,128)(2,1)S(1)} %collective-permute-done.11), channel_id=1, source_target_pairs={{0,8},{8,16},{16,24},{24,28},{28,20},{20,12},{12,4},{4,0},{1,9},{9... | collective-permute-start | bytes 1179656 | tf_op jit(solution)/shard_map/ppermute | solution.py:628
  119.0 19.5 %collective-permute-start.39 = (bf16[96,896]{1,0:T(8,128)(2,1)S(1)}, bf16[96,896]{1,0:T(8,128)(2,1)S(1)}, u32[]{:S(2)}, u32[]{:S(2)}) collective-permute-start(bf16[96,896]{1,0:T(8,128)(2,1)S(1)} %get-tuple-element.27), channel_id=1, source_target_pairs={{2,0},{3,1},{6,4},{7,5},{10,8},{8,10},{14,12},{12,14},{19,17},{17,... | collective-permute-start | bytes 516104 | tf_op jit(solution)/shard_map/ppermute | solution.py:628
  121.7 16.9 %collective-permute-start.33 = (bf16[48,2048]{1,0:T(8,128)(2,1)S(1)}, bf16[48,2048]{1,0:T(8,128)(2,1)S(1)}, u32[]{:S(2)}, u32[]{:S(2)}) collective-permute-start(bf16[48,2048]{1,0:T(8,128)(2,1)S(1)} %get-tuple-element.40), channel_id=1, source_target_pairs={{8,0},{16,8},{24,16},{28,24},{20,28},{12,20},{4,12},{0,4},{9,1},{1... | collective-permute-start | bytes 589832 | tf_op jit(solution)/shard_map/ppermute | solution.py:628
  127.2 12.6 %collective-permute-start.32 = (bf16[48,2048]{1,0:T(8,128)(2,1)S(1)}, bf16[48,2048]{1,0:T(8,128)(2,1)S(1)}, u32[]{:S(2)}, u32[]{:S(2)}) collective-permute-start(bf16[48,2048]{1,0:T(8,128)(2,1)S(1)} %get-tuple-element.39), channel_id=1, source_target_pairs={{8,0},{16,8},{24,16},{28,24},{20,28},{12,20},{4,12},{0,4},{9,1},{1... | collective-permute-start | bytes 589832 | tf_op jit(solution)/shard_map/ppermute | solution.py:628
  (46 other events, 343.9 us)

commit v7 on v6

--- a/solution.py
+++ b/solution.py
@@ -240,7 +240,7 @@
     middle = ranks // 2
     return {
         "p": [list(range(middle - 1)), [middle - 1]],
-        "s": [list(range(middle, ranks - 1)), [ranks - 1]],
+        "s": [[c] for c in range(middle, ranks - 2)] + [[ranks - 2, ranks - 1]],
     }
 
 
@@ -517,55 +517,60 @@
         after[y] = now if before is None else before[y] + now
 
 
-def settle_kernel(masks, per_head, columns, prev_columns, has_total, table, both, near, *refs):
+def settle_kernel(masks, per_head, groups, prev_columns, has_total, table, *refs):
     refs = list(refs)
+    sources = [(refs.pop(0), refs.pop(0)) for _ in groups]
     if prev_columns:
         prev_own, prev_got = refs.pop(0), [refs.pop(0) for _ in masks]
         before = refs.pop(0) if has_total else None
-    block = both.shape[0] // len(columns)
-    sends = 1 if len(columns) == 1 else len(masks)
-    own = refs[sends]
     head = table[PLACE, 1]
-    chip = both[...].astype(jnp.float32) + near[...].astype(jnp.float32)
-    if len(columns) == 1:
-        own[...] = chip
-        refs[0][...] = chip.astype(jnp.bfloat16)
-    else:
-        for k, m in enumerate((0, *masks)):
-            first = table[TARGET, columns[0]] == jnp.bitwise_xor(head, m)
-            piece = jnp.where(first, chip[:block], chip[block:])
-            if m == 0:
-                own[...] = piece
-            else:
-                refs[k - 1][...] = piece.astype(jnp.bfloat16)
+    for columns, (both, near) in zip(groups, sources):
+        chip = both[...].astype(jnp.float32) + near[...].astype(jnp.float32)
+        block = chip.shape[0] // len(columns)
+        one = chip[:block]
+        other = chip[block:] if len(columns) > 1 else None
+        for m in masks if other is not None else masks[:1]:
+            piece = one
+            if other is not None:
+                piece = jnp.where(table[TARGET, columns[0]] == jnp.bitwise_xor(head, m), one, other)
+            refs.pop(0)[...] = piece.astype(jnp.bfloat16)
+        if other is not None:
+            one = jnp.where(table[TARGET, columns[0]] == head, one, other)
+        refs.pop(0)[...] = one
     if prev_columns:
-        add_in(table, per_head, prev_columns, prev_own, prev_got, before, refs[sends + 1])
-
-
-def settle_step(table, masks, per_head, columns, both, near, previous):
-    n = both.shape[0] // len(columns)
-    wide = both.shape[1]
+        add_in(table, per_head, prev_columns, prev_own, prev_got, before, refs.pop(0))
+
+
+def settle_step(table, masks, per_head, groups, sources, previous):
+    n = sources[0][0].shape[0] // len(groups[0])
+    wide = sources[0][0].shape[1]
     vmem = pl.BlockSpec(memory_space=pltpu.MemorySpace.VMEM)
-    args, prev_columns, has_total = [both, near], None, False
+    args, prev_columns, has_total = [x for source in sources for x in source], None, False
     if previous is not None:
         prev_columns, prev_own, prev_got, total = previous
         has_total = total is not None
         args += [prev_own, *prev_got] + ([total] if has_total else [])
-    sends = 1 if len(columns) == 1 else len(masks)
-    out = [jax.ShapeDtypeStruct((n, wide), jnp.bfloat16)] * sends
-    out.append(jax.ShapeDtypeStruct((n, wide), jnp.float32))
+    out = []
+    for columns in groups:
+        sends = len(masks) if len(columns) > 1 else 1
+        out += [jax.ShapeDtypeStruct((n, wide), jnp.bfloat16)] * sends
+        out.append(jax.ShapeDtypeStruct((n, wide), jnp.float32))
     if previous is not None:
         out.append(jax.ShapeDtypeStruct((per_head, n, wide), jnp.float32))
     outs = pl.pallas_call(
-        functools.partial(settle_kernel, masks, per_head, columns, prev_columns, has_total),
+        functools.partial(settle_kernel, masks, per_head, groups, prev_columns, has_total),
         out_shape=out,
         in_specs=[pl.BlockSpec(memory_space=pltpu.MemorySpace.SMEM)] + [vmem] * len(args),
         out_specs=[vmem] * len(out),
         compiler_params=pltpu.CompilerParams(vmem_limit_bytes=4 * 2**20),
         name="settle",
     )(table, *args)
-    to_send = list(outs[:sends]) * (1 if len(columns) > 1 else len(masks))
-    return to_send, outs[sends], outs[sends + 1] if previous is not None else None
+    outs = list(outs)
+    states = []
+    for columns in groups:
+        sends = [outs.pop(0) for _ in (masks if len(columns) > 1 else masks[:1])]
+        states.append((sends * (1 if len(columns) > 1 else len(masks)), outs.pop(0)))
+    return states, outs.pop(0) if previous is not None else None
 
 
 def finish_kernel(per_head, steps, roll, table, info, seen, before, *refs):
@@ -636,7 +641,7 @@
         jnp.broadcast_to(facts[None], (ranks, width)), "dp", split_axis=0, concat_axis=0, tiled=True
     )
     info = jnp.maximum(info, 0)[:, None]
-    table = plan_of(seen, owner_rank, owner_pick, loads, per_head)
+    table = in_hbm(plan_of(seen, owner_rank, owner_pick, loads, per_head))
     q = q_latent.reshape(bundles, roll_count * local_heads, -1)
     qr = q_rope.reshape(bundles, roll_count * local_heads, -1)
 
@@ -690,17 +695,21 @@
 
     masks = list(range(2, heads, 2))
 
-    def settle(columns, both, previous):
-        near = move(both, [(i, i ^ 1) for i in range(heads)], "head")
-        to_send, own, total = settle_step(table, masks, per_head, columns, both, near, previous)
-        got = []
-        for k, m in enumerate(masks):
-            pairs = []
-            for p in range(ranks):
-                for t in sorted({target(p, c) for c in columns}):
-                    pairs.append((p * heads + (t ^ m), p * heads + t))
-            got.append(move(to_send[k], pairs, ("dp", "head")))
-        return columns, own, got, total
+    def settle(groups, products, previous):
+        cores = [(i, i ^ 1) for i in range(heads)]
+        sources = [(both, move(both, cores, "head")) for both in products]
+        made, total = settle_step(table, masks, per_head, groups, sources, previous)
+        states = []
+        for columns, (to_send, own) in zip(groups, made):
+            got = []
+            for k, m in enumerate(masks):
+                pairs = []
+                for p in range(ranks):
+                    for t in sorted({target(p, c) for c in columns}):
+                        pairs.append((p * heads + (t ^ m), p * heads + t))
+                got.append(move(to_send[k], pairs, ("dp", "head")))
+            states.append((columns, own, got))
+        return states, total
 
     arrived = {}
     for tag, values in chunks:
@@ -725,14 +734,19 @@
         left = move(fore_on, ahead)
         right = move(back_on, behind)
         arrived[tag, last] = (jnp.concatenate([left, right], axis=1),)
-    state = settle([0], project([values for _, values in chunks]), None)
-    for k in range(1, last):
-        pieces = [arrived[tag, k][side] for side in (0, 1) for tag, _ in chunks]
-        state = settle([2 * k - 1, 2 * k], project(pieces), state)
-    ends = project([arrived[tag, last][0] for tag, _ in chunks])
-    *before, total = state
-    *final, _ = settle([2 * last - 1], ends, None)
-    return finish(table, info, seen, per_head, roll_count, total, [before, final])
+
+    def pieces(k):
+        return [arrived[tag, k][side] for side in range(2 if k < last else 1) for tag, _ in chunks]
+
+    products = [project([values for _, values in chunks])]
+    products += [project(pieces(k)) for k in range(1, last + 1)]
+    (state,), total = settle([[0]], products[:1], None)
+    for k in range(1, last - 1):
+        columns = [2 * k - 1, 2 * k]
+        (state,), total = settle([columns], products[k : k + 1], (*state, total))
+    groups = [[2 * last - 3, 2 * last - 2], [2 * last - 1]]
+    states, total = settle(groups, products[last - 1 :], (*state, total))
+    return finish(table, info, seen, per_head, roll_count, total, states)
 
 
 def local(*args):

time: 165 us -> 166 us (level)
  waiting for transfers between devices: 54.5 us -> 60.4 us
  starting transfers between devices: 53.4 us -> 48.2 us
    ppermute x48, waiting for transfers between devices: 46.8 us -> 52.7 us  [move(): return lax.ppermute(x, axis, pairs)]
    ppermute x48, starting transfers between devices: 47.2 us -> 41.9 us  [move(): return lax.ppermute(x, axis, pairs)]
    pallas_call x4 -> x5, Pallas kernels: 19.5 us -> 20.8 us  [attend_slots(): pl.pallas_call(functools.partial(slots_kernel, plan, own, [[index for _,...]
    unnamed x42 -> x40, local copies, waits for them, and re-layouts: 9.2 us -> 8.52 us
    pallas_call x5 -> x4, Pallas kernels: 3.67 us -> 3.55 us  [settle_step(): pl.pallas_call(functools.partial(settle_kernel, masks, per_head, groups,...]
  transfers between devices with their start and end apart: 49 -> 49, of which waited for: 17 -> 19; matrix products, arithmetic and copies ran while one was open for 10% -> 10% of each run, Pallas kernels for 16% -> 16%
where the time goes in v7:
time: 166 us; the launch traced here: 164 us
  waiting for transfers between devices  60.4 us (36%)
  starting transfers between devices  48.2 us (29%)
  Pallas kernels  30.3 us (18%)
  local copies, waits for them, and re-layouts  16.1 us (10%)
  matrix products  8.12 us (5%)
    ppermute x48, waiting for transfers between devices, move(): return lax.ppermute(x, axis, pairs)  52.7 us
    ppermute x48, starting transfers between devices, move(): return lax.ppermute(x, axis, pairs)  41.9 us
    pallas_call x5, Pallas kernels, attend_slots(): pl.pallas_call(functools.partial(slots_kernel, plan, own, [[index for _,...  20.8 us
    unnamed x40, local copies, waits for them, and re-layouts  8.52 us
    dot_general x5, matrix products, project(): jnp.dot(jnp.concatenate(pieces), w_out, preferred_element_type=jnp.float32)  8.12 us
    all_to_all x1, waiting for transfers between devices, local_ring(): lax.all_to_all(jnp.broadcast_to(facts[None], (ranks, width)), 'dp', split...  7.73 us
    all_to_all x1, starting transfers between devices, local_ring(): lax.all_to_all(jnp.broadcast_to(facts[None], (ranks, width)), 'dp', split...  6.28 us
    reshape x1, local copies, waits for them, and re-layouts, local_ring(): q = q_latent.reshape(bundles, roll_count * local_heads, -1)  4.2 us
  transfers between devices with their start and end apart: 49, of which 19 were waited for; matrix products, arithmetic and copies ran while one was open for 10% of the time, Pallas kernels for 16%

profile of v7, /device:TPU:0, one launch (start us, length us, event | category | flops | bytes accessed | tf_op | source)
XLA Modules:
  0.0 164.3 jit_solution(11950991284962008116)
XLA Ops:
  1.1 3.1 %collective-permute-start = (bf16[4,144,512]{2,1,0:T(8,128)(2,1)S(1)}, bf16[4,144,512]{2,1,0:T(8,128)(2,1)S(1)}, u32[]{:S(2)}, u32[]{:S(2)}) collective-permute-start(bf16[4,144,512]{2,1,0:T(8,128)(2,1)S(1)} %payload.1), channel_id=1, source_target_pairs={{0,8},{8,16},{16,24},{24,28},{28,20},{20,12},{12,4},{4,0},{1,9},{9... | collective-permute-start | bytes 1769480 | tf_op jit(solution)/shard_map/ppermute | solution.py:633
  5.5 6.3 %all-to-all-start = ((s32[8,1,32]{2,1,0:T(1,128)}), s32[8,1,32]{2,1,0:T(1,128)S(1)}, u32[]{:S(2)}, u32[]{:S(2)}) async-start(s32[8,1,32]{2,1,0:T(1,128)} %broadcast_in_dim.2), calls=%async_computation | async-start | bytes 8192 | tf_op jit(solution)/shard_map/all_to_all | solution.py:640
  13.3 7.7 %all-to-all-done = s32[8,1,32]{2,1,0:T(1,128)S(1)} async-done(((s32[8,1,32]{2,1,0:T(1,128)}), s32[8,1,32]{2,1,0:T(1,128)S(1)}, u32[]{:S(2)}, u32[]{:S(2)}) %all-to-all-start) | async-done | bytes 1056 | tf_op jit(solution)/shard_map/all_to_all | solution.py:640
  26.9 5.5 %collective-permute-done.2.fore = bf16[368,512]{1,0:T(8,128)(2,1)S(1)} collective-permute-done((bf16[368,512]{1,0:T(8,128)(2,1)S(1)}, bf16[368,512]{1,0:T(8,128)(2,1)S(1)}, u32[]{:S(2)}, u32[]{:S(2)}) %collective-permute-start.2) | collective-permute-done | bytes 376864 | tf_op jit(solution)/shard_map/ppermute | solution.py:633
  36.2 2.8 %collective-permute-done.14.back = bf16[208,512]{1,0:T(8,128)(2,1)S(1)} collective-permute-done((bf16[208,512]{1,0:T(8,128)(2,1)S(1)}, bf16[208,512]{1,0:T(8,128)(2,1)S(1)}, u32[]{:S(2)}, u32[]{:S(2)}) %collective-permute-start.14) | collective-permute-done | bytes 213024 | tf_op jit(solution)/shard_map/ppermute | solution.py:633
  43.0 2.1 %collective-permute-done.19.back = bf16[64,512]{1,0:T(8,128)(2,1)S(1)} collective-permute-done((bf16[64,512]{1,0:T(8,128)(2,1)S(1)}, bf16[64,512]{1,0:T(8,128)(2,1)S(1)}, u32[]{:S(2)}, u32[]{:S(2)}) %collective-permute-start.19) | collective-permute-done | bytes 65568 | tf_op jit(solution)/shard_map/ppermute | solution.py:633
  45.9 3.6 %collective-permute-done.18.fore = bf16[80,512]{1,0:T(8,128)(2,1)S(1)} collective-permute-done((bf16[80,512]{1,0:T(8,128)(2,1)S(1)}, bf16[80,512]{1,0:T(8,128)(2,1)S(1)}, u32[]{:S(2)}, u32[]{:S(2)}) %collective-permute-start.18) | collective-permute-done | bytes 81952 | tf_op jit(solution)/shard_map/ppermute | solution.py:633
  54.4 4.1 %collective-permute-done.21.refs_9_ = bf16[1,144,512]{2,1,0:T(8,128)(2,1)} collective-permute-done((bf16[1,144,512]{2,1,0:T(8,128)(2,1)}, bf16[1,144,512]{2,1,0:T(8,128)(2,1)}, u32[]{:S(2)}, u32[]{:S(2)}) %collective-permute-start.21) | collective-permute-done | bytes 147488 | tf_op jit(solution)/shard_map/ppermute | solution.py:633
  58.6 4.2 %reshape.12.refs_0_ = bf16[8,384,512]{2,1,0:T(8,128)(2,1)S(1)} reshape(bf16[96,16384]{1,0:T(8,128)(2,1)} %param.11) | data formatting | bytes 6291456 | tf_op jit(solution)/shard_map/reshape | solution.py:645
  62.8 2.6 %reshape.13.refs_1_ = bf16[8,384,64]{2,1,0:T(8,128)(2,1)} reshape(bf16[96,2048]{1,0:T(8,128)(2,1)} %param.12) | data formatting | bytes 786432 | tf_op jit(solution)/shard_map/reshape | solution.py:646
  70.4 6.9 %attend_slots.5.refs_7_ = f32[36,4096]{1,0:T(8,128)S(1)} custom-call(s32[8,8]{1,0:T(8,128)} %plan.1.table, s32[8,1,32]{2,1,0:T(1,128)S(1)} %broadcast_maximum_fusion.info, bf16[8,384,512]{2,1,0:T(8,128)(2,1)S(1)} %reshape.12.refs_0_, bf16[8,384,64]{2,1,0:T(8,128)(2,1)S(1)} %copy-done.1, bf16[32,512,128]{2,1,0:T(8,128)(2,1)} %refs_2_.9, ...), custom_call_target="tpu_custom_call" | custom-call | tf_op jit(solution)/shard_map/attend_slots/pallas_call | solution.py:493
  77.4 2.8 %attend_slots.6 = bf16[48,4096]{1,0:T(8,128)(2,1)S(1)} custom-call(s32[8,8]{1,0:T(8,128)} %plan.1.table, s32[8,1,32]{2,1,0:T(1,128)S(1)} %broadcast_maximum_fusion.info, bf16[8,384,512]{2,1,0:T(8,128)(2,1)S(1)} %reshape.12.refs_0_, bf16[8,384,64]{2,1,0:T(8,128)(2,1)S(1)} %copy-done.1, bf16[32,512,128]{2,1,0:T(8,128)(2,1)S(1)} %copy-done, ...), custom_call_target="tpu_custom_call" | custom-call | tf_op jit(solution)/shard_map/attend_slots/pallas_call | solution.py:493
  80.8 2.8 %attend_slots.7.refs_11_ = f32[12,4096]{1,0:T(8,128)S(1)} custom-call(s32[8,8]{1,0:T(8,128)} %plan.1.table, s32[8,1,32]{2,1,0:T(1,128)S(1)} %broadcast_maximum_fusion.info, bf16[8,384,512]{2,1,0:T(8,128)(2,1)S(1)} %reshape.12.refs_0_, bf16[8,384,64]{2,1,0:T(8,128)(2,1)S(1)} %copy-done.1, bf16[32,512,128]{2,1,0:T(8,128)(2,1)S(1)} %copy-done, ...), custom_call_target="tpu_custom_call" | custom-call | tf_op jit(solution)/shard_map/attend_slots/pallas_call | solution.py:493
  85.3 3.0 %attend_slots.8.refs_12_ = f32[12,4096]{1,0:T(8,128)S(1)} custom-call(s32[8,8]{1,0:T(8,128)} %plan.1.table, s32[8,1,32]{2,1,0:T(1,128)S(1)} %broadcast_maximum_fusion.info, bf16[8,384,512]{2,1,0:T(8,128)(2,1)S(1)} %reshape.12.refs_0_, bf16[8,384,64]{2,1,0:T(8,128)(2,1)S(1)} %copy-done.1, bf16[32,512,128]{2,1,0:T(8,128)(2,1)S(1)} %copy-done, ...), custom_call_target="tpu_custom_call" | custom-call | tf_op jit(solution)/shard_map/attend_slots/pallas_call | solution.py:493
  88.3 5.3 %attend_slots.9 = bf16[48,4096]{1,0:T(8,128)(2,1)S(1)} custom-call(s32[8,8]{1,0:T(8,128)} %plan.1.table, s32[8,1,32]{2,1,0:T(1,128)S(1)} %broadcast_maximum_fusion.info, bf16[8,384,512]{2,1,0:T(8,128)(2,1)S(1)} %reshape.12.refs_0_, bf16[8,384,64]{2,1,0:T(8,128)(2,1)S(1)} %copy-done.2, bf16[32,512,128]{2,1,0:T(8,128)(2,1)} %refs_2_.9, ...), custom_call_target="tpu_custom_call" | custom-call | tf_op jit(solution)/shard_map/attend_slots/pallas_call | solution.py:493
  99.2 6.5 %collective-permute-done.23 = bf16[48,4096]{1,0:T(8,128)(2,1)S(1)} collective-permute-done((bf16[48,4096]{1,0:T(8,128)(2,1)S(1)}, bf16[48,4096]{1,0:T(8,128)(2,1)S(1)}, u32[]{:S(2)}, u32[]{:S(2)}) %collective-permute-start.23) | collective-permute-done | bytes 393248 | tf_op jit(solution)/shard_map/ppermute | solution.py:633
  110.3 6.0 %collective-permute-done.43.refs_3_ = bf16[96,896]{1,0:T(8,128)(2,1)S(1)} collective-permute-done((bf16[96,896]{1,0:T(8,128)(2,1)S(1)}, bf16[96,896]{1,0:T(8,128)(2,1)S(1)}, u32[]{:S(2)}, u32[]{:S(2)}) %collective-permute-start.43) | collective-permute-done | bytes 172064 | tf_op jit(solution)/shard_map/ppermute | solution.py:633
  123.3 5.0 %collective-permute-done.31 = bf16[48,4096]{1,0:T(8,128)(2,1)S(1)} collective-permute-done((bf16[48,4096]{1,0:T(8,128)(2,1)S(1)}, bf16[48,4096]{1,0:T(8,128)(2,1)S(1)}, u32[]{:S(2)}, u32[]{:S(2)}) %collective-permute-start.31) | collective-permute-done | bytes 393248 | tf_op jit(solution)/shard_map/ppermute | solution.py:633
  131.6 5.0 %collective-permute-done.29 = bf16[48,4096]{1,0:T(8,128)(2,1)S(1)} collective-permute-done((bf16[48,4096]{1,0:T(8,128)(2,1)S(1)}, bf16[48,4096]{1,0:T(8,128)(2,1)S(1)}, u32[]{:S(2)}, u32[]{:S(2)}) %collective-permute-start.29) | collective-permute-done | bytes 393248 | tf_op jit(solution)/shard_map/ppermute | solution.py:633
  136.6 1.9 %fusion.31.refs_0_ = bf16[192,896]{1,0:T(8,128)(2,1)S(1)} fusion(bf16[4096,896]{1,0:T(8,128)(2,1)S(1)} %bitcast.6, bf16[48,4096]{1,0:T(8,128)(2,1)S(1)} %collective-permute-done.31, bf16[48,4096]{1,0:T(8,128)(2,1)S(1)} %collective-permute-done.28, bf16[48,4096]{1,0:T(8,128)(2,1)S(1)} %collective-permute-done.24, ...), kind=kOutput, calls=%fused_computation.29 | convolution fusion | flops 1415749632 | bytes 9256960 | tf_op jit(solution)/shard_map/dot_general | solution.py:690
  138.6 2.1 %collective-permute-start.35 = (bf16[48,2048]{1,0:T(8,128)(2,1)S(1)}, bf16[48,2048]{1,0:T(8,128)(2,1)S(1)}, u32[]{:S(2)}, u32[]{:S(2)}) collective-permute-start(bf16[48,2048]{1,0:T(8,128)(2,1)S(1)} %slice.48), channel_id=1, source_target_pairs={{0,8},{8,16},{16,24},{24,28},{28,20},{20,12},{12,4},{4,0},{1,9},{9... | collective-permute-start | bytes 589832 | tf_op jit(solution)/shard_map/ppermute | solution.py:633
  140.7 2.0 %collective-permute-start.37 = (bf16[48,2048]{1,0:T(8,128)(2,1)S(1)}, bf16[48,2048]{1,0:T(8,128)(2,1)S(1)}, u32[]{:S(2)}, u32[]{:S(2)}) collective-permute-start(bf16[48,2048]{1,0:T(8,128)(2,1)S(1)} %collective-permute-done.25), channel_id=1, source_target_pairs={{0,8},{8,16},{16,24},{24,28},{28,20},{20,12},{12,4},{4,0},{1,9},{9... | collective-permute-start | bytes 589832 | tf_op jit(solution)/shard_map/ppermute | solution.py:633
  155.6 2.1 %collective-permute-start.46 = (bf16[96,896]{1,0:T(8,128)(2,1)S(1)}, bf16[96,896]{1,0:T(8,128)(2,1)S(1)}, u32[]{:S(2)}, u32[]{:S(2)}) collective-permute-start(bf16[96,896]{1,0:T(8,128)(2,1)S(1)} %get-tuple-element.34), channel_id=1, source_target_pairs={{0,2},{1,3},{4,6},{5,7},{11,9},{9,11},{15,13},{13,15},{18,16},{16,... | collective-permute-start | bytes 516104 | tf_op jit(solution)/shard_map/ppermute | solution.py:633
  158.4 4.1 %collective-permute-done.46.refs_1_ = bf16[96,896]{1,0:T(8,128)(2,1)S(1)} collective-permute-done((bf16[96,896]{1,0:T(8,128)(2,1)S(1)}, bf16[96,896]{1,0:T(8,128)(2,1)S(1)}, u32[]{:S(2)}, u32[]{:S(2)}) %collective-permute-start.46) | collective-permute-done | bytes 172064 | tf_op jit(solution)/shard_map/ppermute | solution.py:633
  (150 shorter events, 66.2 us)
Async XLA Ops:
  1.1 20.0 %collective-permute-start = (bf16[4,144,512]{2,1,0:T(8,128)(2,1)S(1)}, bf16[4,144,512]{2,1,0:T(8,128)(2,1)S(1)}, u32[]{:S(2)}, u32[]{:S(2)}) collective-permute-start(bf16[4,144,512]{2,1,0:T(8,128)(2,1)S(1)} %payload.1), channel_id=1, source_target_pairs={{0,8},{8,16},{16,24},{24,28},{28,20},{20,12},{12,4},{4,0},{1,9},{9... | collective-permute-start | bytes 1769480 | tf_op jit(solution)/shard_map/ppermute | solution.py:633
  4.2 16.9 %collective-permute-start.1 = (bf16[4,144,512]{2,1,0:T(8,128)(2,1)S(1)}, bf16[4,144,512]{2,1,0:T(8,128)(2,1)S(1)}, u32[]{:S(2)}, u32[]{:S(2)}) collective-permute-start(bf16[4,144,512]{2,1,0:T(8,128)(2,1)S(1)} %payload.1), channel_id=1, source_target_pairs={{8,0},{16,8},{24,16},{28,24},{20,28},{12,20},{4,12},{0,4},{9,1},{1... | collective-permute-start | bytes 1769480 | tf_op jit(solution)/shard_map/ppermute | solution.py:633
  5.5 15.5 %all-to-all-start = ((s32[8,1,32]{2,1,0:T(1,128)}), s32[8,1,32]{2,1,0:T(1,128)S(1)}, u32[]{:S(2)}, u32[]{:S(2)}) async-start(s32[8,1,32]{2,1,0:T(1,128)} %broadcast_in_dim.2), calls=%async_computation | async-start | bytes 8192 | tf_op jit(solution)/shard_map/all_to_all | solution.py:640
  25.4 15.2 %collective-permute-start.8 = (bf16[2,144,512]{2,1,0:T(8,128)(2,1)S(1)}, bf16[2,144,512]{2,1,0:T(8,128)(2,1)S(1)}, u32[]{:S(2)}, u32[]{:S(2)}) collective-permute-start(bf16[2,144,512]{2,1,0:T(8,128)(2,1)S(1)} %get-tuple-element.23.refs_5_.refs_9_), channel_id=1, source_target_pairs={{0,2},{1,3},{2,0},{3,1},{4,6},{5,7},{6,4},{7,5},{8,10},{9,11},{10,... | collective-permute-start | bytes 884744 | tf_op jit(solution)/shard_map/ppermute | solution.py:633
  39.0 11.5 %collective-permute-start.16 = (bf16[2,144,512]{2,1,0:T(8,128)(2,1)S(1)}, bf16[2,144,512]{2,1,0:T(8,128)(2,1)}, u32[]{:S(2)}, u32[]{:S(2)}) collective-permute-start(bf16[2,144,512]{2,1,0:T(8,128)(2,1)S(1)} %join.4.refs_3_), channel_id=1, source_target_pairs={{0,2},{1,3},{2,0},{3,1},{4,6},{5,7},{6,4},{7,5},{8,10},{9,11},{10,... | collective-permute-start | bytes 884744 | tf_op jit(solution)/shard_map/ppermute | solution.py:633
  45.9 31.4 %collective-permute-start.6 = (bf16[2,144,512]{2,1,0:T(8,128)(2,1)}, bf16[2,144,512]{2,1,0:T(8,128)(2,1)}, u32[]{:S(2)}, u32[]{:S(2)}) collective-permute-start(bf16[2,144,512]{2,1,0:T(8,128)(2,1)} %collective-permute-done.5.refs_5_), channel_id=1, source_target_pairs={{0,1},{1,0},{2,3},{3,2},{4,5},{5,4},{6,7},{7,6},{8,9},{9,8},{10,11... | collective-permute-start | bytes 884744 | tf_op jit(solution)/shard_map/ppermute | solution.py:633
  49.5 34.1 %collective-permute-start.15 = (bf16[2,144,512]{2,1,0:T(8,128)(2,1)S(1)}, bf16[2,144,512]{2,1,0:T(8,128)(2,1)}, u32[]{:S(2)}, u32[]{:S(2)}) collective-permute-start(bf16[2,144,512]{2,1,0:T(8,128)(2,1)S(1)} %join.4.refs_3_), channel_id=1, source_target_pairs={{0,1},{1,0},{2,3},{3,2},{4,5},{5,4},{6,7},{7,6},{8,9},{9,8},{10,11... | collective-permute-start | bytes 884744 | tf_op jit(solution)/shard_map/ppermute | solution.py:633
  50.5 34.7 %collective-permute-start.17 = (bf16[2,144,512]{2,1,0:T(8,128)(2,1)}, bf16[2,144,512]{2,1,0:T(8,128)(2,1)}, u32[]{:S(2)}, u32[]{:S(2)}) collective-permute-start(bf16[2,144,512]{2,1,0:T(8,128)(2,1)} %collective-permute-done.16.refs_5_), channel_id=1, source_target_pairs={{0,1},{1,0},{2,3},{3,2},{4,5},{5,4},{6,7},{7,6},{8,9},{9,8},{10,11... | collective-permute-start | bytes 884744 | tf_op jit(solution)/shard_map/ppermute | solution.py:633
  54.1 34.2 %collective-permute-start.20 = (bf16[1,144,512]{2,1,0:T(8,128)(2,1)}, bf16[1,144,512]{2,1,0:T(8,128)(2,1)}, u32[]{:S(2)}, u32[]{:S(2)}) collective-permute-start(bf16[1,144,512]{2,1,0:T(8,128)(2,1)} %join.5.refs_7_), channel_id=1, source_target_pairs={{0,1},{1,0},{2,3},{3,2},{4,5},{5,4},{6,7},{7,6},{8,9},{9,8},{10,11... | collective-permute-start | bytes 442376 | tf_op jit(solution)/shard_map/ppermute | solution.py:633
  58.5 29.8 %collective-permute-start.22 = (bf16[1,144,512]{2,1,0:T(8,128)(2,1)}, bf16[1,144,512]{2,1,0:T(8,128)(2,1)}, u32[]{:S(2)}, u32[]{:S(2)}) collective-permute-start(bf16[1,144,512]{2,1,0:T(8,128)(2,1)} %collective-permute-done.21.refs_9_), channel_id=1, source_target_pairs={{0,1},{1,0},{2,3},{3,2},{4,5},{5,4},{6,7},{7,6},{8,9},{9,8},{10,11... | collective-permute-start | bytes 442376 | tf_op jit(solution)/shard_map/ppermute | solution.py:633
  80.2 16.9 %collective-permute-start.10 = (bf16[48,4096]{1,0:T(8,128)(2,1)S(1)}, bf16[48,4096]{1,0:T(8,128)(2,1)S(1)}, u32[]{:S(2)}, u32[]{:S(2)}) collective-permute-start(bf16[48,4096]{1,0:T(8,128)(2,1)S(1)} %attend_slots.6), channel_id=1, source_target_pairs={{0,8},{8,16},{16,24},{24,28},{28,20},{20,12},{12,4},{4,0},{1,9},{9... | collective-permute-start | bytes 1179656 | tf_op jit(solution)/shard_map/ppermute | solution.py:633
  83.6 14.2 %collective-permute-start.27 = (bf16[48,4096]{1,0:T(8,128)(2,1)S(1)}, bf16[48,4096]{1,0:T(8,128)(2,1)S(1)}, u32[]{:S(2)}, u32[]{:S(2)}) collective-permute-start(bf16[48,4096]{1,0:T(8,128)(2,1)S(1)} %attend_slots.6), channel_id=1, source_target_pairs={{8,0},{16,8},{24,16},{28,24},{20,28},{12,20},{4,12},{0,4},{9,1},{1... | collective-permute-start | bytes 1179656 | tf_op jit(solution)/shard_map/ppermute | solution.py:633
  93.7 12.0 %collective-permute-start.23 = (bf16[48,4096]{1,0:T(8,128)(2,1)S(1)}, bf16[48,4096]{1,0:T(8,128)(2,1)S(1)}, u32[]{:S(2)}, u32[]{:S(2)}) collective-permute-start(bf16[48,4096]{1,0:T(8,128)(2,1)S(1)} %attend_slots.9), channel_id=1, source_target_pairs={{0,8},{8,16},{16,24},{24,28},{28,20},{20,12},{12,4},{4,0},{1,9},{9... | collective-permute-start | bytes 1179656 | tf_op jit(solution)/shard_map/ppermute | solution.py:633
  94.3 12.0 %collective-permute-start.30 = (bf16[48,4096]{1,0:T(8,128)(2,1)S(1)}, bf16[48,4096]{1,0:T(8,128)(2,1)S(1)}, u32[]{:S(2)}, u32[]{:S(2)}) collective-permute-start(bf16[48,4096]{1,0:T(8,128)(2,1)S(1)} %attend_slots.9), channel_id=1, source_target_pairs={{8,0},{16,8},{24,16},{28,24},{20,28},{12,20},{4,12},{0,4},{9,1},{1... | collective-permute-start | bytes 1179656 | tf_op jit(solution)/shard_map/ppermute | solution.py:633
  97.1 20.7 %collective-permute-start.11 = (bf16[48,4096]{1,0:T(8,128)(2,1)S(1)}, bf16[48,4096]{1,0:T(8,128)(2,1)S(1)}, u32[]{:S(2)}, u32[]{:S(2)}) collective-permute-start(bf16[48,4096]{1,0:T(8,128)(2,1)S(1)} %collective-permute-done.10), channel_id=1, source_target_pairs={{0,8},{8,16},{16,24},{24,28},{28,20},{20,12},{12,4},{4,0},{1,9},{9... | collective-permute-start | bytes 1179656 | tf_op jit(solution)/shard_map/ppermute | solution.py:633
  97.8 20.6 %collective-permute-start.28 = (bf16[48,4096]{1,0:T(8,128)(2,1)S(1)}, bf16[48,4096]{1,0:T(8,128)(2,1)S(1)}, u32[]{:S(2)}, u32[]{:S(2)}) collective-permute-start(bf16[48,4096]{1,0:T(8,128)(2,1)S(1)} %collective-permute-done.27), channel_id=1, source_target_pairs={{8,0},{16,8},{24,16},{28,24},{20,28},{12,20},{4,12},{0,4},{9,1},{1... | collective-permute-start | bytes 1179656 | tf_op jit(solution)/shard_map/ppermute | solution.py:633
  105.7 16.9 %collective-permute-start.24 = (bf16[48,4096]{1,0:T(8,128)(2,1)S(1)}, bf16[48,4096]{1,0:T(8,128)(2,1)S(1)}, u32[]{:S(2)}, u32[]{:S(2)}) collective-permute-start(bf16[48,4096]{1,0:T(8,128)(2,1)S(1)} %collective-permute-done.23), channel_id=1, source_target_pairs={{0,8},{8,16},{16,24},{24,28},{28,20},{20,12},{12,4},{4,0},{1,9},{9... | collective-permute-start | bytes 1179656 | tf_op jit(solution)/shard_map/ppermute | solution.py:633
  108.2 11.6 %collective-permute-start.41 = (bf16[192,896]{1,0:T(8,128)(2,1)S(1)}, bf16[192,896]{1,0:T(8,128)(2,1)S(1)}, u32[]{:S(2)}, u32[]{:S(2)}) collective-permute-start(bf16[192,896]{1,0:T(8,128)(2,1)S(1)} %fusion.28.refs_0_), channel_id=1, source_target_pairs={{0,1},{1,0},{2,3},{3,2},{4,5},{5,4},{6,7},{7,6},{8,9},{9,8},{10,11... | collective-permute-start | bytes 1032200 | tf_op jit(solution)/shard_map/ppermute | solution.py:633
  116.3 12.0 %collective-permute-start.31 = (bf16[48,4096]{1,0:T(8,128)(2,1)S(1)}, bf16[48,4096]{1,0:T(8,128)(2,1)S(1)}, u32[]{:S(2)}, u32[]{:S(2)}) collective-permute-start(bf16[48,4096]{1,0:T(8,128)(2,1)S(1)} %collective-permute-done.30), channel_id=1, source_target_pairs={{8,0},{16,8},{24,16},{28,24},{20,28},{12,20},{4,12},{0,4},{9,1},{1... | collective-permute-start | bytes 1179656 | tf_op jit(solution)/shard_map/ppermute | solution.py:633
  117.8 13.2 %collective-permute-start.12 = (bf16[48,4096]{1,0:T(8,128)(2,1)S(1)}, bf16[48,4096]{1,0:T(8,128)(2,1)S(1)}, u32[]{:S(2)}, u32[]{:S(2)}) collective-permute-start(bf16[48,4096]{1,0:T(8,128)(2,1)S(1)} %collective-permute-done.11), channel_id=1, source_target_pairs={{0,8},{8,16},{16,24},{24,28},{28,20},{20,12},{12,4},{4,0},{1,9},{9... | collective-permute-start | bytes 1179656 | tf_op jit(solution)/shard_map/ppermute | solution.py:633
  118.4 18.2 %collective-permute-start.29 = (bf16[48,4096]{1,0:T(8,128)(2,1)S(1)}, bf16[48,4096]{1,0:T(8,128)(2,1)S(1)}, u32[]{:S(2)}, u32[]{:S(2)}) collective-permute-start(bf16[48,4096]{1,0:T(8,128)(2,1)S(1)} %collective-permute-done.28), channel_id=1, source_target_pairs={{8,0},{16,8},{24,16},{28,24},{20,28},{12,20},{4,12},{0,4},{9,1},{1... | collective-permute-start | bytes 1179656 | tf_op jit(solution)/shard_map/ppermute | solution.py:633
  120.7 17.8 %collective-permute-start.44 = (bf16[96,896]{1,0:T(8,128)(2,1)S(1)}, bf16[96,896]{1,0:T(8,128)(2,1)S(1)}, u32[]{:S(2)}, u32[]{:S(2)}) collective-permute-start(bf16[96,896]{1,0:T(8,128)(2,1)S(1)} %get-tuple-element.27), channel_id=1, source_target_pairs={{2,0},{3,1},{6,4},{7,5},{10,8},{8,10},{14,12},{12,14},{19,17},{17,... | collective-permute-start | bytes 516104 | tf_op jit(solution)/shard_map/ppermute | solution.py:633
  122.6 16.0 %collective-permute-start.25 = (bf16[48,2048]{1,0:T(8,128)(2,1)S(1)}, bf16[48,2048]{1,0:T(8,128)(2,1)S(1)}, u32[]{:S(2)}, u32[]{:S(2)}) collective-permute-start(bf16[48,2048]{1,0:T(8,128)(2,1)S(1)} %get-tuple-element.37), channel_id=1, source_target_pairs={{0,8},{8,16},{16,24},{24,28},{28,20},{20,12},{12,4},{4,0},{1,9},{9... | collective-permute-start | bytes 589832 | tf_op jit(solution)/shard_map/ppermute | solution.py:633
  128.4 12.4 %collective-permute-start.33 = (bf16[48,2048]{1,0:T(8,128)(2,1)S(1)}, bf16[48,2048]{1,0:T(8,128)(2,1)S(1)}, u32[]{:S(2)}, u32[]{:S(2)}) collective-permute-start(bf16[48,2048]{1,0:T(8,128)(2,1)S(1)} %get-tuple-element.40), channel_id=1, source_target_pairs={{8,0},{16,8},{24,16},{28,24},{20,28},{12,20},{4,12},{0,4},{9,1},{1... | collective-permute-start | bytes 589832 | tf_op jit(solution)/shard_map/ppermute | solution.py:633
  (45 other events, 333.9 us)

commit v8 on v7

--- a/solution.py
+++ b/solution.py
@@ -744,8 +744,10 @@
     for k in range(1, last - 1):
         columns = [2 * k - 1, 2 * k]
         (state,), total = settle([columns], products[k : k + 1], (*state, total))
-    groups = [[2 * last - 3, 2 * last - 2], [2 * last - 1]]
-    states, total = settle(groups, products[last - 1 :], (*state, total))
+    columns = [2 * last - 3, 2 * last - 2]
+    before, total = settle([columns], products[last - 1 : last], (*state, total))
+    final, _ = settle([[2 * last - 1]], products[last:], None)
+    states = before + final
     return finish(table, info, seen, per_head, roll_count, total, states)
 
 

time: 166 us -> 166 us (level)
  starting transfers between devices: 48.2 us -> 52.8 us
  waiting for transfers between devices: 60.4 us -> 55.9 us
    ppermute x48, starting transfers between devices: 41.9 us -> 46.6 us  [move(): return lax.ppermute(x, axis, pairs)]
    ppermute x48, waiting for transfers between devices: 52.7 us -> 48.1 us  [move(): return lax.ppermute(x, axis, pairs)]
    pallas_call x4 -> x5, Pallas kernels: 3.55 us -> 4.28 us  [settle_step(): pl.pallas_call(functools.partial(settle_kernel, masks, per_head, groups,...]
  transfers between devices with their start and end apart: 49 -> 49, of which waited for: 19 -> 18; matrix products, arithmetic and copies ran while one was open for 10% -> 10% of each run, Pallas kernels for 16% -> 16%
where the time goes in v8:
time: 166 us; the launch traced here: 165 us
  waiting for transfers between devices  55.9 us (34%)
  starting transfers between devices  52.8 us (32%)
  Pallas kernels  31 us (19%)
  local copies, waits for them, and re-layouts  16.1 us (10%)
  matrix products  8.11 us (5%)
    ppermute x48, waiting for transfers between devices, move(): return lax.ppermute(x, axis, pairs)  48.1 us
    ppermute x48, starting transfers between devices, move(): return lax.ppermute(x, axis, pairs)  46.6 us
    pallas_call x5, Pallas kernels, attend_slots(): pl.pallas_call(functools.partial(slots_kernel, plan, own, [[index for _,...  20.8 us
    unnamed x40, local copies, waits for them, and re-layouts  8.52 us
    dot_general x5, matrix products, project(): jnp.dot(jnp.concatenate(pieces), w_out, preferred_element_type=jnp.float32)  8.11 us
    all_to_all x1, waiting for transfers between devices, local_ring(): lax.all_to_all(jnp.broadcast_to(facts[None], (ranks, width)), 'dp', split...  7.73 us
    all_to_all x1, starting transfers between devices, local_ring(): lax.all_to_all(jnp.broadcast_to(facts[None], (ranks, width)), 'dp', split...  6.28 us
    pallas_call x5, Pallas kernels, settle_step(): pl.pallas_call(functools.partial(settle_kernel, masks, per_head, groups,...  4.28 us
  transfers between devices with their start and end apart: 49, of which 18 were waited for; matrix products, arithmetic and copies ran while one was open for 10% of the time, Pallas kernels for 16%

profile of v8, /device:TPU:0, one launch (start us, length us, event | category | flops | bytes accessed | tf_op | source)
XLA Modules:
  0.0 165.2 jit_solution(4768220499304017175)
XLA Ops:
  1.1 3.1 %collective-permute-start = (bf16[4,144,512]{2,1,0:T(8,128)(2,1)S(1)}, bf16[4,144,512]{2,1,0:T(8,128)(2,1)S(1)}, u32[]{:S(2)}, u32[]{:S(2)}) collective-permute-start(bf16[4,144,512]{2,1,0:T(8,128)(2,1)S(1)} %payload.1), channel_id=1, source_target_pairs={{0,8},{8,16},{16,24},{24,28},{28,20},{20,12},{12,4},{4,0},{1,9},{9... | collective-permute-start | bytes 1769480 | tf_op jit(solution)/shard_map/ppermute | solution.py:633
  5.5 6.3 %all-to-all-start = ((s32[8,1,32]{2,1,0:T(1,128)}), s32[8,1,32]{2,1,0:T(1,128)S(1)}, u32[]{:S(2)}, u32[]{:S(2)}) async-start(s32[8,1,32]{2,1,0:T(1,128)} %broadcast_in_dim.2), calls=%async_computation | async-start | bytes 8192 | tf_op jit(solution)/shard_map/all_to_all | solution.py:640
  13.3 7.7 %all-to-all-done = s32[8,1,32]{2,1,0:T(1,128)S(1)} async-done(((s32[8,1,32]{2,1,0:T(1,128)}), s32[8,1,32]{2,1,0:T(1,128)S(1)}, u32[]{:S(2)}, u32[]{:S(2)}) %all-to-all-start) | async-done | bytes 1056 | tf_op jit(solution)/shard_map/all_to_all | solution.py:640
  26.9 5.5 %collective-permute-done.2.fore = bf16[368,512]{1,0:T(8,128)(2,1)S(1)} collective-permute-done((bf16[368,512]{1,0:T(8,128)(2,1)S(1)}, bf16[368,512]{1,0:T(8,128)(2,1)S(1)}, u32[]{:S(2)}, u32[]{:S(2)}) %collective-permute-start.2) | collective-permute-done | bytes 376864 | tf_op jit(solution)/shard_map/ppermute | solution.py:633
  36.2 2.8 %collective-permute-done.14.back = bf16[208,512]{1,0:T(8,128)(2,1)S(1)} collective-permute-done((bf16[208,512]{1,0:T(8,128)(2,1)S(1)}, bf16[208,512]{1,0:T(8,128)(2,1)S(1)}, u32[]{:S(2)}, u32[]{:S(2)}) %collective-permute-start.14) | collective-permute-done | bytes 213024 | tf_op jit(solution)/shard_map/ppermute | solution.py:633
  43.0 2.1 %collective-permute-done.19.back = bf16[64,512]{1,0:T(8,128)(2,1)S(1)} collective-permute-done((bf16[64,512]{1,0:T(8,128)(2,1)S(1)}, bf16[64,512]{1,0:T(8,128)(2,1)S(1)}, u32[]{:S(2)}, u32[]{:S(2)}) %collective-permute-start.19) | collective-permute-done | bytes 65568 | tf_op jit(solution)/shard_map/ppermute | solution.py:633
  45.9 3.6 %collective-permute-done.18.fore = bf16[80,512]{1,0:T(8,128)(2,1)S(1)} collective-permute-done((bf16[80,512]{1,0:T(8,128)(2,1)S(1)}, bf16[80,512]{1,0:T(8,128)(2,1)S(1)}, u32[]{:S(2)}, u32[]{:S(2)}) %collective-permute-start.18) | collective-permute-done | bytes 81952 | tf_op jit(solution)/shard_map/ppermute | solution.py:633
  54.4 4.1 %collective-permute-done.21.refs_9_ = bf16[1,144,512]{2,1,0:T(8,128)(2,1)} collective-permute-done((bf16[1,144,512]{2,1,0:T(8,128)(2,1)}, bf16[1,144,512]{2,1,0:T(8,128)(2,1)}, u32[]{:S(2)}, u32[]{:S(2)}) %collective-permute-start.21) | collective-permute-done | bytes 147488 | tf_op jit(solution)/shard_map/ppermute | solution.py:633
  58.6 4.2 %reshape.12.refs_0_ = bf16[8,384,512]{2,1,0:T(8,128)(2,1)S(1)} reshape(bf16[96,16384]{1,0:T(8,128)(2,1)} %param.11) | data formatting | bytes 6291456 | tf_op jit(solution)/shard_map/reshape | solution.py:645
  62.8 2.6 %reshape.13.refs_1_ = bf16[8,384,64]{2,1,0:T(8,128)(2,1)} reshape(bf16[96,2048]{1,0:T(8,128)(2,1)} %param.12) | data formatting | bytes 786432 | tf_op jit(solution)/shard_map/reshape | solution.py:646
  70.4 6.9 %attend_slots.5.refs_7_ = f32[36,4096]{1,0:T(8,128)S(1)} custom-call(s32[8,8]{1,0:T(8,128)} %plan.1.table, s32[8,1,32]{2,1,0:T(1,128)S(1)} %broadcast_maximum_fusion.info, bf16[8,384,512]{2,1,0:T(8,128)(2,1)S(1)} %reshape.12.refs_0_, bf16[8,384,64]{2,1,0:T(8,128)(2,1)S(1)} %copy-done.1, bf16[32,512,128]{2,1,0:T(8,128)(2,1)} %refs_2_.9, ...), custom_call_target="tpu_custom_call" | custom-call | tf_op jit(solution)/shard_map/attend_slots/pallas_call | solution.py:493
  77.4 2.8 %attend_slots.6 = bf16[48,4096]{1,0:T(8,128)(2,1)S(1)} custom-call(s32[8,8]{1,0:T(8,128)} %plan.1.table, s32[8,1,32]{2,1,0:T(1,128)S(1)} %broadcast_maximum_fusion.info, bf16[8,384,512]{2,1,0:T(8,128)(2,1)S(1)} %reshape.12.refs_0_, bf16[8,384,64]{2,1,0:T(8,128)(2,1)S(1)} %copy-done.1, bf16[32,512,128]{2,1,0:T(8,128)(2,1)S(1)} %copy-done, ...), custom_call_target="tpu_custom_call" | custom-call | tf_op jit(solution)/shard_map/attend_slots/pallas_call | solution.py:493
  81.7 2.8 %attend_slots.7.refs_11_ = f32[12,4096]{1,0:T(8,128)S(1)} custom-call(s32[8,8]{1,0:T(8,128)} %plan.1.table, s32[8,1,32]{2,1,0:T(1,128)S(1)} %broadcast_maximum_fusion.info, bf16[8,384,512]{2,1,0:T(8,128)(2,1)S(1)} %reshape.12.refs_0_, bf16[8,384,64]{2,1,0:T(8,128)(2,1)S(1)} %copy-done.1, bf16[32,512,128]{2,1,0:T(8,128)(2,1)S(1)} %copy-done, ...), custom_call_target="tpu_custom_call" | custom-call | tf_op jit(solution)/shard_map/attend_slots/pallas_call | solution.py:493
  85.3 3.0 %attend_slots.8.refs_12_ = f32[12,4096]{1,0:T(8,128)S(1)} custom-call(s32[8,8]{1,0:T(8,128)} %plan.1.table, s32[8,1,32]{2,1,0:T(1,128)S(1)} %broadcast_maximum_fusion.info, bf16[8,384,512]{2,1,0:T(8,128)(2,1)S(1)} %reshape.12.refs_0_, bf16[8,384,64]{2,1,0:T(8,128)(2,1)S(1)} %copy-done.1, bf16[32,512,128]{2,1,0:T(8,128)(2,1)S(1)} %copy-done, ...), custom_call_target="tpu_custom_call" | custom-call | tf_op jit(solution)/shard_map/attend_slots/pallas_call | solution.py:493
  88.3 5.3 %attend_slots.9 = bf16[48,4096]{1,0:T(8,128)(2,1)S(1)} custom-call(s32[8,8]{1,0:T(8,128)} %plan.1.table, s32[8,1,32]{2,1,0:T(1,128)S(1)} %broadcast_maximum_fusion.info, bf16[8,384,512]{2,1,0:T(8,128)(2,1)S(1)} %reshape.12.refs_0_, bf16[8,384,64]{2,1,0:T(8,128)(2,1)S(1)} %copy-done.2, bf16[32,512,128]{2,1,0:T(8,128)(2,1)} %refs_2_.9, ...), custom_call_target="tpu_custom_call" | custom-call | tf_op jit(solution)/shard_map/attend_slots/pallas_call | solution.py:493
  99.2 6.5 %collective-permute-done.30 = bf16[48,4096]{1,0:T(8,128)(2,1)S(1)} collective-permute-done((bf16[48,4096]{1,0:T(8,128)(2,1)S(1)}, bf16[48,4096]{1,0:T(8,128)(2,1)S(1)}, u32[]{:S(2)}, u32[]{:S(2)}) %collective-permute-start.30) | collective-permute-done | bytes 393248 | tf_op jit(solution)/shard_map/ppermute | solution.py:633
  111.2 6.0 %collective-permute-done.38.refs_3_ = bf16[96,896]{1,0:T(8,128)(2,1)S(1)} collective-permute-done((bf16[96,896]{1,0:T(8,128)(2,1)S(1)}, bf16[96,896]{1,0:T(8,128)(2,1)S(1)}, u32[]{:S(2)}, u32[]{:S(2)}) %collective-permute-start.38) | collective-permute-done | bytes 172064 | tf_op jit(solution)/shard_map/ppermute | solution.py:633
  117.2 2.0 %collective-permute-start.29 = (bf16[48,4096]{1,0:T(8,128)(2,1)S(1)}, bf16[48,4096]{1,0:T(8,128)(2,1)S(1)}, u32[]{:S(2)}, u32[]{:S(2)}) collective-permute-start(bf16[48,4096]{1,0:T(8,128)(2,1)S(1)} %collective-permute-done.28), channel_id=1, source_target_pairs={{8,0},{16,8},{24,16},{28,24},{20,28},{12,20},{4,12},{0,4},{9,1},{1... | collective-permute-start | bytes 1179656 | tf_op jit(solution)/shard_map/ppermute | solution.py:633
  124.1 4.1 %collective-permute-done.24 = bf16[48,4096]{1,0:T(8,128)(2,1)S(1)} collective-permute-done((bf16[48,4096]{1,0:T(8,128)(2,1)S(1)}, bf16[48,4096]{1,0:T(8,128)(2,1)S(1)}, u32[]{:S(2)}, u32[]{:S(2)}) %collective-permute-start.24) | collective-permute-done | bytes 393248 | tf_op jit(solution)/shard_map/ppermute | solution.py:633
  131.6 3.5 %collective-permute-done.12 = bf16[48,4096]{1,0:T(8,128)(2,1)S(1)} collective-permute-done((bf16[48,4096]{1,0:T(8,128)(2,1)S(1)}, bf16[48,4096]{1,0:T(8,128)(2,1)S(1)}, u32[]{:S(2)}, u32[]{:S(2)}) %collective-permute-start.12) | collective-permute-done | bytes 393248 | tf_op jit(solution)/shard_map/ppermute | solution.py:633
  135.1 2.5 %collective-permute-start.25 = (bf16[48,2048]{1,0:T(8,128)(2,1)S(1)}, bf16[48,2048]{1,0:T(8,128)(2,1)S(1)}, u32[]{:S(2)}, u32[]{:S(2)}) collective-permute-start(bf16[48,2048]{1,0:T(8,128)(2,1)S(1)} %get-tuple-element.37), channel_id=1, source_target_pairs={{0,8},{8,16},{16,24},{24,28},{28,20},{20,12},{12,4},{4,0},{1,9},{9... | collective-permute-start | bytes 589832 | tf_op jit(solution)/shard_map/ppermute | solution.py:633
  143.6 2.5 %collective-permute-start.44 = (bf16[48,2048]{1,0:T(8,128)(2,1)S(1)}, bf16[48,2048]{1,0:T(8,128)(2,1)S(1)}, u32[]{:S(2)}, u32[]{:S(2)}) collective-permute-start(bf16[48,2048]{1,0:T(8,128)(2,1)S(1)} %collective-permute-done.25), channel_id=1, source_target_pairs={{0,8},{8,16},{16,24},{24,28},{28,20},{20,12},{12,4},{4,0},{1,9},{9... | collective-permute-start | bytes 589832 | tf_op jit(solution)/shard_map/ppermute | solution.py:633
  154.2 4.4 %collective-permute-start.41 = (bf16[96,896]{1,0:T(8,128)(2,1)S(1)}, bf16[96,896]{1,0:T(8,128)(2,1)S(1)}, u32[]{:S(2)}, u32[]{:S(2)}) collective-permute-start(bf16[96,896]{1,0:T(8,128)(2,1)S(1)} %get-tuple-element.34), channel_id=1, source_target_pairs={{0,2},{1,3},{4,6},{5,7},{11,9},{9,11},{15,13},{13,15},{18,16},{16,... | collective-permute-start | bytes 516104 | tf_op jit(solution)/shard_map/ppermute | solution.py:633
  160.1 3.3 %collective-permute-done.41.refs_1_ = bf16[96,896]{1,0:T(8,128)(2,1)S(1)} collective-permute-done((bf16[96,896]{1,0:T(8,128)(2,1)S(1)}, bf16[96,896]{1,0:T(8,128)(2,1)S(1)}, u32[]{:S(2)}, u32[]{:S(2)}) %collective-permute-start.41) | collective-permute-done | bytes 172064 | tf_op jit(solution)/shard_map/ppermute | solution.py:633
  (151 shorter events, 66.9 us)
Async XLA Ops:
  1.1 20.0 %collective-permute-start = (bf16[4,144,512]{2,1,0:T(8,128)(2,1)S(1)}, bf16[4,144,512]{2,1,0:T(8,128)(2,1)S(1)}, u32[]{:S(2)}, u32[]{:S(2)}) collective-permute-start(bf16[4,144,512]{2,1,0:T(8,128)(2,1)S(1)} %payload.1), channel_id=1, source_target_pairs={{0,8},{8,16},{16,24},{24,28},{28,20},{20,12},{12,4},{4,0},{1,9},{9... | collective-permute-start | bytes 1769480 | tf_op jit(solution)/shard_map/ppermute | solution.py:633
  4.2 16.9 %collective-permute-start.1 = (bf16[4,144,512]{2,1,0:T(8,128)(2,1)S(1)}, bf16[4,144,512]{2,1,0:T(8,128)(2,1)S(1)}, u32[]{:S(2)}, u32[]{:S(2)}) collective-permute-start(bf16[4,144,512]{2,1,0:T(8,128)(2,1)S(1)} %payload.1), channel_id=1, source_target_pairs={{8,0},{16,8},{24,16},{28,24},{20,28},{12,20},{4,12},{0,4},{9,1},{1... | collective-permute-start | bytes 1769480 | tf_op jit(solution)/shard_map/ppermute | solution.py:633
  5.5 15.5 %all-to-all-start = ((s32[8,1,32]{2,1,0:T(1,128)}), s32[8,1,32]{2,1,0:T(1,128)S(1)}, u32[]{:S(2)}, u32[]{:S(2)}) async-start(s32[8,1,32]{2,1,0:T(1,128)} %broadcast_in_dim.2), calls=%async_computation | async-start | bytes 8192 | tf_op jit(solution)/shard_map/all_to_all | solution.py:640
  25.4 15.2 %collective-permute-start.8 = (bf16[2,144,512]{2,1,0:T(8,128)(2,1)S(1)}, bf16[2,144,512]{2,1,0:T(8,128)(2,1)S(1)}, u32[]{:S(2)}, u32[]{:S(2)}) collective-permute-start(bf16[2,144,512]{2,1,0:T(8,128)(2,1)S(1)} %get-tuple-element.23.refs_5_.refs_9_), channel_id=1, source_target_pairs={{0,2},{1,3},{2,0},{3,1},{4,6},{5,7},{6,4},{7,5},{8,10},{9,11},{10,... | collective-permute-start | bytes 884744 | tf_op jit(solution)/shard_map/ppermute | solution.py:633
  34.6 11.3 %collective-permute-start.5 = (bf16[2,144,512]{2,1,0:T(8,128)(2,1)S(1)}, bf16[2,144,512]{2,1,0:T(8,128)(2,1)}, u32[]{:S(2)}, u32[]{:S(2)}) collective-permute-start(bf16[2,144,512]{2,1,0:T(8,128)(2,1)S(1)} %join.3.refs_3_), channel_id=1, source_target_pairs={{0,2},{1,3},{2,0},{3,1},{4,6},{5,7},{6,4},{7,5},{8,10},{9,11},{10,... | collective-permute-start | bytes 884744 | tf_op jit(solution)/shard_map/ppermute | solution.py:633
  39.0 11.5 %collective-permute-start.16 = (bf16[2,144,512]{2,1,0:T(8,128)(2,1)S(1)}, bf16[2,144,512]{2,1,0:T(8,128)(2,1)}, u32[]{:S(2)}, u32[]{:S(2)}) collective-permute-start(bf16[2,144,512]{2,1,0:T(8,128)(2,1)S(1)} %join.4.refs_3_), channel_id=1, source_target_pairs={{0,2},{1,3},{2,0},{3,1},{4,6},{5,7},{6,4},{7,5},{8,10},{9,11},{10,... | collective-permute-start | bytes 884744 | tf_op jit(solution)/shard_map/ppermute | solution.py:633
  45.9 31.4 %collective-permute-start.6 = (bf16[2,144,512]{2,1,0:T(8,128)(2,1)}, bf16[2,144,512]{2,1,0:T(8,128)(2,1)}, u32[]{:S(2)}, u32[]{:S(2)}) collective-permute-start(bf16[2,144,512]{2,1,0:T(8,128)(2,1)} %collective-permute-done.5.refs_5_), channel_id=1, source_target_pairs={{0,1},{1,0},{2,3},{3,2},{4,5},{5,4},{6,7},{7,6},{8,9},{9,8},{10,11... | collective-permute-start | bytes 884744 | tf_op jit(solution)/shard_map/ppermute | solution.py:633
  49.5 34.9 %collective-permute-start.15 = (bf16[2,144,512]{2,1,0:T(8,128)(2,1)S(1)}, bf16[2,144,512]{2,1,0:T(8,128)(2,1)}, u32[]{:S(2)}, u32[]{:S(2)}) collective-permute-start(bf16[2,144,512]{2,1,0:T(8,128)(2,1)S(1)} %join.4.refs_3_), channel_id=1, source_target_pairs={{0,1},{1,0},{2,3},{3,2},{4,5},{5,4},{6,7},{7,6},{8,9},{9,8},{10,11... | collective-permute-start | bytes 884744 | tf_op jit(solution)/shard_map/ppermute | solution.py:633
  50.5 34.8 %collective-permute-start.17 = (bf16[2,144,512]{2,1,0:T(8,128)(2,1)}, bf16[2,144,512]{2,1,0:T(8,128)(2,1)}, u32[]{:S(2)}, u32[]{:S(2)}) collective-permute-start(bf16[2,144,512]{2,1,0:T(8,128)(2,1)} %collective-permute-done.16.refs_5_), channel_id=1, source_target_pairs={{0,1},{1,0},{2,3},{3,2},{4,5},{5,4},{6,7},{7,6},{8,9},{9,8},{10,11... | collective-permute-start | bytes 884744 | tf_op jit(solution)/shard_map/ppermute | solution.py:633
  54.2 34.1 %collective-permute-start.20 = (bf16[1,144,512]{2,1,0:T(8,128)(2,1)}, bf16[1,144,512]{2,1,0:T(8,128)(2,1)}, u32[]{:S(2)}, u32[]{:S(2)}) collective-permute-start(bf16[1,144,512]{2,1,0:T(8,128)(2,1)} %join.5.refs_7_), channel_id=1, source_target_pairs={{0,1},{1,0},{2,3},{3,2},{4,5},{5,4},{6,7},{7,6},{8,9},{9,8},{10,11... | collective-permute-start | bytes 442376 | tf_op jit(solution)/shard_map/ppermute | solution.py:633
  58.5 29.8 %collective-permute-start.22 = (bf16[1,144,512]{2,1,0:T(8,128)(2,1)}, bf16[1,144,512]{2,1,0:T(8,128)(2,1)}, u32[]{:S(2)}, u32[]{:S(2)}) collective-permute-start(bf16[1,144,512]{2,1,0:T(8,128)(2,1)} %collective-permute-done.21.refs_9_), channel_id=1, source_target_pairs={{0,1},{1,0},{2,3},{3,2},{4,5},{5,4},{6,7},{7,6},{8,9},{9,8},{10,11... | collective-permute-start | bytes 442376 | tf_op jit(solution)/shard_map/ppermute | solution.py:633
  80.2 16.9 %collective-permute-start.27 = (bf16[48,4096]{1,0:T(8,128)(2,1)S(1)}, bf16[48,4096]{1,0:T(8,128)(2,1)S(1)}, u32[]{:S(2)}, u32[]{:S(2)}) collective-permute-start(bf16[48,4096]{1,0:T(8,128)(2,1)S(1)} %attend_slots.6), channel_id=1, source_target_pairs={{8,0},{16,8},{24,16},{28,24},{20,28},{12,20},{4,12},{0,4},{9,1},{1... | collective-permute-start | bytes 1179656 | tf_op jit(solution)/shard_map/ppermute | solution.py:633
  84.5 14.2 %collective-permute-start.10 = (bf16[48,4096]{1,0:T(8,128)(2,1)S(1)}, bf16[48,4096]{1,0:T(8,128)(2,1)S(1)}, u32[]{:S(2)}, u32[]{:S(2)}) collective-permute-start(bf16[48,4096]{1,0:T(8,128)(2,1)S(1)} %attend_slots.6), channel_id=1, source_target_pairs={{0,8},{8,16},{16,24},{24,28},{28,20},{20,12},{12,4},{4,0},{1,9},{9... | collective-permute-start | bytes 1179656 | tf_op jit(solution)/shard_map/ppermute | solution.py:633
  93.7 12.0 %collective-permute-start.30 = (bf16[48,4096]{1,0:T(8,128)(2,1)S(1)}, bf16[48,4096]{1,0:T(8,128)(2,1)S(1)}, u32[]{:S(2)}, u32[]{:S(2)}) collective-permute-start(bf16[48,4096]{1,0:T(8,128)(2,1)S(1)} %attend_slots.9), channel_id=1, source_target_pairs={{8,0},{16,8},{24,16},{28,24},{20,28},{12,20},{4,12},{0,4},{9,1},{1... | collective-permute-start | bytes 1179656 | tf_op jit(solution)/shard_map/ppermute | solution.py:633
  95.2 12.0 %collective-permute-start.23 = (bf16[48,4096]{1,0:T(8,128)(2,1)S(1)}, bf16[48,4096]{1,0:T(8,128)(2,1)S(1)}, u32[]{:S(2)}, u32[]{:S(2)}) collective-permute-start(bf16[48,4096]{1,0:T(8,128)(2,1)S(1)} %attend_slots.9), channel_id=1, source_target_pairs={{0,8},{8,16},{16,24},{24,28},{28,20},{20,12},{12,4},{4,0},{1,9},{9... | collective-permute-start | bytes 1179656 | tf_op jit(solution)/shard_map/ppermute | solution.py:633
  97.0 12.1 %collective-permute-start.37 = (bf16[96,896]{1,0:T(8,128)(2,1)S(1)}, bf16[96,896]{1,0:T(8,128)(2,1)S(1)}, u32[]{:S(2)}, u32[]{:S(2)}) collective-permute-start(bf16[96,896]{1,0:T(8,128)(2,1)S(1)} %convolution_convert_fusion.1.refs_0_), channel_id=1, source_target_pairs={{0,1},{1,0},{2,3},{3,2},{4,5},{5,4},{6,7},{7,6},{8,9},{9,8},{10,11... | collective-permute-start | bytes 516104 | tf_op jit(solution)/shard_map/ppermute | solution.py:633
  97.1 20.1 %collective-permute-start.28 = (bf16[48,4096]{1,0:T(8,128)(2,1)S(1)}, bf16[48,4096]{1,0:T(8,128)(2,1)S(1)}, u32[]{:S(2)}, u32[]{:S(2)}) collective-permute-start(bf16[48,4096]{1,0:T(8,128)(2,1)S(1)} %collective-permute-done.27), channel_id=1, source_target_pairs={{8,0},{16,8},{24,16},{28,24},{20,28},{12,20},{4,12},{0,4},{9,1},{1... | collective-permute-start | bytes 1179656 | tf_op jit(solution)/shard_map/ppermute | solution.py:633
  98.6 20.6 %collective-permute-start.11 = (bf16[48,4096]{1,0:T(8,128)(2,1)S(1)}, bf16[48,4096]{1,0:T(8,128)(2,1)S(1)}, u32[]{:S(2)}, u32[]{:S(2)}) collective-permute-start(bf16[48,4096]{1,0:T(8,128)(2,1)S(1)} %collective-permute-done.10), channel_id=1, source_target_pairs={{0,8},{8,16},{16,24},{24,28},{28,20},{20,12},{12,4},{4,0},{1,9},{9... | collective-permute-start | bytes 1179656 | tf_op jit(solution)/shard_map/ppermute | solution.py:633
  105.7 16.9 %collective-permute-start.31 = (bf16[48,4096]{1,0:T(8,128)(2,1)S(1)}, bf16[48,4096]{1,0:T(8,128)(2,1)S(1)}, u32[]{:S(2)}, u32[]{:S(2)}) collective-permute-start(bf16[48,4096]{1,0:T(8,128)(2,1)S(1)} %collective-permute-done.30), channel_id=1, source_target_pairs={{8,0},{16,8},{24,16},{28,24},{20,28},{12,20},{4,12},{0,4},{9,1},{1... | collective-permute-start | bytes 1179656 | tf_op jit(solution)/shard_map/ppermute | solution.py:633
  117.2 13.8 %collective-permute-start.29 = (bf16[48,4096]{1,0:T(8,128)(2,1)S(1)}, bf16[48,4096]{1,0:T(8,128)(2,1)S(1)}, u32[]{:S(2)}, u32[]{:S(2)}) collective-permute-start(bf16[48,4096]{1,0:T(8,128)(2,1)S(1)} %collective-permute-done.28), channel_id=1, source_target_pairs={{8,0},{16,8},{24,16},{28,24},{20,28},{12,20},{4,12},{0,4},{9,1},{1... | collective-permute-start | bytes 1179656 | tf_op jit(solution)/shard_map/ppermute | solution.py:633
  119.2 15.9 %collective-permute-start.12 = (bf16[48,4096]{1,0:T(8,128)(2,1)S(1)}, bf16[48,4096]{1,0:T(8,128)(2,1)S(1)}, u32[]{:S(2)}, u32[]{:S(2)}) collective-permute-start(bf16[48,4096]{1,0:T(8,128)(2,1)S(1)} %collective-permute-done.11), channel_id=1, source_target_pairs={{0,8},{8,16},{16,24},{24,28},{28,20},{20,12},{12,4},{4,0},{1,9},{9... | collective-permute-start | bytes 1179656 | tf_op jit(solution)/shard_map/ppermute | solution.py:633
  120.2 19.4 %collective-permute-start.39 = (bf16[96,896]{1,0:T(8,128)(2,1)S(1)}, bf16[96,896]{1,0:T(8,128)(2,1)S(1)}, u32[]{:S(2)}, u32[]{:S(2)}) collective-permute-start(bf16[96,896]{1,0:T(8,128)(2,1)S(1)} %get-tuple-element.27), channel_id=1, source_target_pairs={{2,0},{3,1},{6,4},{7,5},{10,8},{8,10},{14,12},{12,14},{19,17},{17,... | collective-permute-start | bytes 516104 | tf_op jit(solution)/shard_map/ppermute | solution.py:633
  122.6 17.0 %collective-permute-start.33 = (bf16[48,2048]{1,0:T(8,128)(2,1)S(1)}, bf16[48,2048]{1,0:T(8,128)(2,1)S(1)}, u32[]{:S(2)}, u32[]{:S(2)}) collective-permute-start(bf16[48,2048]{1,0:T(8,128)(2,1)S(1)} %get-tuple-element.40), channel_id=1, source_target_pairs={{8,0},{16,8},{24,16},{28,24},{20,28},{12,20},{4,12},{0,4},{9,1},{1... | collective-permute-start | bytes 589832 | tf_op jit(solution)/shard_map/ppermute | solution.py:633
  128.2 11.7 %collective-permute-start.32 = (bf16[48,2048]{1,0:T(8,128)(2,1)S(1)}, bf16[48,2048]{1,0:T(8,128)(2,1)S(1)}, u32[]{:S(2)}, u32[]{:S(2)}) collective-permute-start(bf16[48,2048]{1,0:T(8,128)(2,1)S(1)} %get-tuple-element.39), channel_id=1, source_target_pairs={{8,0},{16,8},{24,16},{28,24},{20,28},{12,20},{4,12},{0,4},{9,1},{1... | collective-permute-start | bytes 589832 | tf_op jit(solution)/shard_map/ppermute | solution.py:633
  (45 other events, 339.5 us)

commit v9 on v8

--- a/solution.py
+++ b/solution.py
@@ -239,7 +239,7 @@
 def chunk_plans(ranks):
     middle = ranks // 2
     return {
-        "p": [list(range(middle - 1)), [middle - 1]],
+        "p": [[0], list(range(1, middle - 1)), [middle - 1]],
         "s": [[c] for c in range(middle, ranks - 2)] + [[ranks - 2, ranks - 1]],
     }
 
@@ -377,12 +377,12 @@
     )(fore, back)
 
 
-def slots_kernel(plan, own, indices, bundles, final, scale, table, info, *refs):
-    count, heads = len(plan), len(indices[0])
+def slots_kernel(plan, own, heads, indices, bundles, final, scale, table, info, *refs):
+    count = len(plan)
     refs = list(refs)
     q_ref, qr_ref, w_hbm = refs.pop(0), refs.pop(0), refs.pop(0)
-    w_ref = w_hbm
-    if count > 1:
+    w_ref, fetch = w_hbm, own or count > 1
+    if fetch:
         w_ref, w_sem = refs.pop(-2), refs.pop(-1)
         w_copy = pltpu.make_async_copy(w_hbm, w_ref, w_sem)
         w_copy.start()
@@ -441,7 +441,7 @@
         return 0
 
     lax.fori_loop(0, count, bundle, 0)
-    if count > 1:
+    if fetch:
         w_copy.wait()
     local_heads, _, value_width = w_ref.shape
     n = mixed.shape[1] // local_heads
@@ -462,18 +462,17 @@
         out_ref[...] = into[...].astype(out_ref.dtype)
 
 
-def attend_slots(plan, table, info, q, qr, full, parts, bundles, w_uv, earlier=None):
+def attend_slots(plan, table, info, q, qr, full, parts, heads, positions, bundles, w_uv, earlier=None):
     own = 1 if full is not None else 0
     final = earlier is not None
     earlier = list(earlier or ())
-    count, heads = len(plan), len(parts[0])
+    count = len(plan)
     _, q_rows, wide = q.shape
     dims = qr.shape[2]
-    positions = (parts[0][0][0].shape[1] - dims // heads) * heads
     local_heads, _, value_width = w_uv.shape
     vmem = pl.BlockSpec(memory_space=pltpu.MemorySpace.VMEM)
     smem = pl.BlockSpec(memory_space=pltpu.MemorySpace.SMEM)
-    fetch = count > 1
+    fetch = own or count > 1
     args = [q, qr, in_hbm(w_uv) if fetch else w_uv]
     in_specs = [vmem, vmem, pl.BlockSpec(memory_space=pl.ANY) if fetch else vmem]
     if own:
@@ -492,8 +491,8 @@
         scratch += [pltpu.VMEM(w_uv.shape, w_uv.dtype), pltpu.SemaphoreType.DMA]
     return pl.pallas_call(
         functools.partial(
-            slots_kernel, plan, own, [[index for _, index in slot] for slot in parts], bundles,
-            final, 1.0 / math.sqrt(VD + ROPE),
+            slots_kernel, plan, own, heads, [[index for _, index in slot] for slot in parts],
+            bundles, final, 1.0 / math.sqrt(VD + ROPE),
         ),
         out_shape=jax.ShapeDtypeStruct(out_shape, jnp.bfloat16 if final else jnp.float32),
         in_specs=[smem] * 2 + in_specs,
@@ -574,12 +573,16 @@
 
 
 def finish_kernel(per_head, steps, roll, table, info, seen, before, *refs):
-    *refs, out, total = refs
+    *refs, out = refs
     each = len(refs) // len(steps)
-    for i, columns in enumerate(steps):
+    parts = []
+    for i in range(len(steps)):
         own, *got = refs[each * i : each * (i + 1)]
-        add_in(table, per_head, columns, own, got, total if i else before, total)
-    n = total.shape[1]
+        part = own[...]
+        for g in got:
+            part = part + g[...].astype(jnp.float32)
+        parts.append(part)
+    n = before.shape[1]
     slots = n // roll
     to = lax.broadcasted_iota(jnp.int32, (n, n), 0)
     source = lax.broadcasted_iota(jnp.int32, (n, n), 1)
@@ -593,7 +596,13 @@
             inside = (to >= b * roll) & (to < (b + 1) * roll)
             wanted = jnp.where(inside, to + (place - b) * roll, wanted)
         pick = jnp.where(wanted == source, 1.0, 0.0).astype(jnp.bfloat16)
-        moved = jnp.dot(pick, total[y].astype(jnp.bfloat16), preferred_element_type=jnp.float32)
+        total = before[y]
+        for columns, part in zip(steps, parts):
+            hit = table[OWNER, columns[0]] == rank
+            for c in columns[1:]:
+                hit = hit | (table[OWNER, c] == rank)
+            total = total + jnp.where(hit, part, 0.0)
+        moved = jnp.dot(pick, total.astype(jnp.bfloat16), preferred_element_type=jnp.float32)
         out[pl.ds(y * n, n), :] = moved.astype(out.dtype)
 
 
@@ -608,7 +617,6 @@
         out_shape=jax.ShapeDtypeStruct((per_head * n, wide), jnp.bfloat16),
         in_specs=[smem] * 3 + [vmem] * (1 + len(args)),
         out_specs=vmem,
-        scratch_shapes=[pltpu.VMEM((per_head, n, wide), jnp.float32)],
         compiler_params=pltpu.CompilerParams(vmem_limit_bytes=6 * 2**20),
         name="finish",
     )(table, info, seen, total, *args)
@@ -634,11 +642,9 @@
 
     payload = payload_of(cache_latent, cache_rope, heads)
     fore, back = move(payload, ahead), move(payload, behind)
-    facts = jnp.concatenate([owner_rank, owner_pick, lengths])
-    width = 32
-    facts = jnp.pad(facts, (0, width - facts.shape[0]))
+    facts = [jnp.broadcast_to(x[None], (ranks, x.shape[0])) for x in (owner_rank, owner_pick, lengths)]
     info = lax.all_to_all(
-        jnp.broadcast_to(facts[None], (ranks, width)), "dp", split_axis=0, concat_axis=0, tiled=True
+        jnp.concatenate(facts, axis=1), "dp", split_axis=0, concat_axis=0, tiled=True
     )
     info = jnp.maximum(info, 0)[:, None]
     table = in_hbm(plan_of(seen, owner_rank, owner_pick, loads, per_head))
@@ -673,7 +679,7 @@
     def attend(plan, full=None, earlier=None):
         return attend_slots(
             plan, table, info, q, qr, full, [groups[c] for c in plan[(full is not None) :]],
-            bundles, w_uv, earlier,
+            heads, cache_latent.shape[1], bundles, w_uv, earlier,
         )
 
     chunks = []

time: 166 us -> 165 us (level)
  local copies, waits for them, and re-layouts: 16.1 us -> 11.4 us
  Pallas kernels: 31 us -> 34.5 us
  waiting for transfers between devices: 55.9 us -> 57.7 us
    unnamed x40 -> x42, local copies, waits for them, and re-layouts: 8.52 us -> 4.72 us
    pallas_call x5 -> x6, Pallas kernels: 20.8 us -> 24.2 us  [attend_slots(): pl.pallas_call(functools.partial(slots_kernel, plan, own, heads, [[index...]
  transfers between devices with their start and end apart: 49 -> 49, of which waited for: 18 -> 18; matrix products, arithmetic and copies ran while one was open for 10% -> 9% of each run, Pallas kernels for 16% -> 19%
where the time goes in v9:
time: 165 us; the launch traced here: 164 us
  waiting for transfers between devices  57.7 us (35%)
  starting transfers between devices  51.2 us (31%)
  Pallas kernels  34.5 us (21%)
  local copies, waits for them, and re-layouts  11.4 us (7%)
  matrix products  8.13 us (5%)
    ppermute x48, waiting for transfers between devices, move(): return lax.ppermute(x, axis, pairs)  49 us
    ppermute x48, starting transfers between devices, move(): return lax.ppermute(x, axis, pairs)  45 us
    pallas_call x6, Pallas kernels, attend_slots(): pl.pallas_call(functools.partial(slots_kernel, plan, own, heads, [[index...  24.2 us
    all_to_all x1, waiting for transfers between devices, local_ring(): lax.all_to_all(jnp.concatenate(facts, axis=1), 'dp', split_axis=0, concat...  8.7 us
    dot_general x5, matrix products, project(): jnp.dot(jnp.concatenate(pieces), w_out, preferred_element_type=jnp.float32)  8.13 us
    all_to_all x1, starting transfers between devices, local_ring(): lax.all_to_all(jnp.concatenate(facts, axis=1), 'dp', split_axis=0, concat...  6.22 us
    unnamed x42, local copies, waits for them, and re-layouts  4.72 us
    pallas_call x5, Pallas kernels, settle_step(): pl.pallas_call(functools.partial(settle_kernel, masks, per_head, groups,...  4.26 us
  transfers between devices with their start and end apart: 49, of which 18 were waited for; matrix products, arithmetic and copies ran while one was open for 9% of the time, Pallas kernels for 19%

profile of v9, /device:TPU:0, one launch (start us, length us, event | category | flops | bytes accessed | tf_op | source)
XLA Modules:
  0.0 164.2 jit_solution(1720430851340950063)
XLA Ops:
  1.1 3.0 %collective-permute-start.1 = (bf16[4,144,512]{2,1,0:T(8,128)(2,1)S(1)}, bf16[4,144,512]{2,1,0:T(8,128)(2,1)S(1)}, u32[]{:S(2)}, u32[]{:S(2)}) collective-permute-start(bf16[4,144,512]{2,1,0:T(8,128)(2,1)S(1)} %payload.1), channel_id=1, source_target_pairs={{8,0},{16,8},{24,16},{28,24},{20,28},{12,20},{4,12},{0,4},{9,1},{1... | collective-permute-start | bytes 1769480 | tf_op jit(solution)/shard_map/ppermute | solution.py:641
  5.7 6.2 %all-to-all-start = ((s32[8,1,20]{2,1,0:T(1,128)}), s32[8,1,20]{2,1,0:T(1,128)S(1)}, u32[]{:S(2)}, u32[]{:S(2)}) async-start(s32[8,1,20]{2,1,0:T(1,128)} %bitcast), calls=%async_computation | async-start | bytes 8192 | tf_op jit(solution)/shard_map/all_to_all | solution.py:646
  13.4 8.7 %all-to-all-done = s32[8,1,20]{2,1,0:T(1,128)S(1)} async-done(((s32[8,1,20]{2,1,0:T(1,128)}), s32[8,1,20]{2,1,0:T(1,128)S(1)}, u32[]{:S(2)}, u32[]{:S(2)}) %all-to-all-start) | async-done | bytes 672 | tf_op jit(solution)/shard_map/all_to_all | solution.py:646
  27.9 5.6 %collective-permute-done.2.fore = bf16[368,512]{1,0:T(8,128)(2,1)S(1)} collective-permute-done((bf16[368,512]{1,0:T(8,128)(2,1)S(1)}, bf16[368,512]{1,0:T(8,128)(2,1)S(1)}, u32[]{:S(2)}, u32[]{:S(2)}) %collective-permute-start.2) | collective-permute-done | bytes 376864 | tf_op jit(solution)/shard_map/ppermute | solution.py:641
  37.2 2.7 %collective-permute-done.14.back = bf16[208,512]{1,0:T(8,128)(2,1)S(1)} collective-permute-done((bf16[208,512]{1,0:T(8,128)(2,1)S(1)}, bf16[208,512]{1,0:T(8,128)(2,1)S(1)}, u32[]{:S(2)}, u32[]{:S(2)}) %collective-permute-start.14) | collective-permute-done | bytes 213024 | tf_op jit(solution)/shard_map/ppermute | solution.py:641
  46.7 3.8 %collective-permute-done.18.fore = bf16[80,512]{1,0:T(8,128)(2,1)S(1)} collective-permute-done((bf16[80,512]{1,0:T(8,128)(2,1)S(1)}, bf16[80,512]{1,0:T(8,128)(2,1)S(1)}, u32[]{:S(2)}, u32[]{:S(2)}) %collective-permute-start.18) | collective-permute-done | bytes 81952 | tf_op jit(solution)/shard_map/ppermute | solution.py:641
  55.4 4.1 %collective-permute-done.21.refs_9_ = bf16[1,144,512]{2,1,0:T(8,128)(2,1)} collective-permute-done((bf16[1,144,512]{2,1,0:T(8,128)(2,1)}, bf16[1,144,512]{2,1,0:T(8,128)(2,1)}, u32[]{:S(2)}, u32[]{:S(2)}) %collective-permute-start.21) | collective-permute-done | bytes 147488 | tf_op jit(solution)/shard_map/ppermute | solution.py:641
  61.3 4.2 %reshape.11.refs_0_ = bf16[8,384,512]{2,1,0:T(8,128)(2,1)S(1)} reshape(bf16[96,16384]{1,0:T(8,128)(2,1)} %param.11) | data formatting | bytes 6291456 | tf_op jit(solution)/shard_map/reshape | solution.py:651
  66.6 5.1 %attend_slots.6.refs_7_ = f32[12,4096]{1,0:T(8,128)S(1)} custom-call(s32[8,8]{1,0:T(8,128)} %plan.1.table, s32[8,1,20]{2,1,0:T(1,128)S(1)} %broadcast_maximum_fusion.info, bf16[8,384,512]{2,1,0:T(8,128)(2,1)S(1)} %reshape.11.refs_0_, bf16[8,384,64]{2,1,0:T(8,128)(2,1)S(1)} %copy-done.1, bf16[32,512,128]{2,1,0:T(8,128)(2,1)} %refs_2_.11, ...), custom_call_target="tpu_custom_call" | custom-call | tf_op jit(solution)/shard_map/attend_slots/pallas_call | solution.py:492
  71.8 5.0 %attend_slots.7.refs_8_ = f32[24,4096]{1,0:T(8,128)S(1)} custom-call(s32[8,8]{1,0:T(8,128)} %plan.1.table, s32[8,1,20]{2,1,0:T(1,128)S(1)} %broadcast_maximum_fusion.info, bf16[8,384,512]{2,1,0:T(8,128)(2,1)S(1)} %reshape.11.refs_0_, bf16[8,384,64]{2,1,0:T(8,128)(2,1)S(1)} %copy-done.2, bf16[32,512,128]{2,1,0:T(8,128)(2,1)} %refs_2_.11, ...), custom_call_target="tpu_custom_call" | custom-call | tf_op jit(solution)/shard_map/attend_slots/pallas_call | solution.py:492
  76.9 2.9 %attend_slots.8 = bf16[48,4096]{1,0:T(8,128)(2,1)S(1)} custom-call(s32[8,8]{1,0:T(8,128)} %plan.1.table, s32[8,1,20]{2,1,0:T(1,128)S(1)} %broadcast_maximum_fusion.info, bf16[8,384,512]{2,1,0:T(8,128)(2,1)S(1)} %reshape.11.refs_0_, bf16[8,384,64]{2,1,0:T(8,128)(2,1)S(1)} %copy-done.2, bf16[32,512,128]{2,1,0:T(8,128)(2,1)S(1)} %copy-done, ...), custom_call_target="tpu_custom_call" | custom-call | tf_op jit(solution)/shard_map/attend_slots/pallas_call | solution.py:492
  80.3 2.7 %attend_slots.9.refs_11_ = f32[12,4096]{1,0:T(8,128)S(1)} custom-call(s32[8,8]{1,0:T(8,128)} %plan.1.table, s32[8,1,20]{2,1,0:T(1,128)S(1)} %broadcast_maximum_fusion.info, bf16[8,384,512]{2,1,0:T(8,128)(2,1)S(1)} %reshape.11.refs_0_, bf16[8,384,64]{2,1,0:T(8,128)(2,1)S(1)} %copy-done.2, bf16[32,512,128]{2,1,0:T(8,128)(2,1)S(1)} %copy-done, ...), custom_call_target="tpu_custom_call" | custom-call | tf_op jit(solution)/shard_map/attend_slots/pallas_call | solution.py:492
  84.8 3.0 %attend_slots.10.refs_12_ = f32[12,4096]{1,0:T(8,128)S(1)} custom-call(s32[8,8]{1,0:T(8,128)} %plan.1.table, s32[8,1,20]{2,1,0:T(1,128)S(1)} %broadcast_maximum_fusion.info, bf16[8,384,512]{2,1,0:T(8,128)(2,1)S(1)} %reshape.11.refs_0_, bf16[8,384,64]{2,1,0:T(8,128)(2,1)S(1)} %copy-done.2, bf16[32,512,128]{2,1,0:T(8,128)(2,1)S(1)} %copy-done, ...), custom_call_target="tpu_custom_call" | custom-call | tf_op jit(solution)/shard_map/attend_slots/pallas_call | solution.py:492
  87.9 5.6 %attend_slots.11 = bf16[48,4096]{1,0:T(8,128)(2,1)S(1)} custom-call(s32[8,8]{1,0:T(8,128)} %plan.1.table, s32[8,1,20]{2,1,0:T(1,128)S(1)} %broadcast_maximum_fusion.info, bf16[8,384,512]{2,1,0:T(8,128)(2,1)S(1)} %reshape.11.refs_0_, bf16[8,384,64]{2,1,0:T(8,128)(2,1)S(1)} %copy-done.2, bf16[32,512,128]{2,1,0:T(8,128)(2,1)} %refs_2_.11, ...), custom_call_target="tpu_custom_call" | custom-call | tf_op jit(solution)/shard_map/attend_slots/pallas_call | solution.py:492
  99.0 6.5 %collective-permute-done.30 = bf16[48,4096]{1,0:T(8,128)(2,1)S(1)} collective-permute-done((bf16[48,4096]{1,0:T(8,128)(2,1)S(1)}, bf16[48,4096]{1,0:T(8,128)(2,1)S(1)}, u32[]{:S(2)}, u32[]{:S(2)}) %collective-permute-start.30) | collective-permute-done | bytes 393248 | tf_op jit(solution)/shard_map/ppermute | solution.py:641
  110.0 6.0 %collective-permute-done.38.refs_3_ = bf16[96,896]{1,0:T(8,128)(2,1)S(1)} collective-permute-done((bf16[96,896]{1,0:T(8,128)(2,1)S(1)}, bf16[96,896]{1,0:T(8,128)(2,1)S(1)}, u32[]{:S(2)}, u32[]{:S(2)}) %collective-permute-start.38) | collective-permute-done | bytes 172064 | tf_op jit(solution)/shard_map/ppermute | solution.py:641
  116.1 2.0 %collective-permute-start.29 = (bf16[48,4096]{1,0:T(8,128)(2,1)S(1)}, bf16[48,4096]{1,0:T(8,128)(2,1)S(1)}, u32[]{:S(2)}, u32[]{:S(2)}) collective-permute-start(bf16[48,4096]{1,0:T(8,128)(2,1)S(1)} %collective-permute-done.28), channel_id=1, source_target_pairs={{8,0},{16,8},{24,16},{28,24},{20,28},{12,20},{4,12},{0,4},{9,1},{1... | collective-permute-start | bytes 1179656 | tf_op jit(solution)/shard_map/ppermute | solution.py:641
  122.9 5.0 %collective-permute-done.24 = bf16[48,4096]{1,0:T(8,128)(2,1)S(1)} collective-permute-done((bf16[48,4096]{1,0:T(8,128)(2,1)S(1)}, bf16[48,4096]{1,0:T(8,128)(2,1)S(1)}, u32[]{:S(2)}, u32[]{:S(2)}) %collective-permute-start.24) | collective-permute-done | bytes 393248 | tf_op jit(solution)/shard_map/ppermute | solution.py:641
  128.7 2.1 %collective-permute-done.29 = bf16[48,4096]{1,0:T(8,128)(2,1)S(1)} collective-permute-done((bf16[48,4096]{1,0:T(8,128)(2,1)S(1)}, bf16[48,4096]{1,0:T(8,128)(2,1)S(1)}, u32[]{:S(2)}, u32[]{:S(2)}) %collective-permute-start.29) | collective-permute-done | bytes 393248 | tf_op jit(solution)/shard_map/ppermute | solution.py:641
  131.3 2.6 %collective-permute-done.12 = bf16[48,4096]{1,0:T(8,128)(2,1)S(1)} collective-permute-done((bf16[48,4096]{1,0:T(8,128)(2,1)S(1)}, bf16[48,4096]{1,0:T(8,128)(2,1)S(1)}, u32[]{:S(2)}, u32[]{:S(2)}) %collective-permute-start.12) | collective-permute-done | bytes 393248 | tf_op jit(solution)/shard_map/ppermute | solution.py:641
  133.8 2.5 %collective-permute-start.26 = (bf16[48,2048]{1,0:T(8,128)(2,1)S(1)}, bf16[48,2048]{1,0:T(8,128)(2,1)S(1)}, u32[]{:S(2)}, u32[]{:S(2)}) collective-permute-start(bf16[48,2048]{1,0:T(8,128)(2,1)S(1)} %get-tuple-element.38), channel_id=1, source_target_pairs={{0,8},{8,16},{16,24},{24,28},{28,20},{20,12},{12,4},{4,0},{1,9},{9... | collective-permute-start | bytes 589832 | tf_op jit(solution)/shard_map/ppermute | solution.py:641
  142.3 2.5 %collective-permute-start.44 = (bf16[48,2048]{1,0:T(8,128)(2,1)S(1)}, bf16[48,2048]{1,0:T(8,128)(2,1)S(1)}, u32[]{:S(2)}, u32[]{:S(2)}) collective-permute-start(bf16[48,2048]{1,0:T(8,128)(2,1)S(1)} %collective-permute-done.25), channel_id=1, source_target_pairs={{0,8},{8,16},{16,24},{24,28},{28,20},{20,12},{12,4},{4,0},{1,9},{9... | collective-permute-start | bytes 589832 | tf_op jit(solution)/shard_map/ppermute | solution.py:641
  153.4 4.4 %collective-permute-start.41 = (bf16[96,896]{1,0:T(8,128)(2,1)S(1)}, bf16[96,896]{1,0:T(8,128)(2,1)S(1)}, u32[]{:S(2)}, u32[]{:S(2)}) collective-permute-start(bf16[96,896]{1,0:T(8,128)(2,1)S(1)} %get-tuple-element.34), channel_id=1, source_target_pairs={{0,2},{1,3},{4,6},{5,7},{11,9},{9,11},{15,13},{13,15},{18,16},{16,... | collective-permute-start | bytes 516104 | tf_op jit(solution)/shard_map/ppermute | solution.py:641
  159.3 3.1 %collective-permute-done.41.refs_1_ = bf16[96,896]{1,0:T(8,128)(2,1)S(1)} collective-permute-done((bf16[96,896]{1,0:T(8,128)(2,1)S(1)}, bf16[96,896]{1,0:T(8,128)(2,1)S(1)}, u32[]{:S(2)}, u32[]{:S(2)}) %collective-permute-start.41) | collective-permute-done | bytes 172064 | tf_op jit(solution)/shard_map/ppermute | solution.py:641
  (153 shorter events, 64.3 us)
Async XLA Ops:
  1.1 20.9 %collective-permute-start.1 = (bf16[4,144,512]{2,1,0:T(8,128)(2,1)S(1)}, bf16[4,144,512]{2,1,0:T(8,128)(2,1)S(1)}, u32[]{:S(2)}, u32[]{:S(2)}) collective-permute-start(bf16[4,144,512]{2,1,0:T(8,128)(2,1)S(1)} %payload.1), channel_id=1, source_target_pairs={{8,0},{16,8},{24,16},{28,24},{20,28},{12,20},{4,12},{0,4},{9,1},{1... | collective-permute-start | bytes 1769480 | tf_op jit(solution)/shard_map/ppermute | solution.py:641
  4.2 17.9 %collective-permute-start = (bf16[4,144,512]{2,1,0:T(8,128)(2,1)S(1)}, bf16[4,144,512]{2,1,0:T(8,128)(2,1)S(1)}, u32[]{:S(2)}, u32[]{:S(2)}) collective-permute-start(bf16[4,144,512]{2,1,0:T(8,128)(2,1)S(1)} %payload.1), channel_id=1, source_target_pairs={{0,8},{8,16},{16,24},{24,28},{28,20},{20,12},{12,4},{4,0},{1,9},{9... | collective-permute-start | bytes 1769480 | tf_op jit(solution)/shard_map/ppermute | solution.py:641
  5.7 16.4 %all-to-all-start = ((s32[8,1,20]{2,1,0:T(1,128)}), s32[8,1,20]{2,1,0:T(1,128)S(1)}, u32[]{:S(2)}, u32[]{:S(2)}) async-start(s32[8,1,20]{2,1,0:T(1,128)} %bitcast), calls=%async_computation | async-start | bytes 8192 | tf_op jit(solution)/shard_map/all_to_all | solution.py:646
  26.4 15.1 %collective-permute-start.8 = (bf16[2,144,512]{2,1,0:T(8,128)(2,1)S(1)}, bf16[2,144,512]{2,1,0:T(8,128)(2,1)S(1)}, u32[]{:S(2)}, u32[]{:S(2)}) collective-permute-start(bf16[2,144,512]{2,1,0:T(8,128)(2,1)S(1)} %get-tuple-element.23.refs_3_.refs_7_), channel_id=1, source_target_pairs={{0,2},{1,3},{2,0},{3,1},{4,6},{5,7},{6,4},{7,5},{8,10},{9,11},{10,... | collective-permute-start | bytes 884744 | tf_op jit(solution)/shard_map/ppermute | solution.py:641
  40.0 11.6 %collective-permute-start.16 = (bf16[2,144,512]{2,1,0:T(8,128)(2,1)S(1)}, bf16[2,144,512]{2,1,0:T(8,128)(2,1)}, u32[]{:S(2)}, u32[]{:S(2)}) collective-permute-start(bf16[2,144,512]{2,1,0:T(8,128)(2,1)S(1)} %join.4.refs_3_), channel_id=1, source_target_pairs={{0,2},{1,3},{2,0},{3,1},{4,6},{5,7},{6,4},{7,5},{8,10},{9,11},{10,... | collective-permute-start | bytes 884744 | tf_op jit(solution)/shard_map/ppermute | solution.py:641
  46.7 30.2 %collective-permute-start.6 = (bf16[2,144,512]{2,1,0:T(8,128)(2,1)}, bf16[2,144,512]{2,1,0:T(8,128)(2,1)}, u32[]{:S(2)}, u32[]{:S(2)}) collective-permute-start(bf16[2,144,512]{2,1,0:T(8,128)(2,1)} %collective-permute-done.5.refs_5_), channel_id=1, source_target_pairs={{0,1},{1,0},{2,3},{3,2},{4,5},{5,4},{6,7},{7,6},{8,9},{9,8},{10,11... | collective-permute-start | bytes 884744 | tf_op jit(solution)/shard_map/ppermute | solution.py:641
  50.5 32.6 %collective-permute-start.15 = (bf16[2,144,512]{2,1,0:T(8,128)(2,1)S(1)}, bf16[2,144,512]{2,1,0:T(8,128)(2,1)}, u32[]{:S(2)}, u32[]{:S(2)}) collective-permute-start(bf16[2,144,512]{2,1,0:T(8,128)(2,1)S(1)} %join.4.refs_3_), channel_id=1, source_target_pairs={{0,1},{1,0},{2,3},{3,2},{4,5},{5,4},{6,7},{7,6},{8,9},{9,8},{10,11... | collective-permute-start | bytes 884744 | tf_op jit(solution)/shard_map/ppermute | solution.py:641
  51.6 33.3 %collective-permute-start.17 = (bf16[2,144,512]{2,1,0:T(8,128)(2,1)}, bf16[2,144,512]{2,1,0:T(8,128)(2,1)}, u32[]{:S(2)}, u32[]{:S(2)}) collective-permute-start(bf16[2,144,512]{2,1,0:T(8,128)(2,1)} %collective-permute-done.16.refs_5_), channel_id=1, source_target_pairs={{0,1},{1,0},{2,3},{3,2},{4,5},{5,4},{6,7},{7,6},{8,9},{9,8},{10,11... | collective-permute-start | bytes 884744 | tf_op jit(solution)/shard_map/ppermute | solution.py:641
  55.2 32.7 %collective-permute-start.20 = (bf16[1,144,512]{2,1,0:T(8,128)(2,1)}, bf16[1,144,512]{2,1,0:T(8,128)(2,1)}, u32[]{:S(2)}, u32[]{:S(2)}) collective-permute-start(bf16[1,144,512]{2,1,0:T(8,128)(2,1)} %join.5.refs_7_), channel_id=1, source_target_pairs={{0,1},{1,0},{2,3},{3,2},{4,5},{5,4},{6,7},{7,6},{8,9},{9,8},{10,11... | collective-permute-start | bytes 442376 | tf_op jit(solution)/shard_map/ppermute | solution.py:641
  59.5 28.3 %collective-permute-start.22 = (bf16[1,144,512]{2,1,0:T(8,128)(2,1)}, bf16[1,144,512]{2,1,0:T(8,128)(2,1)}, u32[]{:S(2)}, u32[]{:S(2)}) collective-permute-start(bf16[1,144,512]{2,1,0:T(8,128)(2,1)} %collective-permute-done.21.refs_9_), channel_id=1, source_target_pairs={{0,1},{1,0},{2,3},{3,2},{4,5},{5,4},{6,7},{7,6},{8,9},{9,8},{10,11... | collective-permute-start | bytes 442376 | tf_op jit(solution)/shard_map/ppermute | solution.py:641
  79.7 17.1 %collective-permute-start.27 = (bf16[48,4096]{1,0:T(8,128)(2,1)S(1)}, bf16[48,4096]{1,0:T(8,128)(2,1)S(1)}, u32[]{:S(2)}, u32[]{:S(2)}) collective-permute-start(bf16[48,4096]{1,0:T(8,128)(2,1)S(1)} %attend_slots.8), channel_id=1, source_target_pairs={{8,0},{16,8},{24,16},{28,24},{20,28},{12,20},{4,12},{0,4},{9,1},{1... | collective-permute-start | bytes 1179656 | tf_op jit(solution)/shard_map/ppermute | solution.py:641
  83.1 14.4 %collective-permute-start.10 = (bf16[48,4096]{1,0:T(8,128)(2,1)S(1)}, bf16[48,4096]{1,0:T(8,128)(2,1)S(1)}, u32[]{:S(2)}, u32[]{:S(2)}) collective-permute-start(bf16[48,4096]{1,0:T(8,128)(2,1)S(1)} %attend_slots.8), channel_id=1, source_target_pairs={{0,8},{8,16},{16,24},{24,28},{28,20},{20,12},{12,4},{4,0},{1,9},{9... | collective-permute-start | bytes 1179656 | tf_op jit(solution)/shard_map/ppermute | solution.py:641
  93.4 12.0 %collective-permute-start.30 = (bf16[48,4096]{1,0:T(8,128)(2,1)S(1)}, bf16[48,4096]{1,0:T(8,128)(2,1)S(1)}, u32[]{:S(2)}, u32[]{:S(2)}) collective-permute-start(bf16[48,4096]{1,0:T(8,128)(2,1)S(1)} %attend_slots.11), channel_id=1, source_target_pairs={{8,0},{16,8},{24,16},{28,24},{20,28},{12,20},{4,12},{0,4},{9,1},{1... | collective-permute-start | bytes 1179656 | tf_op jit(solution)/shard_map/ppermute | solution.py:641
  94.0 12.0 %collective-permute-start.23 = (bf16[48,4096]{1,0:T(8,128)(2,1)S(1)}, bf16[48,4096]{1,0:T(8,128)(2,1)S(1)}, u32[]{:S(2)}, u32[]{:S(2)}) collective-permute-start(bf16[48,4096]{1,0:T(8,128)(2,1)S(1)} %attend_slots.11), channel_id=1, source_target_pairs={{0,8},{8,16},{16,24},{24,28},{28,20},{20,12},{12,4},{4,0},{1,9},{9... | collective-permute-start | bytes 1179656 | tf_op jit(solution)/shard_map/ppermute | solution.py:641
  96.8 11.2 %collective-permute-start.37 = (bf16[96,896]{1,0:T(8,128)(2,1)S(1)}, bf16[96,896]{1,0:T(8,128)(2,1)S(1)}, u32[]{:S(2)}, u32[]{:S(2)}) collective-permute-start(bf16[96,896]{1,0:T(8,128)(2,1)S(1)} %convolution_convert_fusion.1.refs_0_), channel_id=1, source_target_pairs={{0,1},{1,0},{2,3},{3,2},{4,5},{5,4},{6,7},{7,6},{8,9},{9,8},{10,11... | collective-permute-start | bytes 516104 | tf_op jit(solution)/shard_map/ppermute | solution.py:641
  96.9 19.2 %collective-permute-start.28 = (bf16[48,4096]{1,0:T(8,128)(2,1)S(1)}, bf16[48,4096]{1,0:T(8,128)(2,1)S(1)}, u32[]{:S(2)}, u32[]{:S(2)}) collective-permute-start(bf16[48,4096]{1,0:T(8,128)(2,1)S(1)} %collective-permute-done.27), channel_id=1, source_target_pairs={{8,0},{16,8},{24,16},{28,24},{20,28},{12,20},{4,12},{0,4},{9,1},{1... | collective-permute-start | bytes 1179656 | tf_op jit(solution)/shard_map/ppermute | solution.py:641
  97.5 20.6 %collective-permute-start.11 = (bf16[48,4096]{1,0:T(8,128)(2,1)S(1)}, bf16[48,4096]{1,0:T(8,128)(2,1)S(1)}, u32[]{:S(2)}, u32[]{:S(2)}) collective-permute-start(bf16[48,4096]{1,0:T(8,128)(2,1)S(1)} %collective-permute-done.10), channel_id=1, source_target_pairs={{0,8},{8,16},{16,24},{24,28},{28,20},{20,12},{12,4},{4,0},{1,9},{9... | collective-permute-start | bytes 1179656 | tf_op jit(solution)/shard_map/ppermute | solution.py:641
  105.5 16.9 %collective-permute-start.31 = (bf16[48,4096]{1,0:T(8,128)(2,1)S(1)}, bf16[48,4096]{1,0:T(8,128)(2,1)S(1)}, u32[]{:S(2)}, u32[]{:S(2)}) collective-permute-start(bf16[48,4096]{1,0:T(8,128)(2,1)S(1)} %collective-permute-done.30), channel_id=1, source_target_pairs={{8,0},{16,8},{24,16},{28,24},{20,28},{12,20},{4,12},{0,4},{9,1},{1... | collective-permute-start | bytes 1179656 | tf_op jit(solution)/shard_map/ppermute | solution.py:641
  116.0 11.9 %collective-permute-start.24 = (bf16[48,4096]{1,0:T(8,128)(2,1)S(1)}, bf16[48,4096]{1,0:T(8,128)(2,1)S(1)}, u32[]{:S(2)}, u32[]{:S(2)}) collective-permute-start(bf16[48,4096]{1,0:T(8,128)(2,1)S(1)} %collective-permute-done.23), channel_id=1, source_target_pairs={{0,8},{8,16},{16,24},{24,28},{28,20},{20,12},{12,4},{4,0},{1,9},{9... | collective-permute-start | bytes 1179656 | tf_op jit(solution)/shard_map/ppermute | solution.py:641
  116.1 14.7 %collective-permute-start.29 = (bf16[48,4096]{1,0:T(8,128)(2,1)S(1)}, bf16[48,4096]{1,0:T(8,128)(2,1)S(1)}, u32[]{:S(2)}, u32[]{:S(2)}) collective-permute-start(bf16[48,4096]{1,0:T(8,128)(2,1)S(1)} %collective-permute-done.28), channel_id=1, source_target_pairs={{8,0},{16,8},{24,16},{28,24},{20,28},{12,20},{4,12},{0,4},{9,1},{1... | collective-permute-start | bytes 1179656 | tf_op jit(solution)/shard_map/ppermute | solution.py:641
  118.1 15.8 %collective-permute-start.12 = (bf16[48,4096]{1,0:T(8,128)(2,1)S(1)}, bf16[48,4096]{1,0:T(8,128)(2,1)S(1)}, u32[]{:S(2)}, u32[]{:S(2)}) collective-permute-start(bf16[48,4096]{1,0:T(8,128)(2,1)S(1)} %collective-permute-done.11), channel_id=1, source_target_pairs={{0,8},{8,16},{16,24},{24,28},{28,20},{20,12},{12,4},{4,0},{1,9},{9... | collective-permute-start | bytes 1179656 | tf_op jit(solution)/shard_map/ppermute | solution.py:641
  119.0 19.2 %collective-permute-start.39 = (bf16[96,896]{1,0:T(8,128)(2,1)S(1)}, bf16[96,896]{1,0:T(8,128)(2,1)S(1)}, u32[]{:S(2)}, u32[]{:S(2)}) collective-permute-start(bf16[96,896]{1,0:T(8,128)(2,1)S(1)} %get-tuple-element.27), channel_id=1, source_target_pairs={{2,0},{3,1},{6,4},{7,5},{10,8},{8,10},{14,12},{12,14},{19,17},{17,... | collective-permute-start | bytes 516104 | tf_op jit(solution)/shard_map/ppermute | solution.py:641
  122.3 16.1 %collective-permute-start.32 = (bf16[48,2048]{1,0:T(8,128)(2,1)S(1)}, bf16[48,2048]{1,0:T(8,128)(2,1)S(1)}, u32[]{:S(2)}, u32[]{:S(2)}) collective-permute-start(bf16[48,2048]{1,0:T(8,128)(2,1)S(1)} %get-tuple-element.39), channel_id=1, source_target_pairs={{8,0},{16,8},{24,16},{28,24},{20,28},{12,20},{4,12},{0,4},{9,1},{1... | collective-permute-start | bytes 589832 | tf_op jit(solution)/shard_map/ppermute | solution.py:641
  128.0 11.2 %collective-permute-start.33 = (bf16[48,2048]{1,0:T(8,128)(2,1)S(1)}, bf16[48,2048]{1,0:T(8,128)(2,1)S(1)}, u32[]{:S(2)}, u32[]{:S(2)}) collective-permute-start(bf16[48,2048]{1,0:T(8,128)(2,1)S(1)} %get-tuple-element.40), channel_id=1, source_target_pairs={{8,0},{16,8},{24,16},{28,24},{20,28},{12,20},{4,12},{0,4},{9,1},{1... | collective-permute-start | bytes 589832 | tf_op jit(solution)/shard_map/ppermute | solution.py:641
  (46 other events, 394.6 us)

commit v10 on v9

--- a/solution.py
+++ b/solution.py
@@ -239,7 +239,7 @@
 def chunk_plans(ranks):
     middle = ranks // 2
     return {
-        "p": [[0], list(range(1, middle - 1)), [middle - 1]],
+        "p": [list(range(middle - 1)), [middle - 1]],
         "s": [[c] for c in range(middle, ranks - 2)] + [[ranks - 2, ranks - 1]],
     }
 
@@ -377,12 +377,12 @@
     )(fore, back)
 
 
-def slots_kernel(plan, own, heads, indices, bundles, final, scale, table, info, *refs):
-    count = len(plan)
+def slots_kernel(plan, own, indices, bundles, final, scale, table, info, *refs):
+    count, heads = len(plan), len(indices[0])
     refs = list(refs)
     q_ref, qr_ref, w_hbm = refs.pop(0), refs.pop(0), refs.pop(0)
-    w_ref, fetch = w_hbm, own or count > 1
-    if fetch:
+    w_ref = w_hbm
+    if count > 1:
         w_ref, w_sem = refs.pop(-2), refs.pop(-1)
         w_copy = pltpu.make_async_copy(w_hbm, w_ref, w_sem)
         w_copy.start()
@@ -441,7 +441,7 @@
         return 0
 
     lax.fori_loop(0, count, bundle, 0)
-    if fetch:
+    if count > 1:
         w_copy.wait()
     local_heads, _, value_width = w_ref.shape
     n = mixed.shape[1] // local_heads
@@ -462,17 +462,18 @@
         out_ref[...] = into[...].astype(out_ref.dtype)
 
 
-def attend_slots(plan, table, info, q, qr, full, parts, heads, positions, bundles, w_uv, earlier=None):
+def attend_slots(plan, table, info, q, qr, full, parts, bundles, w_uv, earlier=None):
     own = 1 if full is not None else 0
     final = earlier is not None
     earlier = list(earlier or ())
-    count = len(plan)
+    count, heads = len(plan), len(parts[0])
     _, q_rows, wide = q.shape
     dims = qr.shape[2]
+    positions = (parts[0][0][0].shape[1] - dims // heads) * heads
     local_heads, _, value_width = w_uv.shape
     vmem = pl.BlockSpec(memory_space=pltpu.MemorySpace.VMEM)
     smem = pl.BlockSpec(memory_space=pltpu.MemorySpace.SMEM)
-    fetch = own or count > 1
+    fetch = count > 1
     args = [q, qr, in_hbm(w_uv) if fetch else w_uv]
     in_specs = [vmem, vmem, pl.BlockSpec(memory_space=pl.ANY) if fetch else vmem]
     if own:
@@ -491,8 +492,8 @@
         scratch += [pltpu.VMEM(w_uv.shape, w_uv.dtype), pltpu.SemaphoreType.DMA]
     return pl.pallas_call(
         functools.partial(
-            slots_kernel, plan, own, heads, [[index for _, index in slot] for slot in parts],
-            bundles, final, 1.0 / math.sqrt(VD + ROPE),
+            slots_kernel, plan, own, [[index for _, index in slot] for slot in parts], bundles,
+            final, 1.0 / math.sqrt(VD + ROPE),
         ),
         out_shape=jax.ShapeDtypeStruct(out_shape, jnp.bfloat16 if final else jnp.float32),
         in_specs=[smem] * 2 + in_specs,
@@ -679,7 +680,7 @@
     def attend(plan, full=None, earlier=None):
         return attend_slots(
             plan, table, info, q, qr, full, [groups[c] for c in plan[(full is not None) :]],
-            heads, cache_latent.shape[1], bundles, w_uv, earlier,
+            bundles, w_uv, earlier,
         )
 
     chunks = []

time: 165 us -> 166 us (level)
  local copies, waits for them, and re-layouts: 11.4 us -> 16.1 us
  Pallas kernels: 34.5 us -> 31 us
  waiting for transfers between devices: 57.7 us -> 55.9 us
    unnamed x42 -> x40, local copies, waits for them, and re-layouts: 4.72 us -> 8.52 us
    pallas_call x6 -> x5, Pallas kernels: 24.2 us -> 20.8 us  [attend_slots(): pl.pallas_call(functools.partial(slots_kernel, plan, own, [[index for _,...]
  transfers between devices with their start and end apart: 49 -> 49, of which waited for: 18 -> 18; matrix products, arithmetic and copies ran while one was open for 9% -> 10% of each run, Pallas kernels for 19% -> 16%
where the time goes in v10:
time: 166 us; the launch traced here: 165 us
  waiting for transfers between devices  55.9 us (34%)
  starting transfers between devices  52.8 us (32%)
  Pallas kernels  31 us (19%)
  local copies, waits for them, and re-layouts  16.1 us (10%)
  matrix products  8.11 us (5%)
    ppermute x48, waiting for transfers between devices, move(): return lax.ppermute(x, axis, pairs)  48.1 us
    ppermute x48, starting transfers between devices, move(): return lax.ppermute(x, axis, pairs)  46.6 us
    pallas_call x5, Pallas kernels, attend_slots(): pl.pallas_call(functools.partial(slots_kernel, plan, own, [[index for _,...  20.8 us
    unnamed x40, local copies, waits for them, and re-layouts  8.52 us
    dot_general x5, matrix products, project(): jnp.dot(jnp.concatenate(pieces), w_out, preferred_element_type=jnp.float32)  8.11 us
    all_to_all x1, waiting for transfers between devices, local_ring(): lax.all_to_all(jnp.concatenate(facts, axis=1), 'dp', split_axis=0, concat...  7.74 us
    all_to_all x1, starting transfers between devices, local_ring(): lax.all_to_all(jnp.concatenate(facts, axis=1), 'dp', split_axis=0, concat...  6.28 us
    pallas_call x5, Pallas kernels, settle_step(): pl.pallas_call(functools.partial(settle_kernel, masks, per_head, groups,...  4.28 us
  transfers between devices with their start and end apart: 49, of which 18 were waited for; matrix products, arithmetic and copies ran while one was open for 10% of the time, Pallas kernels for 16%

profile of v10, /device:TPU:0, one launch (start us, length us, event | category | flops | bytes accessed | tf_op | source)
XLA Modules:
  0.0 165.2 jit_solution(11715527083422935528)
XLA Ops:
  1.1 3.1 %collective-permute-start = (bf16[4,144,512]{2,1,0:T(8,128)(2,1)S(1)}, bf16[4,144,512]{2,1,0:T(8,128)(2,1)S(1)}, u32[]{:S(2)}, u32[]{:S(2)}) collective-permute-start(bf16[4,144,512]{2,1,0:T(8,128)(2,1)S(1)} %payload.1), channel_id=1, source_target_pairs={{0,8},{8,16},{16,24},{24,28},{28,20},{20,12},{12,4},{4,0},{1,9},{9... | collective-permute-start | bytes 1769480 | tf_op jit(solution)/shard_map/ppermute | solution.py:642
  5.5 6.3 %all-to-all-start = ((s32[8,1,20]{2,1,0:T(1,128)}), s32[8,1,20]{2,1,0:T(1,128)S(1)}, u32[]{:S(2)}, u32[]{:S(2)}) async-start(s32[8,1,20]{2,1,0:T(1,128)} %bitcast), calls=%async_computation | async-start | bytes 8192 | tf_op jit(solution)/shard_map/all_to_all | solution.py:647
  13.3 7.7 %all-to-all-done = s32[8,1,20]{2,1,0:T(1,128)S(1)} async-done(((s32[8,1,20]{2,1,0:T(1,128)}), s32[8,1,20]{2,1,0:T(1,128)S(1)}, u32[]{:S(2)}, u32[]{:S(2)}) %all-to-all-start) | async-done | bytes 672 | tf_op jit(solution)/shard_map/all_to_all | solution.py:647
  26.9 5.5 %collective-permute-done.2.fore = bf16[368,512]{1,0:T(8,128)(2,1)S(1)} collective-permute-done((bf16[368,512]{1,0:T(8,128)(2,1)S(1)}, bf16[368,512]{1,0:T(8,128)(2,1)S(1)}, u32[]{:S(2)}, u32[]{:S(2)}) %collective-permute-start.2) | collective-permute-done | bytes 376864 | tf_op jit(solution)/shard_map/ppermute | solution.py:642
  36.2 2.8 %collective-permute-done.14.back = bf16[208,512]{1,0:T(8,128)(2,1)S(1)} collective-permute-done((bf16[208,512]{1,0:T(8,128)(2,1)S(1)}, bf16[208,512]{1,0:T(8,128)(2,1)S(1)}, u32[]{:S(2)}, u32[]{:S(2)}) %collective-permute-start.14) | collective-permute-done | bytes 213024 | tf_op jit(solution)/shard_map/ppermute | solution.py:642
  43.0 2.1 %collective-permute-done.19.back = bf16[64,512]{1,0:T(8,128)(2,1)S(1)} collective-permute-done((bf16[64,512]{1,0:T(8,128)(2,1)S(1)}, bf16[64,512]{1,0:T(8,128)(2,1)S(1)}, u32[]{:S(2)}, u32[]{:S(2)}) %collective-permute-start.19) | collective-permute-done | bytes 65568 | tf_op jit(solution)/shard_map/ppermute | solution.py:642
  45.9 3.6 %collective-permute-done.18.fore = bf16[80,512]{1,0:T(8,128)(2,1)S(1)} collective-permute-done((bf16[80,512]{1,0:T(8,128)(2,1)S(1)}, bf16[80,512]{1,0:T(8,128)(2,1)S(1)}, u32[]{:S(2)}, u32[]{:S(2)}) %collective-permute-start.18) | collective-permute-done | bytes 81952 | tf_op jit(solution)/shard_map/ppermute | solution.py:642
  54.4 4.1 %collective-permute-done.21.refs_9_ = bf16[1,144,512]{2,1,0:T(8,128)(2,1)} collective-permute-done((bf16[1,144,512]{2,1,0:T(8,128)(2,1)}, bf16[1,144,512]{2,1,0:T(8,128)(2,1)}, u32[]{:S(2)}, u32[]{:S(2)}) %collective-permute-start.21) | collective-permute-done | bytes 147488 | tf_op jit(solution)/shard_map/ppermute | solution.py:642
  58.6 4.2 %reshape.11.refs_0_ = bf16[8,384,512]{2,1,0:T(8,128)(2,1)S(1)} reshape(bf16[96,16384]{1,0:T(8,128)(2,1)} %param.11) | data formatting | bytes 6291456 | tf_op jit(solution)/shard_map/reshape | solution.py:652
  62.8 2.6 %reshape.12.refs_1_ = bf16[8,384,64]{2,1,0:T(8,128)(2,1)} reshape(bf16[96,2048]{1,0:T(8,128)(2,1)} %param.12) | data formatting | bytes 786432 | tf_op jit(solution)/shard_map/reshape | solution.py:653
  70.4 6.9 %attend_slots.5.refs_7_ = f32[36,4096]{1,0:T(8,128)S(1)} custom-call(s32[8,8]{1,0:T(8,128)} %plan.1.table, s32[8,1,20]{2,1,0:T(1,128)S(1)} %broadcast_maximum_fusion.info, bf16[8,384,512]{2,1,0:T(8,128)(2,1)S(1)} %reshape.11.refs_0_, bf16[8,384,64]{2,1,0:T(8,128)(2,1)S(1)} %copy-done.1, bf16[32,512,128]{2,1,0:T(8,128)(2,1)} %refs_2_.9, ...), custom_call_target="tpu_custom_call" | custom-call | tf_op jit(solution)/shard_map/attend_slots/pallas_call | solution.py:493
  77.4 2.8 %attend_slots.6 = bf16[48,4096]{1,0:T(8,128)(2,1)S(1)} custom-call(s32[8,8]{1,0:T(8,128)} %plan.1.table, s32[8,1,20]{2,1,0:T(1,128)S(1)} %broadcast_maximum_fusion.info, bf16[8,384,512]{2,1,0:T(8,128)(2,1)S(1)} %reshape.11.refs_0_, bf16[8,384,64]{2,1,0:T(8,128)(2,1)S(1)} %copy-done.1, bf16[32,512,128]{2,1,0:T(8,128)(2,1)S(1)} %copy-done, ...), custom_call_target="tpu_custom_call" | custom-call | tf_op jit(solution)/shard_map/attend_slots/pallas_call | solution.py:493
  81.7 2.8 %attend_slots.7.refs_11_ = f32[12,4096]{1,0:T(8,128)S(1)} custom-call(s32[8,8]{1,0:T(8,128)} %plan.1.table, s32[8,1,20]{2,1,0:T(1,128)S(1)} %broadcast_maximum_fusion.info, bf16[8,384,512]{2,1,0:T(8,128)(2,1)S(1)} %reshape.11.refs_0_, bf16[8,384,64]{2,1,0:T(8,128)(2,1)S(1)} %copy-done.1, bf16[32,512,128]{2,1,0:T(8,128)(2,1)S(1)} %copy-done, ...), custom_call_target="tpu_custom_call" | custom-call | tf_op jit(solution)/shard_map/attend_slots/pallas_call | solution.py:493
  85.3 3.0 %attend_slots.8.refs_12_ = f32[12,4096]{1,0:T(8,128)S(1)} custom-call(s32[8,8]{1,0:T(8,128)} %plan.1.table, s32[8,1,20]{2,1,0:T(1,128)S(1)} %broadcast_maximum_fusion.info, bf16[8,384,512]{2,1,0:T(8,128)(2,1)S(1)} %reshape.11.refs_0_, bf16[8,384,64]{2,1,0:T(8,128)(2,1)S(1)} %copy-done.1, bf16[32,512,128]{2,1,0:T(8,128)(2,1)S(1)} %copy-done, ...), custom_call_target="tpu_custom_call" | custom-call | tf_op jit(solution)/shard_map/attend_slots/pallas_call | solution.py:493
  88.3 5.3 %attend_slots.9 = bf16[48,4096]{1,0:T(8,128)(2,1)S(1)} custom-call(s32[8,8]{1,0:T(8,128)} %plan.1.table, s32[8,1,20]{2,1,0:T(1,128)S(1)} %broadcast_maximum_fusion.info, bf16[8,384,512]{2,1,0:T(8,128)(2,1)S(1)} %reshape.11.refs_0_, bf16[8,384,64]{2,1,0:T(8,128)(2,1)S(1)} %copy-done.2, bf16[32,512,128]{2,1,0:T(8,128)(2,1)} %refs_2_.9, ...), custom_call_target="tpu_custom_call" | custom-call | tf_op jit(solution)/shard_map/attend_slots/pallas_call | solution.py:493
  99.2 6.5 %collective-permute-done.30 = bf16[48,4096]{1,0:T(8,128)(2,1)S(1)} collective-permute-done((bf16[48,4096]{1,0:T(8,128)(2,1)S(1)}, bf16[48,4096]{1,0:T(8,128)(2,1)S(1)}, u32[]{:S(2)}, u32[]{:S(2)}) %collective-permute-start.30) | collective-permute-done | bytes 393248 | tf_op jit(solution)/shard_map/ppermute | solution.py:642
  111.2 6.0 %collective-permute-done.38.refs_3_ = bf16[96,896]{1,0:T(8,128)(2,1)S(1)} collective-permute-done((bf16[96,896]{1,0:T(8,128)(2,1)S(1)}, bf16[96,896]{1,0:T(8,128)(2,1)S(1)}, u32[]{:S(2)}, u32[]{:S(2)}) %collective-permute-start.38) | collective-permute-done | bytes 172064 | tf_op jit(solution)/shard_map/ppermute | solution.py:642
  117.2 2.0 %collective-permute-start.29 = (bf16[48,4096]{1,0:T(8,128)(2,1)S(1)}, bf16[48,4096]{1,0:T(8,128)(2,1)S(1)}, u32[]{:S(2)}, u32[]{:S(2)}) collective-permute-start(bf16[48,4096]{1,0:T(8,128)(2,1)S(1)} %collective-permute-done.28), channel_id=1, source_target_pairs={{8,0},{16,8},{24,16},{28,24},{20,28},{12,20},{4,12},{0,4},{9,1},{1... | collective-permute-start | bytes 1179656 | tf_op jit(solution)/shard_map/ppermute | solution.py:642
  124.1 4.1 %collective-permute-done.24 = bf16[48,4096]{1,0:T(8,128)(2,1)S(1)} collective-permute-done((bf16[48,4096]{1,0:T(8,128)(2,1)S(1)}, bf16[48,4096]{1,0:T(8,128)(2,1)S(1)}, u32[]{:S(2)}, u32[]{:S(2)}) %collective-permute-start.24) | collective-permute-done | bytes 393248 | tf_op jit(solution)/shard_map/ppermute | solution.py:642
  131.6 3.5 %collective-permute-done.12 = bf16[48,4096]{1,0:T(8,128)(2,1)S(1)} collective-permute-done((bf16[48,4096]{1,0:T(8,128)(2,1)S(1)}, bf16[48,4096]{1,0:T(8,128)(2,1)S(1)}, u32[]{:S(2)}, u32[]{:S(2)}) %collective-permute-start.12) | collective-permute-done | bytes 393248 | tf_op jit(solution)/shard_map/ppermute | solution.py:642
  135.1 2.5 %collective-permute-start.25 = (bf16[48,2048]{1,0:T(8,128)(2,1)S(1)}, bf16[48,2048]{1,0:T(8,128)(2,1)S(1)}, u32[]{:S(2)}, u32[]{:S(2)}) collective-permute-start(bf16[48,2048]{1,0:T(8,128)(2,1)S(1)} %get-tuple-element.37), channel_id=1, source_target_pairs={{0,8},{8,16},{16,24},{24,28},{28,20},{20,12},{12,4},{4,0},{1,9},{9... | collective-permute-start | bytes 589832 | tf_op jit(solution)/shard_map/ppermute | solution.py:642
  143.6 2.5 %collective-permute-start.44 = (bf16[48,2048]{1,0:T(8,128)(2,1)S(1)}, bf16[48,2048]{1,0:T(8,128)(2,1)S(1)}, u32[]{:S(2)}, u32[]{:S(2)}) collective-permute-start(bf16[48,2048]{1,0:T(8,128)(2,1)S(1)} %collective-permute-done.25), channel_id=1, source_target_pairs={{0,8},{8,16},{16,24},{24,28},{28,20},{20,12},{12,4},{4,0},{1,9},{9... | collective-permute-start | bytes 589832 | tf_op jit(solution)/shard_map/ppermute | solution.py:642
  154.2 4.4 %collective-permute-start.41 = (bf16[96,896]{1,0:T(8,128)(2,1)S(1)}, bf16[96,896]{1,0:T(8,128)(2,1)S(1)}, u32[]{:S(2)}, u32[]{:S(2)}) collective-permute-start(bf16[96,896]{1,0:T(8,128)(2,1)S(1)} %get-tuple-element.34), channel_id=1, source_target_pairs={{0,2},{1,3},{4,6},{5,7},{11,9},{9,11},{15,13},{13,15},{18,16},{16,... | collective-permute-start | bytes 516104 | tf_op jit(solution)/shard_map/ppermute | solution.py:642
  160.1 3.3 %collective-permute-done.41.refs_1_ = bf16[96,896]{1,0:T(8,128)(2,1)S(1)} collective-permute-done((bf16[96,896]{1,0:T(8,128)(2,1)S(1)}, bf16[96,896]{1,0:T(8,128)(2,1)S(1)}, u32[]{:S(2)}, u32[]{:S(2)}) %collective-permute-start.41) | collective-permute-done | bytes 172064 | tf_op jit(solution)/shard_map/ppermute | solution.py:642
  (150 shorter events, 66.9 us)
Async XLA Ops:
  1.1 20.0 %collective-permute-start = (bf16[4,144,512]{2,1,0:T(8,128)(2,1)S(1)}, bf16[4,144,512]{2,1,0:T(8,128)(2,1)S(1)}, u32[]{:S(2)}, u32[]{:S(2)}) collective-permute-start(bf16[4,144,512]{2,1,0:T(8,128)(2,1)S(1)} %payload.1), channel_id=1, source_target_pairs={{0,8},{8,16},{16,24},{24,28},{28,20},{20,12},{12,4},{4,0},{1,9},{9... | collective-permute-start | bytes 1769480 | tf_op jit(solution)/shard_map/ppermute | solution.py:642
  4.2 16.9 %collective-permute-start.1 = (bf16[4,144,512]{2,1,0:T(8,128)(2,1)S(1)}, bf16[4,144,512]{2,1,0:T(8,128)(2,1)S(1)}, u32[]{:S(2)}, u32[]{:S(2)}) collective-permute-start(bf16[4,144,512]{2,1,0:T(8,128)(2,1)S(1)} %payload.1), channel_id=1, source_target_pairs={{8,0},{16,8},{24,16},{28,24},{20,28},{12,20},{4,12},{0,4},{9,1},{1... | collective-permute-start | bytes 1769480 | tf_op jit(solution)/shard_map/ppermute | solution.py:642
  5.5 15.5 %all-to-all-start = ((s32[8,1,20]{2,1,0:T(1,128)}), s32[8,1,20]{2,1,0:T(1,128)S(1)}, u32[]{:S(2)}, u32[]{:S(2)}) async-start(s32[8,1,20]{2,1,0:T(1,128)} %bitcast), calls=%async_computation | async-start | bytes 8192 | tf_op jit(solution)/shard_map/all_to_all | solution.py:647
  25.4 15.2 %collective-permute-start.8 = (bf16[2,144,512]{2,1,0:T(8,128)(2,1)S(1)}, bf16[2,144,512]{2,1,0:T(8,128)(2,1)S(1)}, u32[]{:S(2)}, u32[]{:S(2)}) collective-permute-start(bf16[2,144,512]{2,1,0:T(8,128)(2,1)S(1)} %get-tuple-element.23.refs_5_.refs_9_), channel_id=1, source_target_pairs={{0,2},{1,3},{2,0},{3,1},{4,6},{5,7},{6,4},{7,5},{8,10},{9,11},{10,... | collective-permute-start | bytes 884744 | tf_op jit(solution)/shard_map/ppermute | solution.py:642
  34.6 11.3 %collective-permute-start.5 = (bf16[2,144,512]{2,1,0:T(8,128)(2,1)S(1)}, bf16[2,144,512]{2,1,0:T(8,128)(2,1)}, u32[]{:S(2)}, u32[]{:S(2)}) collective-permute-start(bf16[2,144,512]{2,1,0:T(8,128)(2,1)S(1)} %join.3.refs_3_), channel_id=1, source_target_pairs={{0,2},{1,3},{2,0},{3,1},{4,6},{5,7},{6,4},{7,5},{8,10},{9,11},{10,... | collective-permute-start | bytes 884744 | tf_op jit(solution)/shard_map/ppermute | solution.py:642
  39.0 11.5 %collective-permute-start.16 = (bf16[2,144,512]{2,1,0:T(8,128)(2,1)S(1)}, bf16[2,144,512]{2,1,0:T(8,128)(2,1)}, u32[]{:S(2)}, u32[]{:S(2)}) collective-permute-start(bf16[2,144,512]{2,1,0:T(8,128)(2,1)S(1)} %join.4.refs_3_), channel_id=1, source_target_pairs={{0,2},{1,3},{2,0},{3,1},{4,6},{5,7},{6,4},{7,5},{8,10},{9,11},{10,... | collective-permute-start | bytes 884744 | tf_op jit(solution)/shard_map/ppermute | solution.py:642
  45.9 31.4 %collective-permute-start.6 = (bf16[2,144,512]{2,1,0:T(8,128)(2,1)}, bf16[2,144,512]{2,1,0:T(8,128)(2,1)}, u32[]{:S(2)}, u32[]{:S(2)}) collective-permute-start(bf16[2,144,512]{2,1,0:T(8,128)(2,1)} %collective-permute-done.5.refs_5_), channel_id=1, source_target_pairs={{0,1},{1,0},{2,3},{3,2},{4,5},{5,4},{6,7},{7,6},{8,9},{9,8},{10,11... | collective-permute-start | bytes 884744 | tf_op jit(solution)/shard_map/ppermute | solution.py:642
  49.5 34.9 %collective-permute-start.15 = (bf16[2,144,512]{2,1,0:T(8,128)(2,1)S(1)}, bf16[2,144,512]{2,1,0:T(8,128)(2,1)}, u32[]{:S(2)}, u32[]{:S(2)}) collective-permute-start(bf16[2,144,512]{2,1,0:T(8,128)(2,1)S(1)} %join.4.refs_3_), channel_id=1, source_target_pairs={{0,1},{1,0},{2,3},{3,2},{4,5},{5,4},{6,7},{7,6},{8,9},{9,8},{10,11... | collective-permute-start | bytes 884744 | tf_op jit(solution)/shard_map/ppermute | solution.py:642
  50.5 34.8 %collective-permute-start.17 = (bf16[2,144,512]{2,1,0:T(8,128)(2,1)}, bf16[2,144,512]{2,1,0:T(8,128)(2,1)}, u32[]{:S(2)}, u32[]{:S(2)}) collective-permute-start(bf16[2,144,512]{2,1,0:T(8,128)(2,1)} %collective-permute-done.16.refs_5_), channel_id=1, source_target_pairs={{0,1},{1,0},{2,3},{3,2},{4,5},{5,4},{6,7},{7,6},{8,9},{9,8},{10,11... | collective-permute-start | bytes 884744 | tf_op jit(solution)/shard_map/ppermute | solution.py:642
  54.2 34.1 %collective-permute-start.20 = (bf16[1,144,512]{2,1,0:T(8,128)(2,1)}, bf16[1,144,512]{2,1,0:T(8,128)(2,1)}, u32[]{:S(2)}, u32[]{:S(2)}) collective-permute-start(bf16[1,144,512]{2,1,0:T(8,128)(2,1)} %join.5.refs_7_), channel_id=1, source_target_pairs={{0,1},{1,0},{2,3},{3,2},{4,5},{5,4},{6,7},{7,6},{8,9},{9,8},{10,11... | collective-permute-start | bytes 442376 | tf_op jit(solution)/shard_map/ppermute | solution.py:642
  58.5 29.8 %collective-permute-start.22 = (bf16[1,144,512]{2,1,0:T(8,128)(2,1)}, bf16[1,144,512]{2,1,0:T(8,128)(2,1)}, u32[]{:S(2)}, u32[]{:S(2)}) collective-permute-start(bf16[1,144,512]{2,1,0:T(8,128)(2,1)} %collective-permute-done.21.refs_9_), channel_id=1, source_target_pairs={{0,1},{1,0},{2,3},{3,2},{4,5},{5,4},{6,7},{7,6},{8,9},{9,8},{10,11... | collective-permute-start | bytes 442376 | tf_op jit(solution)/shard_map/ppermute | solution.py:642
  80.2 16.9 %collective-permute-start.27 = (bf16[48,4096]{1,0:T(8,128)(2,1)S(1)}, bf16[48,4096]{1,0:T(8,128)(2,1)S(1)}, u32[]{:S(2)}, u32[]{:S(2)}) collective-permute-start(bf16[48,4096]{1,0:T(8,128)(2,1)S(1)} %attend_slots.6), channel_id=1, source_target_pairs={{8,0},{16,8},{24,16},{28,24},{20,28},{12,20},{4,12},{0,4},{9,1},{1... | collective-permute-start | bytes 1179656 | tf_op jit(solution)/shard_map/ppermute | solution.py:642
  84.5 14.2 %collective-permute-start.10 = (bf16[48,4096]{1,0:T(8,128)(2,1)S(1)}, bf16[48,4096]{1,0:T(8,128)(2,1)S(1)}, u32[]{:S(2)}, u32[]{:S(2)}) collective-permute-start(bf16[48,4096]{1,0:T(8,128)(2,1)S(1)} %attend_slots.6), channel_id=1, source_target_pairs={{0,8},{8,16},{16,24},{24,28},{28,20},{20,12},{12,4},{4,0},{1,9},{9... | collective-permute-start | bytes 1179656 | tf_op jit(solution)/shard_map/ppermute | solution.py:642
  93.7 12.0 %collective-permute-start.30 = (bf16[48,4096]{1,0:T(8,128)(2,1)S(1)}, bf16[48,4096]{1,0:T(8,128)(2,1)S(1)}, u32[]{:S(2)}, u32[]{:S(2)}) collective-permute-start(bf16[48,4096]{1,0:T(8,128)(2,1)S(1)} %attend_slots.9), channel_id=1, source_target_pairs={{8,0},{16,8},{24,16},{28,24},{20,28},{12,20},{4,12},{0,4},{9,1},{1... | collective-permute-start | bytes 1179656 | tf_op jit(solution)/shard_map/ppermute | solution.py:642
  95.2 12.0 %collective-permute-start.23 = (bf16[48,4096]{1,0:T(8,128)(2,1)S(1)}, bf16[48,4096]{1,0:T(8,128)(2,1)S(1)}, u32[]{:S(2)}, u32[]{:S(2)}) collective-permute-start(bf16[48,4096]{1,0:T(8,128)(2,1)S(1)} %attend_slots.9), channel_id=1, source_target_pairs={{0,8},{8,16},{16,24},{24,28},{28,20},{20,12},{12,4},{4,0},{1,9},{9... | collective-permute-start | bytes 1179656 | tf_op jit(solution)/shard_map/ppermute | solution.py:642
  97.0 12.1 %collective-permute-start.37 = (bf16[96,896]{1,0:T(8,128)(2,1)S(1)}, bf16[96,896]{1,0:T(8,128)(2,1)S(1)}, u32[]{:S(2)}, u32[]{:S(2)}) collective-permute-start(bf16[96,896]{1,0:T(8,128)(2,1)S(1)} %convolution_convert_fusion.1.refs_0_), channel_id=1, source_target_pairs={{0,1},{1,0},{2,3},{3,2},{4,5},{5,4},{6,7},{7,6},{8,9},{9,8},{10,11... | collective-permute-start | bytes 516104 | tf_op jit(solution)/shard_map/ppermute | solution.py:642
  97.1 20.1 %collective-permute-start.28 = (bf16[48,4096]{1,0:T(8,128)(2,1)S(1)}, bf16[48,4096]{1,0:T(8,128)(2,1)S(1)}, u32[]{:S(2)}, u32[]{:S(2)}) collective-permute-start(bf16[48,4096]{1,0:T(8,128)(2,1)S(1)} %collective-permute-done.27), channel_id=1, source_target_pairs={{8,0},{16,8},{24,16},{28,24},{20,28},{12,20},{4,12},{0,4},{9,1},{1... | collective-permute-start | bytes 1179656 | tf_op jit(solution)/shard_map/ppermute | solution.py:642
  98.6 20.6 %collective-permute-start.11 = (bf16[48,4096]{1,0:T(8,128)(2,1)S(1)}, bf16[48,4096]{1,0:T(8,128)(2,1)S(1)}, u32[]{:S(2)}, u32[]{:S(2)}) collective-permute-start(bf16[48,4096]{1,0:T(8,128)(2,1)S(1)} %collective-permute-done.10), channel_id=1, source_target_pairs={{0,8},{8,16},{16,24},{24,28},{28,20},{20,12},{12,4},{4,0},{1,9},{9... | collective-permute-start | bytes 1179656 | tf_op jit(solution)/shard_map/ppermute | solution.py:642
  105.7 16.9 %collective-permute-start.31 = (bf16[48,4096]{1,0:T(8,128)(2,1)S(1)}, bf16[48,4096]{1,0:T(8,128)(2,1)S(1)}, u32[]{:S(2)}, u32[]{:S(2)}) collective-permute-start(bf16[48,4096]{1,0:T(8,128)(2,1)S(1)} %collective-permute-done.30), channel_id=1, source_target_pairs={{8,0},{16,8},{24,16},{28,24},{20,28},{12,20},{4,12},{0,4},{9,1},{1... | collective-permute-start | bytes 1179656 | tf_op jit(solution)/shard_map/ppermute | solution.py:642
  117.2 13.8 %collective-permute-start.29 = (bf16[48,4096]{1,0:T(8,128)(2,1)S(1)}, bf16[48,4096]{1,0:T(8,128)(2,1)S(1)}, u32[]{:S(2)}, u32[]{:S(2)}) collective-permute-start(bf16[48,4096]{1,0:T(8,128)(2,1)S(1)} %collective-permute-done.28), channel_id=1, source_target_pairs={{8,0},{16,8},{24,16},{28,24},{20,28},{12,20},{4,12},{0,4},{9,1},{1... | collective-permute-start | bytes 1179656 | tf_op jit(solution)/shard_map/ppermute | solution.py:642
  119.2 15.9 %collective-permute-start.12 = (bf16[48,4096]{1,0:T(8,128)(2,1)S(1)}, bf16[48,4096]{1,0:T(8,128)(2,1)S(1)}, u32[]{:S(2)}, u32[]{:S(2)}) collective-permute-start(bf16[48,4096]{1,0:T(8,128)(2,1)S(1)} %collective-permute-done.11), channel_id=1, source_target_pairs={{0,8},{8,16},{16,24},{24,28},{28,20},{20,12},{12,4},{4,0},{1,9},{9... | collective-permute-start | bytes 1179656 | tf_op jit(solution)/shard_map/ppermute | solution.py:642
  120.2 19.4 %collective-permute-start.39 = (bf16[96,896]{1,0:T(8,128)(2,1)S(1)}, bf16[96,896]{1,0:T(8,128)(2,1)S(1)}, u32[]{:S(2)}, u32[]{:S(2)}) collective-permute-start(bf16[96,896]{1,0:T(8,128)(2,1)S(1)} %get-tuple-element.27), channel_id=1, source_target_pairs={{2,0},{3,1},{6,4},{7,5},{10,8},{8,10},{14,12},{12,14},{19,17},{17,... | collective-permute-start | bytes 516104 | tf_op jit(solution)/shard_map/ppermute | solution.py:642
  122.6 17.0 %collective-permute-start.33 = (bf16[48,2048]{1,0:T(8,128)(2,1)S(1)}, bf16[48,2048]{1,0:T(8,128)(2,1)S(1)}, u32[]{:S(2)}, u32[]{:S(2)}) collective-permute-start(bf16[48,2048]{1,0:T(8,128)(2,1)S(1)} %get-tuple-element.40), channel_id=1, source_target_pairs={{8,0},{16,8},{24,16},{28,24},{20,28},{12,20},{4,12},{0,4},{9,1},{1... | collective-permute-start | bytes 589832 | tf_op jit(solution)/shard_map/ppermute | solution.py:642
  128.2 11.7 %collective-permute-start.32 = (bf16[48,2048]{1,0:T(8,128)(2,1)S(1)}, bf16[48,2048]{1,0:T(8,128)(2,1)S(1)}, u32[]{:S(2)}, u32[]{:S(2)}) collective-permute-start(bf16[48,2048]{1,0:T(8,128)(2,1)S(1)} %get-tuple-element.39), channel_id=1, source_target_pairs={{8,0},{16,8},{24,16},{28,24},{20,28},{12,20},{4,12},{0,4},{9,1},{1... | collective-permute-start | bytes 589832 | tf_op jit(solution)/shard_map/ppermute | solution.py:642
  (45 other events, 339.5 us)
